TPU v7x, 32 devices: a whole 2x2x4 slice. The times are simulated.
32 devices in a mesh: wide: 8 (over z, y), narrow: 4 (over x, core).
Axes of the slice: x: 2, y: 2, z: 4, core: 2. Of those that a mesh axis runs over, the one named last changes fastest.
Arguments:
- material_flow_vector: float32 [3, 256, 256, 512], P(None, 'wide', 'narrow'), may hold values from -6 to 6
- tool_push_density: float32 [3, 256, 256, 512], P(None, 'wide', 'narrow'), may hold values from -6 to 6
- tool_warmth_excess: float32 [256, 256, 512], P('wide', 'narrow'), may hold values from 0.7 to 1.3
- substrate_warmth_excess: float32 [128, 128, 128], P('wide', 'narrow'), may hold values from -6 to 6
- spread_coefficient: float32 [128, 128, 128], P('wide', 'narrow'), may hold values from 0.02 to 0.08
- source_owner_sheet: int32 [262144, 1], P(('wide', 'narrow')), may hold values from 0 to 7; in each aligned block of 8192 rows (0 to 8191, 8192 to 16383, ...) at most 3072 rows name the same one
- source_part_line: int32 [262144], P(('wide', 'narrow')), may hold values from 0 to 511
Outputs:
- corrected_flow_vector: float32 [3, 256, 256, 512], P(None, 'wide', 'narrow')
- part_out: float32 [128, 128, 128], P('wide', 'narrow')
Inputs may be any that keep to these rules, and one draw needn't show every extreme that they name: `source_owner_sheet`: among the 8192 blocks of one device, no slab is named by more than 3072 of them.
All inputs are finite; a program needn't handle non-finite values.
Results may differ from a plain program's by a relative error of at most 0.00012.
Values sent between devices are 32-bit elements; how exact they have to be, the bound alone decides.
No kernel may reach another device: no remote copies, remote signals or barrier semaphores. Data moves between devices by JAX's collectives and lax.ppermute only.
A program may use at most 256 MiB of HBM per device.

v0:
```python
import math

import jax
import jax.numpy as jnp
from jax import lax
from jax.sharding import PartitionSpec as P

PASSES = 2
STEPS = 3


time_step = 0.15
rate_base = 0.5
zener_energy = 4.0
stress_exponent = 5.0
penalty = 0.001
dissipation_factor = 0.1
highest = lax.Precision.HIGHEST
half_lane = 64


def with_halo(x, sides, width, wrap):
    for axis, dim in sides:
        size, length = (lax.axis_size(axis), x.shape[dim])
        up = [(i, (i + 1) % size) for i in range(size if wrap else size - 1)]
        down = [(j, i) for i, j in up]
        last = lax.slice_in_dim(x, length - width, length, axis=dim)
        initial = lax.slice_in_dim(x, 0, width, axis=dim)
        before = lax.ppermute(last, axis, up)
        after = lax.ppermute(initial, axis, down)
        x = jnp.concatenate([before, x, after], axis=dim)
    return x


def pad_cells(field):
    return with_halo(field, (("wide", 1), ("narrow", 2)), 1, True)


def narrow_turn(spectrum):
    return lax.all_to_all(spectrum, "narrow", split_axis=2, concat_axis=1, tiled=True)


def wide_turn(spectrum):
    return lax.all_to_all(spectrum, "wide", split_axis=1, concat_axis=0, tiled=True)


def gradients(bordered_array):
    center = bordered_array[:, 1:-1, 1:-1]
    along_x = (bordered_array[:, 2:, 1:-1] - bordered_array[:, :-2, 1:-1]) * 0.5
    along_y = (bordered_array[:, 1:-1, 2:] - bordered_array[:, 1:-1, :-2]) * 0.5
    along_z = (jnp.roll(center, -1, 3) - jnp.roll(center, 1, 3)) * 0.5
    return (along_x, along_y, along_z)


def rate_squared(bordered_array):
    along_x, along_y, along_z = gradients(bordered_array)
    s_xy = 0.5 * (along_y[0] + along_x[1])
    s_xz = 0.5 * (along_z[0] + along_x[2])
    s_yz = 0.5 * (along_z[1] + along_y[2])
    total = (
        along_x[0] ** 2 + along_y[1] ** 2 + along_z[2] ** 2 + 2.0 * (s_xy**2 + s_xz**2 + s_yz**2)
    )
    return rate_base**2 + 2.0 * total


def inverse_sinh(value):
    return jnp.log(value + jnp.sqrt(value * value + 1.0))


def viscosity(rate_sq, zener):
    rate = jnp.sqrt(rate_sq)
    return inverse_sinh((rate * zener) ** (1.0 / stress_exponent)) / (3.0 * rate)


def viscous_term(mu_padded, vel_padded):
    mu_center = mu_padded[1:-1, 1:-1]
    vel_center = vel_padded[:, 1:-1, 1:-1]
    total = 0.5 * (mu_center + mu_padded[2:, 1:-1]) * (
        vel_padded[:, 2:, 1:-1] - vel_center
    ) - 0.5 * (mu_center + mu_padded[:-2, 1:-1]) * (vel_center - vel_padded[:, :-2, 1:-1])
    total = (
        total
        + 0.5 * (mu_center + mu_padded[1:-1, 2:]) * (vel_padded[:, 1:-1, 2:] - vel_center)
        - 0.5 * (mu_center + mu_padded[1:-1, :-2]) * (vel_center - vel_padded[:, 1:-1, :-2])
    )
    total = (
        total
        + 0.5
        * (mu_center + jnp.roll(mu_center, -1, 2))
        * (jnp.roll(vel_center, -1, 3) - vel_center)
        - 0.5 * (mu_center + jnp.roll(mu_center, 1, 2)) * (vel_center - jnp.roll(vel_center, 1, 3))
    )
    return total


def dft_tables(length):
    numbers = jnp.arange(length, dtype=jnp.int32)
    product = numbers[:, None] * numbers[None, :] % length
    angle = product.astype(jnp.float32) * (2.0 * math.pi / length)
    return (jnp.cos(angle), jnp.sin(angle))


def table_product(form, left, table):
    return jnp.einsum(form, left, table, precision=highest)


def forward_section(form, real_part, imag_part, cosine, sine):
    new_real = table_product(form, real_part, cosine) + table_product(form, imag_part, sine)
    new_imag = table_product(form, imag_part, cosine) - table_product(form, real_part, sine)
    return (new_real, new_imag)


def inverse_section(form, real_part, imag_part, cosine, sine):
    new_real = table_product(form, real_part, cosine) - table_product(form, imag_part, sine)
    new_imag = table_product(form, real_part, sine) + table_product(form, imag_part, cosine)
    return (new_real, new_imag)


def sine_squared(waves, count):
    return jnp.sin(waves.astype(jnp.float32) * (2.0 * math.pi / count)) ** 2


def joined(real_part, imag_part):
    return jnp.concatenate([real_part, imag_part], 3)


def project(divergence):
    x_local, y_local, z_cells = divergence.shape
    z_outer = z_cells // half_lane
    cos_z, sin_z = dft_tables(z_cells)
    real_part = table_product("xyz,zk->xyk", divergence, cos_z).reshape(
        x_local, y_local, z_outer, half_lane
    )
    imag_part = -table_product("xyz,zk->xyk", divergence, sin_z).reshape(
        x_local, y_local, z_outer, half_lane
    )
    spectrum = narrow_turn(joined(real_part, imag_part))
    y_cells = spectrum.shape[1]
    z_piece = spectrum.shape[2]
    cos_y, sin_y = dft_tables(y_cells)
    real_part, imag_part = forward_section(
        "xyoi,yq->xqoi", spectrum[..., :half_lane], spectrum[..., half_lane:], cos_y, sin_y
    )
    spectrum = wide_turn(joined(real_part, imag_part))
    x_cells = spectrum.shape[0]
    y_piece = spectrum.shape[1]
    cos_x, sin_x = dft_tables(x_cells)
    real_part, imag_part = forward_section(
        "xqoi,xr->rqoi", spectrum[..., :half_lane], spectrum[..., half_lane:], cos_x, sin_x
    )
    wave_x = jnp.arange(x_cells, dtype=jnp.int32)
    wave_y = lax.axis_index("wide") * y_piece + jnp.arange(y_piece, dtype=jnp.int32)
    outer_z = lax.axis_index("narrow") * z_piece + jnp.arange(z_piece, dtype=jnp.int32)
    wave_z = outer_z[:, None] * half_lane + jnp.arange(half_lane, dtype=jnp.int32)[None, :]
    symbol = (
        sine_squared(wave_x, x_cells)[:, None, None, None]
        + sine_squared(wave_y, y_cells)[None, :, None, None]
        + sine_squared(wave_z, z_cells)[None, None, :, :]
    )
    factor = -1.0 / ((symbol + penalty) * float(x_cells * y_cells * z_cells))
    real_part, imag_part = inverse_section(
        "rqoi,rx->qxoi", real_part * factor, imag_part * factor, cos_x, sin_x
    )
    spectrum = wide_turn(joined(real_part, imag_part))
    real_part, imag_part = inverse_section(
        "yxoi,yq->xoqi", spectrum[..., :half_lane], spectrum[..., half_lane:], cos_y, sin_y
    )
    spectrum = narrow_turn(joined(real_part, imag_part))
    cos_blocks = cos_z.reshape(z_outer, half_lane, z_cells)
    sin_blocks = sin_z.reshape(z_outer, half_lane, z_cells)
    return table_product("xoyi,oiz->xyz", spectrum[..., :half_lane], cos_blocks) - table_product(
        "xoyi,oiz->xyz", spectrum[..., half_lane:], sin_blocks
    )


def substrate_advance(thermal_profile, spread_coefficient):
    bordered_array = with_halo(thermal_profile, (("wide", 0), ("narrow", 1)), 1, False)
    center = bordered_array[1:-1, 1:-1]
    neighbour_voxels = (
        bordered_array[2:, 1:-1]
        + bordered_array[:-2, 1:-1]
        + bordered_array[1:-1, 2:]
        + bordered_array[1:-1, :-2]
    )
    ahead = jnp.pad(center[:, :, 1:], ((0, 0), (0, 0), (0, 1)))
    behind = jnp.pad(center[:, :, :-1], ((0, 0), (0, 0), (1, 0)))
    return center + spread_coefficient * (neighbour_voxels + ahead + behind - 6.0 * center)


def per_device(
    material_flow_vector,
    tool_push_density,
    tool_warmth_excess,
    substrate_warmth_excess,
    spread_coefficient,
    source_owner_sheet,
    source_part_line,
):
    zener = jnp.exp(zener_energy * (1.0 / tool_warmth_excess - 1.0))
    base_pad = pad_cells(material_flow_vector)
    current_pad = base_pad
    current = material_flow_vector
    for section in range(PASSES):
        rate_sq = rate_squared(current_pad)
        mu_field = viscosity(rate_sq, zener)
        mu_padded = pad_cells(mu_field[None])[0]
        current = material_flow_vector + time_step * (
            viscous_term(mu_padded, base_pad) + tool_push_density
        )
        if section + 1 < PASSES:
            current_pad = pad_cells(current)
    heat_cells = mu_field * (rate_sq - rate_base**2)
    along_x, along_y, along_z = gradients(pad_cells(current))
    divergence = along_x[0] + along_y[1] + along_z[2]
    pressure = project(divergence)
    press_x, press_y, press_z = gradients(pad_cells(pressure[None]))
    corrected_flow_vector = current - jnp.concatenate([press_x, press_y, press_z], 0)
    blocks = heat_cells.reshape(-1, 128)
    slab_ids = source_owner_sheet[:, 0]
    slab_count = lax.axis_size("wide")
    component_lines = substrate_warmth_excess.shape[0] * substrate_warmth_excess.shape[1]
    partial_value = (
        jnp.zeros((slab_count * component_lines, 128), jnp.float32)
        .at[slab_ids * component_lines + source_part_line]
        .add(blocks)
    )
    substrate_energy_input = lax.psum_scatter(
        partial_value.reshape(slab_count, component_lines, 128),
        "wide",
        scatter_dimension=0,
        tiled=True,
    )
    thermal_profile = substrate_warmth_excess + dissipation_factor * substrate_energy_input.reshape(
        substrate_warmth_excess.shape
    )
    for section in range(STEPS):
        thermal_profile = substrate_advance(thermal_profile, spread_coefficient)
    return (corrected_flow_vector, thermal_profile)


def solution(mesh):
    return jax.shard_map(
        per_device,
        mesh=mesh,
        in_specs=(
            P(None, "wide", "narrow", None),
            P(None, "wide", "narrow", None),
            P("wide", "narrow", None),
            P("wide", "narrow", None),
            P("wide", "narrow", None),
            P(("wide", "narrow"), None),
            P(("wide", "narrow")),
        ),
        out_specs=(P(None, "wide", "narrow", None), P("wide", "narrow", None)),
        check_vma=False,
    )
```

profile of v0, /device:TPU:1, one launch (start us, length us, event | category | flops | bytes accessed | tf_op | source)
XLA Modules:
  0.0 1415.4 jit_solution(18206457857166424000)
XLA Ops:
  13.7 21.5 %fusion.244 = (f32[3,32,64,511]{3,2,1,0:T(8,128)}, f32[3,32,64,511]{3,2,1,0:T(8,128)}) fusion(f32[3,32,64,512]{3,2,1,0:T(8,128)} %param.7), kind=kLoop, calls=%fused_computation.376 | loop fusion | bytes 50233344 | tf_op jit(solution)/shard_map/jit(_roll_static)/slice | solution.py:51
  55.9 18.0 %subtract_multiply_fusion = f32[3,32,64,512]{3,2,1,0:T(8,128)} fusion(f32[3,32,64,511]{3,2,1,0:T(8,128)} %get-tuple-element.27, f32[3,32,64,1]{3,2,1,0:T(8,128)} %get-tuple-element.29, f32[3,32,64,1]{3,2,1,0:T(8,128)} %get-tuple-element.28, f32[3,32,64,511]{3,2,1,0:T(8,128)} %get-tuple-element.26), kind=kLoop, calls=%fused_computation.28 | loop fusion | flops 12582912 | bytes 37748736 | tf_op jit(solution)/shard_map/mul | solution.py:51
  80.7 16.1 %divide_bitcast_fusion = f32[1,32,64,512]{3,2,1,0:T(8,128)S(1)} fusion(f32[3,32,64,512]{3,2,1,0:T(8,128)} %subtract_multiply_fusion.1, f32[3,32,64,512]{3,2,1,0:T(8,128)} %subtract_multiply_fusion, f32[3,32,64,512]{3,2,1,0:T(8,128)} %get-tuple-element.24, f32[32,64,512]{2,1,0:T(8,128)S(1)} %copy-done.12), kind=kLoop, calls=%fused_computation.155 | loop fusion | flops 30408704 | bytes 46137344 | tf_op jit(solution)/shard_map/broadcast_in_dim | solution.py:206
  118.3 21.9 %fusion.51 = (f32[32,64,512]{2,1,0:T(8,128)}, f32[32,64,512]{2,1,0:T(8,128)}, f32[32,64,512]{2,1,0:T(8,128)}, f32[32,64,512]{2,1,0:T(8,128)}, f32[32,64,512]{2,1,0:T(8,128)}, /*index=5*/f32[32,64,512]{2,1,0:T(8,128)}) fusion(f32[34,66,512]{2,1,0:T(8,128)} %copy-done.1, f32[32,64,511]{2,1,0:T(8,128)} %get-tuple-element.55, ...), kind=kLoop, calls=%fused_computation.110 | loop fusion | flops 14680064 | bytes 54525952 | tf_op jit(solution)/shard_map/mul | solution.py:78
  140.2 42.5 %multiply_add_fusion.1 = f32[3,32,64,512]{3,2,1,0:T(8,128)S(1)} fusion(f32[3,32,64,512]{3,2,1,0:T(8,128)} %param.7, f32[3,32,64,512]{3,2,1,0:T(8,128)} %param.8, f32[3,34,1,512]{3,2,1,0:T(1,128)S(1)} %collective-permute-done.2, f32[3,34,64,512]{3,2,1,0:T(8,128)} %constant_dynamic-update-slice_fusion, f32[3,34,1,512]{3,2,1,0:T(1,128)S(1)} %collective-permute-done.3, ...), kind=kLoop, calls=%fused_computation.27 | loop fusion | flops 81788928 | bytes 102653952 | tf_op jit(solution)/shard_map/add | solution.py:207
  198.3 13.4 collective-permute-done.8
  213.8 15.6 %fusion.8 = f32[3,32,64,512]{3,2,1,0:T(8,128)} fusion(f32[3,32,64,1]{3,2,1,0:T(8,128)S(1)} %get-tuple-element.19, f32[3,32,64,511]{3,2,1,0:T(8,128)} %get-tuple-element.21, f32[3,32,64,511]{3,2,1,0:T(8,128)} %get-tuple-element.20, f32[3,32,64,1]{3,2,1,0:T(8,128)S(1)} %get-tuple-element.18), kind=kLoop, calls=%fused_computation.24 | loop fusion | flops 12582912 | bytes 37748736 | tf_op jit(solution)/shard_map/mul | solution.py:51
  229.5 13.8 fusion.3
  243.3 17.4 %fusion.234 = (f32[32,64,512]{2,1,0:T(8,128)}, f32[32,64,512]{2,1,0:T(8,128)S(1)}) fusion(f32[32,64,512]{2,1,0:T(8,128)} %param.9, f32[3,32,64,512]{3,2,1,0:T(8,128)} %get-tuple-element.7, f32[3,32,64,512]{3,2,1,0:T(8,128)} %fusion.8, f32[3,32,64,512]{3,2,1,0:T(8,128)} %get-tuple-element.6), kind=kLoop, calls=%fused_computation.367 | loop fusion | flops 31457280 | bytes 50331648 | tf_op jit(solution)/shard_map/mul | solution.py:212
  293.9 21.9 %fusion.33 = (f32[32,64,512]{2,1,0:T(8,128)}, f32[32,64,512]{2,1,0:T(8,128)}, f32[32,64,512]{2,1,0:T(8,128)}, f32[32,64,512]{2,1,0:T(8,128)}, f32[32,64,512]{2,1,0:T(8,128)}, /*index=5*/f32[32,64,512]{2,1,0:T(8,128)}) fusion(f32[34,66,512]{2,1,0:T(8,128)} %copy-done.2, f32[32,64,511]{2,1,0:T(8,128)} %get-tuple-element.45, ...), kind=kLoop, calls=%fused_computation.82 | loop fusion | flops 14680064 | bytes 54525952 | tf_op jit(solution)/shard_map/mul | solution.py:78
  315.9 42.6 %multiply_add_fusion = f32[3,32,64,512]{3,2,1,0:T(8,128)S(1)} fusion(f32[3,32,64,512]{3,2,1,0:T(8,128)} %param.7, f32[3,32,64,512]{3,2,1,0:T(8,128)} %param.8, f32[3,34,1,512]{3,2,1,0:T(1,128)S(1)} %collective-permute-done.2, f32[3,34,64,512]{3,2,1,0:T(8,128)} %constant_dynamic-update-slice_fusion, f32[3,34,1,512]{3,2,1,0:T(1,128)S(1)} %collective-permute-done.3, ...), kind=kLoop, calls=%fused_computation.26 | loop fusion | flops 81788928 | bytes 102653952 | tf_op jit(solution)/shard_map/add | solution.py:207
  392.3 15.8 %convolution_negate_fusion = f32[32,64,8,64]{3,1,2,0:T(8,128)} fusion(f32[32,64,512,1]{2,1,3,0:T(8,128)S(1)} %fusion.24, f32[8,64,512,1]{2,1,0,3:T(8,128)S(1)} %bitcast.180), kind=kOutput, calls=%fused_computation.157 | convolution fusion | flops 6443499520 | bytes 9437184 | tf_op jit(solution)/shard_map/xyz,zk->xyk/dot_general | solution.py:104
  408.1 15.8 %fusion.265 = f32[32,64,8,64]{3,1,2,0:T(8,128)} fusion(f32[32,64,512,1]{2,1,3,0:T(8,128)S(1)} %fusion.24, f32[8,64,512,1]{2,1,0,3:T(8,128)S(1)} %bitcast.179), kind=kOutput, calls=%fused_computation.397 | convolution fusion | flops 6442450944 | bytes 9437184 | tf_op jit(solution)/shard_map/xyz,zk->xyk/dot_general | solution.py:104
  424.0 12.0 pad_maximum_fusion.14
  440.2 96.3 %all_to_all.72 = f32[32,64,8,128]{3,1,0,2:T(8,128)S(1)} all-to-all(f32[32,64,8,128]{3,1,0,2:T(8,128)S(1)} %copy.42), channel_id=1, replica_groups=mesh['wide'=8,'narrow'=4] {'narrow'}, dimensions={2} | all-to-all | bytes 16777216 | tf_op jit(solution)/shard_map/all_to_all | solution.py:40
  609.1 13.2 copy.47
  628.3 181.6 %all-to-all-done.1 = f32[32,256,2,128]{3,2,0,1:T(2,128)} async-done(((f32[32,256,2,128]{3,2,0,1:T(2,128)}), f32[32,256,2,128]{3,2,0,1:T(2,128)}, u32[]{:S(2)}, u32[]{:S(2)}) %all-to-all-start.1) | async-done | bytes 8388640 | tf_op jit(solution)/shard_map/all_to_all | solution.py:44
  912.6 13.2 copy.52
  935.8 45.7 %scatter_custom_fusion = f32[4096,128]{1,0:T(8,128)} fusion(s32[8192]{0:T(1024)S(1)} %compare_select_fusion, f32[8192,128]{1,0:T(8,128)} %reshape.294, f32[]{:T(128)} %constant.95.clone.1), kind=kCustom, calls=%fused_computation.172 | custom fusion | flops 1048576 | bytes 2097664 | tf_op jit(solution)/shard_map/scatter-add | solution.py:225
  981.5 147.6 %all-to-all-done.2 = f32[32,256,2,128]{3,2,0,1:T(2,128)} async-done(((f32[32,256,2,128]{3,2,0,1:T(2,128)}), f32[32,256,2,128]{3,2,0,1:T(2,128)}, u32[]{:S(2)}, u32[]{:S(2)}) %all-to-all-start.2) | async-done | bytes 8388640 | tf_op jit(solution)/shard_map/all_to_all | solution.py:44
  1197.1 13.2 copy.57
  1232.9 78.8 %collective-permute-done.26 = f32[18,1,128]{2,1,0:T(1,128)S(1)} collective-permute-done((f32[18,1,128]{2,1,0:T(1,128)S(1)}, f32[18,1,128]{2,1,0:T(1,128)S(1)}, u32[]{:S(2)}, u32[]{:S(2)}) %collective-permute-start.26) | collective-permute-done | bytes 9248 | tf_op jit(solution)/shard_map/ppermute | solution.py:30
  1349.5 14.4 %fusion.13 = f32[32,64,512,1]{2,1,3,0:T(8,128)S(1)} fusion(f32[32,8,64,128]{3,2,1,0:T(8,128)S(1)} %bitcast.156, s32[8,64]{1,0:T(8,128)S(1)} %copy-done.22), kind=kOutput, calls=%fused_computation.34 | convolution fusion | flops 6446120960 | bytes 12584960 | tf_op jit(solution)/shard_map/xoyi,oiz->xyz/dot_general | solution.py:104
  1363.9 11.4 fusion.73
  (251 shorter events, 496.4 us)
Async XLA Ops:
  8.5 30.8 %collective-permute-start.1 = (f32[3,1,64,512]{3,2,1,0:T(8,128)S(1)}, f32[3,1,64,512]{3,2,1,0:T(8,128)S(1)}, u32[]{:S(2)}, u32[]{:S(2)}) collective-permute-start(f32[3,1,64,512]{3,2,1,0:T(8,128)S(1)} %get-tuple-element.31), channel_id=1, source_target_pairs={{0,4},{4,8},{8,12},{12,16},{16,20},{20,24},{24,28},{28,0},{1,5},{5... | collective-permute-start | bytes 1179656 | tf_op jit(solution)/shard_map/ppermute | solution.py:29
  10.6 29.5 %collective-permute-start = (f32[3,1,64,512]{3,2,1,0:T(8,128)S(1)}, f32[3,1,64,512]{3,2,1,0:T(8,128)S(1)}, u32[]{:S(2)}, u32[]{:S(2)}) collective-permute-start(f32[3,1,64,512]{3,2,1,0:T(8,128)S(1)} %get-tuple-element.30), channel_id=1, source_target_pairs={{4,0},{8,4},{12,8},{16,12},{20,16},{24,20},{28,24},{0,28},{5,1},{9... | collective-permute-start | bytes 1179656 | tf_op jit(solution)/shard_map/ppermute | solution.py:30
  53.3 20.6 %collective-permute-start.2 = (f32[3,34,1,512]{3,2,1,0:T(1,128)S(1)}, f32[3,34,1,512]{3,2,1,0:T(1,128)S(1)}, u32[]{:S(2)}, u32[]{:S(2)}) collective-permute-start(f32[3,34,1,512]{3,2,1,0:T(1,128)S(1)} %get-tuple-element.11), channel_id=1, source_target_pairs={{1,0},{2,1},{3,2},{0,3},{5,4},{6,5},{7,6},{4,7},{9,8},{10,9},{11,1... | collective-permute-start | bytes 626696 | tf_op jit(solution)/shard_map/ppermute | solution.py:30
  54.4 19.6 %collective-permute-start.3 = (f32[3,34,1,512]{3,2,1,0:T(1,128)S(1)}, f32[3,34,1,512]{3,2,1,0:T(1,128)S(1)}, u32[]{:S(2)}, u32[]{:S(2)}) collective-permute-start(f32[3,34,1,512]{3,2,1,0:T(1,128)S(1)} %get-tuple-element.10), channel_id=1, source_target_pairs={{0,1},{1,2},{2,3},{3,0},{4,5},{5,6},{6,7},{7,4},{8,9},{9,10},{10,1... | collective-permute-start | bytes 626696 | tf_op jit(solution)/shard_map/ppermute | solution.py:29
  96.8 8.1 collective-permute-start.4
  96.9 8.0 collective-permute-start.5
  192.8 18.8 %collective-permute-start.8 = (f32[3,1,64,512]{3,2,1,0:T(8,128)S(1)}, f32[3,1,64,512]{3,2,1,0:T(8,128)S(1)}, u32[]{:S(2)}, u32[]{:S(2)}) collective-permute-start(f32[3,1,64,512]{3,2,1,0:T(8,128)S(1)} %get-tuple-element.23), channel_id=1, source_target_pairs={{4,0},{8,4},{12,8},{16,12},{20,16},{24,20},{28,24},{0,28},{5,1},{9... | collective-permute-start | bytes 1179656 | tf_op jit(solution)/shard_map/ppermute | solution.py:30
  196.9 14.8 %collective-permute-start.9 = (f32[3,1,64,512]{3,2,1,0:T(8,128)S(1)}, f32[3,1,64,512]{3,2,1,0:T(8,128)S(1)}, u32[]{:S(2)}, u32[]{:S(2)}) collective-permute-start(f32[3,1,64,512]{3,2,1,0:T(8,128)S(1)} %get-tuple-element.22), channel_id=1, source_target_pairs={{0,4},{4,8},{8,12},{12,16},{16,20},{20,24},{24,28},{28,0},{1,5},{5... | collective-permute-start | bytes 1179656 | tf_op jit(solution)/shard_map/ppermute | solution.py:29
  212.1 17.4 %collective-permute-start.10 = (f32[3,34,1,512]{3,2,1,0:T(1,128)S(1)}, f32[3,34,1,512]{3,2,1,0:T(1,128)S(1)}, u32[]{:S(2)}, u32[]{:S(2)}) collective-permute-start(f32[3,34,1,512]{3,2,1,0:T(1,128)S(1)} %get-tuple-element.8), channel_id=1, source_target_pairs={{1,0},{2,1},{3,2},{0,3},{5,4},{6,5},{7,6},{4,7},{9,8},{10,9},{11,1... | collective-permute-start | bytes 626696 | tf_op jit(solution)/shard_map/ppermute | solution.py:30
  212.3 17.2 %collective-permute-start.11 = (f32[3,34,1,512]{3,2,1,0:T(1,128)S(1)}, f32[3,34,1,512]{3,2,1,0:T(1,128)S(1)}, u32[]{:S(2)}, u32[]{:S(2)}) collective-permute-start(f32[3,34,1,512]{3,2,1,0:T(1,128)S(1)} %get-tuple-element.9), channel_id=1, source_target_pairs={{0,1},{1,2},{2,3},{3,0},{4,5},{5,6},{6,7},{7,4},{8,9},{9,10},{10,1... | collective-permute-start | bytes 626696 | tf_op jit(solution)/shard_map/ppermute | solution.py:29
  268.7 8.3 collective-permute-start.12
  269.3 8.0 collective-permute-start.13
  278.7 7.5 collective-permute-start.14
  358.6 18.1 %collective-permute-start.16 = (f32[3,1,64,512]{3,2,1,0:T(8,128)S(1)}, f32[3,1,64,512]{3,2,1,0:T(8,128)S(1)}, u32[]{:S(2)}, u32[]{:S(2)}) collective-permute-start(f32[3,1,64,512]{3,2,1,0:T(8,128)S(1)} %get-tuple-element.13), channel_id=1, source_target_pairs={{4,0},{8,4},{12,8},{16,12},{20,16},{24,20},{28,24},{0,28},{5,1},{9... | collective-permute-start | bytes 1179656 | tf_op jit(solution)/shard_map/ppermute | solution.py:30
  362.3 14.4 %collective-permute-start.17 = (f32[3,1,64,512]{3,2,1,0:T(8,128)S(1)}, f32[3,1,64,512]{3,2,1,0:T(8,128)S(1)}, u32[]{:S(2)}, u32[]{:S(2)}) collective-permute-start(f32[3,1,64,512]{3,2,1,0:T(8,128)S(1)} %get-tuple-element.12), channel_id=1, source_target_pairs={{0,4},{4,8},{8,12},{12,16},{16,20},{20,24},{24,28},{28,0},{1,5},{5... | collective-permute-start | bytes 1179656 | tf_op jit(solution)/shard_map/ppermute | solution.py:29
  377.1 7.6 collective-permute-start.18
  622.3 187.6 %all-to-all-start.1 = ((f32[32,256,2,128]{3,2,0,1:T(2,128)}), f32[32,256,2,128]{3,2,0,1:T(2,128)}, u32[]{:S(2)}, u32[]{:S(2)}) async-start(f32[32,256,2,128]{3,2,0,1:T(2,128)} %copy.47), calls=%async_computation.1 | async-start | bytes 16777216 | tf_op jit(solution)/shard_map/all_to_all | solution.py:44
  925.8 203.3 %all-to-all-start.2 = ((f32[32,256,2,128]{3,2,0,1:T(2,128)}), f32[32,256,2,128]{3,2,0,1:T(2,128)}, u32[]{:S(2)}, u32[]{:S(2)}) async-start(f32[32,256,2,128]{3,2,0,1:T(2,128)} %copy.52), calls=%async_computation.2 | async-start | bytes 16777216 | tf_op jit(solution)/shard_map/all_to_all | solution.py:44
  930.9 288.0 %reduce-scatter.2.cloned.1.call-start = ((), (), s32[]{:S(2)}) async-start(), calls=%async_computation.5 | async-start | bytes 2359296 | tf_op jit(solution)/shard_map/reduce_scatter | solution.py:227
  1210.3 129.8 %all-to-all-start.3 = ((f32[32,2,256,128]{3,1,0,2:T(2,128)}), f32[32,2,256,128]{3,1,0,2:T(2,128)}, u32[]{:S(2)}, u32[]{:S(2)}) async-start(f32[32,2,256,128]{3,1,0,2:T(2,128)} %copy.57), calls=%async_computation.3 | async-start | bytes 16777216 | tf_op jit(solution)/shard_map/all_to_all | solution.py:40
  1226.1 85.6 %collective-permute-start.26 = (f32[18,1,128]{2,1,0:T(1,128)S(1)}, f32[18,1,128]{2,1,0:T(1,128)S(1)}, u32[]{:S(2)}, u32[]{:S(2)}) collective-permute-start(f32[18,1,128]{2,1,0:T(1,128)S(1)} %get-tuple-element.80), channel_id=1, source_target_pairs={{1,0},{2,1},{3,2},{5,4},{6,5},{7,6},{9,8},{10,9},{11,10},{13,12},{... | collective-permute-start | bytes 27656 | tf_op jit(solution)/shard_map/ppermute | solution.py:30
  1229.3 82.5 %collective-permute-start.27 = (f32[18,1,128]{2,1,0:T(1,128)S(1)}, f32[18,1,128]{2,1,0:T(1,128)S(1)}, u32[]{:S(2)}, u32[]{:S(2)}) collective-permute-start(f32[18,1,128]{2,1,0:T(1,128)S(1)} %get-tuple-element.81), channel_id=1, source_target_pairs={{0,1},{1,2},{2,3},{4,5},{5,6},{6,7},{8,9},{9,10},{10,11},{12,13},{... | collective-permute-start | bytes 27656 | tf_op jit(solution)/shard_map/ppermute | solution.py:29
  1377.0 9.3 collective-permute-start.20
  1391.1 7.4 collective-permute-start.22
  (51 other events, 555.9 us)
Sparse Core Ops, SparseCore 0:
  981.7 160.6 reduce-scatter.1
where the time goes:
time: 1420 us
  waiting for transfers between devices  447 us (31%)
  other arithmetic  364 us (26%)
  local copies, waits for them, and re-layouts  223 us (16%)
  matrix products  171 us (12%)
  starting transfers between devices  99.7 us (7%)
  blocking collectives  96.3 us (7%)
  between operations  15.2 us (1%)
    all_to_all x2, waiting for transfers between devices, wide_turn(): lax.all_to_all(spectrum, 'wide', split_axis=1, concat_axis=0, tiled=True)  329 us
    unnamed x16, matrix products  113 us
    ppermute x18, waiting for transfers between devices, with_halo(): after = lax.ppermute(initial, axis, down)  102 us
    all_to_all x1, blocking collectives, narrow_turn(): lax.all_to_all(spectrum, 'narrow', split_axis=2, concat_axis=1, tiled=True)  96.3 us
    add x2, other arithmetic, per_device(): material_flow_vector + time_step * (viscous_term(mu_padded, base_pad) + t...  85.1 us
    dot_general x4, matrix products, table_product(): return jnp.einsum(form, left, table, precision=highest)  57.4 us
    slice x8, local copies, waits for them, and re-layouts, gradients(): along_z = (jnp.roll(center, -1, 3) - jnp.roll(center, 1, 3)) * 0.5  53.1 us
    unnamed x77, local copies, waits for them, and re-layouts  49.7 us
  transfers between devices with their start and end apart: 40, of which 18 were waited for; matrix products, arithmetic and copies ran while one was open for 15% of the time, Pallas kernels for 0%

commit v1 on v0

--- a/solution.py
+++ b/solution.py
@@ -2,7 +2,10 @@
 
 import jax
 import jax.numpy as jnp
+import numpy as np
 from jax import lax
+from jax.experimental import pallas as pl
+from jax.experimental.pallas import tpu as pltpu
 from jax.sharding import PartitionSpec as P
 
 PASSES = 2
@@ -15,8 +18,6 @@
 stress_exponent = 5.0
 penalty = 0.001
 dissipation_factor = 0.1
-highest = lax.Precision.HIGHEST
-half_lane = 64
 
 
 def with_halo(x, sides, width, wrap):
@@ -36,14 +37,6 @@
     return with_halo(field, (("wide", 1), ("narrow", 2)), 1, True)
 
 
-def narrow_turn(spectrum):
-    return lax.all_to_all(spectrum, "narrow", split_axis=2, concat_axis=1, tiled=True)
-
-
-def wide_turn(spectrum):
-    return lax.all_to_all(spectrum, "wide", split_axis=1, concat_axis=0, tiled=True)
-
-
 def gradients(bordered_array):
     center = bordered_array[:, 1:-1, 1:-1]
     along_x = (bordered_array[:, 2:, 1:-1] - bordered_array[:, :-2, 1:-1]) * 0.5
@@ -93,84 +86,299 @@
     return total
 
 
-def dft_tables(length):
-    numbers = jnp.arange(length, dtype=jnp.int32)
-    product = numbers[:, None] * numbers[None, :] % length
-    angle = product.astype(jnp.float32) * (2.0 * math.pi / length)
-    return (jnp.cos(angle), jnp.sin(angle))
-
-
-def table_product(form, left, table):
-    return jnp.einsum(form, left, table, precision=highest)
-
-
-def forward_section(form, real_part, imag_part, cosine, sine):
-    new_real = table_product(form, real_part, cosine) + table_product(form, imag_part, sine)
-    new_imag = table_product(form, imag_part, cosine) - table_product(form, real_part, sine)
-    return (new_real, new_imag)
-
-
-def inverse_section(form, real_part, imag_part, cosine, sine):
-    new_real = table_product(form, real_part, cosine) - table_product(form, imag_part, sine)
-    new_imag = table_product(form, real_part, sine) + table_product(form, imag_part, cosine)
-    return (new_real, new_imag)
-
-
-def sine_squared(waves, count):
-    return jnp.sin(waves.astype(jnp.float32) * (2.0 * math.pi / count)) ** 2
-
-
-def joined(real_part, imag_part):
-    return jnp.concatenate([real_part, imag_part], 3)
-
-
-def project(divergence):
+def cosine_sine_basis(points, period, waves):
+    columns, eigen = [], []
+    for wave in waves:
+        angle = 2.0 * np.pi * ((wave * np.arange(points)) % period) / period
+        single = wave % period == 0 or 2 * wave == period
+        size = math.sqrt((1.0 if single else 2.0) / period)
+        columns.append(np.cos(angle) * size)
+        eigen.append(math.sin(2.0 * math.pi * wave / period) ** 2)
+        if not single:
+            columns.append(np.sin(angle) * size)
+            eigen.append(eigen[-1])
+    return np.stack(columns, 1), np.array(eigen)
+
+
+def halves(table):
+    table = np.asarray(table, np.float32)
+    high = table.astype(jnp.bfloat16)
+    low = (table - high.astype(np.float32)).astype(jnp.bfloat16)
+    return jnp.asarray(high), jnp.asarray(low)
+
+
+def split(value):
+    high = value.astype(jnp.bfloat16)
+    return high, (value - high.astype(jnp.float32)).astype(jnp.bfloat16)
+
+
+def triple_product(left, right):
+    def product(one, two):
+        return lax.dot_general(
+            one, two, (((1,), (0,)), ((), ())), preferred_element_type=jnp.float32
+        )
+
+    return product(left[0], right[0]) + (product(left[0], right[1]) + product(left[1], right[0]))
+
+
+def z_tables(z_cells):
+    half = z_cells // 2
+    even, eigen_even = cosine_sine_basis(half, z_cells, range(0, half + 1, 2))
+    odd, eigen_odd = cosine_sine_basis(half, z_cells, range(1, half, 2))
+    return even, odd, np.concatenate([eigen_even, eigen_odd])
+
+
+def whole(*shape):
+    return pl.BlockSpec(shape, lambda *index: (0,) * len(shape))
+
+
+def z_forward(divergence, count):
     x_local, y_local, z_cells = divergence.shape
-    z_outer = z_cells // half_lane
-    cos_z, sin_z = dft_tables(z_cells)
-    real_part = table_product("xyz,zk->xyk", divergence, cos_z).reshape(
-        x_local, y_local, z_outer, half_lane
-    )
-    imag_part = -table_product("xyz,zk->xyk", divergence, sin_z).reshape(
-        x_local, y_local, z_outer, half_lane
-    )
-    spectrum = narrow_turn(joined(real_part, imag_part))
-    y_cells = spectrum.shape[1]
-    z_piece = spectrum.shape[2]
-    cos_y, sin_y = dft_tables(y_cells)
-    real_part, imag_part = forward_section(
-        "xyoi,yq->xqoi", spectrum[..., :half_lane], spectrum[..., half_lane:], cos_y, sin_y
-    )
-    spectrum = wide_turn(joined(real_part, imag_part))
-    x_cells = spectrum.shape[0]
-    y_piece = spectrum.shape[1]
-    cos_x, sin_x = dft_tables(x_cells)
-    real_part, imag_part = forward_section(
-        "xqoi,xr->rqoi", spectrum[..., :half_lane], spectrum[..., half_lane:], cos_x, sin_x
-    )
-    wave_x = jnp.arange(x_cells, dtype=jnp.int32)
-    wave_y = lax.axis_index("wide") * y_piece + jnp.arange(y_piece, dtype=jnp.int32)
-    outer_z = lax.axis_index("narrow") * z_piece + jnp.arange(z_piece, dtype=jnp.int32)
-    wave_z = outer_z[:, None] * half_lane + jnp.arange(half_lane, dtype=jnp.int32)[None, :]
-    symbol = (
-        sine_squared(wave_x, x_cells)[:, None, None, None]
-        + sine_squared(wave_y, y_cells)[None, :, None, None]
-        + sine_squared(wave_z, z_cells)[None, None, :, :]
-    )
-    factor = -1.0 / ((symbol + penalty) * float(x_cells * y_cells * z_cells))
-    real_part, imag_part = inverse_section(
-        "rqoi,rx->qxoi", real_part * factor, imag_part * factor, cos_x, sin_x
-    )
-    spectrum = wide_turn(joined(real_part, imag_part))
-    real_part, imag_part = inverse_section(
-        "yxoi,yq->xoqi", spectrum[..., :half_lane], spectrum[..., half_lane:], cos_y, sin_y
-    )
-    spectrum = narrow_turn(joined(real_part, imag_part))
-    cos_blocks = cos_z.reshape(z_outer, half_lane, z_cells)
-    sin_blocks = sin_z.reshape(z_outer, half_lane, z_cells)
-    return table_product("xoyi,oiz->xyz", spectrum[..., :half_lane], cos_blocks) - table_product(
-        "xoyi,oiz->xyz", spectrum[..., half_lane:], sin_blocks
-    )
+    half, piece = z_cells // 2, z_cells // count
+    step = min(8, x_local)
+    even, odd, _ = z_tables(z_cells)
+    tables = halves(even) + halves(odd)
+
+    def kernel(div_ref, even_high, even_low, odd_high, odd_low, out_ref):
+        rows = div_ref[...].reshape(step * y_local, z_cells)
+        first, second = rows[:, :half], rows[:, half:]
+        modes = jnp.concatenate(
+            [
+                triple_product(split(first + second), (even_high[...], even_low[...])),
+                triple_product(split(first - second), (odd_high[...], odd_low[...])),
+            ],
+            1,
+        )
+        for n in range(count):
+            out_ref[n] = modes[:, n * piece : (n + 1) * piece].reshape(step, y_local, piece)
+
+    return pl.pallas_call(
+        kernel,
+        grid=(x_local // step,),
+        in_specs=[pl.BlockSpec((step, y_local, z_cells), lambda i: (i, 0, 0))]
+        + [whole(half, half)] * 4,
+        out_specs=pl.BlockSpec((count, step, y_local, piece), lambda i: (0, i, 0, 0)),
+        out_shape=jax.ShapeDtypeStruct((count, x_local, y_local, piece), jnp.float32),
+        name="z_forward",
+    )(divergence, *tables)
+
+
+def z_inverse(spectrum):
+    count, planes, y_local, piece = spectrum.shape
+    z_cells = count * piece
+    half, step = z_cells // 2, planes // 2
+    even, odd, _ = z_tables(z_cells)
+    tables = halves(even.T) + halves(odd.T)
+
+    def kernel(in_ref, even_high, even_low, odd_high, odd_low, out_ref):
+        modes = jnp.concatenate(
+            [in_ref[n].reshape(step * y_local, piece) for n in range(count)], 1
+        )
+        first = triple_product(split(modes[:, :half]), (even_high[...], even_low[...]))
+        second = triple_product(split(modes[:, half:]), (odd_high[...], odd_low[...]))
+        out_ref[...] = jnp.concatenate([first + second, first - second], 1).reshape(
+            step, y_local, z_cells
+        )
+
+    return pl.pallas_call(
+        kernel,
+        grid=(planes // step,),
+        in_specs=[pl.BlockSpec((count, step, y_local, piece), lambda i: (0, i, 0, 0))]
+        + [whole(half, half)] * 4,
+        out_specs=pl.BlockSpec((step, y_local, z_cells), lambda i: (i, 0, 0)),
+        out_shape=jax.ShapeDtypeStruct((planes, y_local, z_cells), jnp.float32),
+        name="z_inverse",
+    )(spectrum, *tables)
+
+
+def y_forward(spectrum, ratio, wide_count):
+    count, x_local, y_local, piece = spectrum.shape
+    y_cells = count * y_local
+    share = y_cells // wide_count
+    table, _ = cosine_sine_basis(y_cells, y_cells, range(y_cells // 2 + 1))
+    tables = halves(table.T)
+
+    def kernel(in_ref, high_ref, low_ref, ratio_ref, modes_ref, carry_ref, sums, power):
+        @pl.when(pl.program_id(0) == 0)
+        def _():
+            sums[...] = jnp.zeros_like(sums)
+            power[...] = jnp.ones_like(power)
+
+        planes = [
+            jnp.concatenate([in_ref[n, side] for n in range(count)], 0) for side in range(2)
+        ]
+        modes = triple_product(
+            (high_ref[...], low_ref[...]), split(jnp.concatenate(planes, 1))
+        )
+        r, pw = ratio_ref[...], power[...]
+        for side in range(2):
+            plane = modes[:, side * piece : (side + 1) * piece]
+            modes_ref[side] = plane
+            sums[side] = plane + r * sums[side]
+            sums[2 + side] = sums[2 + side] + pw * plane
+        power[...] = pw * r
+
+        @pl.when(pl.program_id(0) == x_local // 2 - 1)
+        def _():
+            for kind in range(4):
+                carry_ref[:, kind] = sums[kind].reshape(wide_count, share, piece)
+
+    return pl.pallas_call(
+        kernel,
+        grid=(x_local // 2,),
+        in_specs=[
+            pl.BlockSpec((count, 2, y_local, piece), lambda i: (0, i, 0, 0)),
+            whole(y_cells, y_cells),
+            whole(y_cells, y_cells),
+            whole(y_cells, piece),
+        ],
+        out_specs=[
+            pl.BlockSpec((2, y_cells, piece), lambda i: (i, 0, 0)),
+            whole(wide_count, 4, share, piece),
+        ],
+        out_shape=[
+            jax.ShapeDtypeStruct((x_local, y_cells, piece), jnp.float32),
+            jax.ShapeDtypeStruct((wide_count, 4, share, piece), jnp.float32),
+        ],
+        scratch_shapes=[
+            pltpu.VMEM((4, y_cells, piece), jnp.float32),
+            pltpu.VMEM((y_cells, piece), jnp.float32),
+        ],
+        name="y_forward",
+    )(spectrum, *tables, ratio)
+
+
+def power_of(value, exponent):
+    result = None
+    while exponent:
+        if exponent & 1:
+            result = value if result is None else result * value
+        value = value * value
+        exponent >>= 1
+    return result
+
+
+def join_carries(carries, ratio, block):
+    count, kinds, share, piece = carries.shape
+
+    def kernel(in_ref, ratio_ref, out_ref):
+        step = power_of(ratio_ref[...], block)
+        scale = 1.0 / (1.0 - power_of(step, count))
+        for kind in range(kinds):
+            order = list(range(count)) if kind < 2 else list(range(count))[::-1]
+            total = in_ref[order[0], kind]
+            for w in order[1:]:
+                total = in_ref[w, kind] + step * total
+            total = total * scale
+            for w in order:
+                out_ref[w, kind] = total
+                total = in_ref[w, kind] + step * total
+
+    return pl.pallas_call(
+        kernel,
+        out_shape=jax.ShapeDtypeStruct(carries.shape, jnp.float32),
+        name="join_carries",
+    )(carries, ratio)
+
+
+def y_inverse(modes, carries, ratio, gain, count):
+    x_local, y_cells, piece = modes.shape
+    y_local, pairs = y_cells // count, x_local // 2
+    wide_count, _, share, _ = carries.shape
+    table, _ = cosine_sine_basis(y_cells, y_cells, range(y_cells // 2 + 1))
+    tables = halves(table)
+
+    def kernel(modes_ref, carry_ref, high_ref, low_ref, ratio_ref, gain_ref, out_ref, behind, ahead):
+        step = pl.program_id(0)
+        r = ratio_ref[...]
+
+        def carry(kind):
+            return carry_ref[:, kind].reshape(y_cells, piece)
+
+        @pl.when(step == 0)
+        def _():
+            ahead[0] = carry(0)
+            ahead[1] = carry(1)
+            behind[2 * pairs + 1] = carry(2)
+
+            def back(i, state):
+                even, odd = state
+                m = pairs - 1 - i
+                behind[2 * m + 2] = r * odd
+                behind[2 * m + 1] = r * even
+                return (
+                    modes_ref[2 * m] + r * even,
+                    modes_ref[2 * m + 1] + r * odd,
+                )
+
+            _, odd = lax.fori_loop(0, pairs, back, (carry(2), carry(3)))
+            behind[0] = r * odd
+
+        even_plane = modes_ref[jnp.minimum(2 * step, x_local - 2)]
+        odd_plane = modes_ref[jnp.maximum(2 * step - 1, 1)]
+        even = r * ahead[0] + jnp.where(step < pairs, even_plane, 0.0)
+        odd = jnp.where(step > 0, odd_plane + r * ahead[1], ahead[1])
+        ahead[0] = even
+        ahead[1] = odd
+        gain_value = gain_ref[...]
+        planes = jnp.concatenate(
+            [gain_value * (odd + behind[2 * step]), gain_value * (even + behind[2 * step + 1])], 1
+        )
+        cells = triple_product((high_ref[...], low_ref[...]), split(planes))
+        for n in range(count):
+            for side in range(2):
+                out_ref[n, side] = cells[
+                    n * y_local : (n + 1) * y_local, side * piece : (side + 1) * piece
+                ]
+
+    return pl.pallas_call(
+        kernel,
+        grid=(pairs + 1,),
+        in_specs=[
+            whole(x_local, y_cells, piece),
+            whole(wide_count, 4, share, piece),
+            whole(y_cells, y_cells),
+            whole(y_cells, y_cells),
+            whole(y_cells, piece),
+            whole(y_cells, piece),
+        ],
+        out_specs=pl.BlockSpec((count, 2, y_local, piece), lambda i: (0, i, 0, 0)),
+        out_shape=jax.ShapeDtypeStruct((count, x_local + 2, y_local, piece), jnp.float32),
+        scratch_shapes=[
+            pltpu.VMEM((x_local + 2, y_cells, piece), jnp.float32),
+            pltpu.VMEM((2, y_cells, piece), jnp.float32),
+        ],
+        name="y_inverse",
+    )(modes, carries, *tables, ratio, gain)
+
+
+def turn(value, axis):
+    return lax.all_to_all(value, axis, split_axis=0, concat_axis=0, tiled=True)
+
+
+def project(spectrum):
+    count, x_local, y_local, piece = spectrum.shape
+    y_cells, z_cells = count * y_local, count * piece
+    wide_count = lax.axis_size("wide")
+    _, eigen_y = cosine_sine_basis(y_cells, y_cells, range(y_cells // 2 + 1))
+    eigen_z = jnp.asarray(z_tables(z_cells)[2], jnp.float32)
+    own_z = lax.dynamic_slice_in_dim(eigen_z, lax.axis_index("narrow") * piece, piece)
+    excess = 4.0 * (jnp.asarray(eigen_y, jnp.float32)[:, None] + own_z[None, :] + penalty)
+    root = jnp.sqrt(excess * (4.0 + excess))
+    ratio = 2.0 / (2.0 + excess + root)
+    gain = -4.0 / root
+    share = y_cells // wide_count
+    own_ratio = lax.dynamic_slice_in_dim(ratio, lax.axis_index("wide") * share, share)
+    modes, carries = y_forward(turn(spectrum, "narrow"), ratio, wide_count)
+    carries = turn(join_carries(turn(carries, "wide"), own_ratio, x_local // 2), "wide")
+    return z_inverse(turn(y_inverse(modes, carries, ratio, gain, count), "narrow"))
+
+
+def ring(value_up, value_down, axis):
+    size = lax.axis_size(axis)
+    up = [(i, (i + 1) % size) for i in range(size)]
+    down = [(j, i) for i, j in up]
+    return lax.ppermute(value_up, axis, up), lax.ppermute(value_down, axis, down)
 
 
 def substrate_advance(thermal_profile, spread_coefficient):
@@ -212,9 +420,14 @@
     heat_cells = mu_field * (rate_sq - rate_base**2)
     along_x, along_y, along_z = gradients(pad_cells(current))
     divergence = along_x[0] + along_y[1] + along_z[2]
-    pressure = project(divergence)
-    press_x, press_y, press_z = gradients(pad_cells(pressure[None]))
-    corrected_flow_vector = current - jnp.concatenate([press_x, press_y, press_z], 0)
+    pressure = project(z_forward(divergence, lax.axis_size("narrow")))
+    inner = pressure[1:-1]
+    below, above = ring(inner[:, -1:], inner[:, :1], "narrow")
+    tall = jnp.concatenate([below, inner, above], 1)
+    press_x = (pressure[2:] - pressure[:-2]) * 0.5
+    press_y = (tall[:, 2:] - tall[:, :-2]) * 0.5
+    press_z = (jnp.roll(inner, -1, 2) - jnp.roll(inner, 1, 2)) * 0.5
+    corrected_flow_vector = current - jnp.stack([press_x, press_y, press_z], 0)
     blocks = heat_cells.reshape(-1, 128)
     slab_ids = source_owner_sheet[:, 0]
     slab_count = lax.axis_size("wide")

time: 1420 us -> 665 us (0.47)
  waiting for transfers between devices: 447 us -> 98.8 us
  matrix products: 171 us -> 0 us
  local copies, waits for them, and re-layouts: 223 us -> 81.6 us
  blocking collectives: 96.3 us -> 17.8 us
  other arithmetic: 364 us -> 317 us
  Pallas kernels: 0 us -> 38.1 us
    all_to_all x3, waiting for transfers between devices: 329 us -> 20.9 us  [turn(): return lax.all_to_all(value, axis, split_axis=0, concat_axis=0, tiled=True)]
    unnamed x16 -> x0, matrix products: 113 us -> none
    all_to_all x1, blocking collectives: 96.3 us -> 17.8 us  [turn(): return lax.all_to_all(value, axis, split_axis=0, concat_axis=0, tiled=True)]
    dot_general x4 -> x0, matrix products: 57.4 us -> none  [table_product(): return jnp.einsum(form, left, table, precision=highest)]
    unnamed x77 -> x45, local copies, waits for them, and re-layouts: 49.7 us -> 1.69 us
    pallas_call x0 -> x5, Pallas kernels: none -> 38.1 us  [the longest x1 12.5 us: y_forward(): pl.pallas_call(kernel, grid=(x_local // 2,), in_specs=[pl.BlockSpec((coun...]
    concatenate x4 -> x2, local copies, waits for them, and re-layouts: 43.9 us -> 6.32 us  [per_device(): press_z = (jnp.roll(inner, -1, 2) - jnp.roll(inner, 1, 2)) * 0.5]
    ppermute x18 -> x16, waiting for transfers between devices: 102 us -> 64.8 us  [with_halo(): after = lax.ppermute(initial, axis, down)]
  transfers between devices with their start and end apart: 40 -> 38, of which waited for: 18 -> 17; matrix products, arithmetic and copies ran while one was open for 15% -> 20% of each run, Pallas kernels for 0% -> 4%
where the time goes in v1:
time: 665 us; the launch traced here: 657 us
  other arithmetic  317 us (48%)
  waiting for transfers between devices  98.8 us (15%)
  starting transfers between devices  88.9 us (13%)
  local copies, waits for them, and re-layouts  81.6 us (12%)
  Pallas kernels  38.1 us (6%)
  blocking collectives  17.8 us (3%)
  between operations  14.8 us (2%)
    add x2, other arithmetic, per_device(): material_flow_vector + time_step * (viscous_term(mu_padded, base_pad) + t...  85.9 us
    ppermute x16, waiting for transfers between devices, with_halo(): after = lax.ppermute(initial, axis, down)  64.8 us
    slice x6, local copies, waits for them, and re-layouts, gradients(): along_z = (jnp.roll(center, -1, 3) - jnp.roll(center, 1, 3)) * 0.5  48.2 us
    scatter-add x1, other arithmetic, per_device(): partial_value = jnp.zeros((slab_count * component_lines, 128), jnp.float3...  45.7 us
    mul x2, other arithmetic, viscous_term(): 0.5 * (mu_center + mu_padded[2:, 1:-1])  43.7 us
    ppermute x16, starting transfers between devices, with_halo(): before = lax.ppermute(last, axis, up)  35.7 us
    mul x2, other arithmetic, gradients(): along_z = (jnp.roll(center, -1, 3) - jnp.roll(center, 1, 3)) * 0.5  33.6 us
    ppermute x16, starting transfers between devices, with_halo(): after = lax.ppermute(initial, axis, down)  32.3 us
  transfers between devices with their start and end apart: 38, of which 17 were waited for; matrix products, arithmetic and copies ran while one was open for 20% of the time, Pallas kernels for 4%

profile of v1, /device:TPU:1, one launch (start us, length us, event | category | flops | bytes accessed | tf_op | source)
XLA Modules:
  0.0 657.1 jit_solution(924733168700330174)
XLA Ops:
  13.7 21.7 %fusion.108 = (f32[3,32,64,511]{3,2,1,0:T(8,128)}, f32[3,32,64,511]{3,2,1,0:T(8,128)}) fusion(f32[3,32,64,512]{3,2,1,0:T(8,128)} %param.21), kind=kLoop, calls=%fused_computation.230 | loop fusion | bytes 50233344 | tf_op jit(solution)/shard_map/jit(_roll_static)/slice | solution.py:44
  40.3 10.1 %fusion.6 = (f32[3,32,64,512]{3,2,1,0:T(8,128)}, f32[3,34,64,512]{3,2,1,0:T(8,128)}) fusion(f32[3,32,64,512]{3,2,1,0:T(8,128)S(1)} %bitcast.35, f32[3,1,64,512]{3,2,1,0:T(8,128)S(1)} %collective-permute-done.1, f32[3,1,64,512]{3,2,1,0:T(8,128)S(1)} %collective-permute-done, f32[3,34,64,512]{3,2,1,0:T(8,128)} %constant_dynamic-update-slice_fusion.2), kind=kLoop, calls=%fused_computation.18 | loop fusion | flops 12582912 | bytes 38535168 | tf_op jit(solution)/shard_map/mul | solution.py:42
  56.1 18.0 %subtract_multiply_fusion = f32[3,32,64,512]{3,2,1,0:T(8,128)} fusion(f32[3,32,64,511]{3,2,1,0:T(8,128)} %get-tuple-element.31, f32[3,32,64,1]{3,2,1,0:T(8,128)} %get-tuple-element.33, f32[3,32,64,1]{3,2,1,0:T(8,128)} %get-tuple-element.32, f32[3,32,64,511]{3,2,1,0:T(8,128)} %get-tuple-element.30), kind=kLoop, calls=%fused_computation.28 | loop fusion | flops 12582912 | bytes 37748736 | tf_op jit(solution)/shard_map/mul | solution.py:44
  74.1 6.8 %subtract_multiply_fusion.1 = f32[3,32,64,512]{3,2,1,0:T(8,128)} fusion(f32[3,34,1,512]{3,2,1,0:T(1,128)S(1)} %collective-permute-done.2, f32[3,34,64,512]{3,2,1,0:T(8,128)S(1)} %bitcast.37, f32[3,34,1,512]{3,2,1,0:T(1,128)S(1)} %collective-permute-done.3), kind=kLoop, calls=%fused_computation.29 | loop fusion | flops 12582912 | bytes 26370048 | tf_op jit(solution)/shard_map/mul | solution.py:43
  80.9 16.1 %divide_bitcast_fusion = f32[1,32,64,512]{3,2,1,0:T(8,128)S(1)} fusion(f32[3,32,64,512]{3,2,1,0:T(8,128)} %subtract_multiply_fusion.1, f32[3,32,64,512]{3,2,1,0:T(8,128)} %subtract_multiply_fusion, f32[3,32,64,512]{3,2,1,0:T(8,128)} %get-tuple-element.28, f32[32,64,512]{2,1,0:T(8,128)S(1)} %copy-done.4), kind=kLoop, calls=%fused_computation.134 | loop fusion | flops 30408704 | bytes 46137344 | tf_op jit(solution)/shard_map/broadcast_in_dim | solution.py:414
  118.4 21.9 %fusion.48 = (f32[32,64,512]{2,1,0:T(8,128)}, f32[32,64,512]{2,1,0:T(8,128)}, f32[32,64,512]{2,1,0:T(8,128)}, f32[32,64,512]{2,1,0:T(8,128)}, f32[32,64,512]{2,1,0:T(8,128)}, /*index=5*/f32[32,64,512]{2,1,0:T(8,128)}) fusion(f32[34,66,512]{2,1,0:T(8,128)} %copy-done.1, f32[32,64,511]{2,1,0:T(8,128)} %get-tuple-element.53, ...), kind=kLoop, calls=%fused_computation.100 | loop fusion | flops 14680064 | bytes 54525952 | tf_op jit(solution)/shard_map/mul | solution.py:71
  140.3 43.0 %multiply_add_fusion.1 = f32[3,32,64,512]{3,2,1,0:T(8,128)S(1)} fusion(f32[3,32,64,512]{3,2,1,0:T(8,128)} %param.21, f32[3,32,64,512]{3,2,1,0:T(8,128)} %param.22, f32[3,34,1,512]{3,2,1,0:T(1,128)S(1)} %collective-permute-done.2, f32[3,34,64,512]{3,2,1,0:T(8,128)} %constant_dynamic-update-slice_fusion, f32[3,34,1,512]{3,2,1,0:T(1,128)S(1)} %collective-permute-done.3, ...), kind=kLoop, calls=%fused_computation.27 | loop fusion | flops 81788928 | bytes 102653952 | tf_op jit(solution)/shard_map/add | solution.py:415
  183.3 10.1 %fusion.106 = (f32[3,32,64,511]{3,2,1,0:T(8,128)}, f32[3,32,64,511]{3,2,1,0:T(8,128)}) fusion(f32[3,32,64,512]{3,2,1,0:T(8,128)S(1)} %multiply_add_fusion.1), kind=kLoop, calls=%fused_computation.228 | loop fusion | bytes 50233344 | tf_op jit(solution)/shard_map/jit(_roll_static)/slice | solution.py:44
  198.9 13.4 %collective-permute-done.8 = f32[3,1,64,512]{3,2,1,0:T(8,128)S(1)} collective-permute-done((f32[3,1,64,512]{3,2,1,0:T(8,128)S(1)}, f32[3,1,64,512]{3,2,1,0:T(8,128)S(1)}, u32[]{:S(2)}, u32[]{:S(2)}) %collective-permute-start.8) | collective-permute-done | bytes 393248 | tf_op jit(solution)/shard_map/ppermute | solution.py:31
  214.5 15.6 %fusion.8 = f32[3,32,64,512]{3,2,1,0:T(8,128)} fusion(f32[3,32,64,1]{3,2,1,0:T(8,128)S(1)} %get-tuple-element.23, f32[3,32,64,511]{3,2,1,0:T(8,128)} %get-tuple-element.25, f32[3,32,64,511]{3,2,1,0:T(8,128)} %get-tuple-element.24, f32[3,32,64,1]{3,2,1,0:T(8,128)S(1)} %get-tuple-element.22), kind=kLoop, calls=%fused_computation.24 | loop fusion | flops 12582912 | bytes 37748736 | tf_op jit(solution)/shard_map/mul | solution.py:44
  230.1 13.9 %fusion.3 = (f32[3,32,64,512]{3,2,1,0:T(8,128)}, f32[3,32,64,512]{3,2,1,0:T(8,128)}) fusion(f32[3,32,64,512]{3,2,1,0:T(8,128)S(1)} %multiply_add_fusion.1, f32[3,1,64,512]{3,2,1,0:T(8,128)S(1)} %collective-permute-done.9, f32[3,1,64,512]{3,2,1,0:T(8,128)S(1)} %collective-permute-done.8, f32[3,34,1,512]{3,2,1,0:T(1,128)S(1)} %collective-permute-done.11, ...), kind=kLoop, calls=%fused_computation.11 | loop fusion | flops 37748736 | bytes 38952960 | tf_op jit(solution)/shard_map/mul | solution.py:42
  244.0 17.4 %fusion.98 = (f32[32,64,512]{2,1,0:T(8,128)}, f32[32,64,512]{2,1,0:T(8,128)S(1)}) fusion(f32[32,64,512]{2,1,0:T(8,128)} %param.23, f32[3,32,64,512]{3,2,1,0:T(8,128)} %get-tuple-element.11, f32[3,32,64,512]{3,2,1,0:T(8,128)} %fusion.8, f32[3,32,64,512]{3,2,1,0:T(8,128)} %get-tuple-element.10), kind=kLoop, calls=%fused_computation.221 | loop fusion | flops 31457280 | bytes 50331648 | tf_op jit(solution)/shard_map/mul | solution.py:420
  289.3 21.8 %fusion.30 = (f32[32,64,512]{2,1,0:T(8,128)}, f32[32,64,512]{2,1,0:T(8,128)}, f32[32,64,512]{2,1,0:T(8,128)}, f32[32,64,512]{2,1,0:T(8,128)}, f32[32,64,512]{2,1,0:T(8,128)}, /*index=5*/f32[32,64,512]{2,1,0:T(8,128)}) fusion(f32[34,66,512]{2,1,0:T(8,128)} %copy-done.2, f32[32,64,511]{2,1,0:T(8,128)} %get-tuple-element.43, ...), kind=kLoop, calls=%fused_computation.72 | loop fusion | flops 14680064 | bytes 54525952 | tf_op jit(solution)/shard_map/mul | solution.py:71
  311.1 42.9 %multiply_add_fusion = f32[3,32,64,512]{3,2,1,0:T(8,128)S(1)} fusion(f32[3,32,64,512]{3,2,1,0:T(8,128)} %param.21, f32[3,32,64,512]{3,2,1,0:T(8,128)} %param.22, f32[3,34,1,512]{3,2,1,0:T(1,128)S(1)} %collective-permute-done.2, f32[3,34,64,512]{3,2,1,0:T(8,128)} %constant_dynamic-update-slice_fusion, f32[3,34,1,512]{3,2,1,0:T(1,128)S(1)} %collective-permute-done.3, ...), kind=kLoop, calls=%fused_computation.26 | loop fusion | flops 81788928 | bytes 102653952 | tf_op jit(solution)/shard_map/add | solution.py:415
  357.9 9.9 %fusion.104 = (f32[3,32,64,511]{3,2,1,0:T(8,128)}, f32[3,32,64,511]{3,2,1,0:T(8,128)}) fusion(f32[3,32,64,512]{3,2,1,0:T(8,128)S(1)} %multiply_add_fusion), kind=kLoop, calls=%fused_computation.226 | loop fusion | bytes 50233344 | tf_op jit(solution)/shard_map/jit(_roll_static)/slice | solution.py:44
  380.6 8.8 %fusion.21.div_ref = f32[32,64,512]{2,1,0:T(8,128)} fusion(f32[3,32,64,1]{3,2,1,0:T(8,128)S(1)} %get-tuple-element.19, f32[3,32,64,511]{3,2,1,0:T(8,128)} %get-tuple-element.21, f32[3,32,64,511]{3,2,1,0:T(8,128)} %get-tuple-element.20, f32[3,32,64,1]{3,2,1,0:T(8,128)S(1)} %get-tuple-element.18, f32[3,34,1,512]{3,2,1,0:T(1,128)S(1)} %collective-permute-done.18, ...), kind=kLoop, calls=%fused_computation.50 | loop fusion | flops 18874368 | bytes 43147264 | tf_op jit(solution)/shard_map/add | solution.py:422
  406.5 45.7 %scatter_custom_fusion = f32[4096,128]{1,0:T(8,128)} fusion(s32[8192]{0:T(1024)S(1)} %compare_select_fusion, f32[8192,128]{1,0:T(8,128)} %reshape.143, f32[]{:T(128)} %constant.36.clone.1), kind=kCustom, calls=%fused_computation.138 | custom fusion | flops 1048576 | bytes 2097664 | tf_op jit(solution)/shard_map/scatter-add | solution.py:438
  453.9 12.5 %y_forward.1 = (f32[32,256,128]{2,1,0:T(8,128)}, f32[8,4,32,128]{3,2,1,0:T(8,128)}) custom-call(f32[4,32,64,128]{3,2,1,0:T(8,128)} %all-to-all-done.in_ref, bf16[256,256]{1,0:T(8,128)(2,1)} %constant.91.clone.high_ref, bf16[256,256]{1,0:T(8,128)(2,1)} %constant.92.clone.low_ref, f32[256,128]{1,0:T(8,128)} %get-tuple-element.91.ratio_ref), custom_call_target="tpu_custom_call" | custom-call | tf_op jit(solution)/shard_map/y_forward/pallas_call | solution.py:226
  473.5 20.9 %all-to-all-done.1.in_ref = f32[8,4,32,128]{3,2,1,0:T(8,128)S(1)} async-done(((f32[8,4,32,128]{3,2,1,0:T(8,128)}), f32[8,4,32,128]{3,2,1,0:T(8,128)S(1)}, u32[]{:S(2)}, u32[]{:S(2)}) %all-to-all-start.1) | async-done | bytes 524320 | tf_op jit(solution)/shard_map/all_to_all | solution.py:356
  497.1 17.8 %all_to_all.20.carry_ref = f32[8,4,32,128]{3,2,1,0:T(8,128)} all-to-all(f32[8,4,32,128]{3,2,1,0:T(8,128)} %join_carries.1), channel_id=1, replica_groups=mesh['wide'=8,'narrow'=4] {'wide'}, dimensions={0} | all-to-all | bytes 1048576 | tf_op jit(solution)/shard_map/all_to_all | solution.py:356
  515.0 12.5 %y_inverse.1 = f32[4,34,64,128]{3,2,1,0:T(8,128)} custom-call(f32[32,256,128]{2,1,0:T(8,128)} %get-tuple-element.4.modes_ref, f32[8,4,32,128]{3,2,1,0:T(8,128)} %all_to_all.20.carry_ref, bf16[256,256]{1,0:T(8,128)(2,1)} %constant.93.clone.high_ref, bf16[256,256]{1,0:T(8,128)(2,1)} %constant.94.clone.low_ref, f32[256,128]{1,0:T(8,128)} %get-tuple-element.91.ratio_ref, ...), custom_call_target="tpu_custom_call" | custom-call | tf_op jit(solution)/shard_map/y_inverse/pallas_call | solution.py:334
  527.5 6.6 %all-to-all-start.3 = ((f32[4,34,64,128]{3,2,1,0:T(8,128)}), f32[4,34,64,128]{3,2,1,0:T(8,128)}, u32[]{:S(2)}, u32[]{:S(2)}) async-start(f32[4,34,64,128]{3,2,1,0:T(8,128)} %y_inverse.1), calls=%async_computation.3 | async-start | bytes 8912896 | tf_op jit(solution)/shard_map/all_to_all | solution.py:356
  548.0 36.7 %collective-permute-done.24 = f32[18,1,128]{2,1,0:T(1,128)S(1)} collective-permute-done((f32[18,1,128]{2,1,0:T(1,128)S(1)}, f32[18,1,128]{2,1,0:T(1,128)S(1)}, u32[]{:S(2)}, u32[]{:S(2)}) %collective-permute-start.24) | collective-permute-done | bytes 9248 | tf_op jit(solution)/shard_map/ppermute | solution.py:31
  642.3 7.8 %maximum_subtract_fusion.1 = f32[3,32,64,512]{3,2,1,0:T(8,128)} fusion(f32[3,32,64,512]{3,2,1,0:T(8,128)S(1)} %bitcast.33, f32[1,32,64,512]{3,2,1,0:T(8,128)S(1)} %fusion.69, f32[1,32,64,512]{3,2,1,0:T(8,128)} %fusion.15, f32[1,32,64,512]{3,2,1,0:T(8,128)S(1)} %get-tuple-element.56), kind=kLoop, calls=%fused_computation.25 | loop fusion | flops 9437184 | bytes 37748736 | tf_op jit(solution)/shard_map/sub | solution.py:430
  (171 shorter events, 190.4 us)
Async XLA Ops:
  8.5 31.0 %collective-permute-start.1 = (f32[3,1,64,512]{3,2,1,0:T(8,128)S(1)}, f32[3,1,64,512]{3,2,1,0:T(8,128)S(1)}, u32[]{:S(2)}, u32[]{:S(2)}) collective-permute-start(f32[3,1,64,512]{3,2,1,0:T(8,128)S(1)} %get-tuple-element.35), channel_id=1, source_target_pairs={{0,4},{4,8},{8,12},{12,16},{16,20},{20,24},{24,28},{28,0},{1,5},{5... | collective-permute-start | bytes 1179656 | tf_op jit(solution)/shard_map/ppermute | solution.py:30
  10.6 29.6 %collective-permute-start = (f32[3,1,64,512]{3,2,1,0:T(8,128)S(1)}, f32[3,1,64,512]{3,2,1,0:T(8,128)S(1)}, u32[]{:S(2)}, u32[]{:S(2)}) collective-permute-start(f32[3,1,64,512]{3,2,1,0:T(8,128)S(1)} %get-tuple-element.34), channel_id=1, source_target_pairs={{4,0},{8,4},{12,8},{16,12},{20,16},{24,20},{28,24},{0,28},{5,1},{9... | collective-permute-start | bytes 1179656 | tf_op jit(solution)/shard_map/ppermute | solution.py:31
  53.5 20.5 %collective-permute-start.2 = (f32[3,34,1,512]{3,2,1,0:T(1,128)S(1)}, f32[3,34,1,512]{3,2,1,0:T(1,128)S(1)}, u32[]{:S(2)}, u32[]{:S(2)}) collective-permute-start(f32[3,34,1,512]{3,2,1,0:T(1,128)S(1)} %get-tuple-element.15), channel_id=1, source_target_pairs={{1,0},{2,1},{3,2},{0,3},{5,4},{6,5},{7,6},{4,7},{9,8},{10,9},{11,1... | collective-permute-start | bytes 626696 | tf_op jit(solution)/shard_map/ppermute | solution.py:31
  54.5 19.5 %collective-permute-start.3 = (f32[3,34,1,512]{3,2,1,0:T(1,128)S(1)}, f32[3,34,1,512]{3,2,1,0:T(1,128)S(1)}, u32[]{:S(2)}, u32[]{:S(2)}) collective-permute-start(f32[3,34,1,512]{3,2,1,0:T(1,128)S(1)} %get-tuple-element.14), channel_id=1, source_target_pairs={{0,1},{1,2},{2,3},{3,0},{4,5},{5,6},{6,7},{7,4},{8,9},{9,10},{10,1... | collective-permute-start | bytes 626696 | tf_op jit(solution)/shard_map/ppermute | solution.py:30
  97.0 8.1 %collective-permute-start.4 = (f32[1,1,64,512]{3,2,1,0:T(8,128)S(1)}, f32[1,1,64,512]{3,2,1,0:T(8,128)S(1)}, u32[]{:S(2)}, u32[]{:S(2)}) collective-permute-start(f32[1,1,64,512]{3,2,1,0:T(8,128)S(1)} %get-tuple-element.70), channel_id=1, source_target_pairs={{0,4},{4,8},{8,12},{12,16},{16,20},{20,24},{24,28},{28,0},{1,5},{5... | collective-permute-start | bytes 393224 | tf_op jit(solution)/shard_map/ppermute | solution.py:30
  97.1 8.0 %collective-permute-start.5 = (f32[1,1,64,512]{3,2,1,0:T(8,128)S(1)}, f32[1,1,64,512]{3,2,1,0:T(8,128)S(1)}, u32[]{:S(2)}, u32[]{:S(2)}) collective-permute-start(f32[1,1,64,512]{3,2,1,0:T(8,128)S(1)} %get-tuple-element.71), channel_id=1, source_target_pairs={{4,0},{8,4},{12,8},{16,12},{20,16},{24,20},{28,24},{0,28},{5,1},{9... | collective-permute-start | bytes 393224 | tf_op jit(solution)/shard_map/ppermute | solution.py:31
  193.4 18.8 %collective-permute-start.8 = (f32[3,1,64,512]{3,2,1,0:T(8,128)S(1)}, f32[3,1,64,512]{3,2,1,0:T(8,128)S(1)}, u32[]{:S(2)}, u32[]{:S(2)}) collective-permute-start(f32[3,1,64,512]{3,2,1,0:T(8,128)S(1)} %get-tuple-element.27), channel_id=1, source_target_pairs={{4,0},{8,4},{12,8},{16,12},{20,16},{24,20},{28,24},{0,28},{5,1},{9... | collective-permute-start | bytes 1179656 | tf_op jit(solution)/shard_map/ppermute | solution.py:31
  197.5 14.8 %collective-permute-start.9 = (f32[3,1,64,512]{3,2,1,0:T(8,128)S(1)}, f32[3,1,64,512]{3,2,1,0:T(8,128)S(1)}, u32[]{:S(2)}, u32[]{:S(2)}) collective-permute-start(f32[3,1,64,512]{3,2,1,0:T(8,128)S(1)} %get-tuple-element.26), channel_id=1, source_target_pairs={{0,4},{4,8},{8,12},{12,16},{16,20},{20,24},{24,28},{28,0},{1,5},{5... | collective-permute-start | bytes 1179656 | tf_op jit(solution)/shard_map/ppermute | solution.py:30
  212.7 17.4 %collective-permute-start.10 = (f32[3,34,1,512]{3,2,1,0:T(1,128)S(1)}, f32[3,34,1,512]{3,2,1,0:T(1,128)S(1)}, u32[]{:S(2)}, u32[]{:S(2)}) collective-permute-start(f32[3,34,1,512]{3,2,1,0:T(1,128)S(1)} %get-tuple-element.12), channel_id=1, source_target_pairs={{1,0},{2,1},{3,2},{0,3},{5,4},{6,5},{7,6},{4,7},{9,8},{10,9},{11,1... | collective-permute-start | bytes 626696 | tf_op jit(solution)/shard_map/ppermute | solution.py:31
  212.9 17.2 %collective-permute-start.11 = (f32[3,34,1,512]{3,2,1,0:T(1,128)S(1)}, f32[3,34,1,512]{3,2,1,0:T(1,128)S(1)}, u32[]{:S(2)}, u32[]{:S(2)}) collective-permute-start(f32[3,34,1,512]{3,2,1,0:T(1,128)S(1)} %get-tuple-element.13), channel_id=1, source_target_pairs={{0,1},{1,2},{2,3},{3,0},{4,5},{5,6},{6,7},{7,4},{8,9},{9,10},{10,1... | collective-permute-start | bytes 626696 | tf_op jit(solution)/shard_map/ppermute | solution.py:30
  267.4 8.3 %collective-permute-start.12 = (f32[1,1,64,512]{3,2,1,0:T(8,128)S(1)}, f32[1,1,64,512]{3,2,1,0:T(8,128)S(1)}, u32[]{:S(2)}, u32[]{:S(2)}) collective-permute-start(f32[1,1,64,512]{3,2,1,0:T(8,128)S(1)} %get-tuple-element.68), channel_id=1, source_target_pairs={{0,4},{4,8},{8,12},{12,16},{16,20},{20,24},{24,28},{28,0},{1,5},{5... | collective-permute-start | bytes 393224 | tf_op jit(solution)/shard_map/ppermute | solution.py:30
  268.1 8.0 %collective-permute-start.13 = (f32[1,1,64,512]{3,2,1,0:T(8,128)S(1)}, f32[1,1,64,512]{3,2,1,0:T(8,128)S(1)}, u32[]{:S(2)}, u32[]{:S(2)}) collective-permute-start(f32[1,1,64,512]{3,2,1,0:T(8,128)S(1)} %get-tuple-element.69), channel_id=1, source_target_pairs={{4,0},{8,4},{12,8},{16,12},{20,16},{24,20},{28,24},{0,28},{5,1},{9... | collective-permute-start | bytes 393224 | tf_op jit(solution)/shard_map/ppermute | solution.py:31
  354.2 19.1 %collective-permute-start.16 = (f32[3,1,64,512]{3,2,1,0:T(8,128)S(1)}, f32[3,1,64,512]{3,2,1,0:T(8,128)S(1)}, u32[]{:S(2)}, u32[]{:S(2)}) collective-permute-start(f32[3,1,64,512]{3,2,1,0:T(8,128)S(1)} %get-tuple-element.17), channel_id=1, source_target_pairs={{4,0},{8,4},{12,8},{16,12},{20,16},{24,20},{28,24},{0,28},{5,1},{9... | collective-permute-start | bytes 1179656 | tf_op jit(solution)/shard_map/ppermute | solution.py:31
  357.9 15.4 %collective-permute-start.17 = (f32[3,1,64,512]{3,2,1,0:T(8,128)S(1)}, f32[3,1,64,512]{3,2,1,0:T(8,128)S(1)}, u32[]{:S(2)}, u32[]{:S(2)}) collective-permute-start(f32[3,1,64,512]{3,2,1,0:T(8,128)S(1)} %get-tuple-element.16), channel_id=1, source_target_pairs={{0,4},{4,8},{8,12},{12,16},{16,20},{20,24},{24,28},{28,0},{1,5},{5... | collective-permute-start | bytes 1179656 | tf_op jit(solution)/shard_map/ppermute | solution.py:30
  373.7 6.9 %collective-permute-start.18 = (f32[3,34,1,512]{3,2,1,0:T(1,128)S(1)}, f32[3,34,1,512]{3,2,1,0:T(1,128)S(1)}, u32[]{:S(2)}, u32[]{:S(2)}) collective-permute-start(f32[3,34,1,512]{3,2,1,0:T(1,128)S(1)} %get-tuple-element.9), channel_id=1, source_target_pairs={{1,0},{2,1},{3,2},{0,3},{5,4},{6,5},{7,6},{4,7},{9,8},{10,9},{11,1... | collective-permute-start | bytes 626696 | tf_op jit(solution)/shard_map/ppermute | solution.py:31
  395.4 58.5 %all-to-all-start = ((f32[4,32,64,128]{3,2,1,0:T(8,128)}), f32[4,32,64,128]{3,2,1,0:T(8,128)}, u32[]{:S(2)}, u32[]{:S(2)}) async-start(f32[4,32,64,128]{3,2,1,0:T(8,128)} %z_forward.1), calls=%async_computation | async-start | bytes 8388608 | tf_op jit(solution)/shard_map/all_to_all | solution.py:356
  401.7 132.4 %reduce-scatter.2.cloned.1.call-start = ((), (), s32[]{:S(2)}) async-start(), calls=%async_computation.5 | async-start | bytes 2359296 | tf_op jit(solution)/shard_map/reduce_scatter | solution.py:440
  466.3 28.0 %all-to-all-start.1 = ((f32[8,4,32,128]{3,2,1,0:T(8,128)}), f32[8,4,32,128]{3,2,1,0:T(8,128)S(1)}, u32[]{:S(2)}, u32[]{:S(2)}) async-start(f32[8,4,32,128]{3,2,1,0:T(8,128)} %get-tuple-element.5), calls=%async_computation.1 | async-start | bytes 1048576 | tf_op jit(solution)/shard_map/all_to_all | solution.py:356
  527.5 85.6 %all-to-all-start.3 = ((f32[4,34,64,128]{3,2,1,0:T(8,128)}), f32[4,34,64,128]{3,2,1,0:T(8,128)}, u32[]{:S(2)}, u32[]{:S(2)}) async-start(f32[4,34,64,128]{3,2,1,0:T(8,128)} %y_inverse.1), calls=%async_computation.3 | async-start | bytes 8912896 | tf_op jit(solution)/shard_map/all_to_all | solution.py:356
  541.3 43.4 %collective-permute-start.24 = (f32[18,1,128]{2,1,0:T(1,128)S(1)}, f32[18,1,128]{2,1,0:T(1,128)S(1)}, u32[]{:S(2)}, u32[]{:S(2)}) collective-permute-start(f32[18,1,128]{2,1,0:T(1,128)S(1)} %get-tuple-element.76), channel_id=1, source_target_pairs={{1,0},{2,1},{3,2},{5,4},{6,5},{7,6},{9,8},{10,9},{11,10},{13,12},{... | collective-permute-start | bytes 27656 | tf_op jit(solution)/shard_map/ppermute | solution.py:31
  544.4 40.3 %collective-permute-start.25 = (f32[18,1,128]{2,1,0:T(1,128)S(1)}, f32[18,1,128]{2,1,0:T(1,128)S(1)}, u32[]{:S(2)}, u32[]{:S(2)}) collective-permute-start(f32[18,1,128]{2,1,0:T(1,128)S(1)} %get-tuple-element.77), channel_id=1, source_target_pairs={{0,1},{1,2},{2,3},{4,5},{5,6},{6,7},{8,9},{9,10},{10,11},{12,13},{... | collective-permute-start | bytes 27656 | tf_op jit(solution)/shard_map/ppermute | solution.py:30
  604.4 7.3 %collective-permute-start.32 = (f32[18,1,128]{2,1,0:T(1,128)S(1)}, f32[18,1,128]{2,1,0:T(1,128)S(1)}, u32[]{:S(2)}, u32[]{:S(2)}) collective-permute-start(f32[18,1,128]{2,1,0:T(1,128)S(1)} %get-tuple-element.72), channel_id=1, source_target_pairs={{1,0},{2,1},{3,2},{5,4},{6,5},{7,6},{9,8},{10,9},{11,10},{13,12},{... | collective-permute-start | bytes 27656 | tf_op jit(solution)/shard_map/ppermute | solution.py:31
  631.3 7.6 %collective-permute-start.20 = (f32[32,1,512]{2,1,0:T(1,128)S(1)}, f32[32,1,512]{2,1,0:T(1,128)S(1)}, u32[]{:S(2)}, u32[]{:S(2)}) collective-permute-start(f32[32,1,512]{2,1,0:T(1,128)S(1)} %get-tuple-element.58), channel_id=1, source_target_pairs={{1,0},{2,1},{3,2},{0,3},{5,4},{6,5},{7,6},{4,7},{9,8},{10,9},{11,1... | collective-permute-start | bytes 196616 | tf_op jit(solution)/shard_map/ppermute | solution.py:381
  631.3 7.7 %collective-permute-start.21 = (f32[32,1,512]{2,1,0:T(1,128)S(1)}, f32[32,1,512]{2,1,0:T(1,128)S(1)}, u32[]{:S(2)}, u32[]{:S(2)}) collective-permute-start(f32[32,1,512]{2,1,0:T(1,128)S(1)} %get-tuple-element.59), channel_id=1, source_target_pairs={{0,1},{1,2},{2,3},{3,0},{4,5},{5,6},{6,7},{7,4},{8,9},{9,10},{10,1... | collective-permute-start | bytes 196616 | tf_op jit(solution)/shard_map/ppermute | solution.py:381
  (36 other events, 431.3 us)
Sparse Core Ops, SparseCore 0:
  452.4 75.9 reduce-scatter.1

commit v2 on v1

--- a/solution.py
+++ b/solution.py
@@ -33,57 +33,229 @@
     return x
 
 
-def pad_cells(field):
-    return with_halo(field, (("wide", 1), ("narrow", 2)), 1, True)
-
-
-def gradients(bordered_array):
-    center = bordered_array[:, 1:-1, 1:-1]
-    along_x = (bordered_array[:, 2:, 1:-1] - bordered_array[:, :-2, 1:-1]) * 0.5
-    along_y = (bordered_array[:, 1:-1, 2:] - bordered_array[:, 1:-1, :-2]) * 0.5
-    along_z = (jnp.roll(center, -1, 3) - jnp.roll(center, 1, 3)) * 0.5
-    return (along_x, along_y, along_z)
-
-
-def rate_squared(bordered_array):
-    along_x, along_y, along_z = gradients(bordered_array)
-    s_xy = 0.5 * (along_y[0] + along_x[1])
-    s_xz = 0.5 * (along_z[0] + along_x[2])
-    s_yz = 0.5 * (along_z[1] + along_y[2])
-    total = (
-        along_x[0] ** 2 + along_y[1] ** 2 + along_z[2] ** 2 + 2.0 * (s_xy**2 + s_xz**2 + s_yz**2)
-    )
-    return rate_base**2 + 2.0 * total
-
-
-def inverse_sinh(value):
-    return jnp.log(value + jnp.sqrt(value * value + 1.0))
-
-
-def viscosity(rate_sq, zener):
-    rate = jnp.sqrt(rate_sq)
-    return inverse_sinh((rate * zener) ** (1.0 / stress_exponent)) / (3.0 * rate)
-
-
-def viscous_term(mu_padded, vel_padded):
-    mu_center = mu_padded[1:-1, 1:-1]
-    vel_center = vel_padded[:, 1:-1, 1:-1]
-    total = 0.5 * (mu_center + mu_padded[2:, 1:-1]) * (
-        vel_padded[:, 2:, 1:-1] - vel_center
-    ) - 0.5 * (mu_center + mu_padded[:-2, 1:-1]) * (vel_center - vel_padded[:, :-2, 1:-1])
-    total = (
-        total
-        + 0.5 * (mu_center + mu_padded[1:-1, 2:]) * (vel_padded[:, 1:-1, 2:] - vel_center)
-        - 0.5 * (mu_center + mu_padded[1:-1, :-2]) * (vel_center - vel_padded[:, 1:-1, :-2])
-    )
-    total = (
-        total
-        + 0.5
-        * (mu_center + jnp.roll(mu_center, -1, 2))
-        * (jnp.roll(vel_center, -1, 3) - vel_center)
-        - 0.5 * (mu_center + jnp.roll(mu_center, 1, 2)) * (vel_center - jnp.roll(vel_center, 1, 3))
-    )
-    return total
+def ring(value, axis, dim):
+    size, length = lax.axis_size(axis), value.shape[dim]
+    up = [(i, (i + 1) % size) for i in range(size)]
+    down = [(j, i) for i, j in up]
+    last = lax.slice_in_dim(value, length - 1, length, axis=dim)
+    initial = lax.slice_in_dim(value, 0, 1, axis=dim)
+    return lax.ppermute(last, axis, up), lax.ppermute(initial, axis, down)
+
+
+def row_numbers(width):
+    return lax.broadcasted_iota(jnp.int32, (8, width), 0)
+
+
+def rows_of(strip):
+    return pl.ds(8 * strip, 8)
+
+
+def ahead_row(strip, value, take, edge, strips, rows):
+    following = take(8 * strip + 8) if strip + 1 < strips else edge
+    return jnp.where(rows == 7, following, pltpu.roll(value, 7, 0))
+
+
+def behind_row(strip, value, take, edge, rows):
+    previous = take(8 * strip - 1) if strip else edge
+    return jnp.where(rows == 0, previous, pltpu.roll(value, 1, 0))
+
+
+def plane_copies(source, low, high, target, semaphores, count):
+    def pick(ref, index):
+        return ref.at[:, index] if len(ref.shape) == 4 else ref.at[index]
+
+    def start_all():
+        pltpu.make_async_copy(pick(low, 0), pick(target, 0), semaphores.at[0]).start()
+
+        def body(i, state):
+            pltpu.make_async_copy(
+                pick(source, i), pick(target, i + 1), semaphores.at[i + 1]
+            ).start()
+            return state
+
+        lax.fori_loop(0, count, body, 0)
+        pltpu.make_async_copy(
+            pick(high, 0), pick(target, count + 1), semaphores.at[count + 1]
+        ).start()
+
+    def wait(index):
+        pltpu.make_async_copy(pick(low, 0), pick(target, index), semaphores.at[index]).wait()
+
+    return start_all, wait
+
+
+def await_planes(wait, step, planes):
+    @pl.when(step == 0)
+    def _():
+        wait(0)
+        wait(1)
+
+    for i in range(planes):
+        wait(step * planes + i + 2)
+
+
+anywhere = pl.BlockSpec(memory_space=pl.ANY)
+
+
+def viscosity_kernel_call(flow, x_sides, y_sides, warmth, with_heat):
+    _, x_local, y_local, z_cells = flow.shape
+    planes, strips, z_blocks = 2, y_local // 8, z_cells // 128
+
+    def kernel(flow_ref, low_ref, high_ref, before_ref, after_ref, warmth_ref, *rest):
+        outs, (cells, semaphores) = rest[:-2], rest[-2:]
+        step = pl.program_id(0)
+        start_all, wait = plane_copies(flow_ref, low_ref, high_ref, cells, semaphores, x_local)
+        pl.when(step == 0)(start_all)
+        await_planes(wait, step, planes)
+        rows = row_numbers(z_cells)
+
+        def plane(i, state):
+            j = step * planes + i
+            for s in range(strips):
+                along_x, along_y, along_z = [], [], []
+                for c in range(3):
+                    value = cells[c, j + 1, rows_of(s), :]
+
+                    def take(row):
+                        return cells[c, j + 1, pl.ds(row, 1), :]
+
+                    along_x.append(cells[c, j + 2, rows_of(s), :] - cells[c, j, rows_of(s), :])
+                    along_y.append(
+                        ahead_row(s, value, take, after_ref[c, i], strips, rows)
+                        - behind_row(s, value, take, before_ref[c, i], rows)
+                    )
+                    along_z.append(
+                        pltpu.roll(value, z_cells - 1, 1) - pltpu.roll(value, 1, 1)
+                    )
+                s_xy = along_y[0] + along_x[1]
+                s_xz = along_z[0] + along_x[2]
+                s_yz = along_z[1] + along_y[2]
+                extra = 0.5 * (
+                    along_x[0] * along_x[0] + along_y[1] * along_y[1] + along_z[2] * along_z[2]
+                ) + 0.25 * (s_xy * s_xy + s_xz * s_xz + s_yz * s_yz)
+                rate_sq = rate_base**2 + extra
+                value = jnp.exp(
+                    (0.5 / stress_exponent) * jnp.log(rate_sq)
+                    + (zener_energy / stress_exponent)
+                    * (1.0 / warmth_ref[i, rows_of(s), :] - 1.0)
+                )
+                mu = (
+                    jnp.log(value + jnp.sqrt(value * value + 1.0))
+                    * lax.rsqrt(rate_sq)
+                    * (1.0 / 3.0)
+                )
+                outs[0][i, rows_of(s), :] = mu
+                if with_heat:
+                    heat = mu * (rate_sq - rate_base**2)
+                    for b in range(z_blocks):
+                        outs[1][b, i, rows_of(s), :] = heat[:, b * 128 : (b + 1) * 128]
+            return state
+
+        lax.fori_loop(0, planes, plane, 0)
+
+    row_spec = pl.BlockSpec((3, planes, 1, z_cells), lambda i: (0, i, 0, 0))
+    cell_spec = pl.BlockSpec((planes, y_local, z_cells), lambda i: (i, 0, 0))
+    out_specs = [cell_spec]
+    out_shape = [jax.ShapeDtypeStruct((x_local, y_local, z_cells), jnp.float32)]
+    if with_heat:
+        out_specs.append(pl.BlockSpec((z_blocks, planes, y_local, 128), lambda i: (0, i, 0, 0)))
+        out_shape.append(jax.ShapeDtypeStruct((z_blocks, x_local, y_local, 128), jnp.float32))
+    return pl.pallas_call(
+        kernel,
+        grid=(x_local // planes,),
+        in_specs=[anywhere] * 3 + [row_spec, row_spec, cell_spec],
+        out_specs=out_specs,
+        out_shape=out_shape,
+        scratch_shapes=[
+            pltpu.VMEM((3, x_local + 2, y_local, z_cells), jnp.float32),
+            pltpu.SemaphoreType.DMA((x_local + 2,)),
+        ],
+        name="viscosity",
+    )(flow, *x_sides, *y_sides, warmth)
+
+
+def advance_kernel_call(flow, flow_x, flow_y, mu, mu_x, mu_y, push):
+    _, x_local, y_local, z_cells = flow.shape
+    planes, strips = 2, y_local // 8
+
+    def kernel(
+        flow_ref, flow_low, flow_high, flow_before, flow_after,
+        mu_ref, mu_low, mu_high, mu_before, mu_after, push_ref,
+        out_ref, cells, semaphores, mu_cells, mu_semaphores,
+    ):
+        step = pl.program_id(0)
+        start_flow, wait_flow = plane_copies(
+            flow_ref, flow_low, flow_high, cells, semaphores, x_local
+        )
+        start_mu, wait_mu = plane_copies(
+            mu_ref, mu_low, mu_high, mu_cells, mu_semaphores, x_local
+        )
+
+        @pl.when(step == 0)
+        def _():
+            start_mu()
+            start_flow()
+
+        await_planes(wait_mu, step, planes)
+        await_planes(wait_flow, step, planes)
+        rows = row_numbers(z_cells)
+
+        def plane(i, state):
+            j = step * planes + i
+            for s in range(strips):
+                m = mu_cells[j + 1, rows_of(s), :]
+
+                def take_mu(row):
+                    return mu_cells[j + 1, pl.ds(row, 1), :]
+
+                sum_x_ahead = m + mu_cells[j + 2, rows_of(s), :]
+                sum_x_behind = m + mu_cells[j, rows_of(s), :]
+                sum_y_ahead = m + ahead_row(s, m, take_mu, mu_after[i], strips, rows)
+                sum_y_behind = m + behind_row(s, m, take_mu, mu_before[i], rows)
+                sum_z_ahead = m + pltpu.roll(m, z_cells - 1, 1)
+                for c in range(3):
+                    value = cells[c, j + 1, rows_of(s), :]
+
+                    def take(row):
+                        return cells[c, j + 1, pl.ds(row, 1), :]
+
+                    flux_z = sum_z_ahead * (pltpu.roll(value, z_cells - 1, 1) - value)
+                    total = (
+                        sum_x_ahead * (cells[c, j + 2, rows_of(s), :] - value)
+                        - sum_x_behind * (value - cells[c, j, rows_of(s), :])
+                        + sum_y_ahead
+                        * (ahead_row(s, value, take, flow_after[c, i], strips, rows) - value)
+                        - sum_y_behind
+                        * (value - behind_row(s, value, take, flow_before[c, i], rows))
+                        + (flux_z - pltpu.roll(flux_z, 1, 1))
+                    )
+                    out_ref[c, i, rows_of(s), :] = value + time_step * (
+                        0.5 * total + push_ref[c, i, rows_of(s), :]
+                    )
+            return state
+
+        lax.fori_loop(0, planes, plane, 0)
+
+    row_spec = pl.BlockSpec((3, planes, 1, z_cells), lambda i: (0, i, 0, 0))
+    mu_row_spec = pl.BlockSpec((planes, 1, z_cells), lambda i: (i, 0, 0))
+    block = pl.BlockSpec((3, planes, y_local, z_cells), lambda i: (0, i, 0, 0))
+    return pl.pallas_call(
+        kernel,
+        grid=(x_local // planes,),
+        in_specs=[anywhere] * 3
+        + [row_spec, row_spec]
+        + [anywhere] * 3
+        + [mu_row_spec, mu_row_spec, block],
+        out_specs=block,
+        out_shape=jax.ShapeDtypeStruct(flow.shape, jnp.float32),
+        scratch_shapes=[
+            pltpu.VMEM((3, x_local + 2, y_local, z_cells), jnp.float32),
+            pltpu.SemaphoreType.DMA((x_local + 2,)),
+            pltpu.VMEM((x_local + 2, y_local, z_cells), jnp.float32),
+            pltpu.SemaphoreType.DMA((x_local + 2,)),
+        ],
+        name="advance",
+    )(flow, *flow_x, *flow_y, mu, *mu_x, *mu_y, push)
 
 
 def cosine_sine_basis(points, period, waves):
@@ -132,16 +304,47 @@
     return pl.BlockSpec(shape, lambda *index: (0,) * len(shape))
 
 
-def z_forward(divergence, count):
-    x_local, y_local, z_cells = divergence.shape
-    half, piece = z_cells // 2, z_cells // count
+def divergence_modes(flow, x_sides, y_sides, count):
+    _, x_local, y_local, z_cells = flow.shape
+    half, piece, strips = z_cells // 2, z_cells // count, y_local // 8
     step = min(8, x_local)
     even, odd, _ = z_tables(z_cells)
     tables = halves(even) + halves(odd)
 
-    def kernel(div_ref, even_high, even_low, odd_high, odd_low, out_ref):
-        rows = div_ref[...].reshape(step * y_local, z_cells)
-        first, second = rows[:, :half], rows[:, half:]
+    def kernel(
+        first_ref, low_ref, high_ref, second_ref, before_ref, after_ref, third_ref,
+        even_high, even_low, odd_high, odd_low, out_ref, cells, semaphores, work,
+    ):
+        start_all, wait = plane_copies(
+            first_ref.at[0], low_ref, high_ref, cells, semaphores, x_local
+        )
+        grid_step = pl.program_id(0)
+        pl.when(grid_step == 0)(start_all)
+        await_planes(wait, grid_step, step)
+        rows = row_numbers(z_cells)
+
+        def plane(i, state):
+            j = grid_step * step + i
+            for s in range(strips):
+                value = second_ref[0, i, rows_of(s), :]
+
+                def take(row):
+                    return second_ref[0, i, pl.ds(row, 1), :]
+
+                along = third_ref[0, i, rows_of(s), :]
+                work[i, rows_of(s), :] = 0.5 * (
+                    (cells[j + 2, rows_of(s), :] - cells[j, rows_of(s), :])
+                    + (
+                        ahead_row(s, value, take, after_ref[i], strips, rows)
+                        - behind_row(s, value, take, before_ref[i], rows)
+                    )
+                    + (pltpu.roll(along, z_cells - 1, 1) - pltpu.roll(along, 1, 1))
+                )
+            return state
+
+        lax.fori_loop(0, step, plane, 0)
+        lines = work[...].reshape(step * y_local, z_cells)
+        first, second = lines[:, :half], lines[:, half:]
         modes = jnp.concatenate(
             [
                 triple_product(split(first + second), (even_high[...], even_low[...])),
@@ -152,15 +355,29 @@
         for n in range(count):
             out_ref[n] = modes[:, n * piece : (n + 1) * piece].reshape(step, y_local, piece)
 
+    row_spec = pl.BlockSpec((step, 1, z_cells), lambda i: (i, 0, 0))
     return pl.pallas_call(
         kernel,
         grid=(x_local // step,),
-        in_specs=[pl.BlockSpec((step, y_local, z_cells), lambda i: (i, 0, 0))]
+        in_specs=[
+            anywhere,
+            anywhere,
+            anywhere,
+            pl.BlockSpec((1, step, y_local, z_cells), lambda i: (1, i, 0, 0)),
+            row_spec,
+            row_spec,
+            pl.BlockSpec((1, step, y_local, z_cells), lambda i: (2, i, 0, 0)),
+        ]
         + [whole(half, half)] * 4,
         out_specs=pl.BlockSpec((count, step, y_local, piece), lambda i: (0, i, 0, 0)),
         out_shape=jax.ShapeDtypeStruct((count, x_local, y_local, piece), jnp.float32),
-        name="z_forward",
-    )(divergence, *tables)
+        scratch_shapes=[
+            pltpu.VMEM((x_local + 2, y_local, z_cells), jnp.float32),
+            pltpu.SemaphoreType.DMA((x_local + 2,)),
+            pltpu.VMEM((step, y_local, z_cells), jnp.float32),
+        ],
+        name="divergence_modes",
+    )(flow, *x_sides, flow, *y_sides, flow, *tables)
 
 
 def z_inverse(spectrum):
@@ -374,25 +591,60 @@
     return z_inverse(turn(y_inverse(modes, carries, ratio, gain, count), "narrow"))
 
 
-def ring(value_up, value_down, axis):
-    size = lax.axis_size(axis)
-    up = [(i, (i + 1) % size) for i in range(size)]
-    down = [(j, i) for i, j in up]
-    return lax.ppermute(value_up, axis, up), lax.ppermute(value_down, axis, down)
-
-
-def substrate_advance(thermal_profile, spread_coefficient):
-    bordered_array = with_halo(thermal_profile, (("wide", 0), ("narrow", 1)), 1, False)
-    center = bordered_array[1:-1, 1:-1]
-    neighbour_voxels = (
-        bordered_array[2:, 1:-1]
-        + bordered_array[:-2, 1:-1]
-        + bordered_array[1:-1, 2:]
-        + bordered_array[1:-1, :-2]
-    )
-    ahead = jnp.pad(center[:, :, 1:], ((0, 0), (0, 0), (0, 1)))
-    behind = jnp.pad(center[:, :, :-1], ((0, 0), (0, 0), (1, 0)))
-    return center + spread_coefficient * (neighbour_voxels + ahead + behind - 6.0 * center)
+def correct(flow, pressure, y_sides):
+    _, x_local, y_local, z_cells = flow.shape
+    planes, strips = 2, y_local // 8
+
+    def kernel(flow_ref, pressure_ref, before_ref, after_ref, out_ref):
+        step = pl.program_id(0)
+        rows = row_numbers(z_cells)
+
+        def plane(i, state):
+            j = step * planes + i
+            for s in range(strips):
+                value = pressure_ref[j + 1, rows_of(s), :]
+
+                def take(row):
+                    return pressure_ref[j + 1, pl.ds(row, 1), :]
+
+                slopes = (
+                    pressure_ref[j + 2, rows_of(s), :] - pressure_ref[j, rows_of(s), :],
+                    ahead_row(s, value, take, after_ref[i], strips, rows)
+                    - behind_row(s, value, take, before_ref[i], rows),
+                    pltpu.roll(value, z_cells - 1, 1) - pltpu.roll(value, 1, 1),
+                )
+                for c in range(3):
+                    out_ref[c, i, rows_of(s), :] = flow_ref[c, i, rows_of(s), :] - 0.5 * slopes[c]
+            return state
+
+        lax.fori_loop(0, planes, plane, 0)
+
+    row_spec = pl.BlockSpec((planes, 1, z_cells), lambda i: (i, 0, 0))
+    block = pl.BlockSpec((3, planes, y_local, z_cells), lambda i: (0, i, 0, 0))
+    return pl.pallas_call(
+        kernel,
+        grid=(x_local // planes,),
+        in_specs=[block, whole(x_local + 2, y_local, z_cells), row_spec, row_spec],
+        out_specs=block,
+        out_shape=jax.ShapeDtypeStruct(flow.shape, jnp.float32),
+        name="correct",
+    )(flow, pressure, *y_sides)
+
+
+def conduct(profile, spread):
+    sides = (("wide", 0), ("narrow", 1))
+    spread = with_halo(spread, sides, STEPS - 1, False)
+    profile = with_halo(profile, sides, STEPS, False)
+    for step in range(STEPS):
+        center = profile[1:-1, 1:-1]
+        near = (
+            profile[2:, 1:-1] + profile[:-2, 1:-1] + profile[1:-1, 2:] + profile[1:-1, :-2]
+        )
+        ahead = jnp.pad(center[:, :, 1:], ((0, 0), (0, 0), (0, 1)))
+        behind = jnp.pad(center[:, :, :-1], ((0, 0), (0, 0), (1, 0)))
+        profile = center + spread * (near + ahead + behind - 6.0 * center)
+        spread = spread[1:-1, 1:-1]
+    return profile
 
 
 def per_device(
@@ -404,38 +656,42 @@
     source_owner_sheet,
     source_part_line,
 ):
-    zener = jnp.exp(zener_energy * (1.0 / tool_warmth_excess - 1.0))
-    base_pad = pad_cells(material_flow_vector)
-    current_pad = base_pad
-    current = material_flow_vector
+    flow_x = ring(material_flow_vector, "wide", 1)
+    flow_y = ring(material_flow_vector, "narrow", 2)
+    current, current_x, current_y = material_flow_vector, flow_x, flow_y
     for section in range(PASSES):
-        rate_sq = rate_squared(current_pad)
-        mu_field = viscosity(rate_sq, zener)
-        mu_padded = pad_cells(mu_field[None])[0]
-        current = material_flow_vector + time_step * (
-            viscous_term(mu_padded, base_pad) + tool_push_density
-        )
-        if section + 1 < PASSES:
-            current_pad = pad_cells(current)
-    heat_cells = mu_field * (rate_sq - rate_base**2)
-    along_x, along_y, along_z = gradients(pad_cells(current))
-    divergence = along_x[0] + along_y[1] + along_z[2]
-    pressure = project(z_forward(divergence, lax.axis_size("narrow")))
-    inner = pressure[1:-1]
-    below, above = ring(inner[:, -1:], inner[:, :1], "narrow")
-    tall = jnp.concatenate([below, inner, above], 1)
-    press_x = (pressure[2:] - pressure[:-2]) * 0.5
-    press_y = (tall[:, 2:] - tall[:, :-2]) * 0.5
-    press_z = (jnp.roll(inner, -1, 2) - jnp.roll(inner, 1, 2)) * 0.5
-    corrected_flow_vector = current - jnp.stack([press_x, press_y, press_z], 0)
-    blocks = heat_cells.reshape(-1, 128)
-    slab_ids = source_owner_sheet[:, 0]
+        last = section + 1 == PASSES
+        fields = viscosity_kernel_call(current, current_x, current_y, tool_warmth_excess, last)
+        mu_field = fields[0]
+        current = advance_kernel_call(
+            material_flow_vector,
+            flow_x,
+            flow_y,
+            mu_field,
+            ring(mu_field, "wide", 0),
+            ring(mu_field, "narrow", 1),
+            tool_push_density,
+        )
+        if not last:
+            current_x = ring(current, "wide", 1)
+            current_y = ring(current, "narrow", 2)
+    heat_cells = fields[1]
+    modes = divergence_modes(
+        current,
+        ring(current[0], "wide", 0),
+        ring(current[1], "narrow", 1),
+        lax.axis_size("narrow"),
+    )
+    pressure = project(modes)
+    corrected_flow_vector = correct(current, pressure, ring(pressure[1:-1], "narrow", 1))
+    z_blocks = heat_cells.shape[0]
     slab_count = lax.axis_size("wide")
     component_lines = substrate_warmth_excess.shape[0] * substrate_warmth_excess.shape[1]
+    targets = source_owner_sheet[:, 0] * component_lines + source_part_line
     partial_value = (
         jnp.zeros((slab_count * component_lines, 128), jnp.float32)
-        .at[slab_ids * component_lines + source_part_line]
-        .add(blocks)
+        .at[targets.reshape(-1, z_blocks).T.reshape(-1)]
+        .add(heat_cells.reshape(-1, 128))
     )
     substrate_energy_input = lax.psum_scatter(
         partial_value.reshape(slab_count, component_lines, 128),
@@ -446,9 +702,7 @@
     thermal_profile = substrate_warmth_excess + dissipation_factor * substrate_energy_input.reshape(
         substrate_warmth_excess.shape
     )
-    for section in range(STEPS):
-        thermal_profile = substrate_advance(thermal_profile, spread_coefficient)
-    return (corrected_flow_vector, thermal_profile)
+    return (corrected_flow_vector, conduct(thermal_profile, spread_coefficient))
 
 
 def solution(mesh):

time: 665 us -> 445 us (0.67)
  other arithmetic: 317 us -> 49.2 us
  Pallas kernels: 38.1 us -> 179 us
  local copies, waits for them, and re-layouts: 81.6 us -> 27 us
  waiting for transfers between devices: 98.8 us -> 79.5 us
  starting transfers between devices: 88.9 us -> 75.2 us
    pallas_call x1 -> x6, Pallas kernels: 5.96 us -> 148 us  [the longest x2 77.1 us: advance_kernel_call(): pl.pallas_call(kernel, grid=(x_local // planes,), in_specs=[anywhere] * 3...]
    mul x10 -> x1, other arithmetic: 131 us -> 0.03 us  [per_device(): targets = source_owner_sheet[:, 0] * component_lines + source_part_line]
    add x6 -> x3, other arithmetic: 96 us -> 1.15 us  [the longest x2 1.15 us: conduct(): profile = center + spread * (near + ahead + behind - 6.0 * center)]
    ppermute x16 -> x4, waiting for transfers between devices: 64.8 us -> 5.98 us  [with_halo(): after = lax.ppermute(initial, axis, down)]
    slice x14, local copies, waits for them, and re-layouts: 62 us -> 14.4 us  [the longest x11 13.9 us: ring(): initial = lax.slice_in_dim(value, 0, 1, axis=dim)]
    ppermute x2 -> x22, starting transfers between devices: 2.29 us -> 35.1 us  [ring(): return (lax.ppermute(last, axis, up), lax.ppermute(initial, axis, down))]
    ppermute x2 -> x22, waiting for transfers between devices: 0.01 us -> 31.5 us  [ring(): return (lax.ppermute(last, axis, up), lax.ppermute(initial, axis, down))]
    ppermute x16 -> x4, starting transfers between devices: 32.3 us -> 6.43 us  [with_halo(): after = lax.ppermute(initial, axis, down)]
  transfers between devices with their start and end apart: 38 -> 34, of which waited for: 17 -> 15; matrix products, arithmetic and copies ran while one was open for 20% -> 14% of each run, Pallas kernels for 4% -> 6%
where the time goes in v2:
time: 445 us; the launch traced here: 443 us
  Pallas kernels  179 us (40%)
  waiting for transfers between devices  79.5 us (18%)
  starting transfers between devices  75.2 us (17%)
  other arithmetic  49.2 us (11%)
  local copies, waits for them, and re-layouts  27 us (6%)
  blocking collectives  17.8 us (4%)
  between operations  14.5 us (3%)
    pallas_call x2, Pallas kernels, advance_kernel_call(): pl.pallas_call(kernel, grid=(x_local // planes,), in_specs=[anywhere] * 3...  77.1 us
    scatter-add x1, other arithmetic, per_device(): partial_value = jnp.zeros((slab_count * component_lines, 128), jnp.float3...  45.7 us
    pallas_call x2, Pallas kernels, viscosity_kernel_call(): pl.pallas_call(kernel, grid=(x_local // planes,), in_specs=[anywhere] * 3...  40.8 us
    ppermute x22, starting transfers between devices, ring(): return (lax.ppermute(last, axis, up), lax.ppermute(initial, axis, down))  35.1 us
    ppermute x22, waiting for transfers between devices, ring(): return (lax.ppermute(last, axis, up), lax.ppermute(initial, axis, down))  31.5 us
    ppermute x4, waiting for transfers between devices, with_halo(): before = lax.ppermute(last, axis, up)  21.5 us
    all_to_all x3, waiting for transfers between devices, turn(): return lax.all_to_all(value, axis, split_axis=0, concat_axis=0, tiled=True)  20.5 us
    pallas_call x1, Pallas kernels, correct(): pl.pallas_call(kernel, grid=(x_local // planes,), in_specs=[block, whole(...  18.1 us
  transfers between devices with their start and end apart: 34, of which 15 were waited for; matrix products, arithmetic and copies ran while one was open for 14% of the time, Pallas kernels for 6%

profile of v2, /device:TPU:1, one launch (start us, length us, event | category | flops | bytes accessed | tf_op | source)
XLA Modules:
  0.0 442.7 jit_solution(18315681569676786551)
XLA Ops:
  8.3 5.1 %collective-permute-start.1 = (f32[3,1,64,512]{3,2,1,0:T(8,128)S(1)}, f32[3,1,64,512]{3,2,1,0:T(8,128)S(1)}, u32[]{:S(2)}, u32[]{:S(2)}) collective-permute-start(f32[3,1,64,512]{3,2,1,0:T(8,128)S(1)} %get-tuple-element.18), channel_id=1, source_target_pairs={{4,0},{8,4},{12,8},{16,12},{20,16},{24,20},{28,24},{0,28},{5,1},{9... | collective-permute-start | bytes 1179656 | tf_op jit(solution)/shard_map/ppermute | solution.py:42
  17.9 5.1 %collective-permute-done.3.after_ref.flow_after = f32[3,32,1,512]{3,2,1,0:T(1,128)S(1)} collective-permute-done((f32[3,32,1,512]{3,2,1,0:T(1,128)S(1)}, f32[3,32,1,512]{3,2,1,0:T(1,128)S(1)}, u32[]{:S(2)}, u32[]{:S(2)}) %collective-permute-start.3) | collective-permute-done | bytes 196640 | tf_op jit(solution)/shard_map/ppermute | solution.py:42
  23.0 4.7 %collective-permute-done.1.high_ref.flow_high = f32[3,1,64,512]{3,2,1,0:T(8,128)S(1)} collective-permute-done((f32[3,1,64,512]{3,2,1,0:T(8,128)S(1)}, f32[3,1,64,512]{3,2,1,0:T(8,128)S(1)}, u32[]{:S(2)}, u32[]{:S(2)}) %collective-permute-start.1) | collective-permute-done | bytes 393248 | tf_op jit(solution)/shard_map/ppermute | solution.py:42
  29.4 19.9 %viscosity.2.mu_ref = f32[32,64,512]{2,1,0:T(8,128)} custom-call(f32[3,32,64,512]{3,2,1,0:T(8,128)} %flow_ref.5, f32[3,1,64,512]{3,2,1,0:T(8,128)} %copy-done.1, f32[3,1,64,512]{3,2,1,0:T(8,128)} %copy-done, f32[3,32,1,512]{3,2,1,0:T(1,128)} %copy-done.4, f32[3,32,1,512]{3,2,1,0:T(1,128)} %copy-done.3, f32[32,64,512]{2,1,0:T(8,128)} %warmth_ref.3), custom_call_target="tpu_custom_call" | custom-call | tf_op jit(solution)/shard_map/viscosity/pallas_call | solution.py:163
  62.4 38.5 %advance.2.flow_ref = f32[3,32,64,512]{3,2,1,0:T(8,128)} custom-call(f32[3,32,64,512]{3,2,1,0:T(8,128)} %flow_ref.5, f32[3,1,64,512]{3,2,1,0:T(8,128)} %copy-done.1, f32[3,1,64,512]{3,2,1,0:T(8,128)} %copy-done, f32[3,32,1,512]{3,2,1,0:T(1,128)} %copy-done.4, f32[3,32,1,512]{3,2,1,0:T(1,128)} %copy-done.3, f32[32,64,512]{2,1,0:T(8,128)} %viscosity.2.mu_ref, ...), custom_call_target="tpu_custom_call" | custom-call | tf_op jit(solution)/shard_map/advance/pallas_call | solution.py:242
  102.1 4.5 %collective-permute-start.9 = (f32[3,1,64,512]{3,2,1,0:T(8,128)S(1)}, f32[3,1,64,512]{3,2,1,0:T(8,128)S(1)}, u32[]{:S(2)}, u32[]{:S(2)}) collective-permute-start(f32[3,1,64,512]{3,2,1,0:T(8,128)S(1)} %get-tuple-element.14), channel_id=1, source_target_pairs={{4,0},{8,4},{12,8},{16,12},{20,16},{24,20},{28,24},{0,28},{5,1},{9... | collective-permute-start | bytes 1179656 | tf_op jit(solution)/shard_map/ppermute | solution.py:42
  110.7 5.7 %collective-permute-done.11.after_ref = f32[3,32,1,512]{3,2,1,0:T(1,128)S(1)} collective-permute-done((f32[3,32,1,512]{3,2,1,0:T(1,128)S(1)}, f32[3,32,1,512]{3,2,1,0:T(1,128)S(1)}, u32[]{:S(2)}, u32[]{:S(2)}) %collective-permute-start.11) | collective-permute-done | bytes 196640 | tf_op jit(solution)/shard_map/ppermute | solution.py:42
  121.0 20.9 %viscosity.3 = (f32[32,64,512]{2,1,0:T(8,128)}, f32[4,32,64,128]{3,2,1,0:T(8,128)}) custom-call(f32[3,32,64,512]{3,2,1,0:T(8,128)} %advance.2.flow_ref, f32[3,1,64,512]{3,2,1,0:T(8,128)} %copy-done.7, f32[3,1,64,512]{3,2,1,0:T(8,128)} %copy-done.6, f32[3,32,1,512]{3,2,1,0:T(1,128)} %copy-done.10, f32[3,32,1,512]{3,2,1,0:T(1,128)} %copy-done.9, ...), custom_call_target="tpu_custom_call" | custom-call | tf_op jit(solution)/shard_map/viscosity/pallas_call | solution.py:163
  143.0 5.2 %collective-permute-start.13 = (f32[1,64,512]{2,1,0:T(8,128)S(1)}, f32[1,64,512]{2,1,0:T(8,128)S(1)}, u32[]{:S(2)}, u32[]{:S(2)}) collective-permute-start(f32[1,64,512]{2,1,0:T(8,128)S(1)} %get-tuple-element.26), channel_id=1, source_target_pairs={{4,0},{8,4},{12,8},{16,12},{20,16},{24,20},{28,24},{0,28},{5,1},{9... | collective-permute-start | bytes 393224 | tf_op jit(solution)/shard_map/ppermute | solution.py:42
  155.3 38.5 %advance.3.first_ref.second_ref.third_ref.flow_ref = f32[3,32,64,512]{3,2,1,0:T(8,128)} custom-call(f32[3,32,64,512]{3,2,1,0:T(8,128)} %flow_ref.5, f32[3,1,64,512]{3,2,1,0:T(8,128)} %copy-done.1, f32[3,1,64,512]{3,2,1,0:T(8,128)} %copy-done, f32[3,32,1,512]{3,2,1,0:T(1,128)} %copy-done.4, f32[3,32,1,512]{3,2,1,0:T(1,128)} %copy-done.3, ...), custom_call_target="tpu_custom_call" | custom-call | tf_op jit(solution)/shard_map/advance/pallas_call | solution.py:242
  208.5 11.5 %divergence_modes.1 = f32[4,32,64,128]{3,2,1,0:T(8,128)} custom-call(f32[3,32,64,512]{3,2,1,0:T(8,128)} %advance.3.first_ref.second_ref.third_ref.flow_ref, f32[1,64,512]{2,1,0:T(8,128)} %copy-done.15, f32[1,64,512]{2,1,0:T(8,128)} %copy-done.12, f32[3,32,64,512]{3,2,1,0:T(8,128)} %advance.3.first_ref.second_ref.third_ref.flow_ref, ...), custom_call_target="tpu_custom_call" | custom-call | tf_op jit(solution)/shard_map/divergence_modes/pallas_call | solution.py:359
  220.1 7.8 %all-to-all-start = ((f32[4,32,64,128]{3,2,1,0:T(8,128)}), f32[4,32,64,128]{3,2,1,0:T(8,128)}, u32[]{:S(2)}, u32[]{:S(2)}) async-start(f32[4,32,64,128]{3,2,1,0:T(8,128)} %divergence_modes.1), calls=%async_computation | async-start | bytes 8388608 | tf_op jit(solution)/shard_map/all_to_all | solution.py:573
  229.5 45.7 %scatter_custom_fusion = f32[4096,128]{1,0:T(8,128)} fusion(s32[8192]{0:T(1024)S(1)} %bitcast.22, f32[8192,128]{1,0:T(8,128)} %bitcast.23, f32[]{:T(128)} %constant.26.clone.1), kind=kCustom, calls=%fused_computation.2 | custom fusion | flops 1048576 | bytes 2097664 | tf_op jit(solution)/shard_map/scatter-add | solution.py:694
  276.9 12.5 %y_forward.1 = (f32[32,256,128]{2,1,0:T(8,128)}, f32[8,4,32,128]{3,2,1,0:T(8,128)}) custom-call(f32[4,32,64,128]{3,2,1,0:T(8,128)} %all-to-all-done.in_ref, bf16[256,256]{1,0:T(8,128)(2,1)} %constant.74.clone.high_ref, bf16[256,256]{1,0:T(8,128)(2,1)} %constant.75.clone.low_ref, f32[256,128]{1,0:T(8,128)} %get-tuple-element.49.ratio_ref), custom_call_target="tpu_custom_call" | custom-call | tf_op jit(solution)/shard_map/y_forward/pallas_call | solution.py:443
  294.1 20.5 %all-to-all-done.1.in_ref = f32[8,4,32,128]{3,2,1,0:T(8,128)S(1)} async-done(((f32[8,4,32,128]{3,2,1,0:T(8,128)}), f32[8,4,32,128]{3,2,1,0:T(8,128)S(1)}, u32[]{:S(2)}, u32[]{:S(2)}) %all-to-all-start.1) | async-done | bytes 524320 | tf_op jit(solution)/shard_map/all_to_all | solution.py:573
  317.4 17.8 %all_to_all.20.carry_ref = f32[8,4,32,128]{3,2,1,0:T(8,128)} all-to-all(f32[8,4,32,128]{3,2,1,0:T(8,128)} %join_carries.1), channel_id=1, replica_groups=mesh['wide'=8,'narrow'=4] {'wide'}, dimensions={0} | all-to-all | bytes 1048576 | tf_op jit(solution)/shard_map/all_to_all | solution.py:573
  335.2 12.4 %y_inverse.1 = f32[4,34,64,128]{3,2,1,0:T(8,128)} custom-call(f32[32,256,128]{2,1,0:T(8,128)} %get-tuple-element.7.modes_ref, f32[8,4,32,128]{3,2,1,0:T(8,128)} %all_to_all.20.carry_ref, bf16[256,256]{1,0:T(8,128)(2,1)} %constant.76.clone.high_ref, bf16[256,256]{1,0:T(8,128)(2,1)} %constant.77.clone.low_ref, f32[256,128]{1,0:T(8,128)} %get-tuple-element.49.ratio_ref, ...), custom_call_target="tpu_custom_call" | custom-call | tf_op jit(solution)/shard_map/y_inverse/pallas_call | solution.py:551
  347.6 6.7 %all-to-all-start.3 = ((f32[4,34,64,128]{3,2,1,0:T(8,128)}), f32[4,34,64,128]{3,2,1,0:T(8,128)}, u32[]{:S(2)}, u32[]{:S(2)}) async-start(f32[4,34,64,128]{3,2,1,0:T(8,128)} %y_inverse.1), calls=%async_computation.3 | async-start | bytes 8912896 | tf_op jit(solution)/shard_map/all_to_all | solution.py:573
  359.8 4.0 collective-permute-start.22
  365.1 4.2 collective-permute-done.23
  369.4 4.9 %collective-permute-start.24 = (f32[22,3,128]{2,1,0:T(4,128)S(1)}, f32[22,3,128]{2,1,0:T(4,128)S(1)}, u32[]{:S(2)}, u32[]{:S(2)}) collective-permute-start(f32[22,3,128]{2,1,0:T(4,128)S(1)} %get-tuple-element.40), channel_id=1, source_target_pairs={{0,1},{1,2},{2,3},{4,5},{5,6},{6,7},{8,9},{9,10},{10,11},{12,13},{... | collective-permute-start | bytes 101384 | tf_op jit(solution)/shard_map/ppermute | solution.py:30
  381.7 21.5 %collective-permute-done.24 = f32[22,3,128]{2,1,0:T(4,128)S(1)} collective-permute-done((f32[22,3,128]{2,1,0:T(4,128)S(1)}, f32[22,3,128]{2,1,0:T(4,128)S(1)}, u32[]{:S(2)}, u32[]{:S(2)}) %collective-permute-start.24) | collective-permute-done | bytes 33824 | tf_op jit(solution)/shard_map/ppermute | solution.py:30
  406.2 5.2 %z_inverse.1.pressure_ref = f32[34,64,512]{2,1,0:T(8,128)} custom-call(f32[4,34,64,128]{3,2,1,0:T(8,128)} %all-to-all-done.3.in_ref, bf16[256,256]{1,0:T(8,128)(2,1)} %constant.78.clone.even_high, bf16[256,256]{1,0:T(8,128)(2,1)} %constant.79.clone.even_low, bf16[256,256]{1,0:T(8,128)(2,1)} %constant.80.clone.odd_high, bf16[256,256]{1,0:T(8,128)(2,1)} %constant.81.clone.odd_low), custom_call_target="tpu_custom_call" | custom-call | tf_op jit(solution)/shard_map/z_inverse/pallas_call | solution.py:400
  417.7 18.1 %correct.1 = f32[3,32,64,512]{3,2,1,0:T(8,128)} custom-call(f32[3,32,64,512]{3,2,1,0:T(8,128)} %advance.3.first_ref.second_ref.third_ref.flow_ref, f32[34,64,512]{2,1,0:T(8,128)} %z_inverse.1.pressure_ref, f32[32,1,512]{2,1,0:T(1,128)} %copy-done.24, f32[32,1,512]{2,1,0:T(1,128)} %copy-done.23), custom_call_target="tpu_custom_call" | custom-call | tf_op jit(solution)/shard_map/correct/pallas_call | solution.py:624
  (150 shorter events, 87.3 us)
Async XLA Ops:
  8.3 19.4 %collective-permute-start.1 = (f32[3,1,64,512]{3,2,1,0:T(8,128)S(1)}, f32[3,1,64,512]{3,2,1,0:T(8,128)S(1)}, u32[]{:S(2)}, u32[]{:S(2)}) collective-permute-start(f32[3,1,64,512]{3,2,1,0:T(8,128)S(1)} %get-tuple-element.18), channel_id=1, source_target_pairs={{4,0},{8,4},{12,8},{16,12},{20,16},{24,20},{28,24},{0,28},{5,1},{9... | collective-permute-start | bytes 1179656 | tf_op jit(solution)/shard_map/ppermute | solution.py:42
  13.5 15.1 %collective-permute-start = (f32[3,1,64,512]{3,2,1,0:T(8,128)S(1)}, f32[3,1,64,512]{3,2,1,0:T(8,128)S(1)}, u32[]{:S(2)}, u32[]{:S(2)}) collective-permute-start(f32[3,1,64,512]{3,2,1,0:T(8,128)S(1)} %get-tuple-element.19), channel_id=1, source_target_pairs={{0,4},{4,8},{8,12},{12,16},{16,20},{20,24},{24,28},{28,0},{1,5},{5... | collective-permute-start | bytes 1179656 | tf_op jit(solution)/shard_map/ppermute | solution.py:42
  15.8 7.2 %collective-permute-start.3 = (f32[3,32,1,512]{3,2,1,0:T(1,128)S(1)}, f32[3,32,1,512]{3,2,1,0:T(1,128)S(1)}, u32[]{:S(2)}, u32[]{:S(2)}) collective-permute-start(f32[3,32,1,512]{3,2,1,0:T(1,128)S(1)} %get-tuple-element.16), channel_id=1, source_target_pairs={{1,0},{2,1},{3,2},{0,3},{5,4},{6,5},{7,6},{4,7},{9,8},{10,9},{11,1... | collective-permute-start | bytes 589832 | tf_op jit(solution)/shard_map/ppermute | solution.py:42
  16.8 6.2 %collective-permute-start.2 = (f32[3,32,1,512]{3,2,1,0:T(1,128)S(1)}, f32[3,32,1,512]{3,2,1,0:T(1,128)S(1)}, u32[]{:S(2)}, u32[]{:S(2)}) collective-permute-start(f32[3,32,1,512]{3,2,1,0:T(1,128)S(1)} %get-tuple-element.17), channel_id=1, source_target_pairs={{0,1},{1,2},{2,3},{3,0},{4,5},{5,6},{6,7},{7,4},{8,9},{9,10},{10,1... | collective-permute-start | bytes 589832 | tf_op jit(solution)/shard_map/ppermute | solution.py:42
  50.3 10.8 %collective-permute-start.5 = (f32[1,64,512]{2,1,0:T(8,128)S(1)}, f32[1,64,512]{2,1,0:T(8,128)S(1)}, u32[]{:S(2)}, u32[]{:S(2)}) collective-permute-start(f32[1,64,512]{2,1,0:T(8,128)S(1)} %get-tuple-element.30), channel_id=1, source_target_pairs={{4,0},{8,4},{12,8},{16,12},{20,16},{24,20},{28,24},{0,28},{5,1},{9... | collective-permute-start | bytes 393224 | tf_op jit(solution)/shard_map/ppermute | solution.py:42
  53.6 7.5 %collective-permute-start.4 = (f32[1,64,512]{2,1,0:T(8,128)S(1)}, f32[1,64,512]{2,1,0:T(8,128)S(1)}, u32[]{:S(2)}, u32[]{:S(2)}) collective-permute-start(f32[1,64,512]{2,1,0:T(8,128)S(1)} %get-tuple-element.31), channel_id=1, source_target_pairs={{0,4},{4,8},{8,12},{12,16},{16,20},{20,24},{24,28},{28,0},{1,5},{5... | collective-permute-start | bytes 393224 | tf_op jit(solution)/shard_map/ppermute | solution.py:42
  54.9 6.2 %collective-permute-start.7 = (f32[32,1,512]{2,1,0:T(1,128)S(1)}, f32[32,1,512]{2,1,0:T(1,128)S(1)}, u32[]{:S(2)}, u32[]{:S(2)}) collective-permute-start(f32[32,1,512]{2,1,0:T(1,128)S(1)} %get-tuple-element.28), channel_id=1, source_target_pairs={{1,0},{2,1},{3,2},{0,3},{5,4},{6,5},{7,6},{4,7},{9,8},{10,9},{11,1... | collective-permute-start | bytes 196616 | tf_op jit(solution)/shard_map/ppermute | solution.py:42
  102.1 14.3 %collective-permute-start.9 = (f32[3,1,64,512]{3,2,1,0:T(8,128)S(1)}, f32[3,1,64,512]{3,2,1,0:T(8,128)S(1)}, u32[]{:S(2)}, u32[]{:S(2)}) collective-permute-start(f32[3,1,64,512]{3,2,1,0:T(8,128)S(1)} %get-tuple-element.14), channel_id=1, source_target_pairs={{4,0},{8,4},{12,8},{16,12},{20,16},{24,20},{28,24},{0,28},{5,1},{9... | collective-permute-start | bytes 1179656 | tf_op jit(solution)/shard_map/ppermute | solution.py:42
  106.6 13.6 %collective-permute-start.8 = (f32[3,1,64,512]{3,2,1,0:T(8,128)S(1)}, f32[3,1,64,512]{3,2,1,0:T(8,128)S(1)}, u32[]{:S(2)}, u32[]{:S(2)}) collective-permute-start(f32[3,1,64,512]{3,2,1,0:T(8,128)S(1)} %get-tuple-element.15), channel_id=1, source_target_pairs={{0,4},{4,8},{8,12},{12,16},{16,20},{20,24},{24,28},{28,0},{1,5},{5... | collective-permute-start | bytes 1179656 | tf_op jit(solution)/shard_map/ppermute | solution.py:42
  108.9 7.5 %collective-permute-start.11 = (f32[3,32,1,512]{3,2,1,0:T(1,128)S(1)}, f32[3,32,1,512]{3,2,1,0:T(1,128)S(1)}, u32[]{:S(2)}, u32[]{:S(2)}) collective-permute-start(f32[3,32,1,512]{3,2,1,0:T(1,128)S(1)} %get-tuple-element.12), channel_id=1, source_target_pairs={{1,0},{2,1},{3,2},{0,3},{5,4},{6,5},{7,6},{4,7},{9,8},{10,9},{11,1... | collective-permute-start | bytes 589832 | tf_op jit(solution)/shard_map/ppermute | solution.py:42
  109.6 6.8 %collective-permute-start.10 = (f32[3,32,1,512]{3,2,1,0:T(1,128)S(1)}, f32[3,32,1,512]{3,2,1,0:T(1,128)S(1)}, u32[]{:S(2)}, u32[]{:S(2)}) collective-permute-start(f32[3,32,1,512]{3,2,1,0:T(1,128)S(1)} %get-tuple-element.13), channel_id=1, source_target_pairs={{0,1},{1,2},{2,3},{3,0},{4,5},{5,6},{6,7},{7,4},{8,9},{9,10},{10,1... | collective-permute-start | bytes 589832 | tf_op jit(solution)/shard_map/ppermute | solution.py:42
  143.0 10.3 %collective-permute-start.13 = (f32[1,64,512]{2,1,0:T(8,128)S(1)}, f32[1,64,512]{2,1,0:T(8,128)S(1)}, u32[]{:S(2)}, u32[]{:S(2)}) collective-permute-start(f32[1,64,512]{2,1,0:T(8,128)S(1)} %get-tuple-element.26), channel_id=1, source_target_pairs={{4,0},{8,4},{12,8},{16,12},{20,16},{24,20},{28,24},{0,28},{5,1},{9... | collective-permute-start | bytes 393224 | tf_op jit(solution)/shard_map/ppermute | solution.py:42
  148.2 6.5 %collective-permute-start.12 = (f32[1,64,512]{2,1,0:T(8,128)S(1)}, f32[1,64,512]{2,1,0:T(8,128)S(1)}, u32[]{:S(2)}, u32[]{:S(2)}) collective-permute-start(f32[1,64,512]{2,1,0:T(8,128)S(1)} %get-tuple-element.27), channel_id=1, source_target_pairs={{0,4},{4,8},{8,12},{12,16},{16,20},{20,24},{24,28},{28,0},{1,5},{5... | collective-permute-start | bytes 393224 | tf_op jit(solution)/shard_map/ppermute | solution.py:42
  197.6 8.2 %collective-permute-start.17 = (f32[1,64,512]{2,1,0:T(8,128)S(1)}, f32[1,64,512]{2,1,0:T(8,128)S(1)}, u32[]{:S(2)}, u32[]{:S(2)}) collective-permute-start(f32[1,64,512]{2,1,0:T(8,128)S(1)} %get-tuple-element.10), channel_id=1, source_target_pairs={{4,0},{8,4},{12,8},{16,12},{20,16},{24,20},{28,24},{0,28},{5,1},{9... | collective-permute-start | bytes 393224 | tf_op jit(solution)/shard_map/ppermute | solution.py:42
  201.4 6.5 %collective-permute-start.16 = (f32[1,64,512]{2,1,0:T(8,128)S(1)}, f32[1,64,512]{2,1,0:T(8,128)S(1)}, u32[]{:S(2)}, u32[]{:S(2)}) collective-permute-start(f32[1,64,512]{2,1,0:T(8,128)S(1)} %get-tuple-element.11), channel_id=1, source_target_pairs={{0,4},{4,8},{8,12},{12,16},{16,20},{20,24},{24,28},{28,0},{1,5},{5... | collective-permute-start | bytes 393224 | tf_op jit(solution)/shard_map/ppermute | solution.py:42
  220.1 56.7 %all-to-all-start = ((f32[4,32,64,128]{3,2,1,0:T(8,128)}), f32[4,32,64,128]{3,2,1,0:T(8,128)}, u32[]{:S(2)}, u32[]{:S(2)}) async-start(f32[4,32,64,128]{3,2,1,0:T(8,128)} %divergence_modes.1), calls=%async_computation | async-start | bytes 8388608 | tf_op jit(solution)/shard_map/all_to_all | solution.py:573
  227.9 130.8 %reduce-scatter.2.cloned.1.call-start = ((), (), s32[]{:S(2)}) async-start(), calls=%async_computation.5 | async-start | bytes 2359296 | tf_op jit(solution)/shard_map/reduce_scatter | solution.py:696
  289.3 25.3 %all-to-all-start.1 = ((f32[8,4,32,128]{3,2,1,0:T(8,128)}), f32[8,4,32,128]{3,2,1,0:T(8,128)S(1)}, u32[]{:S(2)}, u32[]{:S(2)}) async-start(f32[8,4,32,128]{3,2,1,0:T(8,128)} %get-tuple-element.8), calls=%async_computation.1 | async-start | bytes 1048576 | tf_op jit(solution)/shard_map/all_to_all | solution.py:573
  347.6 58.6 %all-to-all-start.3 = ((f32[4,34,64,128]{3,2,1,0:T(8,128)}), f32[4,34,64,128]{3,2,1,0:T(8,128)}, u32[]{:S(2)}, u32[]{:S(2)}) async-start(f32[4,34,64,128]{3,2,1,0:T(8,128)} %y_inverse.1), calls=%async_computation.3 | async-start | bytes 8912896 | tf_op jit(solution)/shard_map/all_to_all | solution.py:573
  357.4 7.7 %collective-permute-start.27 = (f32[2,32,128]{2,1,0:T(8,128)S(1)}, f32[2,32,128]{2,1,0:T(8,128)S(1)}, u32[]{:S(2)}, u32[]{:S(2)}) collective-permute-start(f32[2,32,128]{2,1,0:T(8,128)S(1)} %get-tuple-element.44), channel_id=1, source_target_pairs={{4,0},{8,4},{12,8},{16,12},{20,16},{24,20},{28,24},{5,1},{9,5},{13... | collective-permute-start | bytes 98312 | tf_op jit(solution)/shard_map/ppermute | solution.py:31
  369.4 33.9 %collective-permute-start.24 = (f32[22,3,128]{2,1,0:T(4,128)S(1)}, f32[22,3,128]{2,1,0:T(4,128)S(1)}, u32[]{:S(2)}, u32[]{:S(2)}) collective-permute-start(f32[22,3,128]{2,1,0:T(4,128)S(1)} %get-tuple-element.40), channel_id=1, source_target_pairs={{0,1},{1,2},{2,3},{4,5},{5,6},{6,7},{8,9},{9,10},{10,11},{12,13},{... | collective-permute-start | bytes 101384 | tf_op jit(solution)/shard_map/ppermute | solution.py:30
  374.2 30.8 %collective-permute-start.25 = (f32[22,3,128]{2,1,0:T(4,128)S(1)}, f32[22,3,128]{2,1,0:T(4,128)S(1)}, u32[]{:S(2)}, u32[]{:S(2)}) collective-permute-start(f32[22,3,128]{2,1,0:T(4,128)S(1)} %get-tuple-element.41), channel_id=1, source_target_pairs={{1,0},{2,1},{3,2},{5,4},{6,5},{7,6},{9,8},{10,9},{11,10},{13,12},{... | collective-permute-start | bytes 101384 | tf_op jit(solution)/shard_map/ppermute | solution.py:31
  376.2 29.1 %collective-permute-start.28 = (f32[20,2,128]{2,1,0:T(2,128)S(1)}, f32[20,2,128]{2,1,0:T(2,128)S(1)}, u32[]{:S(2)}, u32[]{:S(2)}) collective-permute-start(f32[20,2,128]{2,1,0:T(2,128)S(1)} %get-tuple-element.42), channel_id=1, source_target_pairs={{0,1},{1,2},{2,3},{4,5},{5,6},{6,7},{8,9},{9,10},{10,11},{12,13},{... | collective-permute-start | bytes 61448 | tf_op jit(solution)/shard_map/ppermute | solution.py:30
  379.8 25.5 %collective-permute-start.29 = (f32[20,2,128]{2,1,0:T(2,128)S(1)}, f32[20,2,128]{2,1,0:T(2,128)S(1)}, u32[]{:S(2)}, u32[]{:S(2)}) collective-permute-start(f32[20,2,128]{2,1,0:T(2,128)S(1)} %get-tuple-element.43), channel_id=1, source_target_pairs={{1,0},{2,1},{3,2},{5,4},{6,5},{7,6},{9,8},{10,9},{11,10},{13,12},{... | collective-permute-start | bytes 61448 | tf_op jit(solution)/shard_map/ppermute | solution.py:31
  (38 other events, 163.8 us)
Sparse Core Ops, SparseCore 0:
  275.4 72.6 reduce-scatter.1

commit v3 on v1

--- a/solution.py
+++ b/solution.py
@@ -33,57 +33,361 @@
     return x
 
 
-def pad_cells(field):
-    return with_halo(field, (("wide", 1), ("narrow", 2)), 1, True)
-
-
-def gradients(bordered_array):
-    center = bordered_array[:, 1:-1, 1:-1]
-    along_x = (bordered_array[:, 2:, 1:-1] - bordered_array[:, :-2, 1:-1]) * 0.5
-    along_y = (bordered_array[:, 1:-1, 2:] - bordered_array[:, 1:-1, :-2]) * 0.5
-    along_z = (jnp.roll(center, -1, 3) - jnp.roll(center, 1, 3)) * 0.5
-    return (along_x, along_y, along_z)
-
-
-def rate_squared(bordered_array):
-    along_x, along_y, along_z = gradients(bordered_array)
-    s_xy = 0.5 * (along_y[0] + along_x[1])
-    s_xz = 0.5 * (along_z[0] + along_x[2])
-    s_yz = 0.5 * (along_z[1] + along_y[2])
-    total = (
-        along_x[0] ** 2 + along_y[1] ** 2 + along_z[2] ** 2 + 2.0 * (s_xy**2 + s_xz**2 + s_yz**2)
-    )
-    return rate_base**2 + 2.0 * total
-
-
-def inverse_sinh(value):
-    return jnp.log(value + jnp.sqrt(value * value + 1.0))
-
-
-def viscosity(rate_sq, zener):
-    rate = jnp.sqrt(rate_sq)
-    return inverse_sinh((rate * zener) ** (1.0 / stress_exponent)) / (3.0 * rate)
-
-
-def viscous_term(mu_padded, vel_padded):
-    mu_center = mu_padded[1:-1, 1:-1]
-    vel_center = vel_padded[:, 1:-1, 1:-1]
-    total = 0.5 * (mu_center + mu_padded[2:, 1:-1]) * (
-        vel_padded[:, 2:, 1:-1] - vel_center
-    ) - 0.5 * (mu_center + mu_padded[:-2, 1:-1]) * (vel_center - vel_padded[:, :-2, 1:-1])
-    total = (
-        total
-        + 0.5 * (mu_center + mu_padded[1:-1, 2:]) * (vel_padded[:, 1:-1, 2:] - vel_center)
-        - 0.5 * (mu_center + mu_padded[1:-1, :-2]) * (vel_center - vel_padded[:, 1:-1, :-2])
-    )
-    total = (
-        total
-        + 0.5
-        * (mu_center + jnp.roll(mu_center, -1, 2))
-        * (jnp.roll(vel_center, -1, 3) - vel_center)
-        - 0.5 * (mu_center + jnp.roll(mu_center, 1, 2)) * (vel_center - jnp.roll(vel_center, 1, 3))
-    )
-    return total
+def ring(value, axis, dim):
+    size, length = lax.axis_size(axis), value.shape[dim]
+    up = [(i, (i + 1) % size) for i in range(size)]
+    down = [(j, i) for i, j in up]
+    last = lax.slice_in_dim(value, length - 1, length, axis=dim)
+    initial = lax.slice_in_dim(value, 0, 1, axis=dim)
+    return lax.ppermute(last, axis, up), lax.ppermute(initial, axis, down)
+
+
+anywhere = pl.BlockSpec(memory_space=pl.ANY)
+in_vmem = pl.BlockSpec(memory_space=pltpu.VMEM)
+scaled_mu = 0.5 * time_step
+
+
+def row_numbers(width):
+    return lax.broadcasted_iota(jnp.int32, (8, width), 0)
+
+
+def rows_of(strip):
+    return pl.ds(8 * strip, 8)
+
+
+def pick(ref, index):
+    return ref.at[:, index] if len(ref.shape) == 4 else ref.at[index]
+
+
+class Planes:
+    def __init__(self, source, target, semaphores, listed=None):
+        self.source, self.target, self.semaphores = source, target, semaphores
+        self.listed = listed
+
+    def copy(self, slot, ref, plane):
+        return pltpu.make_async_copy(
+            pick(ref, plane), pick(self.target, slot), self.semaphores.at[slot]
+        )
+
+    def start(self, slot, plane=None):
+        if self.listed is None:
+            self.copy(slot, self.source, slot if plane is None else plane).start()
+        else:
+            self.copy(slot, *self.listed[slot]).start()
+
+    def wait(self, slot):
+        self.copy(slot, self.source, 0).wait()
+
+
+def edge_list(ref, low, high, x_local):
+    return [(low, 0), (ref, 0), (ref, 1), (ref, x_local - 2), (ref, x_local - 1), (high, 0)]
+
+
+def viscosity_plane(cells, slot, edges, warmth, warm_slot, outs, out_slot, y_local, z_cells):
+    strips, rows = y_local // 8, row_numbers(z_cells)
+    before, after = edges
+    values = [[cells[c, slot, rows_of(s), :] for s in range(strips)] for c in range(3)]
+    up = [[pltpu.roll(v, 7, 0) for v in row] for row in values]
+    down = [[pltpu.roll(v, 1, 0) for v in row] for row in values]
+    for s in range(strips):
+        along_x, along_y, along_z = [], [], []
+        for c in range(3):
+            value = values[c][s]
+            along_x.append(cells[c, slot + 1, rows_of(s), :] - cells[c, slot - 1, rows_of(s), :])
+            ahead = jnp.where(rows == 7, up[c][s + 1] if s + 1 < strips else after(c), up[c][s])
+            behind = jnp.where(rows == 0, down[c][s - 1] if s else before(c), down[c][s])
+            along_y.append(ahead - behind)
+            along_z.append(pltpu.roll(value, z_cells - 1, 1) - pltpu.roll(value, 1, 1))
+        s_xy = along_y[0] + along_x[1]
+        s_xz = along_z[0] + along_x[2]
+        s_yz = along_z[1] + along_y[2]
+        extra = 0.5 * (
+            along_x[0] * along_x[0] + along_y[1] * along_y[1] + along_z[2] * along_z[2]
+        ) + 0.25 * (s_xy * s_xy + s_xz * s_xz + s_yz * s_yz)
+        rate_sq = rate_base**2 + extra
+        value = jnp.exp(
+            (0.5 / stress_exponent) * jnp.log(rate_sq)
+            + (zener_energy / stress_exponent) * (1.0 / warmth[warm_slot, rows_of(s), :] - 1.0)
+        )
+        square = value * value + 1.0
+        mu = jnp.log(value + square * lax.rsqrt(square)) * lax.rsqrt(rate_sq)
+        outs[0][out_slot, rows_of(s), :] = mu * (scaled_mu / 3.0)
+        if len(outs) > 1:
+            heat = (mu * (1.0 / 3.0)) * extra
+            for b in range(z_cells // 128):
+                outs[1][b, out_slot, rows_of(s), :] = heat[:, b * 128 : (b + 1) * 128]
+
+
+def viscosity_call(flow, y_sides, warmth, with_heat, x_sides=None, inner=None):
+    _, x_local, y_local, z_cells = flow.shape
+    z_blocks = z_cells // 128
+    edge = x_sides is not None
+    slots, made = (6, 2) if edge else (x_local, x_local - 2)
+    outputs = 2 if with_heat else 1
+
+    def kernel(*refs):
+        flow_ref, before_ref, after_ref, warmth_ref = refs[:4]
+        rest = list(refs[4:])
+        listed = None
+        if edge:
+            low, high = rest[:2]
+            listed = edge_list(flow_ref, low, high, x_local)
+            rest = rest[2 + outputs :]
+        out_refs, rest = rest[:outputs], rest[outputs:]
+        cells, cell_sem, warm, warm_sem = rest[:4]
+        outs, out_sems = rest[4 : 4 + outputs], rest[4 + outputs :]
+        flow_planes = Planes(flow_ref, cells, cell_sem, listed)
+        warm_planes = Planes(warmth_ref, warm, warm_sem)
+
+        def plane_of(i):
+            return i * (x_local - 1) if edge else i + 1
+
+        def slot_of(i):
+            return 3 * i + 1 if edge else i + 1
+
+        def stored(k, i):
+            return pltpu.make_async_copy(
+                pick(outs[k], i), pick(out_refs[k], plane_of(i)), out_sems[k].at[i]
+            )
+
+        if edge:
+            for slot in range(6):
+                flow_planes.start(slot)
+            for i in range(2):
+                warm_planes.start(i, plane_of(i))
+        else:
+            flow_planes.start(0)
+            flow_planes.start(1)
+
+            def begin(i, state):
+                flow_planes.start(i + 2)
+                warm_planes.start(i, i + 1)
+                return state
+
+            lax.fori_loop(0, made, begin, 0)
+            flow_planes.wait(0)
+            flow_planes.wait(1)
+
+        def body(i, state):
+            slot, plane = slot_of(i), plane_of(i)
+            if edge:
+                flow_planes.wait(slot - 1)
+                flow_planes.wait(slot)
+            flow_planes.wait(slot + 1)
+            warm_planes.wait(i)
+            viscosity_plane(
+                cells,
+                slot,
+                (lambda c: before_ref[c, plane], lambda c: after_ref[c, plane]),
+                warm,
+                i,
+                outs,
+                i,
+                y_local,
+                z_cells,
+            )
+            for k in range(outputs):
+                stored(k, i).start()
+            return state
+
+        lax.fori_loop(0, made, body, 0)
+
+        def finish(i, state):
+            for k in range(outputs):
+                stored(k, i).wait()
+            return state
+
+        lax.fori_loop(0, made, finish, 0)
+
+    shapes = [(x_local, y_local, z_cells), (z_blocks, x_local, y_local, 128)][:outputs]
+    held = [(made, y_local, z_cells), (z_blocks, made, y_local, 128)][:outputs]
+    operands = [flow, *y_sides, warmth]
+    specs = [anywhere, in_vmem, in_vmem, anywhere]
+    aliases = {}
+    if edge:
+        operands += [*x_sides, *inner]
+        specs += [anywhere] * (2 + outputs)
+        aliases = {6 + k: k for k in range(outputs)}
+    return pl.pallas_call(
+        kernel,
+        in_specs=specs,
+        out_specs=[anywhere] * outputs,
+        out_shape=[jax.ShapeDtypeStruct(shape, jnp.float32) for shape in shapes],
+        input_output_aliases=aliases,
+        scratch_shapes=[
+            pltpu.VMEM((3, slots, y_local, z_cells), jnp.float32),
+            pltpu.SemaphoreType.DMA((slots,)),
+            pltpu.VMEM((made, y_local, z_cells), jnp.float32),
+            pltpu.SemaphoreType.DMA((made,)),
+        ]
+        + [pltpu.VMEM(shape, jnp.float32) for shape in held]
+        + [pltpu.SemaphoreType.DMA((made,))] * outputs,
+        compiler_params=pltpu.CompilerParams(vmem_limit_bytes=vmem_limit),
+        name="viscosity_edge" if edge else "viscosity_inner",
+    )(*operands)
+
+
+vmem_limit = 48 << 20
+
+
+def advance_plane(cells, mu, slot, edges, push, out_slot, flux, y_local, z_cells):
+    strips, rows = y_local // 8, row_numbers(z_cells)
+    flow_before, flow_after, mu_before, mu_after = edges
+    m = [mu[slot, rows_of(s), :] for s in range(strips)]
+    m_up = [pltpu.roll(v, 7, 0) for v in m]
+    sums_y = [
+        m[s] + jnp.where(rows == 7, m_up[s + 1] if s + 1 < strips else mu_after(), m_up[s])
+        for s in range(strips)
+    ]
+    first_sum = mu_before() + mu[slot, pl.ds(0, 1), :]
+    values = [[cells[c, slot, rows_of(s), :] for s in range(strips)] for c in range(3)]
+    up = [[pltpu.roll(v, 7, 0) for v in row] for row in values]
+    carried = [
+        first_sum * (cells[c, slot, pl.ds(0, 1), :] - flow_before(c)) for c in range(3)
+    ]
+    for s in range(strips):
+        sum_x = m[s] + mu[slot + 1, rows_of(s), :]
+        sum_z = m[s] + pltpu.roll(m[s], z_cells - 1, 1)
+        for c in range(3):
+            value = values[c][s]
+            flux_x = sum_x * (cells[c, slot + 1, rows_of(s), :] - value)
+            ahead = jnp.where(
+                rows == 7, up[c][s + 1] if s + 1 < strips else flow_after(c), up[c][s]
+            )
+            flux_y = sums_y[s] * (ahead - value)
+            flux_z = sum_z * (pltpu.roll(value, z_cells - 1, 1) - value)
+            turned = pltpu.roll(flux_y, 1, 0)
+            total = (flux_x - flux[c, rows_of(s), :]) + (
+                flux_y - jnp.where(rows == 0, carried[c], turned)
+            ) + (flux_z - pltpu.roll(flux_z, 1, 1))
+            flux[c, rows_of(s), :] = flux_x
+            carried[c] = turned
+            push[c, out_slot, rows_of(s), :] = (
+                value + time_step * push[c, out_slot, rows_of(s), :] + total
+            )
+
+
+def first_flux(cells, mu, slot, flux, y_local):
+    for s in range(y_local // 8):
+        sum_x = mu[slot - 1, rows_of(s), :] + mu[slot, rows_of(s), :]
+        for c in range(3):
+            flux[c, rows_of(s), :] = sum_x * (
+                cells[c, slot, rows_of(s), :] - cells[c, slot - 1, rows_of(s), :]
+            )
+
+
+def advance_call(flow, flow_y, mu, mu_y, push, flow_x=None, mu_x=None, inner=None):
+    _, x_local, y_local, z_cells = flow.shape
+    edge = flow_x is not None
+    slots, made = (6, 2) if edge else (x_local, x_local - 2)
+
+    def kernel(*refs):
+        flow_ref, flow_before, flow_after, mu_ref, mu_before, mu_after, push_ref = refs[:7]
+        rest = refs[7:]
+        flow_listed = mu_listed = None
+        if edge:
+            flow_listed = edge_list(flow_ref, rest[0], rest[1], x_local)
+            mu_listed = edge_list(mu_ref, rest[2], rest[3], x_local)
+            rest = rest[5:]
+        out_ref, cells, cell_sem, mu_cells, mu_sem, work, work_sem, out_sem, flux = rest
+        flow_planes = Planes(flow_ref, cells, cell_sem, flow_listed)
+        mu_planes = Planes(mu_ref, mu_cells, mu_sem, mu_listed)
+        push_planes = Planes(push_ref, work, work_sem)
+
+        def plane_of(i):
+            return i * (x_local - 1) if edge else i + 1
+
+        def stored(i):
+            return pltpu.make_async_copy(
+                pick(work, i), pick(out_ref, plane_of(i)), out_sem.at[i]
+            )
+
+        if edge:
+            for slot in range(6):
+                flow_planes.start(slot)
+                mu_planes.start(slot)
+            for i in range(2):
+                push_planes.start(i, plane_of(i))
+        else:
+            for slot in range(2):
+                flow_planes.start(slot)
+                mu_planes.start(slot)
+
+            def begin(i, state):
+                flow_planes.start(i + 2)
+                mu_planes.start(i + 2)
+                push_planes.start(i, i + 1)
+                return state
+
+            lax.fori_loop(0, made, begin, 0)
+            for slot in range(2):
+                flow_planes.wait(slot)
+                mu_planes.wait(slot)
+            first_flux(cells, mu_cells, 1, flux, y_local)
+
+        def body(i, state):
+            slot, plane = (3 * i + 1 if edge else i + 1), plane_of(i)
+            if edge:
+                for back in range(2):
+                    flow_planes.wait(slot - back)
+                    mu_planes.wait(slot - back)
+                first_flux(cells, mu_cells, slot, flux, y_local)
+            flow_planes.wait(slot + 1)
+            mu_planes.wait(slot + 1)
+            push_planes.wait(i)
+            advance_plane(
+                cells,
+                mu_cells,
+                slot,
+                (
+                    lambda c: flow_before[c, plane],
+                    lambda c: flow_after[c, plane],
+                    lambda: mu_before[plane],
+                    lambda: mu_after[plane],
+                ),
+                work,
+                i,
+                flux,
+                y_local,
+                z_cells,
+            )
+            stored(i).start()
+            return state
+
+        lax.fori_loop(0, made, body, 0)
+
+        def finish(i, state):
+            stored(i).wait()
+            return state
+
+        lax.fori_loop(0, made, finish, 0)
+
+    operands = [flow, *flow_y, mu, *mu_y, push]
+    specs = [anywhere, in_vmem, in_vmem, anywhere, in_vmem, in_vmem, anywhere]
+    aliases = {}
+    if edge:
+        operands += [*flow_x, *mu_x, inner]
+        specs += [anywhere] * 5
+        aliases = {11: 0}
+    return pl.pallas_call(
+        kernel,
+        in_specs=specs,
+        out_specs=anywhere,
+        out_shape=jax.ShapeDtypeStruct(flow.shape, jnp.float32),
+        input_output_aliases=aliases,
+        scratch_shapes=[
+            pltpu.VMEM((3, slots, y_local, z_cells), jnp.float32),
+            pltpu.SemaphoreType.DMA((slots,)),
+            pltpu.VMEM((slots, y_local, z_cells), jnp.float32),
+            pltpu.SemaphoreType.DMA((slots,)),
+            pltpu.VMEM((3, made, y_local, z_cells), jnp.float32),
+            pltpu.SemaphoreType.DMA((made,)),
+            pltpu.SemaphoreType.DMA((made,)),
+            pltpu.VMEM((3, y_local, z_cells), jnp.float32),
+        ],
+        compiler_params=pltpu.CompilerParams(vmem_limit_bytes=vmem_limit),
+        name="advance_edge" if edge else "advance_inner",
+    )(*operands)
 
 
 def cosine_sine_basis(points, period, waves):
@@ -132,63 +436,282 @@
     return pl.BlockSpec(shape, lambda *index: (0,) * len(shape))
 
 
-def z_forward(divergence, count):
-    x_local, y_local, z_cells = divergence.shape
-    half, piece = z_cells // 2, z_cells // count
+def modes_of(lines, even_high, even_low, odd_high, odd_low):
+    half = lines.shape[1] // 2
+    first, second = lines[:, :half], lines[:, half:]
+    return jnp.concatenate(
+        [
+            triple_product(split(first + second), (even_high[...], even_low[...])),
+            triple_product(split(first - second), (odd_high[...], odd_low[...])),
+        ],
+        1,
+    )
+
+
+def cells_of(modes, even_high, even_low, odd_high, odd_low):
+    half = modes.shape[1] // 2
+    first = triple_product(split(modes[:, :half]), (even_high[...], even_low[...]))
+    second = triple_product(split(modes[:, half:]), (odd_high[...], odd_low[...]))
+    return jnp.concatenate([first + second, first - second], 1)
+
+
+def divergence_modes(flow, count):
+    _, x_local, y_local, z_cells = flow.shape
+    half, piece, strips = z_cells // 2, z_cells // count, y_local // 8
     step = min(8, x_local)
     even, odd, _ = z_tables(z_cells)
     tables = halves(even) + halves(odd)
 
-    def kernel(div_ref, even_high, even_low, odd_high, odd_low, out_ref):
-        rows = div_ref[...].reshape(step * y_local, z_cells)
-        first, second = rows[:, :half], rows[:, half:]
-        modes = jnp.concatenate(
-            [
-                triple_product(split(first + second), (even_high[...], even_low[...])),
-                triple_product(split(first - second), (odd_high[...], odd_low[...])),
-            ],
-            1,
-        )
-        for n in range(count):
-            out_ref[n] = modes[:, n * piece : (n + 1) * piece].reshape(step, y_local, piece)
+    def kernel(
+        flow_ref, even_high, even_low, odd_high, odd_low, out_ref,
+        cells, semaphores, work, made, out_sem,
+    ):
+        planes = Planes(flow_ref, cells, semaphores)
+        rows = row_numbers(z_cells)
+
+        def begin(i, state):
+            planes.start(i)
+            return state
+
+        lax.fori_loop(0, x_local, begin, 0)
+        planes.wait(0)
+
+        def stored(k):
+            part = pl.ds(k * step, step)
+            return pltpu.make_async_copy(made.at[:, part], out_ref.at[:, part], out_sem.at[k])
+
+        def group(k, state):
+            def plane(i, state):
+                j = k * step + i
+
+                @pl.when(j + 1 < x_local)
+                def _():
+                    planes.wait(j + 1)
+
+                nearer = jnp.where(j > 0, 0.5, 0.0)
+                further = jnp.where(j + 1 < x_local, 0.5, 0.0)
+                last, following = jnp.maximum(j - 1, 0), jnp.minimum(j + 1, x_local - 1)
+                across = [cells[1, j, rows_of(s), :] for s in range(strips)]
+                up = [pltpu.roll(v, 7, 0) for v in across]
+                down = [pltpu.roll(v, 1, 0) for v in across]
+                for s in range(strips):
+                    ahead = jnp.where(rows == 7, up[s + 1] if s + 1 < strips else 0.0, up[s])
+                    behind = jnp.where(rows == 0, down[s - 1] if s else 0.0, down[s])
+                    along = cells[2, j, rows_of(s), :]
+                    work[i, rows_of(s), :] = (
+                        further * cells[0, following, rows_of(s), :]
+                        - nearer * cells[0, last, rows_of(s), :]
+                    ) + 0.5 * (
+                        (ahead - behind)
+                        + (pltpu.roll(along, z_cells - 1, 1) - pltpu.roll(along, 1, 1))
+                    )
+                return state
+
+            lax.fori_loop(0, step, plane, 0)
+            modes = modes_of(
+                work[...].reshape(step * y_local, z_cells), even_high, even_low, odd_high, odd_low
+            )
+            for n in range(count):
+                made[n, pl.ds(k * step, step)] = modes[:, n * piece : (n + 1) * piece].reshape(
+                    step, y_local, piece
+                )
+            stored(k).start()
+            return state
+
+        groups = x_local // step
+        lax.fori_loop(0, groups, group, 0)
+        for k in range(groups):
+            stored(k).wait()
 
     return pl.pallas_call(
         kernel,
-        grid=(x_local // step,),
-        in_specs=[pl.BlockSpec((step, y_local, z_cells), lambda i: (i, 0, 0))]
-        + [whole(half, half)] * 4,
-        out_specs=pl.BlockSpec((count, step, y_local, piece), lambda i: (0, i, 0, 0)),
+        in_specs=[anywhere] + [in_vmem] * 4,
+        out_specs=anywhere,
         out_shape=jax.ShapeDtypeStruct((count, x_local, y_local, piece), jnp.float32),
-        name="z_forward",
-    )(divergence, *tables)
-
-
-def z_inverse(spectrum):
+        scratch_shapes=[
+            pltpu.VMEM((3, x_local, y_local, z_cells), jnp.float32),
+            pltpu.SemaphoreType.DMA((x_local,)),
+            pltpu.VMEM((step, y_local, z_cells), jnp.float32),
+            pltpu.VMEM((count, x_local, y_local, piece), jnp.float32),
+            pltpu.SemaphoreType.DMA((x_local // step,)),
+        ],
+        compiler_params=pltpu.CompilerParams(vmem_limit_bytes=vmem_limit),
+        name="divergence_modes",
+    )(flow, *tables)
+
+
+def add_halo_modes(modes, x_sides, y_sides):
+    count, x_local, y_local, piece = modes.shape
+    z_cells = count * piece
+    even, odd, _ = z_tables(z_cells)
+    tables = halves(even) + halves(odd)
+
+    def kernel(
+        modes_ref, low_ref, high_ref, before_ref, after_ref,
+        even_high, even_low, odd_high, odd_low, out_ref, ends, lines, semaphores,
+    ):
+        def moves(back):
+            pairs = [
+                (ends.at[k], modes_ref.at[:, plane])
+                for k, plane in enumerate((0, x_local - 1))
+            ] + [
+                (lines.at[k], modes_ref.at[:, 1 : x_local - 1, 8 * s : 8 * s + 8])
+                for k, s in enumerate((0, y_local // 8 - 1))
+            ]
+            if back:
+                pairs = [
+                    (ends.at[k], out_ref.at[:, plane])
+                    for k, plane in enumerate((0, x_local - 1))
+                ] + [
+                    (lines.at[k], out_ref.at[:, 1 : x_local - 1, 8 * s : 8 * s + 8])
+                    for k, s in enumerate((0, y_local // 8 - 1))
+                ]
+                return [
+                    pltpu.make_async_copy(here, there, semaphores.at[4 + i])
+                    for i, (here, there) in enumerate(pairs)
+                ]
+            return [
+                pltpu.make_async_copy(there, here, semaphores.at[i])
+                for i, (here, there) in enumerate(pairs)
+            ]
+
+        loads, stores = moves(False), moves(True)
+        for load in loads:
+            load.start()
+        added = modes_of(
+            jnp.concatenate(
+                [-0.5 * low_ref[0], 0.5 * high_ref[0], -0.5 * before_ref[...], 0.5 * after_ref[...]],
+                0,
+            ),
+            even_high,
+            even_low,
+            odd_high,
+            odd_low,
+        )
+        for load in loads:
+            load.wait()
+        rows = row_numbers(piece)
+        for n in range(count):
+            block = added[:, n * piece : (n + 1) * piece]
+            side = [block[2 * y_local + k * x_local :][:x_local] for k in range(2)]
+            for k, plane in enumerate((0, x_local - 1)):
+                ends[k, n] = ends[k, n] + block[k * y_local : (k + 1) * y_local]
+                for j, (strip, row) in enumerate(((0, 0), (y_local // 8 - 1, 7))):
+                    part = pl.ds(8 * strip, 8)
+                    ends[k, n, part, :] = ends[k, n, part, :] + jnp.where(
+                        rows == row, side[j][plane : plane + 1], 0.0
+                    )
+            for j, row in enumerate((0, 7)):
+                for x in range(1, x_local - 1):
+                    lines[j, n, x - 1] = lines[j, n, x - 1] + jnp.where(
+                        rows == row, side[j][x : x + 1], 0.0
+                    )
+        for store in stores:
+            store.start()
+        for store in stores:
+            store.wait()
+
+    return pl.pallas_call(
+        kernel,
+        in_specs=[anywhere] + [in_vmem] * 8,
+        out_specs=anywhere,
+        out_shape=jax.ShapeDtypeStruct(modes.shape, jnp.float32),
+        input_output_aliases={0: 0},
+        scratch_shapes=[
+            pltpu.VMEM((2, count, y_local, piece), jnp.float32),
+            pltpu.VMEM((2, count, x_local - 2, 8, piece), jnp.float32),
+            pltpu.SemaphoreType.DMA((8,)),
+        ],
+        compiler_params=pltpu.CompilerParams(vmem_limit_bytes=16 << 20),
+        name="add_halo_modes",
+    )(modes, *x_sides, *y_sides, *tables)
+
+
+def corrected(flow, spectrum, y_sides):
     count, planes, y_local, piece = spectrum.shape
-    z_cells = count * piece
-    half, step = z_cells // 2, planes // 2
+    x_local, z_cells = planes - 2, count * piece
+    strips, part = y_local // 8, planes // 2
     even, odd, _ = z_tables(z_cells)
     tables = halves(even.T) + halves(odd.T)
 
-    def kernel(in_ref, even_high, even_low, odd_high, odd_low, out_ref):
-        modes = jnp.concatenate(
-            [in_ref[n].reshape(step * y_local, piece) for n in range(count)], 1
+    def kernel(
+        flow_ref, in_ref, before_ref, after_ref,
+        even_high, even_low, odd_high, odd_low, out_ref,
+        modes, mode_sem, pressure, sides, work, out_sem,
+    ):
+        table_refs = (even_high, even_low, odd_high, odd_low)
+
+        def load(k):
+            span = pl.ds(k * part, part)
+            return pltpu.make_async_copy(in_ref.at[:, span], modes.at[:, span], mode_sem.at[k])
+
+        load(0).start()
+        load(1).start()
+        sides[...] = cells_of(
+            jnp.concatenate(
+                [
+                    jnp.concatenate([ref[n] for n in range(count)], 1)
+                    for ref in (before_ref, after_ref)
+                ],
+                0,
+            ),
+            *table_refs,
         )
-        first = triple_product(split(modes[:, :half]), (even_high[...], even_low[...]))
-        second = triple_product(split(modes[:, half:]), (odd_high[...], odd_low[...]))
-        out_ref[...] = jnp.concatenate([first + second, first - second], 1).reshape(
-            step, y_local, z_cells
-        )
+        rows = row_numbers(z_cells)
+
+        def stored(i):
+            return pltpu.make_async_copy(pick(work, i), pick(out_ref, i), out_sem.at[i])
+
+        def plane(j, state):
+            values = [pressure[j + 1, rows_of(s), :] for s in range(strips)]
+            up = [pltpu.roll(v, 7, 0) for v in values]
+            down = [pltpu.roll(v, 1, 0) for v in values]
+            for s in range(strips):
+                ahead = up[s + 1] if s + 1 < strips else sides[pl.ds(x_local + j, 1), :]
+                behind = down[s - 1] if s else sides[pl.ds(j, 1), :]
+                slopes = (
+                    pressure[j + 2, rows_of(s), :] - pressure[j, rows_of(s), :],
+                    jnp.where(rows == 7, ahead, up[s]) - jnp.where(rows == 0, behind, down[s]),
+                    pltpu.roll(values[s], z_cells - 1, 1) - pltpu.roll(values[s], 1, 1),
+                )
+                for c in range(3):
+                    work[c, j, rows_of(s), :] = flow_ref[c, j, rows_of(s), :] - 0.5 * slopes[c]
+            stored(j).start()
+            return state
+
+        for k in range(2):
+            load(k).wait()
+            span = pl.ds(k * part, part)
+            pressure[span] = cells_of(
+                jnp.concatenate(
+                    [modes[n, span].reshape(part * y_local, piece) for n in range(count)], 1
+                ),
+                *table_refs,
+            ).reshape(part, y_local, z_cells)
+            lax.fori_loop(k * (part - 2), (part - 2) if k == 0 else x_local, plane, 0)
+
+        def finish(i, state):
+            stored(i).wait()
+            return state
+
+        lax.fori_loop(0, x_local, finish, 0)
 
     return pl.pallas_call(
         kernel,
-        grid=(planes // step,),
-        in_specs=[pl.BlockSpec((count, step, y_local, piece), lambda i: (0, i, 0, 0))]
-        + [whole(half, half)] * 4,
-        out_specs=pl.BlockSpec((step, y_local, z_cells), lambda i: (i, 0, 0)),
-        out_shape=jax.ShapeDtypeStruct((planes, y_local, z_cells), jnp.float32),
-        name="z_inverse",
-    )(spectrum, *tables)
+        in_specs=[in_vmem, anywhere] + [in_vmem] * 6,
+        out_specs=anywhere,
+        out_shape=jax.ShapeDtypeStruct(flow.shape, jnp.float32),
+        scratch_shapes=[
+            pltpu.VMEM(spectrum.shape, jnp.float32),
+            pltpu.SemaphoreType.DMA((2,)),
+            pltpu.VMEM((planes, y_local, z_cells), jnp.float32),
+            pltpu.VMEM((2 * x_local, z_cells), jnp.float32),
+            pltpu.VMEM(flow.shape, jnp.float32),
+            pltpu.SemaphoreType.DMA((x_local,)),
+        ],
+        compiler_params=pltpu.CompilerParams(vmem_limit_bytes=36 << 20),
+        name="corrected",
+    )(flow, spectrum, *y_sides, *tables)
 
 
 def y_forward(spectrum, ratio, wide_count):
@@ -371,28 +894,23 @@
     own_ratio = lax.dynamic_slice_in_dim(ratio, lax.axis_index("wide") * share, share)
     modes, carries = y_forward(turn(spectrum, "narrow"), ratio, wide_count)
     carries = turn(join_carries(turn(carries, "wide"), own_ratio, x_local // 2), "wide")
-    return z_inverse(turn(y_inverse(modes, carries, ratio, gain, count), "narrow"))
-
-
-def ring(value_up, value_down, axis):
-    size = lax.axis_size(axis)
-    up = [(i, (i + 1) % size) for i in range(size)]
-    down = [(j, i) for i, j in up]
-    return lax.ppermute(value_up, axis, up), lax.ppermute(value_down, axis, down)
-
-
-def substrate_advance(thermal_profile, spread_coefficient):
-    bordered_array = with_halo(thermal_profile, (("wide", 0), ("narrow", 1)), 1, False)
-    center = bordered_array[1:-1, 1:-1]
-    neighbour_voxels = (
-        bordered_array[2:, 1:-1]
-        + bordered_array[:-2, 1:-1]
-        + bordered_array[1:-1, 2:]
-        + bordered_array[1:-1, :-2]
-    )
-    ahead = jnp.pad(center[:, :, 1:], ((0, 0), (0, 0), (0, 1)))
-    behind = jnp.pad(center[:, :, :-1], ((0, 0), (0, 0), (1, 0)))
-    return center + spread_coefficient * (neighbour_voxels + ahead + behind - 6.0 * center)
+    return turn(y_inverse(modes, carries, ratio, gain, count), "narrow")
+
+
+def conduct(profile, spread):
+    sides = (("wide", 0), ("narrow", 1))
+    spread = with_halo(spread, sides, STEPS - 1, False)
+    profile = with_halo(profile, sides, STEPS, False)
+    for step in range(STEPS):
+        center = profile[1:-1, 1:-1]
+        near = (
+            profile[2:, 1:-1] + profile[:-2, 1:-1] + profile[1:-1, 2:] + profile[1:-1, :-2]
+        )
+        ahead = jnp.pad(center[:, :, 1:], ((0, 0), (0, 0), (0, 1)))
+        behind = jnp.pad(center[:, :, :-1], ((0, 0), (0, 0), (1, 0)))
+        profile = center + spread * (near + ahead + behind - 6.0 * center)
+        spread = spread[1:-1, 1:-1]
+    return profile
 
 
 def per_device(
@@ -404,38 +922,36 @@
     source_owner_sheet,
     source_part_line,
 ):
-    zener = jnp.exp(zener_energy * (1.0 / tool_warmth_excess - 1.0))
-    base_pad = pad_cells(material_flow_vector)
-    current_pad = base_pad
-    current = material_flow_vector
+    flow = material_flow_vector
+    flow_x, flow_y = ring(flow, "wide", 1), ring(flow, "narrow", 2)
+    current, current_x, current_y = flow, flow_x, flow_y
     for section in range(PASSES):
-        rate_sq = rate_squared(current_pad)
-        mu_field = viscosity(rate_sq, zener)
-        mu_padded = pad_cells(mu_field[None])[0]
-        current = material_flow_vector + time_step * (
-            viscous_term(mu_padded, base_pad) + tool_push_density
-        )
-        if section + 1 < PASSES:
-            current_pad = pad_cells(current)
-    heat_cells = mu_field * (rate_sq - rate_base**2)
-    along_x, along_y, along_z = gradients(pad_cells(current))
-    divergence = along_x[0] + along_y[1] + along_z[2]
-    pressure = project(z_forward(divergence, lax.axis_size("narrow")))
-    inner = pressure[1:-1]
-    below, above = ring(inner[:, -1:], inner[:, :1], "narrow")
-    tall = jnp.concatenate([below, inner, above], 1)
-    press_x = (pressure[2:] - pressure[:-2]) * 0.5
-    press_y = (tall[:, 2:] - tall[:, :-2]) * 0.5
-    press_z = (jnp.roll(inner, -1, 2) - jnp.roll(inner, 1, 2)) * 0.5
-    corrected_flow_vector = current - jnp.stack([press_x, press_y, press_z], 0)
-    blocks = heat_cells.reshape(-1, 128)
-    slab_ids = source_owner_sheet[:, 0]
+        last = section + 1 == PASSES
+        inner = viscosity_call(current, current_y, tool_warmth_excess, last)
+        fields = viscosity_call(current, current_y, tool_warmth_excess, last, current_x, inner)
+        mu = fields[0]
+        mu_x, mu_y = ring(mu, "wide", 0), ring(mu, "narrow", 1)
+        inner = advance_call(flow, flow_y, mu, mu_y, tool_push_density)
+        current = advance_call(flow, flow_y, mu, mu_y, tool_push_density, flow_x, mu_x, inner)
+        if not last:
+            current_x, current_y = ring(current, "wide", 1), ring(current, "narrow", 2)
+    heat_cells = fields[1]
+    end_x = ring(current[0], "wide", 0)
+    end_y = [side[:, 0] for side in ring(current[1], "narrow", 1)]
+    modes = divergence_modes(current, lax.axis_size("narrow"))
+    spectrum = project(add_halo_modes(modes, end_x, end_y))
+    inner = spectrum[:, 1:-1]
+    corrected_flow_vector = corrected(
+        current, spectrum, [side[:, :, 0] for side in ring(inner, "narrow", 2)]
+    )
+    z_blocks = heat_cells.shape[0]
     slab_count = lax.axis_size("wide")
     component_lines = substrate_warmth_excess.shape[0] * substrate_warmth_excess.shape[1]
+    targets = source_owner_sheet[:, 0] * component_lines + source_part_line
     partial_value = (
         jnp.zeros((slab_count * component_lines, 128), jnp.float32)
-        .at[slab_ids * component_lines + source_part_line]
-        .add(blocks)
+        .at[targets.reshape(-1, z_blocks).T.reshape(-1)]
+        .add(heat_cells.reshape(-1, 128))
     )
     substrate_energy_input = lax.psum_scatter(
         partial_value.reshape(slab_count, component_lines, 128),
@@ -446,9 +962,7 @@
     thermal_profile = substrate_warmth_excess + dissipation_factor * substrate_energy_input.reshape(
         substrate_warmth_excess.shape
     )
-    for section in range(STEPS):
-        thermal_profile = substrate_advance(thermal_profile, spread_coefficient)
-    return (corrected_flow_vector, thermal_profile)
+    return (corrected_flow_vector, conduct(thermal_profile, spread_coefficient))
 
 
 def solution(mesh):

time: 665 us -> 416 us (0.63)
  other arithmetic: 317 us -> 49.2 us
  Pallas kernels: 38.1 us -> 170 us
  local copies, waits for them, and re-layouts: 81.6 us -> 26.2 us
  waiting for transfers between devices: 98.8 us -> 68.3 us
  starting transfers between devices: 88.9 us -> 67.7 us
    pallas_call x2 -> x11, Pallas kernels: 11.1 us -> 143 us  [the longest x4 81.7 us: advance_call(): pl.pallas_call(kernel, in_specs=specs, out_specs=anywhere, out_shape=jax....]
    mul x10 -> x1, other arithmetic: 131 us -> 0.03 us  [per_device(): targets = source_owner_sheet[:, 0] * component_lines + source_part_line]
    add x6 -> x3, other arithmetic: 96 us -> 1.16 us  [the longest x2 1.15 us: conduct(): profile = center + spread * (near + ahead + behind - 6.0 * center)]
    ppermute x16 -> x4, waiting for transfers between devices: 64.8 us -> 5.89 us  [with_halo(): after = lax.ppermute(initial, axis, down)]
    slice x14 -> x15, local copies, waits for them, and re-layouts: 62 us -> 12.8 us  [the longest x11 9.52 us: ring(): initial = lax.slice_in_dim(value, 0, 1, axis=dim)]
    ppermute x2 -> x22, starting transfers between devices: 2.29 us -> 30.3 us  [ring(): return (lax.ppermute(last, axis, up), lax.ppermute(initial, axis, down))]
    ppermute x16 -> x4, starting transfers between devices: 32.3 us -> 6.43 us  [with_halo(): after = lax.ppermute(initial, axis, down)]
    broadcast_in_dim x2 -> x0, other arithmetic: 22 us -> none  [per_device(): mu_padded = pad_cells(mu_field[None])[0]]
  transfers between devices with their start and end apart: 38 -> 34, of which waited for: 17 -> 14; matrix products, arithmetic and copies ran while one was open for 20% -> 14% of each run, Pallas kernels for 4% -> 35%
where the time goes in v3:
time: 416 us; the launch traced here: 414 us
  Pallas kernels  170 us (41%)
  waiting for transfers between devices  68.3 us (16%)
  starting transfers between devices  67.7 us (16%)
  other arithmetic  49.2 us (12%)
  local copies, waits for them, and re-layouts  26.2 us (6%)
  blocking collectives  17.9 us (4%)
  between operations  14.7 us (4%)
    pallas_call x4, Pallas kernels, advance_call(): pl.pallas_call(kernel, in_specs=specs, out_specs=anywhere, out_shape=jax....  81.7 us
    scatter-add x1, other arithmetic, per_device(): partial_value = jnp.zeros((slab_count * component_lines, 128), jnp.float3...  45.7 us
    pallas_call x4, Pallas kernels, viscosity_call(): pl.pallas_call(kernel, in_specs=specs, out_specs=[anywhere] * outputs, ou...  42.8 us
    ppermute x22, starting transfers between devices, ring(): return (lax.ppermute(last, axis, up), lax.ppermute(initial, axis, down))  30.3 us
    ppermute x4, waiting for transfers between devices, with_halo(): before = lax.ppermute(last, axis, up)  21.4 us
    ppermute x22, waiting for transfers between devices, ring(): return (lax.ppermute(last, axis, up), lax.ppermute(initial, axis, down))  21.2 us
    all_to_all x3, waiting for transfers between devices, turn(): return lax.all_to_all(value, axis, split_axis=0, concat_axis=0, tiled=True)  19.8 us
    all_to_all x1, blocking collectives, turn(): return lax.all_to_all(value, axis, split_axis=0, concat_axis=0, tiled=True)  17.9 us
  transfers between devices with their start and end apart: 34, of which 14 were waited for; matrix products, arithmetic and copies ran while one was open for 14% of the time, Pallas kernels for 35%

profile of v3, /device:TPU:1, one launch (start us, length us, event | category | flops | bytes accessed | tf_op | source)
XLA Modules:
  0.0 414.3 jit_solution(16048586022582475019)
XLA Ops:
  23.7 17.8 %viscosity_inner.2.refs_6_ = f32[32,64,512]{2,1,0:T(8,128)S(1)} custom-call(f32[3,32,64,512]{3,2,1,0:T(8,128)} %refs_0_.11, f32[3,32,1,512]{3,2,1,0:T(1,128)S(1)} %collective-permute-done.refs_1_, f32[3,32,1,512]{3,2,1,0:T(1,128)S(1)} %collective-permute-done.1.refs_2_, f32[32,64,512]{2,1,0:T(8,128)} %refs_3_.7), custom_call_target="tpu_custom_call" | custom-call | tf_op jit(solution)/shard_map/viscosity_inner/pallas_call | solution.py:211
  44.2 4.1 %collective-permute-start.7 = (f32[1,64,512]{2,1,0:T(8,128)S(1)}, f32[1,64,512]{2,1,0:T(8,128)S(1)}, u32[]{:S(2)}, u32[]{:S(2)}) collective-permute-start(f32[1,64,512]{2,1,0:T(8,128)S(1)} %get-tuple-element.32), channel_id=1, source_target_pairs={{4,0},{8,4},{12,8},{16,12},{20,16},{24,20},{28,24},{0,28},{5,1},{9... | collective-permute-start | bytes 393224 | tf_op jit(solution)/shard_map/ppermute | solution.py:42
  53.6 35.8 %advance_inner.2.refs_11_ = f32[3,32,64,512]{3,2,1,0:T(8,128)} custom-call(f32[3,32,64,512]{3,2,1,0:T(8,128)} %refs_0_.11, f32[3,32,1,512]{3,2,1,0:T(1,128)S(1)} %collective-permute-done.refs_1_, f32[3,32,1,512]{3,2,1,0:T(1,128)S(1)} %collective-permute-done.1.refs_2_, f32[32,64,512]{2,1,0:T(8,128)S(1)} %viscosity_edge.2.refs_3_, ...), custom_call_target="tpu_custom_call" | custom-call | tf_op jit(solution)/shard_map/advance_inner/pallas_call | solution.py:372
  89.4 5.1 %advance_edge.2.refs_0_ = f32[3,32,64,512]{3,2,1,0:T(8,128)} custom-call(f32[3,32,64,512]{3,2,1,0:T(8,128)} %refs_0_.11, f32[3,32,1,512]{3,2,1,0:T(1,128)S(1)} %collective-permute-done.refs_1_, f32[3,32,1,512]{3,2,1,0:T(1,128)S(1)} %collective-permute-done.1.refs_2_, f32[32,64,512]{2,1,0:T(8,128)S(1)} %viscosity_edge.2.refs_3_, ...), custom_call_target="tpu_custom_call", output_to_operand_aliasing={{}: (11, {})} | custom-call | tf_op jit(solution)/shard_map/advance_edge/pallas_call | solution.py:372
  95.8 4.1 %collective-permute-start.11 = (f32[3,1,64,512]{3,2,1,0:T(8,128)S(1)}, f32[3,1,64,512]{3,2,1,0:T(8,128)S(1)}, u32[]{:S(2)}, u32[]{:S(2)}) collective-permute-start(f32[3,1,64,512]{3,2,1,0:T(8,128)S(1)} %get-tuple-element.16), channel_id=1, source_target_pairs={{4,0},{8,4},{12,8},{16,12},{20,16},{24,20},{28,24},{0,28},{5,1},{9... | collective-permute-start | bytes 1179656 | tf_op jit(solution)/shard_map/ppermute | solution.py:42
  103.0 4.3 %collective-permute-done.8.refs_1_ = f32[3,32,1,512]{3,2,1,0:T(1,128)S(1)} collective-permute-done((f32[3,32,1,512]{3,2,1,0:T(1,128)S(1)}, f32[3,32,1,512]{3,2,1,0:T(1,128)S(1)}, u32[]{:S(2)}, u32[]{:S(2)}) %collective-permute-start.8) | collective-permute-done | bytes 196640 | tf_op jit(solution)/shard_map/ppermute | solution.py:42
  108.3 19.1 %viscosity_inner.3 = (f32[32,64,512]{2,1,0:T(8,128)S(1)}, f32[4,32,64,128]{3,2,1,0:T(8,128)}) custom-call(f32[3,32,64,512]{3,2,1,0:T(8,128)} %advance_edge.2.refs_0_, f32[3,32,1,512]{3,2,1,0:T(1,128)S(1)} %collective-permute-done.8.refs_1_, f32[3,32,1,512]{3,2,1,0:T(1,128)S(1)} %collective-permute-done.9.refs_2_, f32[32,64,512]{2,1,0:T(8,128)} %refs_3_.7), custom_call_target="tpu_custom_call" | custom-call | tf_op jit(solution)/shard_map/viscosity_inner/pallas_call | solution.py:211
  130.9 4.1 %collective-permute-start.15 = (f32[1,64,512]{2,1,0:T(8,128)S(1)}, f32[1,64,512]{2,1,0:T(8,128)S(1)}, u32[]{:S(2)}, u32[]{:S(2)}) collective-permute-start(f32[1,64,512]{2,1,0:T(8,128)S(1)} %get-tuple-element.28), channel_id=1, source_target_pairs={{4,0},{8,4},{12,8},{16,12},{20,16},{24,20},{28,24},{0,28},{5,1},{9... | collective-permute-start | bytes 393224 | tf_op jit(solution)/shard_map/ppermute | solution.py:42
  140.8 35.8 %advance_inner.3.refs_11_ = f32[3,32,64,512]{3,2,1,0:T(8,128)} custom-call(f32[3,32,64,512]{3,2,1,0:T(8,128)} %refs_0_.11, f32[3,32,1,512]{3,2,1,0:T(1,128)S(1)} %collective-permute-done.refs_1_, f32[3,32,1,512]{3,2,1,0:T(1,128)S(1)} %collective-permute-done.1.refs_2_, f32[32,64,512]{2,1,0:T(8,128)S(1)} %get-tuple-element.10.refs_3_, ...), custom_call_target="tpu_custom_call" | custom-call | tf_op jit(solution)/shard_map/advance_inner/pallas_call | solution.py:372
  176.6 5.1 %advance_edge.3.flow_ref = f32[3,32,64,512]{3,2,1,0:T(8,128)} custom-call(f32[3,32,64,512]{3,2,1,0:T(8,128)} %refs_0_.11, f32[3,32,1,512]{3,2,1,0:T(1,128)S(1)} %collective-permute-done.refs_1_, f32[3,32,1,512]{3,2,1,0:T(1,128)S(1)} %collective-permute-done.1.refs_2_, f32[32,64,512]{2,1,0:T(8,128)S(1)} %get-tuple-element.10.refs_3_, ...), custom_call_target="tpu_custom_call", output_to_operand_aliasing={{}: (11, {})} | custom-call | tf_op jit(solution)/shard_map/advance_edge/pallas_call | solution.py:372
  188.0 4.1 %collective-permute-start.17 = (f32[1,64,512]{2,1,0:T(8,128)S(1)}, f32[1,64,512]{2,1,0:T(8,128)S(1)}, u32[]{:S(2)}, u32[]{:S(2)}) collective-permute-start(f32[1,64,512]{2,1,0:T(8,128)S(1)} %get-tuple-element.14), channel_id=1, source_target_pairs={{4,0},{8,4},{12,8},{16,12},{20,16},{24,20},{28,24},{0,28},{5,1},{9... | collective-permute-start | bytes 393224 | tf_op jit(solution)/shard_map/ppermute | solution.py:42
  193.3 8.6 %divergence_modes.1.modes_ref = f32[4,32,64,128]{3,2,1,0:T(8,128)S(1)} custom-call(f32[3,32,64,512]{3,2,1,0:T(8,128)} %advance_edge.3.flow_ref, bf16[256,256]{1,0:T(8,128)(2,1)S(1)} %copy-done.2, bf16[256,256]{1,0:T(8,128)(2,1)S(1)} %copy-done.3, bf16[256,256]{1,0:T(8,128)(2,1)S(1)} %copy-done.4, bf16[256,256]{1,0:T(8,128)(2,1)S(1)} %copy-done.5), custom_call_target="tpu_custom_call" | custom-call | tf_op jit(solution)/shard_map/divergence_modes/pallas_call | solution.py:526
  204.9 5.0 %all-to-all-start = ((f32[4,32,64,128]{3,2,1,0:T(8,128)}), f32[4,32,64,128]{3,2,1,0:T(8,128)}, u32[]{:S(2)}, u32[]{:S(2)}) async-start(f32[4,32,64,128]{3,2,1,0:T(8,128)} %copy-done.1), calls=%async_computation | async-start | bytes 8388608 | tf_op jit(solution)/shard_map/all_to_all | solution.py:879
  211.6 45.7 %scatter_custom_fusion = f32[4096,128]{1,0:T(8,128)} fusion(s32[8192]{0:T(1024)S(1)} %bitcast.37, f32[8192,128]{1,0:T(8,128)} %bitcast.29, f32[]{:T(128)} %constant.26.clone.1), kind=kCustom, calls=%fused_computation.2 | custom fusion | flops 1048576 | bytes 2097664 | tf_op jit(solution)/shard_map/scatter-add | solution.py:954
  258.9 12.5 %y_forward.1 = (f32[32,256,128]{2,1,0:T(8,128)}, f32[8,4,32,128]{3,2,1,0:T(8,128)}) custom-call(f32[4,32,64,128]{3,2,1,0:T(8,128)} %all-to-all-done.in_ref, bf16[256,256]{1,0:T(8,128)(2,1)} %constant.74.clone.high_ref, bf16[256,256]{1,0:T(8,128)(2,1)} %constant.75.clone.low_ref, f32[256,128]{1,0:T(8,128)} %get-tuple-element.53.ratio_ref), custom_call_target="tpu_custom_call" | custom-call | tf_op jit(solution)/shard_map/y_forward/pallas_call | solution.py:749
  276.2 19.8 %all-to-all-done.1.in_ref = f32[8,4,32,128]{3,2,1,0:T(8,128)S(1)} async-done(((f32[8,4,32,128]{3,2,1,0:T(8,128)}), f32[8,4,32,128]{3,2,1,0:T(8,128)S(1)}, u32[]{:S(2)}, u32[]{:S(2)}) %all-to-all-start.1) | async-done | bytes 524320 | tf_op jit(solution)/shard_map/all_to_all | solution.py:879
  298.8 17.9 %all_to_all.20.carry_ref = f32[8,4,32,128]{3,2,1,0:T(8,128)} all-to-all(f32[8,4,32,128]{3,2,1,0:T(8,128)} %join_carries.1), channel_id=1, replica_groups=mesh['wide'=8,'narrow'=4] {'wide'}, dimensions={0} | all-to-all | bytes 1048576 | tf_op jit(solution)/shard_map/all_to_all | solution.py:879
  316.6 12.5 %y_inverse.1 = f32[4,34,64,128]{3,2,1,0:T(8,128)} custom-call(f32[32,256,128]{2,1,0:T(8,128)} %get-tuple-element.11.modes_ref, f32[8,4,32,128]{3,2,1,0:T(8,128)} %all_to_all.20.carry_ref, bf16[256,256]{1,0:T(8,128)(2,1)} %constant.76.clone.high_ref, bf16[256,256]{1,0:T(8,128)(2,1)} %constant.77.clone.low_ref, f32[256,128]{1,0:T(8,128)} %get-tuple-element.53.ratio_ref, ...), custom_call_target="tpu_custom_call" | custom-call | tf_op jit(solution)/shard_map/y_inverse/pallas_call | solution.py:857
  329.1 6.8 %all-to-all-start.3 = ((f32[4,34,64,128]{3,2,1,0:T(8,128)}), f32[4,34,64,128]{3,2,1,0:T(8,128)}, u32[]{:S(2)}, u32[]{:S(2)}) async-start(f32[4,34,64,128]{3,2,1,0:T(8,128)} %y_inverse.1), calls=%async_computation.3 | async-start | bytes 8912896 | tf_op jit(solution)/shard_map/all_to_all | solution.py:879
  346.8 4.1 collective-permute-done.23
  350.9 4.9 %collective-permute-start.24 = (f32[22,3,128]{2,1,0:T(4,128)S(1)}, f32[22,3,128]{2,1,0:T(4,128)S(1)}, u32[]{:S(2)}, u32[]{:S(2)}) collective-permute-start(f32[22,3,128]{2,1,0:T(4,128)S(1)} %get-tuple-element.44), channel_id=1, source_target_pairs={{0,1},{1,2},{2,3},{4,5},{5,6},{6,7},{8,9},{9,10},{10,11},{12,13},{... | collective-permute-start | bytes 101384 | tf_op jit(solution)/shard_map/ppermute | solution.py:30
  363.4 21.4 %collective-permute-done.24 = f32[22,3,128]{2,1,0:T(4,128)S(1)} collective-permute-done((f32[22,3,128]{2,1,0:T(4,128)S(1)}, f32[22,3,128]{2,1,0:T(4,128)S(1)}, u32[]{:S(2)}, u32[]{:S(2)}) %collective-permute-start.24) | collective-permute-done | bytes 33824 | tf_op jit(solution)/shard_map/ppermute | solution.py:30
  393.6 4.6 %copy-done = f32[3,32,64,512]{3,2,1,0:T(8,128)S(1)} copy-done((f32[3,32,64,512]{3,2,1,0:T(8,128)S(1)}, f32[3,32,64,512]{3,2,1,0:T(8,128)}, u32[]{:S(2)}) %copy-start) | copy-done | bytes 12582936
  398.2 9.3 %corrected.1 = f32[3,32,64,512]{3,2,1,0:T(8,128)} custom-call(f32[3,32,64,512]{3,2,1,0:T(8,128)S(1)} %copy-done, f32[4,34,64,128]{3,2,1,0:T(8,128)} %all-to-all-done.3.in_ref, f32[4,32,128]{2,1,0:T(8,128)S(1)} %bitcast.25, f32[4,32,128]{2,1,0:T(8,128)S(1)} %bitcast.26, bf16[256,256]{1,0:T(8,128)(2,1)S(1)} %copy-done.6, bf16[256,256]{1,0:T(8,128)(2,1)S(1)} %copy-done.7, ...), custom_call_target="tpu_custom_call" | custom-call | tf_op jit(solution)/shard_map/corrected/pallas_call | solution.py:699
  (131 shorter events, 87.2 us)
Async XLA Ops:
  8.4 33.1 %collective-permute-start.2 = (f32[3,1,64,512]{3,2,1,0:T(8,128)S(1)}, f32[3,1,64,512]{3,2,1,0:T(8,128)S(1)}, u32[]{:S(2)}, u32[]{:S(2)}) collective-permute-start(f32[3,1,64,512]{3,2,1,0:T(8,128)S(1)} %get-tuple-element.21), channel_id=1, source_target_pairs={{0,4},{4,8},{8,12},{12,16},{16,20},{20,24},{24,28},{28,0},{1,5},{5... | collective-permute-start | bytes 1179656 | tf_op jit(solution)/shard_map/ppermute | solution.py:42
  10.5 31.0 %collective-permute-start.3 = (f32[3,1,64,512]{3,2,1,0:T(8,128)S(1)}, f32[3,1,64,512]{3,2,1,0:T(8,128)S(1)}, u32[]{:S(2)}, u32[]{:S(2)}) collective-permute-start(f32[3,1,64,512]{3,2,1,0:T(8,128)S(1)} %get-tuple-element.20), channel_id=1, source_target_pairs={{4,0},{8,4},{12,8},{16,12},{20,16},{24,20},{28,24},{0,28},{5,1},{9... | collective-permute-start | bytes 1179656 | tf_op jit(solution)/shard_map/ppermute | solution.py:42
  15.9 6.2 %collective-permute-start = (f32[3,32,1,512]{3,2,1,0:T(1,128)S(1)}, f32[3,32,1,512]{3,2,1,0:T(1,128)S(1)}, u32[]{:S(2)}, u32[]{:S(2)}) collective-permute-start(f32[3,32,1,512]{3,2,1,0:T(1,128)S(1)} %get-tuple-element.23), channel_id=1, source_target_pairs={{0,1},{1,2},{2,3},{3,0},{4,5},{5,6},{6,7},{7,4},{8,9},{9,10},{10,1... | collective-permute-start | bytes 589832 | tf_op jit(solution)/shard_map/ppermute | solution.py:42
  18.1 5.6 %collective-permute-start.1 = (f32[3,32,1,512]{3,2,1,0:T(1,128)S(1)}, f32[3,32,1,512]{3,2,1,0:T(1,128)S(1)}, u32[]{:S(2)}, u32[]{:S(2)}) collective-permute-start(f32[3,32,1,512]{3,2,1,0:T(1,128)S(1)} %get-tuple-element.22), channel_id=1, source_target_pairs={{1,0},{2,1},{3,2},{0,3},{5,4},{6,5},{7,6},{4,7},{9,8},{10,9},{11,1... | collective-permute-start | bytes 589832 | tf_op jit(solution)/shard_map/ppermute | solution.py:42
  44.1 45.3 %collective-permute-start.6 = (f32[1,64,512]{2,1,0:T(8,128)S(1)}, f32[1,64,512]{2,1,0:T(8,128)S(1)}, u32[]{:S(2)}, u32[]{:S(2)}) collective-permute-start(f32[1,64,512]{2,1,0:T(8,128)S(1)} %get-tuple-element.33), channel_id=1, source_target_pairs={{0,4},{4,8},{8,12},{12,16},{16,20},{20,24},{24,28},{28,0},{1,5},{5... | collective-permute-start | bytes 393224 | tf_op jit(solution)/shard_map/ppermute | solution.py:42
  44.2 45.2 %collective-permute-start.7 = (f32[1,64,512]{2,1,0:T(8,128)S(1)}, f32[1,64,512]{2,1,0:T(8,128)S(1)}, u32[]{:S(2)}, u32[]{:S(2)}) collective-permute-start(f32[1,64,512]{2,1,0:T(8,128)S(1)} %get-tuple-element.32), channel_id=1, source_target_pairs={{4,0},{8,4},{12,8},{16,12},{20,16},{24,20},{28,24},{0,28},{5,1},{9... | collective-permute-start | bytes 393224 | tf_op jit(solution)/shard_map/ppermute | solution.py:42
  95.7 31.8 %collective-permute-start.10 = (f32[3,1,64,512]{3,2,1,0:T(8,128)S(1)}, f32[3,1,64,512]{3,2,1,0:T(8,128)S(1)}, u32[]{:S(2)}, u32[]{:S(2)}) collective-permute-start(f32[3,1,64,512]{3,2,1,0:T(8,128)S(1)} %get-tuple-element.17), channel_id=1, source_target_pairs={{0,4},{4,8},{8,12},{12,16},{16,20},{20,24},{24,28},{28,0},{1,5},{5... | collective-permute-start | bytes 1179656 | tf_op jit(solution)/shard_map/ppermute | solution.py:42
  95.8 31.7 %collective-permute-start.11 = (f32[3,1,64,512]{3,2,1,0:T(8,128)S(1)}, f32[3,1,64,512]{3,2,1,0:T(8,128)S(1)}, u32[]{:S(2)}, u32[]{:S(2)}) collective-permute-start(f32[3,1,64,512]{3,2,1,0:T(8,128)S(1)} %get-tuple-element.16), channel_id=1, source_target_pairs={{4,0},{8,4},{12,8},{16,12},{20,16},{24,20},{28,24},{0,28},{5,1},{9... | collective-permute-start | bytes 1179656 | tf_op jit(solution)/shard_map/ppermute | solution.py:42
  130.8 45.8 %collective-permute-start.14 = (f32[1,64,512]{2,1,0:T(8,128)S(1)}, f32[1,64,512]{2,1,0:T(8,128)S(1)}, u32[]{:S(2)}, u32[]{:S(2)}) collective-permute-start(f32[1,64,512]{2,1,0:T(8,128)S(1)} %get-tuple-element.29), channel_id=1, source_target_pairs={{0,4},{4,8},{8,12},{12,16},{16,20},{20,24},{24,28},{28,0},{1,5},{5... | collective-permute-start | bytes 393224 | tf_op jit(solution)/shard_map/ppermute | solution.py:42
  130.9 45.7 %collective-permute-start.15 = (f32[1,64,512]{2,1,0:T(8,128)S(1)}, f32[1,64,512]{2,1,0:T(8,128)S(1)}, u32[]{:S(2)}, u32[]{:S(2)}) collective-permute-start(f32[1,64,512]{2,1,0:T(8,128)S(1)} %get-tuple-element.28), channel_id=1, source_target_pairs={{4,0},{8,4},{12,8},{16,12},{20,16},{24,20},{28,24},{0,28},{5,1},{9... | collective-permute-start | bytes 393224 | tf_op jit(solution)/shard_map/ppermute | solution.py:42
  187.9 13.9 %collective-permute-start.16 = (f32[1,64,512]{2,1,0:T(8,128)S(1)}, f32[1,64,512]{2,1,0:T(8,128)S(1)}, u32[]{:S(2)}, u32[]{:S(2)}) collective-permute-start(f32[1,64,512]{2,1,0:T(8,128)S(1)} %get-tuple-element.15), channel_id=1, source_target_pairs={{0,4},{4,8},{8,12},{12,16},{16,20},{20,24},{24,28},{28,0},{1,5},{5... | collective-permute-start | bytes 393224 | tf_op jit(solution)/shard_map/ppermute | solution.py:42
  188.0 13.9 %collective-permute-start.17 = (f32[1,64,512]{2,1,0:T(8,128)S(1)}, f32[1,64,512]{2,1,0:T(8,128)S(1)}, u32[]{:S(2)}, u32[]{:S(2)}) collective-permute-start(f32[1,64,512]{2,1,0:T(8,128)S(1)} %get-tuple-element.14), channel_id=1, source_target_pairs={{4,0},{8,4},{12,8},{16,12},{20,16},{24,20},{28,24},{0,28},{5,1},{9... | collective-permute-start | bytes 393224 | tf_op jit(solution)/shard_map/ppermute | solution.py:42
  192.2 9.7 %collective-permute-start.18 = (f32[32,1,512]{2,0,1:T(8,128)S(1)}, f32[32,1,512]{2,0,1:T(8,128)S(1)}, u32[]{:S(2)}, u32[]{:S(2)}) collective-permute-start(f32[32,1,512]{2,0,1:T(8,128)S(1)} %get-tuple-element.27), channel_id=1, source_target_pairs={{0,1},{1,2},{2,3},{3,0},{4,5},{5,6},{6,7},{7,4},{8,9},{9,10},{10,1... | collective-permute-start | bytes 196616 | tf_op jit(solution)/shard_map/ppermute | solution.py:42
  193.2 8.7 %collective-permute-start.19 = (f32[32,1,512]{2,0,1:T(8,128)S(1)}, f32[32,1,512]{2,0,1:T(8,128)S(1)}, u32[]{:S(2)}, u32[]{:S(2)}) collective-permute-start(f32[32,1,512]{2,0,1:T(8,128)S(1)} %get-tuple-element.26), channel_id=1, source_target_pairs={{1,0},{2,1},{3,2},{0,3},{5,4},{6,5},{7,6},{4,7},{9,8},{10,9},{11,1... | collective-permute-start | bytes 196616 | tf_op jit(solution)/shard_map/ppermute | solution.py:42
  204.9 54.0 %all-to-all-start = ((f32[4,32,64,128]{3,2,1,0:T(8,128)}), f32[4,32,64,128]{3,2,1,0:T(8,128)}, u32[]{:S(2)}, u32[]{:S(2)}) async-start(f32[4,32,64,128]{3,2,1,0:T(8,128)} %copy-done.1), calls=%async_computation | async-start | bytes 8388608 | tf_op jit(solution)/shard_map/all_to_all | solution.py:879
  209.9 130.5 %reduce-scatter.2.cloned.1.call-start = ((), (), s32[]{:S(2)}) async-start(), calls=%async_computation.5 | async-start | bytes 2359296 | tf_op jit(solution)/shard_map/reduce_scatter | solution.py:956
  271.4 24.6 %all-to-all-start.1 = ((f32[8,4,32,128]{3,2,1,0:T(8,128)}), f32[8,4,32,128]{3,2,1,0:T(8,128)S(1)}, u32[]{:S(2)}, u32[]{:S(2)}) async-start(f32[8,4,32,128]{3,2,1,0:T(8,128)} %get-tuple-element.12), calls=%async_computation.1 | async-start | bytes 1048576 | tf_op jit(solution)/shard_map/all_to_all | solution.py:879
  329.1 58.7 %all-to-all-start.3 = ((f32[4,34,64,128]{3,2,1,0:T(8,128)}), f32[4,34,64,128]{3,2,1,0:T(8,128)}, u32[]{:S(2)}, u32[]{:S(2)}) async-start(f32[4,34,64,128]{3,2,1,0:T(8,128)} %y_inverse.1), calls=%async_computation.3 | async-start | bytes 8912896 | tf_op jit(solution)/shard_map/all_to_all | solution.py:879
  339.0 7.7 %collective-permute-start.27 = (f32[2,32,128]{2,1,0:T(8,128)S(1)}, f32[2,32,128]{2,1,0:T(8,128)S(1)}, u32[]{:S(2)}, u32[]{:S(2)}) collective-permute-start(f32[2,32,128]{2,1,0:T(8,128)S(1)} %get-tuple-element.48), channel_id=1, source_target_pairs={{4,0},{8,4},{12,8},{16,12},{20,16},{24,20},{28,24},{5,1},{9,5},{13... | collective-permute-start | bytes 98312 | tf_op jit(solution)/shard_map/ppermute | solution.py:31
  345.5 5.4 %collective-permute-start.23 = (f32[3,32,128]{2,1,0:T(8,128)S(1)}, f32[3,32,128]{2,1,0:T(8,128)S(1)}, u32[]{:S(2)}, u32[]{:S(2)}) collective-permute-start(f32[3,32,128]{2,1,0:T(8,128)S(1)} %get-tuple-element.51), channel_id=1, source_target_pairs={{4,0},{8,4},{12,8},{16,12},{20,16},{24,20},{28,24},{5,1},{9,5},{13... | collective-permute-start | bytes 147464 | tf_op jit(solution)/shard_map/ppermute | solution.py:31
  350.9 33.9 %collective-permute-start.24 = (f32[22,3,128]{2,1,0:T(4,128)S(1)}, f32[22,3,128]{2,1,0:T(4,128)S(1)}, u32[]{:S(2)}, u32[]{:S(2)}) collective-permute-start(f32[22,3,128]{2,1,0:T(4,128)S(1)} %get-tuple-element.44), channel_id=1, source_target_pairs={{0,1},{1,2},{2,3},{4,5},{5,6},{6,7},{8,9},{9,10},{10,11},{12,13},{... | collective-permute-start | bytes 101384 | tf_op jit(solution)/shard_map/ppermute | solution.py:30
  355.9 30.8 %collective-permute-start.25 = (f32[22,3,128]{2,1,0:T(4,128)S(1)}, f32[22,3,128]{2,1,0:T(4,128)S(1)}, u32[]{:S(2)}, u32[]{:S(2)}) collective-permute-start(f32[22,3,128]{2,1,0:T(4,128)S(1)} %get-tuple-element.45), channel_id=1, source_target_pairs={{1,0},{2,1},{3,2},{5,4},{6,5},{7,6},{9,8},{10,9},{11,10},{13,12},{... | collective-permute-start | bytes 101384 | tf_op jit(solution)/shard_map/ppermute | solution.py:31
  357.8 29.1 %collective-permute-start.28 = (f32[20,2,128]{2,1,0:T(2,128)S(1)}, f32[20,2,128]{2,1,0:T(2,128)S(1)}, u32[]{:S(2)}, u32[]{:S(2)}) collective-permute-start(f32[20,2,128]{2,1,0:T(2,128)S(1)} %get-tuple-element.46), channel_id=1, source_target_pairs={{0,1},{1,2},{2,3},{4,5},{5,6},{6,7},{8,9},{9,10},{10,11},{12,13},{... | collective-permute-start | bytes 61448 | tf_op jit(solution)/shard_map/ppermute | solution.py:30
  361.5 25.4 %collective-permute-start.29 = (f32[20,2,128]{2,1,0:T(2,128)S(1)}, f32[20,2,128]{2,1,0:T(2,128)S(1)}, u32[]{:S(2)}, u32[]{:S(2)}) collective-permute-start(f32[20,2,128]{2,1,0:T(2,128)S(1)} %get-tuple-element.47), channel_id=1, source_target_pairs={{1,0},{2,1},{3,2},{5,4},{6,5},{7,6},{9,8},{10,9},{11,10},{13,12},{... | collective-permute-start | bytes 61448 | tf_op jit(solution)/shard_map/ppermute | solution.py:31
  (26 other events, 181.3 us)
Sparse Core Ops, SparseCore 0:
  257.4 70.7 reduce-scatter.1

commit v4 on v3

--- a/solution.py
+++ b/solution.py
@@ -247,7 +247,8 @@
     ]
     for s in range(strips):
         sum_x = m[s] + mu[slot + 1, rows_of(s), :]
-        sum_z = m[s] + pltpu.roll(m[s], z_cells - 1, 1)
+        sum_z_ahead = m[s] + pltpu.roll(m[s], z_cells - 1, 1)
+        sum_z_behind = m[s] + pltpu.roll(m[s], 1, 1)
         for c in range(3):
             value = values[c][s]
             flux_x = sum_x * (cells[c, slot + 1, rows_of(s), :] - value)
@@ -255,11 +256,13 @@
                 rows == 7, up[c][s + 1] if s + 1 < strips else flow_after(c), up[c][s]
             )
             flux_y = sums_y[s] * (ahead - value)
-            flux_z = sum_z * (pltpu.roll(value, z_cells - 1, 1) - value)
             turned = pltpu.roll(flux_y, 1, 0)
             total = (flux_x - flux[c, rows_of(s), :]) + (
                 flux_y - jnp.where(rows == 0, carried[c], turned)
-            ) + (flux_z - pltpu.roll(flux_z, 1, 1))
+            ) + (
+                sum_z_ahead * (pltpu.roll(value, z_cells - 1, 1) - value)
+                - sum_z_behind * (value - pltpu.roll(value, 1, 1))
+            )
             flux[c, rows_of(s), :] = flux_x
             carried[c] = turned
             push[c, out_slot, rows_of(s), :] = (
@@ -535,7 +538,6 @@
             pltpu.VMEM((count, x_local, y_local, piece), jnp.float32),
             pltpu.SemaphoreType.DMA((x_local // step,)),
         ],
-        compiler_params=pltpu.CompilerParams(vmem_limit_bytes=vmem_limit),
         name="divergence_modes",
     )(flow, *tables)
 
@@ -622,7 +624,6 @@
             pltpu.VMEM((2, count, x_local - 2, 8, piece), jnp.float32),
             pltpu.SemaphoreType.DMA((8,)),
         ],
-        compiler_params=pltpu.CompilerParams(vmem_limit_bytes=16 << 20),
         name="add_halo_modes",
     )(modes, *x_sides, *y_sides, *tables)
 
@@ -637,8 +638,9 @@
     def kernel(
         flow_ref, in_ref, before_ref, after_ref,
         even_high, even_low, odd_high, odd_low, out_ref,
-        modes, mode_sem, pressure, sides, work, out_sem,
+        modes, mode_sem, pressure, sides, work, flow_sem, out_sem,
     ):
+        flow_planes = Planes(flow_ref, work, flow_sem)
         table_refs = (even_high, even_low, odd_high, odd_low)
 
         def load(k):
@@ -647,6 +649,12 @@
 
         load(0).start()
         load(1).start()
+
+        def begin(i, state):
+            flow_planes.start(i)
+            return state
+
+        lax.fori_loop(0, x_local, begin, 0)
         sides[...] = cells_of(
             jnp.concatenate(
                 [
@@ -663,6 +671,7 @@
             return pltpu.make_async_copy(pick(work, i), pick(out_ref, i), out_sem.at[i])
 
         def plane(j, state):
+            flow_planes.wait(j)
             values = [pressure[j + 1, rows_of(s), :] for s in range(strips)]
             up = [pltpu.roll(v, 7, 0) for v in values]
             down = [pltpu.roll(v, 1, 0) for v in values]
@@ -675,7 +684,7 @@
                     pltpu.roll(values[s], z_cells - 1, 1) - pltpu.roll(values[s], 1, 1),
                 )
                 for c in range(3):
-                    work[c, j, rows_of(s), :] = flow_ref[c, j, rows_of(s), :] - 0.5 * slopes[c]
+                    work[c, j, rows_of(s), :] = work[c, j, rows_of(s), :] - 0.5 * slopes[c]
             stored(j).start()
             return state
 
@@ -698,7 +707,7 @@
 
     return pl.pallas_call(
         kernel,
-        in_specs=[in_vmem, anywhere] + [in_vmem] * 6,
+        in_specs=[anywhere, anywhere] + [in_vmem] * 6,
         out_specs=anywhere,
         out_shape=jax.ShapeDtypeStruct(flow.shape, jnp.float32),
         scratch_shapes=[
@@ -708,8 +717,9 @@
             pltpu.VMEM((2 * x_local, z_cells), jnp.float32),
             pltpu.VMEM(flow.shape, jnp.float32),
             pltpu.SemaphoreType.DMA((x_local,)),
-        ],
-        compiler_params=pltpu.CompilerParams(vmem_limit_bytes=36 << 20),
+            pltpu.SemaphoreType.DMA((x_local,)),
+        ],
+        compiler_params=pltpu.CompilerParams(vmem_limit_bytes=vmem_limit),
         name="corrected",
     )(flow, spectrum, *y_sides, *tables)
 

time: 416 us -> 381 us (0.916)
  Pallas kernels: 170 us -> 141 us
  local copies, waits for them, and re-layouts: 26.2 us -> 20.3 us
    pallas_call x4, Pallas kernels: 81.7 us -> 46.5 us  [advance_call(): pl.pallas_call(kernel, in_specs=specs, out_specs=anywhere, out_shape=jax....]
    unnamed x36 -> x32, local copies, waits for them, and re-layouts: 9.96 us -> 4.03 us
  transfers between devices with their start and end apart: 34 -> 34, of which waited for: 14 -> 14; matrix products, arithmetic and copies ran while one was open for 14% -> 15% of each run, Pallas kernels for 35% -> 30%
where the time goes in v4:
time: 381 us; the launch traced here: 379 us
  Pallas kernels  141 us (37%)
  waiting for transfers between devices  68.5 us (18%)
  starting transfers between devices  67.5 us (18%)
  other arithmetic  49.2 us (13%)
  local copies, waits for them, and re-layouts  20.3 us (5%)
  blocking collectives  17.9 us (5%)
  between operations  14.7 us (4%)
    pallas_call x4, Pallas kernels, advance_call(): pl.pallas_call(kernel, in_specs=specs, out_specs=anywhere, out_shape=jax....  46.5 us
    scatter-add x1, other arithmetic, per_device(): partial_value = jnp.zeros((slab_count * component_lines, 128), jnp.float3...  45.8 us
    pallas_call x4, Pallas kernels, viscosity_call(): pl.pallas_call(kernel, in_specs=specs, out_specs=[anywhere] * outputs, ou...  42.8 us
    ppermute x22, starting transfers between devices, ring(): return (lax.ppermute(last, axis, up), lax.ppermute(initial, axis, down))  30.3 us
    ppermute x4, waiting for transfers between devices, with_halo(): before = lax.ppermute(last, axis, up)  21.5 us
    ppermute x22, waiting for transfers between devices, ring(): return (lax.ppermute(last, axis, up), lax.ppermute(initial, axis, down))  21.2 us
    all_to_all x3, waiting for transfers between devices, turn(): return lax.all_to_all(value, axis, split_axis=0, concat_axis=0, tiled=True)  19.9 us
    all_to_all x1, blocking collectives, turn(): return lax.all_to_all(value, axis, split_axis=0, concat_axis=0, tiled=True)  17.9 us
  transfers between devices with their start and end apart: 34, of which 14 were waited for; matrix products, arithmetic and copies ran while one was open for 15% of the time, Pallas kernels for 30%

profile of v4, /device:TPU:1, one launch (start us, length us, event | category | flops | bytes accessed | tf_op | source)
XLA Modules:
  0.0 379.2 jit_solution(758505800036675488)
XLA Ops:
  18.1 4.0 %collective-permute-done.refs_1_ = f32[3,32,1,512]{3,2,1,0:T(1,128)S(1)} collective-permute-done((f32[3,32,1,512]{3,2,1,0:T(1,128)S(1)}, f32[3,32,1,512]{3,2,1,0:T(1,128)S(1)}, u32[]{:S(2)}, u32[]{:S(2)}) %collective-permute-start) | collective-permute-done | bytes 196640 | tf_op jit(solution)/shard_map/ppermute | solution.py:42
  23.7 17.8 %viscosity_inner.2.refs_6_ = f32[32,64,512]{2,1,0:T(8,128)S(1)} custom-call(f32[3,32,64,512]{3,2,1,0:T(8,128)} %refs_0_.11, f32[3,32,1,512]{3,2,1,0:T(1,128)S(1)} %collective-permute-done.refs_1_, f32[3,32,1,512]{3,2,1,0:T(1,128)S(1)} %collective-permute-done.1.refs_2_, f32[32,64,512]{2,1,0:T(8,128)} %refs_3_.7), custom_call_target="tpu_custom_call" | custom-call | tf_op jit(solution)/shard_map/viscosity_inner/pallas_call | solution.py:211
  44.2 4.1 %collective-permute-start.7 = (f32[1,64,512]{2,1,0:T(8,128)S(1)}, f32[1,64,512]{2,1,0:T(8,128)S(1)}, u32[]{:S(2)}, u32[]{:S(2)}) collective-permute-start(f32[1,64,512]{2,1,0:T(8,128)S(1)} %get-tuple-element.32), channel_id=1, source_target_pairs={{4,0},{8,4},{12,8},{16,12},{20,16},{24,20},{28,24},{0,28},{5,1},{9... | collective-permute-start | bytes 393224 | tf_op jit(solution)/shard_map/ppermute | solution.py:42
  53.6 19.3 %advance_inner.2.refs_11_ = f32[3,32,64,512]{3,2,1,0:T(8,128)} custom-call(f32[3,32,64,512]{3,2,1,0:T(8,128)} %refs_0_.11, f32[3,32,1,512]{3,2,1,0:T(1,128)S(1)} %collective-permute-done.refs_1_, f32[3,32,1,512]{3,2,1,0:T(1,128)S(1)} %collective-permute-done.1.refs_2_, f32[32,64,512]{2,1,0:T(8,128)S(1)} %viscosity_edge.2.refs_3_, ...), custom_call_target="tpu_custom_call" | custom-call | tf_op jit(solution)/shard_map/advance_inner/pallas_call | solution.py:375
  78.2 4.1 %collective-permute-start.11 = (f32[3,1,64,512]{3,2,1,0:T(8,128)S(1)}, f32[3,1,64,512]{3,2,1,0:T(8,128)S(1)}, u32[]{:S(2)}, u32[]{:S(2)}) collective-permute-start(f32[3,1,64,512]{3,2,1,0:T(8,128)S(1)} %get-tuple-element.16), channel_id=1, source_target_pairs={{4,0},{8,4},{12,8},{16,12},{20,16},{24,20},{28,24},{0,28},{5,1},{9... | collective-permute-start | bytes 1179656 | tf_op jit(solution)/shard_map/ppermute | solution.py:42
  85.4 4.3 %collective-permute-done.8.refs_1_ = f32[3,32,1,512]{3,2,1,0:T(1,128)S(1)} collective-permute-done((f32[3,32,1,512]{3,2,1,0:T(1,128)S(1)}, f32[3,32,1,512]{3,2,1,0:T(1,128)S(1)}, u32[]{:S(2)}, u32[]{:S(2)}) %collective-permute-start.8) | collective-permute-done | bytes 196640 | tf_op jit(solution)/shard_map/ppermute | solution.py:42
  90.7 19.1 %viscosity_inner.3 = (f32[32,64,512]{2,1,0:T(8,128)S(1)}, f32[4,32,64,128]{3,2,1,0:T(8,128)}) custom-call(f32[3,32,64,512]{3,2,1,0:T(8,128)} %advance_edge.2.refs_0_, f32[3,32,1,512]{3,2,1,0:T(1,128)S(1)} %collective-permute-done.8.refs_1_, f32[3,32,1,512]{3,2,1,0:T(1,128)S(1)} %collective-permute-done.9.refs_2_, f32[32,64,512]{2,1,0:T(8,128)} %refs_3_.7), custom_call_target="tpu_custom_call" | custom-call | tf_op jit(solution)/shard_map/viscosity_inner/pallas_call | solution.py:211
  113.3 4.1 %collective-permute-start.15 = (f32[1,64,512]{2,1,0:T(8,128)S(1)}, f32[1,64,512]{2,1,0:T(8,128)S(1)}, u32[]{:S(2)}, u32[]{:S(2)}) collective-permute-start(f32[1,64,512]{2,1,0:T(8,128)S(1)} %get-tuple-element.28), channel_id=1, source_target_pairs={{4,0},{8,4},{12,8},{16,12},{20,16},{24,20},{28,24},{0,28},{5,1},{9... | collective-permute-start | bytes 393224 | tf_op jit(solution)/shard_map/ppermute | solution.py:42
  123.2 19.3 %advance_inner.3.refs_11_ = f32[3,32,64,512]{3,2,1,0:T(8,128)} custom-call(f32[3,32,64,512]{3,2,1,0:T(8,128)} %refs_0_.11, f32[3,32,1,512]{3,2,1,0:T(1,128)S(1)} %collective-permute-done.refs_1_, f32[3,32,1,512]{3,2,1,0:T(1,128)S(1)} %collective-permute-done.1.refs_2_, f32[32,64,512]{2,1,0:T(8,128)S(1)} %get-tuple-element.10.refs_3_, ...), custom_call_target="tpu_custom_call" | custom-call | tf_op jit(solution)/shard_map/advance_inner/pallas_call | solution.py:375
  142.5 4.0 %advance_edge.3.flow_ref = f32[3,32,64,512]{3,2,1,0:T(8,128)} custom-call(f32[3,32,64,512]{3,2,1,0:T(8,128)} %refs_0_.11, f32[3,32,1,512]{3,2,1,0:T(1,128)S(1)} %collective-permute-done.refs_1_, f32[3,32,1,512]{3,2,1,0:T(1,128)S(1)} %collective-permute-done.1.refs_2_, f32[32,64,512]{2,1,0:T(8,128)S(1)} %get-tuple-element.10.refs_3_, ...), custom_call_target="tpu_custom_call", output_to_operand_aliasing={{}: (11, {})} | custom-call | tf_op jit(solution)/shard_map/advance_edge/pallas_call | solution.py:375
  152.8 4.1 %collective-permute-start.17 = (f32[1,64,512]{2,1,0:T(8,128)S(1)}, f32[1,64,512]{2,1,0:T(8,128)S(1)}, u32[]{:S(2)}, u32[]{:S(2)}) collective-permute-start(f32[1,64,512]{2,1,0:T(8,128)S(1)} %get-tuple-element.14), channel_id=1, source_target_pairs={{4,0},{8,4},{12,8},{16,12},{20,16},{24,20},{28,24},{0,28},{5,1},{9... | collective-permute-start | bytes 393224 | tf_op jit(solution)/shard_map/ppermute | solution.py:42
  158.0 10.3 %divergence_modes.1.modes_ref = f32[4,32,64,128]{3,2,1,0:T(8,128)} custom-call(f32[3,32,64,512]{3,2,1,0:T(8,128)} %advance_edge.3.flow_ref, bf16[256,256]{1,0:T(8,128)(2,1)} %constant.68.clone.even_high, bf16[256,256]{1,0:T(8,128)(2,1)} %constant.69.clone.even_low, bf16[256,256]{1,0:T(8,128)(2,1)} %constant.70.clone.odd_high, ...), custom_call_target="tpu_custom_call" | custom-call | tf_op jit(solution)/shard_map/divergence_modes/pallas_call | solution.py:529
  172.9 4.9 %all-to-all-start = ((f32[4,32,64,128]{3,2,1,0:T(8,128)}), f32[4,32,64,128]{3,2,1,0:T(8,128)}, u32[]{:S(2)}, u32[]{:S(2)}) async-start(f32[4,32,64,128]{3,2,1,0:T(8,128)} %add_halo_modes.1), calls=%async_computation | async-start | bytes 8388608 | tf_op jit(solution)/shard_map/all_to_all | solution.py:889
  179.4 45.8 %scatter_custom_fusion = f32[4096,128]{1,0:T(8,128)} fusion(s32[8192]{0:T(1024)S(1)} %bitcast.37, f32[8192,128]{1,0:T(8,128)} %bitcast.27, f32[]{:T(128)} %constant.26.clone.1), kind=kCustom, calls=%fused_computation.2 | custom fusion | flops 1048576 | bytes 2097664 | tf_op jit(solution)/shard_map/scatter-add | solution.py:964
  226.8 12.4 %y_forward.1 = (f32[32,256,128]{2,1,0:T(8,128)}, f32[8,4,32,128]{3,2,1,0:T(8,128)}) custom-call(f32[4,32,64,128]{3,2,1,0:T(8,128)} %all-to-all-done.in_ref, bf16[256,256]{1,0:T(8,128)(2,1)} %constant.74.clone.high_ref, bf16[256,256]{1,0:T(8,128)(2,1)} %constant.75.clone.low_ref, f32[256,128]{1,0:T(8,128)} %get-tuple-element.53.ratio_ref), custom_call_target="tpu_custom_call" | custom-call | tf_op jit(solution)/shard_map/y_forward/pallas_call | solution.py:759
  244.1 19.8 %all-to-all-done.1.in_ref = f32[8,4,32,128]{3,2,1,0:T(8,128)S(1)} async-done(((f32[8,4,32,128]{3,2,1,0:T(8,128)}), f32[8,4,32,128]{3,2,1,0:T(8,128)S(1)}, u32[]{:S(2)}, u32[]{:S(2)}) %all-to-all-start.1) | async-done | bytes 524320 | tf_op jit(solution)/shard_map/all_to_all | solution.py:889
  266.7 17.9 %all_to_all.20.carry_ref = f32[8,4,32,128]{3,2,1,0:T(8,128)} all-to-all(f32[8,4,32,128]{3,2,1,0:T(8,128)} %join_carries.1), channel_id=1, replica_groups=mesh['wide'=8,'narrow'=4] {'wide'}, dimensions={0} | all-to-all | bytes 1048576 | tf_op jit(solution)/shard_map/all_to_all | solution.py:889
  284.6 12.4 %y_inverse.1 = f32[4,34,64,128]{3,2,1,0:T(8,128)} custom-call(f32[32,256,128]{2,1,0:T(8,128)} %get-tuple-element.11.modes_ref, f32[8,4,32,128]{3,2,1,0:T(8,128)} %all_to_all.20.carry_ref, bf16[256,256]{1,0:T(8,128)(2,1)} %constant.76.clone.high_ref, bf16[256,256]{1,0:T(8,128)(2,1)} %constant.77.clone.low_ref, f32[256,128]{1,0:T(8,128)} %get-tuple-element.53.ratio_ref, ...), custom_call_target="tpu_custom_call" | custom-call | tf_op jit(solution)/shard_map/y_inverse/pallas_call | solution.py:867
  296.9 6.7 %all-to-all-start.3 = ((f32[4,34,64,128]{3,2,1,0:T(8,128)}), f32[4,34,64,128]{3,2,1,0:T(8,128)}, u32[]{:S(2)}, u32[]{:S(2)}) async-start(f32[4,34,64,128]{3,2,1,0:T(8,128)} %y_inverse.1), calls=%async_computation.3 | async-start | bytes 8912896 | tf_op jit(solution)/shard_map/all_to_all | solution.py:889
  309.2 4.0 %collective-permute-start.22 = (f32[3,32,128]{2,1,0:T(8,128)S(1)}, f32[3,32,128]{2,1,0:T(8,128)S(1)}, u32[]{:S(2)}, u32[]{:S(2)}) collective-permute-start(f32[3,32,128]{2,1,0:T(8,128)S(1)} %get-tuple-element.50), channel_id=1, source_target_pairs={{0,4},{4,8},{8,12},{12,16},{16,20},{20,24},{24,28},{1,5},{5,9},{9,... | collective-permute-start | bytes 147464 | tf_op jit(solution)/shard_map/ppermute | solution.py:30
  314.6 4.1 %collective-permute-done.23 = f32[3,32,128]{2,1,0:T(8,128)S(1)} collective-permute-done((f32[3,32,128]{2,1,0:T(8,128)S(1)}, f32[3,32,128]{2,1,0:T(8,128)S(1)}, u32[]{:S(2)}, u32[]{:S(2)}) %collective-permute-start.23) | collective-permute-done | bytes 49184 | tf_op jit(solution)/shard_map/ppermute | solution.py:31
  318.7 4.9 %collective-permute-start.24 = (f32[22,3,128]{2,1,0:T(4,128)S(1)}, f32[22,3,128]{2,1,0:T(4,128)S(1)}, u32[]{:S(2)}, u32[]{:S(2)}) collective-permute-start(f32[22,3,128]{2,1,0:T(4,128)S(1)} %get-tuple-element.44), channel_id=1, source_target_pairs={{0,1},{1,2},{2,3},{4,5},{5,6},{6,7},{8,9},{9,10},{10,11},{12,13},{... | collective-permute-start | bytes 101384 | tf_op jit(solution)/shard_map/ppermute | solution.py:30
  331.2 21.5 %collective-permute-done.24 = f32[22,3,128]{2,1,0:T(4,128)S(1)} collective-permute-done((f32[22,3,128]{2,1,0:T(4,128)S(1)}, f32[22,3,128]{2,1,0:T(4,128)S(1)}, u32[]{:S(2)}, u32[]{:S(2)}) %collective-permute-start.24) | collective-permute-done | bytes 33824 | tf_op jit(solution)/shard_map/ppermute | solution.py:30
  361.4 11.0 %corrected.1 = f32[3,32,64,512]{3,2,1,0:T(8,128)} custom-call(f32[3,32,64,512]{3,2,1,0:T(8,128)} %advance_edge.3.flow_ref, f32[4,34,64,128]{3,2,1,0:T(8,128)} %all-to-all-done.3.in_ref, f32[4,32,128]{2,1,0:T(8,128)S(1)} %bitcast.23, f32[4,32,128]{2,1,0:T(8,128)S(1)} %bitcast.24, bf16[256,256]{1,0:T(8,128)(2,1)S(1)} %copy-done, ...), custom_call_target="tpu_custom_call" | custom-call | tf_op jit(solution)/shard_map/corrected/pallas_call | solution.py:708
  (127 shorter events, 84.5 us)
Async XLA Ops:
  8.4 33.1 %collective-permute-start.2 = (f32[3,1,64,512]{3,2,1,0:T(8,128)S(1)}, f32[3,1,64,512]{3,2,1,0:T(8,128)S(1)}, u32[]{:S(2)}, u32[]{:S(2)}) collective-permute-start(f32[3,1,64,512]{3,2,1,0:T(8,128)S(1)} %get-tuple-element.21), channel_id=1, source_target_pairs={{0,4},{4,8},{8,12},{12,16},{16,20},{20,24},{24,28},{28,0},{1,5},{5... | collective-permute-start | bytes 1179656 | tf_op jit(solution)/shard_map/ppermute | solution.py:42
  10.5 31.0 %collective-permute-start.3 = (f32[3,1,64,512]{3,2,1,0:T(8,128)S(1)}, f32[3,1,64,512]{3,2,1,0:T(8,128)S(1)}, u32[]{:S(2)}, u32[]{:S(2)}) collective-permute-start(f32[3,1,64,512]{3,2,1,0:T(8,128)S(1)} %get-tuple-element.20), channel_id=1, source_target_pairs={{4,0},{8,4},{12,8},{16,12},{20,16},{24,20},{28,24},{0,28},{5,1},{9... | collective-permute-start | bytes 1179656 | tf_op jit(solution)/shard_map/ppermute | solution.py:42
  15.9 6.2 %collective-permute-start = (f32[3,32,1,512]{3,2,1,0:T(1,128)S(1)}, f32[3,32,1,512]{3,2,1,0:T(1,128)S(1)}, u32[]{:S(2)}, u32[]{:S(2)}) collective-permute-start(f32[3,32,1,512]{3,2,1,0:T(1,128)S(1)} %get-tuple-element.23), channel_id=1, source_target_pairs={{0,1},{1,2},{2,3},{3,0},{4,5},{5,6},{6,7},{7,4},{8,9},{9,10},{10,1... | collective-permute-start | bytes 589832 | tf_op jit(solution)/shard_map/ppermute | solution.py:42
  18.1 5.6 %collective-permute-start.1 = (f32[3,32,1,512]{3,2,1,0:T(1,128)S(1)}, f32[3,32,1,512]{3,2,1,0:T(1,128)S(1)}, u32[]{:S(2)}, u32[]{:S(2)}) collective-permute-start(f32[3,32,1,512]{3,2,1,0:T(1,128)S(1)} %get-tuple-element.22), channel_id=1, source_target_pairs={{1,0},{2,1},{3,2},{0,3},{5,4},{6,5},{7,6},{4,7},{9,8},{10,9},{11,1... | collective-permute-start | bytes 589832 | tf_op jit(solution)/shard_map/ppermute | solution.py:42
  44.1 28.8 %collective-permute-start.6 = (f32[1,64,512]{2,1,0:T(8,128)S(1)}, f32[1,64,512]{2,1,0:T(8,128)S(1)}, u32[]{:S(2)}, u32[]{:S(2)}) collective-permute-start(f32[1,64,512]{2,1,0:T(8,128)S(1)} %get-tuple-element.33), channel_id=1, source_target_pairs={{0,4},{4,8},{8,12},{12,16},{16,20},{20,24},{24,28},{28,0},{1,5},{5... | collective-permute-start | bytes 393224 | tf_op jit(solution)/shard_map/ppermute | solution.py:42
  44.2 28.7 %collective-permute-start.7 = (f32[1,64,512]{2,1,0:T(8,128)S(1)}, f32[1,64,512]{2,1,0:T(8,128)S(1)}, u32[]{:S(2)}, u32[]{:S(2)}) collective-permute-start(f32[1,64,512]{2,1,0:T(8,128)S(1)} %get-tuple-element.32), channel_id=1, source_target_pairs={{4,0},{8,4},{12,8},{16,12},{20,16},{24,20},{28,24},{0,28},{5,1},{9... | collective-permute-start | bytes 393224 | tf_op jit(solution)/shard_map/ppermute | solution.py:42
  78.1 31.8 %collective-permute-start.10 = (f32[3,1,64,512]{3,2,1,0:T(8,128)S(1)}, f32[3,1,64,512]{3,2,1,0:T(8,128)S(1)}, u32[]{:S(2)}, u32[]{:S(2)}) collective-permute-start(f32[3,1,64,512]{3,2,1,0:T(8,128)S(1)} %get-tuple-element.17), channel_id=1, source_target_pairs={{0,4},{4,8},{8,12},{12,16},{16,20},{20,24},{24,28},{28,0},{1,5},{5... | collective-permute-start | bytes 1179656 | tf_op jit(solution)/shard_map/ppermute | solution.py:42
  78.2 31.7 %collective-permute-start.11 = (f32[3,1,64,512]{3,2,1,0:T(8,128)S(1)}, f32[3,1,64,512]{3,2,1,0:T(8,128)S(1)}, u32[]{:S(2)}, u32[]{:S(2)}) collective-permute-start(f32[3,1,64,512]{3,2,1,0:T(8,128)S(1)} %get-tuple-element.16), channel_id=1, source_target_pairs={{4,0},{8,4},{12,8},{16,12},{20,16},{24,20},{28,24},{0,28},{5,1},{9... | collective-permute-start | bytes 1179656 | tf_op jit(solution)/shard_map/ppermute | solution.py:42
  113.2 29.3 %collective-permute-start.14 = (f32[1,64,512]{2,1,0:T(8,128)S(1)}, f32[1,64,512]{2,1,0:T(8,128)S(1)}, u32[]{:S(2)}, u32[]{:S(2)}) collective-permute-start(f32[1,64,512]{2,1,0:T(8,128)S(1)} %get-tuple-element.29), channel_id=1, source_target_pairs={{0,4},{4,8},{8,12},{12,16},{16,20},{20,24},{24,28},{28,0},{1,5},{5... | collective-permute-start | bytes 393224 | tf_op jit(solution)/shard_map/ppermute | solution.py:42
  113.3 29.2 %collective-permute-start.15 = (f32[1,64,512]{2,1,0:T(8,128)S(1)}, f32[1,64,512]{2,1,0:T(8,128)S(1)}, u32[]{:S(2)}, u32[]{:S(2)}) collective-permute-start(f32[1,64,512]{2,1,0:T(8,128)S(1)} %get-tuple-element.28), channel_id=1, source_target_pairs={{4,0},{8,4},{12,8},{16,12},{20,16},{24,20},{28,24},{0,28},{5,1},{9... | collective-permute-start | bytes 393224 | tf_op jit(solution)/shard_map/ppermute | solution.py:42
  152.7 15.7 %collective-permute-start.16 = (f32[1,64,512]{2,1,0:T(8,128)S(1)}, f32[1,64,512]{2,1,0:T(8,128)S(1)}, u32[]{:S(2)}, u32[]{:S(2)}) collective-permute-start(f32[1,64,512]{2,1,0:T(8,128)S(1)} %get-tuple-element.15), channel_id=1, source_target_pairs={{0,4},{4,8},{8,12},{12,16},{16,20},{20,24},{24,28},{28,0},{1,5},{5... | collective-permute-start | bytes 393224 | tf_op jit(solution)/shard_map/ppermute | solution.py:42
  152.8 15.6 %collective-permute-start.17 = (f32[1,64,512]{2,1,0:T(8,128)S(1)}, f32[1,64,512]{2,1,0:T(8,128)S(1)}, u32[]{:S(2)}, u32[]{:S(2)}) collective-permute-start(f32[1,64,512]{2,1,0:T(8,128)S(1)} %get-tuple-element.14), channel_id=1, source_target_pairs={{4,0},{8,4},{12,8},{16,12},{20,16},{24,20},{28,24},{0,28},{5,1},{9... | collective-permute-start | bytes 393224 | tf_op jit(solution)/shard_map/ppermute | solution.py:42
  156.9 11.4 %collective-permute-start.18 = (f32[32,1,512]{2,0,1:T(8,128)S(1)}, f32[32,1,512]{2,0,1:T(8,128)S(1)}, u32[]{:S(2)}, u32[]{:S(2)}) collective-permute-start(f32[32,1,512]{2,0,1:T(8,128)S(1)} %get-tuple-element.27), channel_id=1, source_target_pairs={{0,1},{1,2},{2,3},{3,0},{4,5},{5,6},{6,7},{7,4},{8,9},{9,10},{10,1... | collective-permute-start | bytes 196616 | tf_op jit(solution)/shard_map/ppermute | solution.py:42
  158.0 10.4 %collective-permute-start.19 = (f32[32,1,512]{2,0,1:T(8,128)S(1)}, f32[32,1,512]{2,0,1:T(8,128)S(1)}, u32[]{:S(2)}, u32[]{:S(2)}) collective-permute-start(f32[32,1,512]{2,0,1:T(8,128)S(1)} %get-tuple-element.26), channel_id=1, source_target_pairs={{1,0},{2,1},{3,2},{0,3},{5,4},{6,5},{7,6},{4,7},{9,8},{10,9},{11,1... | collective-permute-start | bytes 196616 | tf_op jit(solution)/shard_map/ppermute | solution.py:42
  172.9 53.9 %all-to-all-start = ((f32[4,32,64,128]{3,2,1,0:T(8,128)}), f32[4,32,64,128]{3,2,1,0:T(8,128)}, u32[]{:S(2)}, u32[]{:S(2)}) async-start(f32[4,32,64,128]{3,2,1,0:T(8,128)} %add_halo_modes.1), calls=%async_computation | async-start | bytes 8388608 | tf_op jit(solution)/shard_map/all_to_all | solution.py:889
  177.8 130.4 %reduce-scatter.2.cloned.1.call-start = ((), (), s32[]{:S(2)}) async-start(), calls=%async_computation.5 | async-start | bytes 2359296 | tf_op jit(solution)/shard_map/reduce_scatter | solution.py:966
  239.3 24.7 %all-to-all-start.1 = ((f32[8,4,32,128]{3,2,1,0:T(8,128)}), f32[8,4,32,128]{3,2,1,0:T(8,128)S(1)}, u32[]{:S(2)}, u32[]{:S(2)}) async-start(f32[8,4,32,128]{3,2,1,0:T(8,128)} %get-tuple-element.12), calls=%async_computation.1 | async-start | bytes 1048576 | tf_op jit(solution)/shard_map/all_to_all | solution.py:889
  296.9 58.7 %all-to-all-start.3 = ((f32[4,34,64,128]{3,2,1,0:T(8,128)}), f32[4,34,64,128]{3,2,1,0:T(8,128)}, u32[]{:S(2)}, u32[]{:S(2)}) async-start(f32[4,34,64,128]{3,2,1,0:T(8,128)} %y_inverse.1), calls=%async_computation.3 | async-start | bytes 8912896 | tf_op jit(solution)/shard_map/all_to_all | solution.py:889
  306.8 7.7 %collective-permute-start.27 = (f32[2,32,128]{2,1,0:T(8,128)S(1)}, f32[2,32,128]{2,1,0:T(8,128)S(1)}, u32[]{:S(2)}, u32[]{:S(2)}) collective-permute-start(f32[2,32,128]{2,1,0:T(8,128)S(1)} %get-tuple-element.48), channel_id=1, source_target_pairs={{4,0},{8,4},{12,8},{16,12},{20,16},{24,20},{28,24},{5,1},{9,5},{13... | collective-permute-start | bytes 98312 | tf_op jit(solution)/shard_map/ppermute | solution.py:31
  313.2 5.4 %collective-permute-start.23 = (f32[3,32,128]{2,1,0:T(8,128)S(1)}, f32[3,32,128]{2,1,0:T(8,128)S(1)}, u32[]{:S(2)}, u32[]{:S(2)}) collective-permute-start(f32[3,32,128]{2,1,0:T(8,128)S(1)} %get-tuple-element.51), channel_id=1, source_target_pairs={{4,0},{8,4},{12,8},{16,12},{20,16},{24,20},{28,24},{5,1},{9,5},{13... | collective-permute-start | bytes 147464 | tf_op jit(solution)/shard_map/ppermute | solution.py:31
  318.7 33.9 %collective-permute-start.24 = (f32[22,3,128]{2,1,0:T(4,128)S(1)}, f32[22,3,128]{2,1,0:T(4,128)S(1)}, u32[]{:S(2)}, u32[]{:S(2)}) collective-permute-start(f32[22,3,128]{2,1,0:T(4,128)S(1)} %get-tuple-element.44), channel_id=1, source_target_pairs={{0,1},{1,2},{2,3},{4,5},{5,6},{6,7},{8,9},{9,10},{10,11},{12,13},{... | collective-permute-start | bytes 101384 | tf_op jit(solution)/shard_map/ppermute | solution.py:30
  323.6 30.8 %collective-permute-start.25 = (f32[22,3,128]{2,1,0:T(4,128)S(1)}, f32[22,3,128]{2,1,0:T(4,128)S(1)}, u32[]{:S(2)}, u32[]{:S(2)}) collective-permute-start(f32[22,3,128]{2,1,0:T(4,128)S(1)} %get-tuple-element.45), channel_id=1, source_target_pairs={{1,0},{2,1},{3,2},{5,4},{6,5},{7,6},{9,8},{10,9},{11,10},{13,12},{... | collective-permute-start | bytes 101384 | tf_op jit(solution)/shard_map/ppermute | solution.py:31
  325.6 29.1 %collective-permute-start.28 = (f32[20,2,128]{2,1,0:T(2,128)S(1)}, f32[20,2,128]{2,1,0:T(2,128)S(1)}, u32[]{:S(2)}, u32[]{:S(2)}) collective-permute-start(f32[20,2,128]{2,1,0:T(2,128)S(1)} %get-tuple-element.46), channel_id=1, source_target_pairs={{0,1},{1,2},{2,3},{4,5},{5,6},{6,7},{8,9},{9,10},{10,11},{12,13},{... | collective-permute-start | bytes 61448 | tf_op jit(solution)/shard_map/ppermute | solution.py:30
  329.2 25.4 %collective-permute-start.29 = (f32[20,2,128]{2,1,0:T(2,128)S(1)}, f32[20,2,128]{2,1,0:T(2,128)S(1)}, u32[]{:S(2)}, u32[]{:S(2)}) collective-permute-start(f32[20,2,128]{2,1,0:T(2,128)S(1)} %get-tuple-element.47), channel_id=1, source_target_pairs={{1,0},{2,1},{3,2},{5,4},{6,5},{7,6},{9,8},{10,9},{11,10},{13,12},{... | collective-permute-start | bytes 61448 | tf_op jit(solution)/shard_map/ppermute | solution.py:31
  (24 other events, 146.1 us)
Sparse Core Ops, SparseCore 0:
  225.3 70.7 reduce-scatter.1

commit v5 on v4

--- a/solution.py
+++ b/solution.py
@@ -7,6 +7,7 @@
 from jax.experimental import pallas as pl
 from jax.experimental.pallas import tpu as pltpu
 from jax.sharding import PartitionSpec as P
+
 
 PASSES = 2
 STEPS = 3
@@ -33,16 +34,20 @@
     return x
 
 
+def shift(value, axis, by):
+    size = lax.axis_size(axis)
+    return lax.ppermute(value, axis, [(i, (i + by) % size) for i in range(size)])
+
+
 def ring(value, axis, dim):
-    size, length = lax.axis_size(axis), value.shape[dim]
-    up = [(i, (i + 1) % size) for i in range(size)]
-    down = [(j, i) for i, j in up]
+    length = value.shape[dim]
     last = lax.slice_in_dim(value, length - 1, length, axis=dim)
     initial = lax.slice_in_dim(value, 0, 1, axis=dim)
-    return lax.ppermute(last, axis, up), lax.ppermute(initial, axis, down)
+    return shift(last, axis, 1), shift(initial, axis, -1)
 
 
 anywhere = pl.BlockSpec(memory_space=pl.ANY)
+in_smem = pl.BlockSpec(memory_space=pltpu.SMEM)
 in_vmem = pl.BlockSpec(memory_space=pltpu.VMEM)
 scaled_mu = 0.5 * time_step
 
@@ -435,10 +440,6 @@
     return even, odd, np.concatenate([eigen_even, eigen_odd])
 
 
-def whole(*shape):
-    return pl.BlockSpec(shape, lambda *index: (0,) * len(shape))
-
-
 def modes_of(lines, even_high, even_low, odd_high, odd_low):
     half = lines.shape[1] // 2
     first, second = lines[:, :half], lines[:, half:]
@@ -458,39 +459,50 @@
     return jnp.concatenate([first + second, first - second], 1)
 
 
-def divergence_modes(flow, count):
+def divergence_modes(flow, own, count):
     _, x_local, y_local, z_cells = flow.shape
-    half, piece, strips = z_cells // 2, z_cells // count, y_local // 8
-    step = min(8, x_local)
+    piece, strips = z_cells // count, y_local // 8
+    step, pairs = min(8, x_local), x_local // 2
+    groups = x_local // step
     even, odd, _ = z_tables(z_cells)
     tables = halves(even) + halves(odd)
 
     def kernel(
-        flow_ref, even_high, even_low, odd_high, odd_low, out_ref,
-        cells, semaphores, work, made, out_sem,
+        flow_ref, own_ref, even_high, even_low, odd_high, odd_low, *rest
     ):
-        planes = Planes(flow_ref, cells, semaphores)
+        out_refs, rest = rest[: 2 * count], rest[2 * count :]
+        cells, semaphores, work, first, second, out_sem = rest
         rows = row_numbers(z_cells)
-
-        def begin(i, state):
-            planes.start(i)
-            return state
-
-        lax.fori_loop(0, x_local, begin, 0)
-        planes.wait(0)
-
-        def stored(k):
+        me = own_ref[0]
+
+        def load(k):
             part = pl.ds(k * step, step)
-            return pltpu.make_async_copy(made.at[:, part], out_ref.at[:, part], out_sem.at[k])
+            return pltpu.make_async_copy(
+                flow_ref.at[:, part], cells.at[:, part], semaphores.at[k]
+            )
+
+        for k in range(groups):
+            load(k).start()
+        load(0).wait()
+
+        def stored(k, parity):
+            part = pl.ds(k * (step // 2), step // 2)
+            return [
+                pltpu.make_async_copy(
+                    (first, second)[parity].at[me ^ n, part],
+                    out_refs[parity * count + n].at[part],
+                    out_sem.at[2 * k + parity, n],
+                )
+                for n in range(count)
+            ]
 
         def group(k, state):
+            @pl.when(k + 1 < groups)
+            def _():
+                load(k + 1).wait()
+
             def plane(i, state):
                 j = k * step + i
-
-                @pl.when(j + 1 < x_local)
-                def _():
-                    planes.wait(j + 1)
-
                 nearer = jnp.where(j > 0, 0.5, 0.0)
                 further = jnp.where(j + 1 < x_local, 0.5, 0.0)
                 last, following = jnp.maximum(j - 1, 0), jnp.minimum(j + 1, x_local - 1)
@@ -515,99 +527,97 @@
                 work[...].reshape(step * y_local, z_cells), even_high, even_low, odd_high, odd_low
             )
             for n in range(count):
-                made[n, pl.ds(k * step, step)] = modes[:, n * piece : (n + 1) * piece].reshape(
-                    step, y_local, piece
-                )
-            stored(k).start()
+                for i in range(step):
+                    (first, second)[i % 2][n, k * (step // 2) + i // 2] = modes[
+                        i * y_local : (i + 1) * y_local, n * piece : (n + 1) * piece
+                    ]
+            for parity in range(2):
+                for copy in stored(k, parity):
+                    copy.start()
             return state
 
-        groups = x_local // step
         lax.fori_loop(0, groups, group, 0)
         for k in range(groups):
-            stored(k).wait()
-
-    return pl.pallas_call(
+            for parity in range(2):
+                for copy in stored(k, parity):
+                    copy.wait()
+
+    made = (count, pairs, y_local, piece)
+    outputs = pl.pallas_call(
         kernel,
-        in_specs=[anywhere] + [in_vmem] * 4,
-        out_specs=anywhere,
-        out_shape=jax.ShapeDtypeStruct((count, x_local, y_local, piece), jnp.float32),
+        in_specs=[anywhere, in_smem] + [in_vmem] * 4,
+        out_specs=[anywhere] * (2 * count),
+        out_shape=[jax.ShapeDtypeStruct(made[1:], jnp.float32)] * (2 * count),
         scratch_shapes=[
             pltpu.VMEM((3, x_local, y_local, z_cells), jnp.float32),
-            pltpu.SemaphoreType.DMA((x_local,)),
+            pltpu.SemaphoreType.DMA((groups,)),
             pltpu.VMEM((step, y_local, z_cells), jnp.float32),
-            pltpu.VMEM((count, x_local, y_local, piece), jnp.float32),
-            pltpu.SemaphoreType.DMA((x_local // step,)),
+            pltpu.VMEM(made, jnp.float32),
+            pltpu.VMEM(made, jnp.float32),
+            pltpu.SemaphoreType.DMA((2 * groups, count)),
         ],
         name="divergence_modes",
-    )(flow, *tables)
-
-
-def add_halo_modes(modes, x_sides, y_sides):
-    count, x_local, y_local, piece = modes.shape
+    )(flow, own, *tables)
+    return outputs[:count], outputs[count:]
+
+
+def add_halo_modes(modes, own, end, y_sides, parity):
+    count = len(modes)
+    pairs, y_local, piece = modes[0].shape
     z_cells = count * piece
+    tail = pairs - 1 if parity else 0
     even, odd, _ = z_tables(z_cells)
     tables = halves(even) + halves(odd)
-
-    def kernel(
-        modes_ref, low_ref, high_ref, before_ref, after_ref,
-        even_high, even_low, odd_high, odd_low, out_ref, ends, lines, semaphores,
-    ):
-        def moves(back):
-            pairs = [
-                (ends.at[k], modes_ref.at[:, plane])
-                for k, plane in enumerate((0, x_local - 1))
-            ] + [
-                (lines.at[k], modes_ref.at[:, 1 : x_local - 1, 8 * s : 8 * s + 8])
-                for k, s in enumerate((0, y_local // 8 - 1))
+    strips = (0, y_local // 8 - 1)
+
+    def kernel(*refs):
+        modes_refs, refs = refs[:count], refs[count:]
+        own_ref, end_ref, before_ref, after_ref = refs[:4]
+        table_refs, refs = refs[4:8], refs[8:]
+        out_refs, (plane, lines, added, semaphores) = refs[:count], refs[count:]
+
+        def moves(refs):
+            return [(plane.at[n], refs[n].at[tail]) for n in range(count)] + [
+                (lines.at[k, n], refs[n].at[:, 8 * s : 8 * s + 8])
+                for k, s in enumerate(strips)
+                for n in range(count)
             ]
-            if back:
-                pairs = [
-                    (ends.at[k], out_ref.at[:, plane])
-                    for k, plane in enumerate((0, x_local - 1))
-                ] + [
-                    (lines.at[k], out_ref.at[:, 1 : x_local - 1, 8 * s : 8 * s + 8])
-                    for k, s in enumerate((0, y_local // 8 - 1))
-                ]
-                return [
-                    pltpu.make_async_copy(here, there, semaphores.at[4 + i])
-                    for i, (here, there) in enumerate(pairs)
-                ]
-            return [
-                pltpu.make_async_copy(there, here, semaphores.at[i])
-                for i, (here, there) in enumerate(pairs)
-            ]
-
-        loads, stores = moves(False), moves(True)
+
+        loads = [
+            pltpu.make_async_copy(there, here, semaphores.at[i])
+            for i, (here, there) in enumerate(moves(modes_refs))
+        ]
         for load in loads:
             load.start()
-        added = modes_of(
+        sign = 0.5 if parity else -0.5
+        result = modes_of(
             jnp.concatenate(
-                [-0.5 * low_ref[0], 0.5 * high_ref[0], -0.5 * before_ref[...], 0.5 * after_ref[...]],
-                0,
+                [sign * end_ref[0], -0.5 * before_ref[...], 0.5 * after_ref[...]], 0
             ),
-            even_high,
-            even_low,
-            odd_high,
-            odd_low,
+            *table_refs,
         )
+        for n in range(count):
+            added[n] = result[:, n * piece : (n + 1) * piece]
         for load in loads:
             load.wait()
         rows = row_numbers(piece)
         for n in range(count):
-            block = added[:, n * piece : (n + 1) * piece]
-            side = [block[2 * y_local + k * x_local :][:x_local] for k in range(2)]
-            for k, plane in enumerate((0, x_local - 1)):
-                ends[k, n] = ends[k, n] + block[k * y_local : (k + 1) * y_local]
-                for j, (strip, row) in enumerate(((0, 0), (y_local // 8 - 1, 7))):
-                    part = pl.ds(8 * strip, 8)
-                    ends[k, n, part, :] = ends[k, n, part, :] + jnp.where(
-                        rows == row, side[j][plane : plane + 1], 0.0
-                    )
+            block = added.at[own_ref[0] ^ n]
             for j, row in enumerate((0, 7)):
-                for x in range(1, x_local - 1):
-                    lines[j, n, x - 1] = lines[j, n, x - 1] + jnp.where(
-                        rows == row, side[j][x : x + 1], 0.0
-                    )
+                for x in range(pairs):
+                    side = block[pl.ds(y_local + j * pairs + x, 1), :]
+                    lines[j, n, x] = lines[j, n, x] + jnp.where(rows == row, side, 0.0)
+            plane[n] = plane[n] + block[pl.ds(0, y_local), :]
+            for j, s in enumerate(strips):
+                lines[j, n, tail] = lines[j, n, tail] + block[rows_of(s), :]
+        inside = [
+            (plane.at[n, 8 : y_local - 8], out_refs[n].at[tail, 8 : y_local - 8])
+            for n in range(count)
+        ]
+        stores = [
+            pltpu.make_async_copy(here, there, semaphores.at[3 * count + i])
+            for i, (here, there) in enumerate(inside + moves(out_refs)[count:])
+        ]
         for store in stores:
             store.start()
         for store in stores:
@@ -615,53 +625,102 @@
 
     return pl.pallas_call(
         kernel,
-        in_specs=[anywhere] + [in_vmem] * 8,
-        out_specs=anywhere,
-        out_shape=jax.ShapeDtypeStruct(modes.shape, jnp.float32),
-        input_output_aliases={0: 0},
+        in_specs=[anywhere] * count + [in_smem] + [in_vmem] * 7,
+        out_specs=[anywhere] * count,
+        out_shape=[jax.ShapeDtypeStruct(modes[0].shape, jnp.float32)] * count,
+        input_output_aliases={n: n for n in range(count)},
         scratch_shapes=[
-            pltpu.VMEM((2, count, y_local, piece), jnp.float32),
-            pltpu.VMEM((2, count, x_local - 2, 8, piece), jnp.float32),
-            pltpu.SemaphoreType.DMA((8,)),
+            pltpu.VMEM((count, y_local, piece), jnp.float32),
+            pltpu.VMEM((2, count, pairs, 8, piece), jnp.float32),
+            pltpu.VMEM((count, y_local + 2 * pairs, piece), jnp.float32),
+            pltpu.SemaphoreType.DMA((6 * count,)),
         ],
         name="add_halo_modes",
-    )(modes, *x_sides, *y_sides, *tables)
-
-
-def corrected(flow, spectrum, y_sides):
-    count, planes, y_local, piece = spectrum.shape
-    x_local, z_cells = planes - 2, count * piece
-    strips, part = y_local // 8, planes // 2
+    )(*modes, own, end, *y_sides, *tables)
+
+
+def pressure_planes(spectrum, own):
+    count = len(spectrum)
+    planes, y_local, piece = spectrum[0].shape
+    z_cells = count * piece
     even, odd, _ = z_tables(z_cells)
     tables = halves(even.T) + halves(odd.T)
 
-    def kernel(
-        flow_ref, in_ref, before_ref, after_ref,
-        even_high, even_low, odd_high, odd_low, out_ref,
-        modes, mode_sem, pressure, sides, work, flow_sem, out_sem,
-    ):
-        flow_planes = Planes(flow_ref, work, flow_sem)
-        table_refs = (even_high, even_low, odd_high, odd_low)
+    def kernel(*refs):
+        in_refs, refs = refs[:count], refs[count:]
+        own_ref, table_refs, (out_ref, modes, semaphores) = refs[0], refs[1:5], refs[5:]
+        loads = [
+            pltpu.make_async_copy(in_refs[k], modes.at[own_ref[0] ^ k], semaphores.at[k])
+            for k in range(count)
+        ]
+        for load in loads:
+            load.start()
+        for load in loads:
+            load.wait()
+        out_ref[...] = cells_of(
+            jnp.concatenate(
+                [modes[n].reshape(planes * y_local, piece) for n in range(count)], 1
+            ),
+            *table_refs,
+        ).reshape(planes, y_local, z_cells)
+
+    return pl.pallas_call(
+        kernel,
+        in_specs=[anywhere] * count + [in_smem] + [in_vmem] * 4,
+        out_specs=in_vmem,
+        out_shape=jax.ShapeDtypeStruct((planes, y_local, z_cells), jnp.float32),
+        scratch_shapes=[
+            pltpu.VMEM((count, planes, y_local, piece), jnp.float32),
+            pltpu.SemaphoreType.DMA((count,)),
+        ],
+        compiler_params=pltpu.CompilerParams(vmem_limit_bytes=vmem_limit),
+        name="pressure_planes",
+    )(*spectrum, own, *tables)
+
+
+def corrected(flow, even_pressure, odd_spectrum, own, sides):
+    count = len(odd_spectrum)
+    planes, y_local, piece = odd_spectrum[0].shape
+    pairs = planes - 1
+    x_local, z_cells = 2 * pairs, count * piece
+    strips, cut = y_local // 8, planes // 2 + 1
+    spans = ((0, cut), (cut, planes))
+    even, odd, _ = z_tables(z_cells)
+    tables = halves(even.T) + halves(odd.T)
+
+    def kernel(*refs):
+        in_refs, refs = refs[:count], refs[count:]
+        own_ref, flow_ref, even_ref, side_ref = refs[:4]
+        table_refs, refs = refs[4:8], refs[8:]
+        out_ref, modes, mode_sem, pressure, lines, work, flow_sem, out_sem = refs
+        me = own_ref[0]
 
         def load(k):
-            span = pl.ds(k * part, part)
-            return pltpu.make_async_copy(in_ref.at[:, span], modes.at[:, span], mode_sem.at[k])
-
-        load(0).start()
-        load(1).start()
-
-        def begin(i, state):
-            flow_planes.start(i)
-            return state
-
-        lax.fori_loop(0, x_local, begin, 0)
-        sides[...] = cells_of(
+            span = pl.ds(spans[k][0], spans[k][1] - spans[k][0])
+            return [
+                pltpu.make_async_copy(
+                    in_refs[n].at[span], modes.at[me ^ n, span], mode_sem.at[k, n]
+                )
+                for n in range(count)
+            ]
+
+        def brought(k):
+            span = pl.ds(k * pairs, pairs)
+            return pltpu.make_async_copy(flow_ref.at[:, span], work.at[:, span], flow_sem.at[k])
+
+        for k in range(2):
+            for copy in load(k):
+                copy.start()
+        for k in range(2):
+            brought(k).start()
+        senders = ((me + count - 1) % count, (me + 1) % count)
+        lines[...] = cells_of(
             jnp.concatenate(
                 [
-                    jnp.concatenate([ref[n] for n in range(count)], 1)
-                    for ref in (before_ref, after_ref)
+                    jnp.concatenate([side_ref[i, senders[i % 2] ^ n] for i in range(4)], 0)
+                    for n in range(count)
                 ],
-                0,
+                1,
             ),
             *table_refs,
         )
@@ -670,34 +729,45 @@
         def stored(i):
             return pltpu.make_async_copy(pick(work, i), pick(out_ref, i), out_sem.at[i])
 
-        def plane(j, state):
-            flow_planes.wait(j)
-            values = [pressure[j + 1, rows_of(s), :] for s in range(strips)]
+        def correct(j, center, low, high, side):
+            values = [center[rows_of(s), :] for s in range(strips)]
             up = [pltpu.roll(v, 7, 0) for v in values]
             down = [pltpu.roll(v, 1, 0) for v in values]
             for s in range(strips):
-                ahead = up[s + 1] if s + 1 < strips else sides[pl.ds(x_local + j, 1), :]
-                behind = down[s - 1] if s else sides[pl.ds(j, 1), :]
+                ahead = up[s + 1] if s + 1 < strips else lines[pl.ds(side + pairs, 1), :]
+                behind = down[s - 1] if s else lines[pl.ds(side, 1), :]
                 slopes = (
-                    pressure[j + 2, rows_of(s), :] - pressure[j, rows_of(s), :],
+                    high[rows_of(s), :] - low[rows_of(s), :],
                     jnp.where(rows == 7, ahead, up[s]) - jnp.where(rows == 0, behind, down[s]),
                     pltpu.roll(values[s], z_cells - 1, 1) - pltpu.roll(values[s], 1, 1),
                 )
                 for c in range(3):
                     work[c, j, rows_of(s), :] = work[c, j, rows_of(s), :] - 0.5 * slopes[c]
             stored(j).start()
+
+        def pair(k, state):
+            correct(2 * k, even_ref.at[k], pressure.at[k], pressure.at[k + 1], k)
+            correct(
+                2 * k + 1, pressure.at[k + 1], even_ref.at[k], even_ref.at[k + 1], 2 * pairs + k
+            )
             return state
 
         for k in range(2):
-            load(k).wait()
-            span = pl.ds(k * part, part)
-            pressure[span] = cells_of(
+            for copy in load(k):
+                copy.wait()
+            start, stop = spans[k]
+            pressure[start:stop] = cells_of(
                 jnp.concatenate(
-                    [modes[n, span].reshape(part * y_local, piece) for n in range(count)], 1
+                    [
+                        modes[n, start:stop].reshape((stop - start) * y_local, piece)
+                        for n in range(count)
+                    ],
+                    1,
                 ),
                 *table_refs,
-            ).reshape(part, y_local, z_cells)
-            lax.fori_loop(k * (part - 2), (part - 2) if k == 0 else x_local, plane, 0)
+            ).reshape(stop - start, y_local, z_cells)
+            brought(k).wait()
+            lax.fori_loop(*((0, cut - 1) if k == 0 else (cut - 1, pairs)), pair, 0)
 
         def finish(i, state):
             stored(i).wait()
@@ -707,78 +777,94 @@
 
     return pl.pallas_call(
         kernel,
-        in_specs=[anywhere, anywhere] + [in_vmem] * 6,
+        in_specs=[anywhere] * count + [in_smem, anywhere] + [in_vmem] * 6,
         out_specs=anywhere,
         out_shape=jax.ShapeDtypeStruct(flow.shape, jnp.float32),
         scratch_shapes=[
-            pltpu.VMEM(spectrum.shape, jnp.float32),
+            pltpu.VMEM((count, planes, y_local, piece), jnp.float32),
+            pltpu.SemaphoreType.DMA((2, count)),
+            pltpu.VMEM((planes, y_local, z_cells), jnp.float32),
+            pltpu.VMEM((4 * pairs, z_cells), jnp.float32),
+            pltpu.VMEM(flow.shape, jnp.float32),
             pltpu.SemaphoreType.DMA((2,)),
-            pltpu.VMEM((planes, y_local, z_cells), jnp.float32),
-            pltpu.VMEM((2 * x_local, z_cells), jnp.float32),
-            pltpu.VMEM(flow.shape, jnp.float32),
-            pltpu.SemaphoreType.DMA((x_local,)),
             pltpu.SemaphoreType.DMA((x_local,)),
         ],
         compiler_params=pltpu.CompilerParams(vmem_limit_bytes=vmem_limit),
         name="corrected",
-    )(flow, spectrum, *y_sides, *tables)
-
-
-def y_forward(spectrum, ratio, wide_count):
-    count, x_local, y_local, piece = spectrum.shape
+    )(*odd_spectrum, own, flow, even_pressure, sides, *tables)
+
+
+def y_forward(spectrum, own, ratio, wide_count):
+    count = len(spectrum)
+    pairs, y_local, piece = spectrum[0].shape
     y_cells = count * y_local
-    share = y_cells // wide_count
+    share, steps, group = y_cells // wide_count, pairs // 2, max(2, pairs // 4)
     table, _ = cosine_sine_basis(y_cells, y_cells, range(y_cells // 2 + 1))
     tables = halves(table.T)
 
-    def kernel(in_ref, high_ref, low_ref, ratio_ref, modes_ref, carry_ref, sums, power):
-        @pl.when(pl.program_id(0) == 0)
-        def _():
-            sums[...] = jnp.zeros_like(sums)
-            power[...] = jnp.ones_like(power)
-
-        planes = [
-            jnp.concatenate([in_ref[n, side] for n in range(count)], 0) for side in range(2)
-        ]
-        modes = triple_product(
-            (high_ref[...], low_ref[...]), split(jnp.concatenate(planes, 1))
-        )
-        r, pw = ratio_ref[...], power[...]
-        for side in range(2):
-            plane = modes[:, side * piece : (side + 1) * piece]
-            modes_ref[side] = plane
-            sums[side] = plane + r * sums[side]
-            sums[2 + side] = sums[2 + side] + pw * plane
-        power[...] = pw * r
-
-        @pl.when(pl.program_id(0) == x_local // 2 - 1)
-        def _():
-            for kind in range(4):
-                carry_ref[:, kind] = sums[kind].reshape(wide_count, share, piece)
+    def kernel(*refs):
+        in_refs, refs = refs[:count], refs[count:]
+        own_ref, high_ref, low_ref, ratio_ref, modes_ref, carry_ref = refs[:6]
+        lines, sems, sums, power = refs[6:]
+
+        def load(k):
+            part = pl.ds(k * group, group)
+            return [
+                pltpu.make_async_copy(
+                    in_refs[n].at[part], lines.at[own_ref[0] ^ n, part], sems.at[k, n]
+                )
+                for n in range(count)
+            ]
+
+        for k in range(pairs // group):
+            for copy in load(k):
+                copy.start()
+        sums[...] = jnp.zeros_like(sums)
+        power[...] = jnp.ones_like(power)
+
+        def body(k, state):
+            @pl.when(k % (group // 2) == 0)
+            def _():
+                for copy in load(k // (group // 2)):
+                    copy.wait()
+
+            planes = [
+                jnp.concatenate([lines[n, 2 * k + side] for n in range(count)], 0)
+                for side in range(2)
+            ]
+            modes = triple_product(
+                (high_ref[...], low_ref[...]), split(jnp.concatenate(planes, 1))
+            )
+            r, pw = ratio_ref[...], power[...]
+            one, two = modes[:, :piece], modes[:, piece:]
+            modes_ref[2 * k] = one
+            modes_ref[2 * k + 1] = two
+            sums[0] = two + r * (one + r * sums[0])
+            sums[1] = sums[1] + pw * (one + r * two)
+            power[...] = pw * (r * r)
+            return state
+
+        lax.fori_loop(0, steps, body, 0)
+        for kind in range(2):
+            carry_ref[:, kind] = sums[kind].reshape(wide_count, share, piece)
 
     return pl.pallas_call(
         kernel,
-        grid=(x_local // 2,),
-        in_specs=[
-            pl.BlockSpec((count, 2, y_local, piece), lambda i: (0, i, 0, 0)),
-            whole(y_cells, y_cells),
-            whole(y_cells, y_cells),
-            whole(y_cells, piece),
-        ],
-        out_specs=[
-            pl.BlockSpec((2, y_cells, piece), lambda i: (i, 0, 0)),
-            whole(wide_count, 4, share, piece),
-        ],
+        in_specs=[anywhere] * count + [in_smem] + [in_vmem] * 3,
+        out_specs=[in_vmem, in_vmem],
         out_shape=[
-            jax.ShapeDtypeStruct((x_local, y_cells, piece), jnp.float32),
-            jax.ShapeDtypeStruct((wide_count, 4, share, piece), jnp.float32),
+            jax.ShapeDtypeStruct((pairs, y_cells, piece), jnp.float32),
+            jax.ShapeDtypeStruct((wide_count, 2, share, piece), jnp.float32),
         ],
         scratch_shapes=[
-            pltpu.VMEM((4, y_cells, piece), jnp.float32),
+            pltpu.VMEM((count, pairs, y_local, piece), jnp.float32),
+            pltpu.SemaphoreType.DMA((pairs // group, count)),
+            pltpu.VMEM((2, y_cells, piece), jnp.float32),
             pltpu.VMEM((y_cells, piece), jnp.float32),
         ],
+        compiler_params=pltpu.CompilerParams(vmem_limit_bytes=24 << 20),
         name="y_forward",
-    )(spectrum, *tables, ratio)
+    )(*spectrum, own, *tables, ratio)
 
 
 def power_of(value, exponent):
@@ -792,13 +878,13 @@
 
 
 def join_carries(carries, ratio, block):
-    count, kinds, share, piece = carries.shape
+    count, kinds, _, _ = carries.shape
 
     def kernel(in_ref, ratio_ref, out_ref):
         step = power_of(ratio_ref[...], block)
         scale = 1.0 / (1.0 - power_of(step, count))
         for kind in range(kinds):
-            order = list(range(count)) if kind < 2 else list(range(count))[::-1]
+            order = list(range(count)) if kind == 0 else list(range(count))[::-1]
             total = in_ref[order[0], kind]
             for w in order[1:]:
                 total = in_ref[w, kind] + step * total
@@ -809,88 +895,107 @@
 
     return pl.pallas_call(
         kernel,
+        in_specs=[in_vmem] * 2,
+        out_specs=in_vmem,
         out_shape=jax.ShapeDtypeStruct(carries.shape, jnp.float32),
+        compiler_params=pltpu.CompilerParams(vmem_limit_bytes=24 << 20),
         name="join_carries",
     )(carries, ratio)
 
 
-def y_inverse(modes, carries, ratio, gain, count):
-    x_local, y_cells, piece = modes.shape
-    y_local, pairs = y_cells // count, x_local // 2
-    wide_count, _, share, _ = carries.shape
+def y_inverse(modes, carries, own, ratio, gain, count, parity):
+    pairs, y_cells, piece = modes.shape
+    y_local = y_cells // count
     table, _ = cosine_sine_basis(y_cells, y_cells, range(y_cells // 2 + 1))
     tables = halves(table)
 
-    def kernel(modes_ref, carry_ref, high_ref, low_ref, ratio_ref, gain_ref, out_ref, behind, ahead):
-        step = pl.program_id(0)
-        r = ratio_ref[...]
+    def kernel(own_ref, modes_ref, carry_ref, high_ref, low_ref, ratio_ref, gain_ref, *rest):
+        out_refs, (behind, state, cells, sems) = rest[:count], rest[count:]
 
         def carry(kind):
             return carry_ref[:, kind].reshape(y_cells, piece)
 
-        @pl.when(step == 0)
-        def _():
-            ahead[0] = carry(0)
-            ahead[1] = carry(1)
-            behind[2 * pairs + 1] = carry(2)
-
-            def back(i, state):
-                even, odd = state
-                m = pairs - 1 - i
-                behind[2 * m + 2] = r * odd
-                behind[2 * m + 1] = r * even
-                return (
-                    modes_ref[2 * m] + r * even,
-                    modes_ref[2 * m + 1] + r * odd,
+        def stored(k, size):
+            part = pl.ds(k, size)
+            return [
+                pltpu.make_async_copy(
+                    cells.at[own_ref[0] ^ n, part], out_refs[n].at[part], sems.at[k, n]
                 )
-
-            _, odd = lax.fori_loop(0, pairs, back, (carry(2), carry(3)))
-            behind[0] = r * odd
-
-        even_plane = modes_ref[jnp.minimum(2 * step, x_local - 2)]
-        odd_plane = modes_ref[jnp.maximum(2 * step - 1, 1)]
-        even = r * ahead[0] + jnp.where(step < pairs, even_plane, 0.0)
-        odd = jnp.where(step > 0, odd_plane + r * ahead[1], ahead[1])
-        ahead[0] = even
-        ahead[1] = odd
-        gain_value = gain_ref[...]
-        planes = jnp.concatenate(
-            [gain_value * (odd + behind[2 * step]), gain_value * (even + behind[2 * step + 1])], 1
-        )
-        cells = triple_product((high_ref[...], low_ref[...]), split(planes))
-        for n in range(count):
-            for side in range(2):
-                out_ref[n, side] = cells[
-                    n * y_local : (n + 1) * y_local, side * piece : (side + 1) * piece
-                ]
-
+                for n in range(count)
+            ]
+
+        def emit(planes, k):
+            size = len(planes)
+            gain_value = gain_ref[...]
+            joined = jnp.concatenate([gain_value * plane for plane in planes], 1)
+            result = triple_product((high_ref[...], low_ref[...]), split(joined))
+            for n in range(count):
+                for side in range(size):
+                    cells[n, k + side] = result[
+                        n * y_local : (n + 1) * y_local, side * piece : (side + 1) * piece
+                    ]
+            for copy in stored(k, size):
+                copy.start()
+
+        r = ratio_ref[...]
+        state[0] = carry(0)
+        state[1] = carry(1)
+
+        def back(i, done):
+            m = pairs - 1 - i
+            value = state[1]
+            behind[m] = ratio_ref[...] * value
+            state[1] = modes_ref[m] + ratio_ref[...] * value
+            return done
+
+        lax.fori_loop(0, pairs, back, 0)
+        if parity:
+            emit([state[0] + r * state[1]], 0)
+
+        def body(t, done):
+            r = ratio_ref[...]
+            one = modes_ref[2 * t] + r * state[0]
+            two = modes_ref[2 * t + 1] + r * one
+            state[0] = two
+            emit([one + behind[2 * t], two + behind[2 * t + 1]], 2 * t + parity)
+            return done
+
+        lax.fori_loop(0, pairs // 2, body, 0)
+        if not parity:
+            emit([r * state[0] + carry(1)], pairs)
+        for copy in stored(0 if parity else pairs, 1):
+            copy.wait()
+
+        def finish(t, done):
+            for copy in stored(2 * t + parity, 2):
+                copy.wait()
+
+            return done
+
+        lax.fori_loop(0, pairs // 2, finish, 0)
+
+    made = (count, pairs + 1, y_local, piece)
     return pl.pallas_call(
         kernel,
-        grid=(pairs + 1,),
-        in_specs=[
-            whole(x_local, y_cells, piece),
-            whole(wide_count, 4, share, piece),
-            whole(y_cells, y_cells),
-            whole(y_cells, y_cells),
-            whole(y_cells, piece),
-            whole(y_cells, piece),
+        in_specs=[in_smem] + [in_vmem] * 6,
+        out_specs=[anywhere] * count,
+        out_shape=[jax.ShapeDtypeStruct(made[1:], jnp.float32)] * count,
+        scratch_shapes=[
+            pltpu.VMEM((pairs, y_cells, piece), jnp.float32),
+            pltpu.VMEM((2, y_cells, piece), jnp.float32),
+            pltpu.VMEM(made, jnp.float32),
+            pltpu.SemaphoreType.DMA((pairs + 1, count)),
         ],
-        out_specs=pl.BlockSpec((count, 2, y_local, piece), lambda i: (0, i, 0, 0)),
-        out_shape=jax.ShapeDtypeStruct((count, x_local + 2, y_local, piece), jnp.float32),
-        scratch_shapes=[
-            pltpu.VMEM((x_local + 2, y_cells, piece), jnp.float32),
-            pltpu.VMEM((2, y_cells, piece), jnp.float32),
-        ],
+        compiler_params=pltpu.CompilerParams(vmem_limit_bytes=vmem_limit),
         name="y_inverse",
-    )(modes, carries, *tables, ratio, gain)
+    )(own, modes, carries, *tables, ratio, gain)
 
 
 def turn(value, axis):
     return lax.all_to_all(value, axis, split_axis=0, concat_axis=0, tiled=True)
 
 
-def project(spectrum):
-    count, x_local, y_local, piece = spectrum.shape
+def solve_tables(count, y_local, piece):
     y_cells, z_cells = count * y_local, count * piece
     wide_count = lax.axis_size("wide")
     _, eigen_y = cosine_sine_basis(y_cells, y_cells, range(y_cells // 2 + 1))
@@ -899,19 +1004,38 @@
     excess = 4.0 * (jnp.asarray(eigen_y, jnp.float32)[:, None] + own_z[None, :] + penalty)
     root = jnp.sqrt(excess * (4.0 + excess))
     ratio = 2.0 / (2.0 + excess + root)
-    gain = -4.0 / root
     share = y_cells // wide_count
     own_ratio = lax.dynamic_slice_in_dim(ratio, lax.axis_index("wide") * share, share)
-    modes, carries = y_forward(turn(spectrum, "narrow"), ratio, wide_count)
-    carries = turn(join_carries(turn(carries, "wide"), own_ratio, x_local // 2), "wide")
-    return turn(y_inverse(modes, carries, ratio, gain, count), "narrow")
+    return ratio, -4.0 / root, own_ratio
+
+
+def swap(blocks, axis):
+    size = len(blocks)
+    return [blocks[0]] + [
+        lax.ppermute(blocks[k], axis, [(i, i ^ k) for i in range(size)]) for k in range(1, size)
+    ]
+
+
+def project(spectra, own, tables):
+    count, pairs = len(spectra[0]), spectra[0][0].shape[0]
+    ratio, gain, own_ratio = tables
+    turned = []
+    for spectrum in spectra:
+        turned.append(swap(spectrum, "narrow"))
+    solved = [y_forward(spectrum, own, ratio, lax.axis_size("wide")) for spectrum in turned]
+    carries = [turn(carry, "wide") for _, carry in solved]
+    joined = [turn(join_carries(carry, own_ratio, pairs), "wide") for carry in carries]
+    return [
+        swap(y_inverse(solved[p][0], joined[p], own, ratio, gain, count, p), "narrow")
+        for p in range(2)
+    ]
 
 
 def conduct(profile, spread):
     sides = (("wide", 0), ("narrow", 1))
     spread = with_halo(spread, sides, STEPS - 1, False)
     profile = with_halo(profile, sides, STEPS, False)
-    for step in range(STEPS):
+    for _ in range(STEPS):
         center = profile[1:-1, 1:-1]
         near = (
             profile[2:, 1:-1] + profile[:-2, 1:-1] + profile[1:-1, 2:] + profile[1:-1, :-2]
@@ -923,7 +1047,7 @@
     return profile
 
 
-def per_device(
+def device_step(
     material_flow_vector,
     tool_push_density,
     tool_warmth_excess,
@@ -945,15 +1069,30 @@
         current = advance_call(flow, flow_y, mu, mu_y, tool_push_density, flow_x, mu_x, inner)
         if not last:
             current_x, current_y = ring(current, "wide", 1), ring(current, "narrow", 2)
-    heat_cells = fields[1]
+    _, x_local, y_local, z_cells = flow.shape
+    count = lax.axis_size("narrow")
+    pairs, piece = x_local // 2, z_cells // count
+    tables = solve_tables(count, y_local, piece)
     end_x = ring(current[0], "wide", 0)
-    end_y = [side[:, 0] for side in ring(current[1], "narrow", 1)]
-    modes = divergence_modes(current, lax.axis_size("narrow"))
-    spectrum = project(add_halo_modes(modes, end_x, end_y))
-    inner = spectrum[:, 1:-1]
-    corrected_flow_vector = corrected(
-        current, spectrum, [side[:, :, 0] for side in ring(inner, "narrow", 2)]
-    )
+    lowest, highest = current[1, :, :1], current[1, :, y_local - 1 :]
+    end_y = [
+        side.reshape(pairs, 2, z_cells)
+        for side in (shift(highest, "narrow", 1), shift(lowest, "narrow", -1))
+    ]
+    own = lax.axis_index("narrow").astype(jnp.int32).reshape(1)
+    modes = divergence_modes(current, own, count)
+    modes = [
+        add_halo_modes(modes[p], own, end_x[p], [side[:, p] for side in end_y], p)
+        for p in range(2)
+    ]
+    heat_cells, kept = lax.optimization_barrier((fields[1], (modes[0][0], modes[1][0])))
+    modes = [[kept[p], *modes[p][1:]] for p in range(2)]
+    spectra = project(modes, own, tables)
+    sides = []
+    for p in range(2):
+        for row, by in ((y_local - 1, 1), (0, -1)):
+            lines = jnp.stack([block[p : p + pairs, row] for block in spectra[p]])
+            sides.append(shift(lines, "narrow", by))
     z_blocks = heat_cells.shape[0]
     slab_count = lax.axis_size("wide")
     component_lines = substrate_warmth_excess.shape[0] * substrate_warmth_excess.shape[1]
@@ -972,12 +1111,17 @@
     thermal_profile = substrate_warmth_excess + dissipation_factor * substrate_energy_input.reshape(
         substrate_warmth_excess.shape
     )
-    return (corrected_flow_vector, conduct(thermal_profile, spread_coefficient))
+    part_out = conduct(thermal_profile, spread_coefficient)
+    part_out, sides = lax.optimization_barrier((part_out, jnp.stack(sides)))
+    corrected_flow_vector = corrected(
+        current, pressure_planes(spectra[0], own), spectra[1], own, sides
+    )
+    return (corrected_flow_vector, part_out)
 
 
 def solution(mesh):
     return jax.shard_map(
-        per_device,
+        device_step,
         mesh=mesh,
         in_specs=(
             P(None, "wide", "narrow", None),

time: 381 us -> 408 us (1.071)
  local copies, waits for them, and re-layouts: 20.3 us -> 44.6 us
  starting transfers between devices: 67.5 us -> 87 us
  blocking collectives: 17.9 us -> 0 us
    ppermute x22 -> x36, waiting for transfers between devices: 21.2 us -> 54.8 us  [the longest x12 40 us: swap(): lax.ppermute(blocks[k], axis, [(i, i ^ k) for i in range(size)])]
    ppermute x4, waiting for transfers between devices: 21.5 us -> 0.01 us  [with_halo(): before = lax.ppermute(last, axis, up)]
    unnamed x32 -> x69, local copies, waits for them, and re-layouts: 4.03 us -> 25.3 us
    all_to_all x1 -> x0, blocking collectives: 17.9 us -> none  [turn(): return lax.all_to_all(value, axis, split_axis=0, concat_axis=0, tiled=True)]
    ppermute x22 -> x36, starting transfers between devices: 30.3 us -> 43.1 us  [the longest x24 31.5 us: shift(): lax.ppermute(value, axis, [(i, (i + by) % size) for i in range(size)])]
    all_to_all x3 -> x4, waiting for transfers between devices: 19.9 us -> 7.96 us  [turn(): return lax.all_to_all(value, axis, split_axis=0, concat_axis=0, tiled=True)]
    all_to_all x3 -> x4, starting transfers between devices: 15.1 us -> 24.4 us  [turn(): return lax.all_to_all(value, axis, split_axis=0, concat_axis=0, tiled=True)]
    pallas_call x6 -> x11, Pallas kernels: 51.8 us -> 53.9 us  [the longest x2 12 us: y_inverse(): pl.pallas_call(kernel, in_specs=[in_smem] + [in_vmem] * 6, out_specs=[any...]
  transfers between devices with their start and end apart: 34 -> 49, of which waited for: 14 -> 14; matrix products, arithmetic and copies ran while one was open for 15% -> 16% of each run, Pallas kernels for 30% -> 29%
where the time goes in v5:
time: 408 us; the launch traced here: 406 us
  Pallas kernels  143 us (35%)
  starting transfers between devices  87 us (21%)
  waiting for transfers between devices  65.9 us (16%)
  other arithmetic  49.9 us (12%)
  local copies, waits for them, and re-layouts  44.6 us (11%)
  between operations  15 us (4%)
    pallas_call x4, Pallas kernels, advance_call(): pl.pallas_call(kernel, in_specs=specs, out_specs=anywhere, out_shape=jax....  46.5 us
    scatter-add x1, other arithmetic, device_step(): partial_value = jnp.zeros((slab_count * component_lines, 128), jnp.float3...  45.7 us
    pallas_call x4, Pallas kernels, viscosity_call(): pl.pallas_call(kernel, in_specs=specs, out_specs=[anywhere] * outputs, ou...  42.8 us
    ppermute x12, waiting for transfers between devices, swap(): lax.ppermute(blocks[k], axis, [(i, i ^ k) for i in range(size)])  40 us
    ppermute x24, starting transfers between devices, shift(): lax.ppermute(value, axis, [(i, (i + by) % size) for i in range(size)])  31.5 us
    unnamed x69, local copies, waits for them, and re-layouts  25.3 us
    all_to_all x4, starting transfers between devices, turn(): return lax.all_to_all(value, axis, split_axis=0, concat_axis=0, tiled=True)  24.4 us
    ppermute x24, waiting for transfers between devices, shift(): lax.ppermute(value, axis, [(i, (i + by) % size) for i in range(size)])  14.7 us
  transfers between devices with their start and end apart: 49, of which 14 were waited for; matrix products, arithmetic and copies ran while one was open for 16% of the time, Pallas kernels for 29%

profile of v5, /device:TPU:1, one launch (start us, length us, event | category | flops | bytes accessed | tf_op | source)
XLA Modules:
  0.0 405.5 jit_solution(15969162091354661422)
XLA Ops:
  23.7 17.8 %viscosity_inner.2.refs_6_ = f32[32,64,512]{2,1,0:T(8,128)S(1)} custom-call(f32[3,32,64,512]{3,2,1,0:T(8,128)} %refs_0_.11, f32[3,32,1,512]{3,2,1,0:T(1,128)S(1)} %collective-permute-done.refs_1_, f32[3,32,1,512]{3,2,1,0:T(1,128)S(1)} %collective-permute-done.1.refs_2_, f32[32,64,512]{2,1,0:T(8,128)} %refs_3_.7), custom_call_target="tpu_custom_call" | custom-call | tf_op jit(solution)/shard_map/viscosity_inner/pallas_call | solution.py:216
  44.2 4.1 %collective-permute-start.7 = (f32[1,64,512]{2,1,0:T(8,128)S(1)}, f32[1,64,512]{2,1,0:T(8,128)S(1)}, u32[]{:S(2)}, u32[]{:S(2)}) collective-permute-start(f32[1,64,512]{2,1,0:T(8,128)S(1)} %get-tuple-element.92), channel_id=1, source_target_pairs={{0,28},{4,0},{8,4},{12,8},{16,12},{20,16},{24,20},{28,24},{1,29},{... | collective-permute-start | bytes 393224 | tf_op jit(solution)/shard_map/ppermute | solution.py:39
  53.7 19.3 %advance_inner.2.refs_11_ = f32[3,32,64,512]{3,2,1,0:T(8,128)} custom-call(f32[3,32,64,512]{3,2,1,0:T(8,128)} %refs_0_.11, f32[3,32,1,512]{3,2,1,0:T(1,128)S(1)} %collective-permute-done.refs_1_, f32[3,32,1,512]{3,2,1,0:T(1,128)S(1)} %collective-permute-done.1.refs_2_, f32[32,64,512]{2,1,0:T(8,128)S(1)} %viscosity_edge.2.refs_3_, ...), custom_call_target="tpu_custom_call" | custom-call | tf_op jit(solution)/shard_map/advance_inner/pallas_call | solution.py:380
  78.2 4.1 %collective-permute-start.11 = (f32[3,1,64,512]{3,2,1,0:T(8,128)S(1)}, f32[3,1,64,512]{3,2,1,0:T(8,128)S(1)}, u32[]{:S(2)}, u32[]{:S(2)}) collective-permute-start(f32[3,1,64,512]{3,2,1,0:T(8,128)S(1)} %get-tuple-element.80), channel_id=1, source_target_pairs={{0,28},{4,0},{8,4},{12,8},{16,12},{20,16},{24,20},{28,24},{1,29},{... | collective-permute-start | bytes 1179656 | tf_op jit(solution)/shard_map/ppermute | solution.py:39
  85.4 4.3 %collective-permute-done.8.refs_1_ = f32[3,32,1,512]{3,2,1,0:T(1,128)S(1)} collective-permute-done((f32[3,32,1,512]{3,2,1,0:T(1,128)S(1)}, f32[3,32,1,512]{3,2,1,0:T(1,128)S(1)}, u32[]{:S(2)}, u32[]{:S(2)}) %collective-permute-start.8) | collective-permute-done | bytes 196640 | tf_op jit(solution)/shard_map/ppermute | solution.py:39
  90.8 19.1 %viscosity_inner.3 = (f32[32,64,512]{2,1,0:T(8,128)S(1)}, f32[4,32,64,128]{3,2,1,0:T(8,128)}) custom-call(f32[3,32,64,512]{3,2,1,0:T(8,128)} %advance_edge.2.refs_0_, f32[3,32,1,512]{3,2,1,0:T(1,128)S(1)} %collective-permute-done.8.refs_1_, f32[3,32,1,512]{3,2,1,0:T(1,128)S(1)} %collective-permute-done.9.refs_2_, f32[32,64,512]{2,1,0:T(8,128)} %refs_3_.7), custom_call_target="tpu_custom_call" | custom-call | tf_op jit(solution)/shard_map/viscosity_inner/pallas_call | solution.py:216
  116.8 4.2 %collective-permute-start.15 = (f32[1,64,512]{2,1,0:T(8,128)S(1)}, f32[1,64,512]{2,1,0:T(8,128)S(1)}, u32[]{:S(2)}, u32[]{:S(2)}) collective-permute-start(f32[1,64,512]{2,1,0:T(8,128)S(1)} %get-tuple-element.88), channel_id=1, source_target_pairs={{0,28},{4,0},{8,4},{12,8},{16,12},{20,16},{24,20},{28,24},{1,29},{... | collective-permute-start | bytes 393224 | tf_op jit(solution)/shard_map/ppermute | solution.py:39
  124.7 19.3 %advance_inner.3.refs_11_ = f32[3,32,64,512]{3,2,1,0:T(8,128)} custom-call(f32[3,32,64,512]{3,2,1,0:T(8,128)} %refs_0_.11, f32[3,32,1,512]{3,2,1,0:T(1,128)S(1)} %collective-permute-done.refs_1_, f32[3,32,1,512]{3,2,1,0:T(1,128)S(1)} %collective-permute-done.1.refs_2_, f32[32,64,512]{2,1,0:T(8,128)S(1)} %copy-done.1, ...), custom_call_target="tpu_custom_call" | custom-call | tf_op jit(solution)/shard_map/advance_inner/pallas_call | solution.py:380
  152.7 12.0 %divergence_modes.1 = (f32[16,64,128]{2,1,0:T(8,128)}, f32[16,64,128]{2,1,0:T(8,128)}, f32[16,64,128]{2,1,0:T(8,128)}, f32[16,64,128]{2,1,0:T(8,128)}, f32[16,64...) custom-call(f32[3,32,64,512]{3,2,1,0:T(8,128)} %advance_edge.3.flow_ref.refs_5_, ...), custom_call_target="tpu_custom_call" | custom-call | tf_op jit(solution)/shard_map/divergence_modes/pallas_call | solution.py:546
  170.2 4.4 %collective-permute-start.19 = (f32[1,64,512]{2,1,0:T(8,128)S(1)}, f32[1,64,512]{2,1,0:T(8,128)S(1)}, u32[]{:S(2)}, u32[]{:S(2)}) collective-permute-start(f32[1,64,512]{2,1,0:T(8,128)S(1)} %get-tuple-element.76), channel_id=1, source_target_pairs={{0,28},{4,0},{8,4},{12,8},{16,12},{20,16},{24,20},{28,24},{1,29},{... | collective-permute-start | bytes 393224 | tf_op jit(solution)/shard_map/ppermute | solution.py:39
  181.8 45.7 %scatter_custom_fusion = f32[4096,128]{1,0:T(8,128)} fusion(s32[8192]{0:T(1024)S(1)} %bitcast.82, f32[8192,128]{1,0:T(8,128)} %bitcast.76, f32[]{:T(128)} %constant.26.clone.1), kind=kCustom, calls=%fused_computation.1 | custom fusion | flops 1048576 | bytes 2097664 | tf_op jit(solution)/shard_map/scatter-add | solution.py:1103
  232.6 5.2 %y_forward.3 = (f32[16,256,128]{2,1,0:T(8,128)S(1)}, f32[8,2,32,128]{3,2,1,0:T(8,128)S(1)}) custom-call(f32[16,64,128]{2,1,0:T(8,128)S(1)} %copy-done.6, f32[16,64,128]{2,1,0:T(8,128)S(1)} %collective-permute-done.26.refs_1_, f32[16,64,128]{2,1,0:T(8,128)S(1)} %collective-permute-done.27.refs_2_, f32[16,64,128]{2,1,0:T(8,128)S(1)} %collective-permute-done.28.refs_3_, ...), custom_call_target="tpu_custom_call" | custom-call | tf_op jit(solution)/shard_map/y_forward/pallas_call | solution.py:851
  239.9 6.2 %all-to-all-start.2 = ((f32[8,2,32,128]{3,2,1,0:T(8,128)}), f32[8,2,32,128]{3,2,1,0:T(8,128)S(1)}, u32[]{:S(2)}, u32[]{:S(2)}) async-start(f32[8,2,32,128]{3,2,1,0:T(8,128)} %copy-done.24), calls=%async_computation.2 | async-start | bytes 524288 | tf_op jit(solution)/shard_map/all_to_all | solution.py:995
  246.8 7.6 %collective-permute-done.22.refs_3_ = f32[16,64,128]{2,1,0:T(8,128)} collective-permute-done((f32[16,64,128]{2,1,0:T(8,128)}, f32[16,64,128]{2,1,0:T(8,128)}, u32[]{:S(2)}, u32[]{:S(2)}) %collective-permute-start.22) | collective-permute-done | bytes 524320 | tf_op jit(solution)/shard_map/ppermute | solution.py:1015
  261.9 6.2 %all-to-all-start = ((f32[8,2,32,128]{3,2,1,0:T(8,128)}), f32[8,2,32,128]{3,2,1,0:T(8,128)S(1)}, u32[]{:S(2)}, u32[]{:S(2)}) async-start(f32[8,2,32,128]{3,2,1,0:T(8,128)} %copy-done.23), calls=%async_computation | async-start | bytes 524288 | tf_op jit(solution)/shard_map/all_to_all | solution.py:995
  268.8 7.6 %all-to-all-done.in_ref = f32[8,2,32,128]{3,2,1,0:T(8,128)S(1)} async-done(((f32[8,2,32,128]{3,2,1,0:T(8,128)}), f32[8,2,32,128]{3,2,1,0:T(8,128)S(1)}, u32[]{:S(2)}, u32[]{:S(2)}) %all-to-all-start) | async-done | bytes 262176 | tf_op jit(solution)/shard_map/all_to_all | solution.py:995
  276.4 4.4 %all-to-all-start.3 = ((f32[8,2,32,128]{3,2,1,0:T(8,128)}), f32[8,2,32,128]{3,2,1,0:T(8,128)S(1)}, u32[]{:S(2)}, u32[]{:S(2)}) async-start(f32[8,2,32,128]{3,2,1,0:T(8,128)} %join_carries.3), calls=%async_computation.3 | async-start | bytes 524288 | tf_op jit(solution)/shard_map/all_to_all | solution.py:995
  288.4 7.7 %all-to-all-start.1 = ((f32[8,2,32,128]{3,2,1,0:T(8,128)}), f32[8,2,32,128]{3,2,1,0:T(8,128)S(1)}, u32[]{:S(2)}, u32[]{:S(2)}) async-start(f32[8,2,32,128]{3,2,1,0:T(8,128)} %join_carries.2), calls=%async_computation.1 | async-start | bytes 524288 | tf_op jit(solution)/shard_map/all_to_all | solution.py:995
  300.1 5.2 %y_inverse.3 = (f32[17,64,128]{2,1,0:T(8,128)S(1)}, f32[17,64,128]{2,1,0:T(8,128)}, f32[17,64,128]{2,1,0:T(8,128)}, f32[17,64,128]{2,1,0:T(8,128)}) custom-call(s32[1]{0:T(128)} %bitcast.own_ref.refs_4_, f32[16,256,128]{2,1,0:T(8,128)S(1)} %copy-done.4, f32[8,2,32,128]{3,2,1,0:T(8,128)S(1)} %all-to-all-done.3.carry_ref, bf16[256,256]{1,0:T(8,128)(2,1)S(1)} %copy-done.13, ...), custom_call_target="tpu_custom_call" | custom-call | tf_op jit(solution)/shard_map/y_inverse/pallas_call | solution.py:978
  316.6 6.8 %y_inverse.2 = (f32[17,64,128]{2,1,0:T(8,128)S(1)}, f32[17,64,128]{2,1,0:T(8,128)S(1)}, f32[17,64,128]{2,1,0:T(8,128)S(1)}, f32[17,64,128]{2,1,0:T(8,128)S(1)}) custom-call(s32[1]{0:T(128)} %bitcast.own_ref.refs_4_, f32[16,256,128]{2,1,0:T(8,128)S(1)} %get-tuple-element.57.modes_ref, f32[8,2,32,128]{3,2,1,0:T(8,128)S(1)} %copy-done.8, ...), custom_call_target="tpu_custom_call" | custom-call | tf_op jit(solution)/shard_map/y_inverse/pallas_call | solution.py:978
  328.5 10.1 %collective-permute-done.31.refs_3_ = f32[17,64,128]{2,1,0:T(8,128)} collective-permute-done((f32[17,64,128]{2,1,0:T(8,128)}, f32[17,64,128]{2,1,0:T(8,128)}, u32[]{:S(2)}, u32[]{:S(2)}) %collective-permute-start.31) | collective-permute-done | bytes 557088 | tf_op jit(solution)/shard_map/ppermute | solution.py:1015
  340.1 9.2 %collective-permute-done.24.refs_2_ = f32[17,64,128]{2,1,0:T(8,128)S(1)} collective-permute-done((f32[17,64,128]{2,1,0:T(8,128)S(1)}, f32[17,64,128]{2,1,0:T(8,128)S(1)}, u32[]{:S(2)}, u32[]{:S(2)}) %collective-permute-start.24) | collective-permute-done | bytes 557088 | tf_op jit(solution)/shard_map/ppermute | solution.py:1015
  349.3 12.7 %collective-permute-done.25.refs_3_ = f32[17,64,128]{2,1,0:T(8,128)S(1)} collective-permute-done((f32[17,64,128]{2,1,0:T(8,128)S(1)}, f32[17,64,128]{2,1,0:T(8,128)S(1)}, u32[]{:S(2)}, u32[]{:S(2)}) %collective-permute-start.25) | collective-permute-done | bytes 557088 | tf_op jit(solution)/shard_map/ppermute | solution.py:1015
  388.9 9.8 %corrected.1 = f32[3,32,64,512]{3,2,1,0:T(8,128)} custom-call(f32[17,64,128]{2,1,0:T(8,128)S(1)} %get-tuple-element.59.refs_0_, f32[17,64,128]{2,1,0:T(8,128)S(1)} %collective-permute-done.23.refs_1_, f32[17,64,128]{2,1,0:T(8,128)S(1)} %collective-permute-done.24.refs_2_, f32[17,64,128]{2,1,0:T(8,128)S(1)} %collective-permute-done.25.refs_3_, ...), custom_call_target="tpu_custom_call" | custom-call | tf_op jit(solution)/shard_map/corrected/pallas_call | solution.py:778
  (219 shorter events, 137.6 us)
Async XLA Ops:
  7.2 354.9 %reduce-scatter.2.cloned.1.call-start = ((), (), s32[]{:S(2)}) async-start(), calls=%async_computation.5 | async-start | bytes 2359296 | tf_op jit(solution)/shard_map/reduce_scatter | solution.py:1105
  8.4 33.1 %collective-permute-start.2 = (f32[3,1,64,512]{3,2,1,0:T(8,128)S(1)}, f32[3,1,64,512]{3,2,1,0:T(8,128)S(1)}, u32[]{:S(2)}, u32[]{:S(2)}) collective-permute-start(f32[3,1,64,512]{3,2,1,0:T(8,128)S(1)} %get-tuple-element.85), channel_id=1, source_target_pairs={{0,4},{4,8},{8,12},{12,16},{16,20},{20,24},{24,28},{28,0},{1,5},{5... | collective-permute-start | bytes 1179656 | tf_op jit(solution)/shard_map/ppermute | solution.py:39
  10.5 31.0 %collective-permute-start.3 = (f32[3,1,64,512]{3,2,1,0:T(8,128)S(1)}, f32[3,1,64,512]{3,2,1,0:T(8,128)S(1)}, u32[]{:S(2)}, u32[]{:S(2)}) collective-permute-start(f32[3,1,64,512]{3,2,1,0:T(8,128)S(1)} %get-tuple-element.84), channel_id=1, source_target_pairs={{0,28},{4,0},{8,4},{12,8},{16,12},{20,16},{24,20},{28,24},{1,29},{... | collective-permute-start | bytes 1179656 | tf_op jit(solution)/shard_map/ppermute | solution.py:39
  44.2 28.8 %collective-permute-start.6 = (f32[1,64,512]{2,1,0:T(8,128)S(1)}, f32[1,64,512]{2,1,0:T(8,128)S(1)}, u32[]{:S(2)}, u32[]{:S(2)}) collective-permute-start(f32[1,64,512]{2,1,0:T(8,128)S(1)} %get-tuple-element.93), channel_id=1, source_target_pairs={{0,4},{4,8},{8,12},{12,16},{16,20},{20,24},{24,28},{28,0},{1,5},{5... | collective-permute-start | bytes 393224 | tf_op jit(solution)/shard_map/ppermute | solution.py:39
  44.2 28.7 %collective-permute-start.7 = (f32[1,64,512]{2,1,0:T(8,128)S(1)}, f32[1,64,512]{2,1,0:T(8,128)S(1)}, u32[]{:S(2)}, u32[]{:S(2)}) collective-permute-start(f32[1,64,512]{2,1,0:T(8,128)S(1)} %get-tuple-element.92), channel_id=1, source_target_pairs={{0,28},{4,0},{8,4},{12,8},{16,12},{20,16},{24,20},{28,24},{1,29},{... | collective-permute-start | bytes 393224 | tf_op jit(solution)/shard_map/ppermute | solution.py:39
  78.1 31.8 %collective-permute-start.10 = (f32[3,1,64,512]{3,2,1,0:T(8,128)S(1)}, f32[3,1,64,512]{3,2,1,0:T(8,128)S(1)}, u32[]{:S(2)}, u32[]{:S(2)}) collective-permute-start(f32[3,1,64,512]{3,2,1,0:T(8,128)S(1)} %get-tuple-element.81), channel_id=1, source_target_pairs={{0,4},{4,8},{8,12},{12,16},{16,20},{20,24},{24,28},{28,0},{1,5},{5... | collective-permute-start | bytes 1179656 | tf_op jit(solution)/shard_map/ppermute | solution.py:39
  78.2 31.7 %collective-permute-start.11 = (f32[3,1,64,512]{3,2,1,0:T(8,128)S(1)}, f32[3,1,64,512]{3,2,1,0:T(8,128)S(1)}, u32[]{:S(2)}, u32[]{:S(2)}) collective-permute-start(f32[3,1,64,512]{3,2,1,0:T(8,128)S(1)} %get-tuple-element.80), channel_id=1, source_target_pairs={{0,28},{4,0},{8,4},{12,8},{16,12},{20,16},{24,20},{28,24},{1,29},{... | collective-permute-start | bytes 1179656 | tf_op jit(solution)/shard_map/ppermute | solution.py:39
  116.8 27.2 %collective-permute-start.14 = (f32[1,64,512]{2,1,0:T(8,128)S(1)}, f32[1,64,512]{2,1,0:T(8,128)S(1)}, u32[]{:S(2)}, u32[]{:S(2)}) collective-permute-start(f32[1,64,512]{2,1,0:T(8,128)S(1)} %get-tuple-element.89), channel_id=1, source_target_pairs={{0,4},{4,8},{8,12},{12,16},{16,20},{20,24},{24,28},{28,0},{1,5},{5... | collective-permute-start | bytes 393224 | tf_op jit(solution)/shard_map/ppermute | solution.py:39
  116.8 27.2 %collective-permute-start.15 = (f32[1,64,512]{2,1,0:T(8,128)S(1)}, f32[1,64,512]{2,1,0:T(8,128)S(1)}, u32[]{:S(2)}, u32[]{:S(2)}) collective-permute-start(f32[1,64,512]{2,1,0:T(8,128)S(1)} %get-tuple-element.88), channel_id=1, source_target_pairs={{0,28},{4,0},{8,4},{12,8},{16,12},{20,16},{24,20},{28,24},{1,29},{... | collective-permute-start | bytes 393224 | tf_op jit(solution)/shard_map/ppermute | solution.py:39
  170.0 59.8 %collective-permute-start.26 = (f32[16,64,128]{2,1,0:T(8,128)}, f32[16,64,128]{2,1,0:T(8,128)S(1)}, u32[]{:S(2)}, u32[]{:S(2)}) collective-permute-start(f32[16,64,128]{2,1,0:T(8,128)} %get-tuple-element.64), channel_id=1, source_target_pairs={{0,1},{1,0},{2,3},{3,2},{4,5},{5,4},{6,7},{7,6},{8,9},{9,8},{10,11... | collective-permute-start | bytes 1572872 | tf_op jit(solution)/shard_map/ppermute | solution.py:1015
  174.6 56.2 %collective-permute-start.27 = (f32[16,64,128]{2,1,0:T(8,128)}, f32[16,64,128]{2,1,0:T(8,128)S(1)}, u32[]{:S(2)}, u32[]{:S(2)}) collective-permute-start(f32[16,64,128]{2,1,0:T(8,128)} %get-tuple-element.65), channel_id=1, source_target_pairs={{0,2},{1,3},{2,0},{3,1},{4,6},{5,7},{6,4},{7,5},{8,10},{9,11},{10,... | collective-permute-start | bytes 1572872 | tf_op jit(solution)/shard_map/ppermute | solution.py:1015
  175.4 55.3 %collective-permute-start.28 = (f32[16,64,128]{2,1,0:T(8,128)}, f32[16,64,128]{2,1,0:T(8,128)S(1)}, u32[]{:S(2)}, u32[]{:S(2)}) collective-permute-start(f32[16,64,128]{2,1,0:T(8,128)} %get-tuple-element.66), channel_id=1, source_target_pairs={{0,3},{1,2},{2,1},{3,0},{4,7},{5,6},{6,5},{7,4},{8,11},{9,10},{10,... | collective-permute-start | bytes 1572872 | tf_op jit(solution)/shard_map/ppermute | solution.py:1015
  228.3 17.8 %collective-permute-start.20 = (f32[16,64,128]{2,1,0:T(8,128)}, f32[16,64,128]{2,1,0:T(8,128)S(1)}, u32[]{:S(2)}, u32[]{:S(2)}) collective-permute-start(f32[16,64,128]{2,1,0:T(8,128)} %get-tuple-element.54), channel_id=1, source_target_pairs={{0,1},{1,0},{2,3},{3,2},{4,5},{5,4},{6,7},{7,6},{8,9},{9,8},{10,11... | collective-permute-start | bytes 1572872 | tf_op jit(solution)/shard_map/ppermute | solution.py:1015
  228.9 17.9 %collective-permute-start.21 = (f32[16,64,128]{2,1,0:T(8,128)}, f32[16,64,128]{2,1,0:T(8,128)}, u32[]{:S(2)}, u32[]{:S(2)}) collective-permute-start(f32[16,64,128]{2,1,0:T(8,128)} %get-tuple-element.55), channel_id=1, source_target_pairs={{0,2},{1,3},{2,0},{3,1},{4,6},{5,7},{6,4},{7,5},{8,10},{9,11},{10,... | collective-permute-start | bytes 1572872 | tf_op jit(solution)/shard_map/ppermute | solution.py:1015
  229.8 24.6 %collective-permute-start.22 = (f32[16,64,128]{2,1,0:T(8,128)}, f32[16,64,128]{2,1,0:T(8,128)}, u32[]{:S(2)}, u32[]{:S(2)}) collective-permute-start(f32[16,64,128]{2,1,0:T(8,128)} %get-tuple-element.56), channel_id=1, source_target_pairs={{0,3},{1,2},{2,1},{3,0},{4,7},{5,6},{6,5},{7,4},{8,11},{9,10},{10,... | collective-permute-start | bytes 1572872 | tf_op jit(solution)/shard_map/ppermute | solution.py:1015
  239.9 22.0 %all-to-all-start.2 = ((f32[8,2,32,128]{3,2,1,0:T(8,128)}), f32[8,2,32,128]{3,2,1,0:T(8,128)S(1)}, u32[]{:S(2)}, u32[]{:S(2)}) async-start(f32[8,2,32,128]{3,2,1,0:T(8,128)} %copy-done.24), calls=%async_computation.2 | async-start | bytes 524288 | tf_op jit(solution)/shard_map/all_to_all | solution.py:995
  288.4 24.7 %all-to-all-start.1 = ((f32[8,2,32,128]{3,2,1,0:T(8,128)}), f32[8,2,32,128]{3,2,1,0:T(8,128)S(1)}, u32[]{:S(2)}, u32[]{:S(2)}) async-start(f32[8,2,32,128]{3,2,1,0:T(8,128)} %join_carries.2), calls=%async_computation.1 | async-start | bytes 524288 | tf_op jit(solution)/shard_map/all_to_all | solution.py:995
  305.4 18.4 %collective-permute-start.29 = (f32[17,64,128]{2,1,0:T(8,128)}, f32[17,64,128]{2,1,0:T(8,128)}, u32[]{:S(2)}, u32[]{:S(2)}) collective-permute-start(f32[17,64,128]{2,1,0:T(8,128)} %get-tuple-element.70), channel_id=1, source_target_pairs={{0,1},{1,0},{2,3},{3,2},{4,5},{5,4},{6,7},{7,6},{8,9},{9,8},{10,11... | collective-permute-start | bytes 1671176 | tf_op jit(solution)/shard_map/ppermute | solution.py:1015
  308.7 78.4 %collective-permute-start.38 = (f32[20,2,128]{2,1,0:T(2,128)S(1)}, f32[20,2,128]{2,1,0:T(2,128)S(1)}, u32[]{:S(2)}, u32[]{:S(2)}) collective-permute-start(f32[20,2,128]{2,1,0:T(2,128)S(1)} %get-tuple-element.122), channel_id=1, source_target_pairs={{0,1},{1,2},{2,3},{4,5},{5,6},{6,7},{8,9},{9,10},{10,11},{12,13},{... | collective-permute-start | bytes 61448 | tf_op jit(solution)/shard_map/ppermute | solution.py:31
  311.3 27.3 %collective-permute-start.31 = (f32[17,64,128]{2,1,0:T(8,128)}, f32[17,64,128]{2,1,0:T(8,128)}, u32[]{:S(2)}, u32[]{:S(2)}) collective-permute-start(f32[17,64,128]{2,1,0:T(8,128)} %get-tuple-element.72), channel_id=1, source_target_pairs={{0,3},{1,2},{2,1},{3,0},{4,7},{5,6},{6,5},{7,4},{8,11},{9,10},{10,... | collective-permute-start | bytes 1671176 | tf_op jit(solution)/shard_map/ppermute | solution.py:1015
  323.8 25.5 %collective-permute-start.24 = (f32[17,64,128]{2,1,0:T(8,128)S(1)}, f32[17,64,128]{2,1,0:T(8,128)S(1)}, u32[]{:S(2)}, u32[]{:S(2)}) collective-permute-start(f32[17,64,128]{2,1,0:T(8,128)S(1)} %get-tuple-element.61), channel_id=1, source_target_pairs={{0,2},{1,3},{2,0},{3,1},{4,6},{5,7},{6,4},{7,5},{8,10},{9,11},{10,... | collective-permute-start | bytes 1671176 | tf_op jit(solution)/shard_map/ppermute | solution.py:1015
  325.5 36.5 %collective-permute-start.25 = (f32[17,64,128]{2,1,0:T(8,128)S(1)}, f32[17,64,128]{2,1,0:T(8,128)S(1)}, u32[]{:S(2)}, u32[]{:S(2)}) collective-permute-start(f32[17,64,128]{2,1,0:T(8,128)S(1)} %get-tuple-element.62), channel_id=1, source_target_pairs={{0,3},{1,2},{2,1},{3,0},{4,7},{5,6},{6,5},{7,4},{8,11},{9,10},{10,... | collective-permute-start | bytes 1671176 | tf_op jit(solution)/shard_map/ppermute | solution.py:1015
  339.5 36.4 %collective-permute-start.40 = (f32[4,16,128]{2,1,0:T(8,128)S(1)}, f32[4,16,128]{2,1,0:T(8,128)S(1)}, u32[]{:S(2)}, u32[]{:S(2)}) collective-permute-start(f32[4,16,128]{2,1,0:T(8,128)S(1)} %pad_maximum_fusion.6), channel_id=1, source_target_pairs={{0,1},{1,2},{2,3},{3,0},{4,5},{5,6},{6,7},{7,4},{8,9},{9,10},{10,1... | collective-permute-start | bytes 98312 | tf_op jit(solution)/shard_map/ppermute | solution.py:39
  339.6 39.3 %collective-permute-start.41 = (f32[4,16,128]{2,1,0:T(8,128)S(1)}, f32[4,16,128]{2,1,0:T(8,128)S(1)}, u32[]{:S(2)}, u32[]{:S(2)}) collective-permute-start(f32[4,16,128]{2,1,0:T(8,128)S(1)} %pad_maximum_fusion.7), channel_id=1, source_target_pairs={{0,3},{1,0},{2,1},{3,2},{4,7},{5,4},{6,5},{7,6},{8,11},{9,8},{10,9... | collective-permute-start | bytes 98312 | tf_op jit(solution)/shard_map/ppermute | solution.py:39
  (58 other events, 503.9 us)
Sparse Core Ops, SparseCore 0:
  227.6 74.0 reduce-scatter.1

commit v6 on v4

--- a/solution.py
+++ b/solution.py
@@ -33,13 +33,16 @@
     return x
 
 
+def shift(value, axis, by):
+    size = lax.axis_size(axis)
+    return lax.ppermute(value, axis, [(i, (i + by) % size) for i in range(size)])
+
+
 def ring(value, axis, dim):
-    size, length = lax.axis_size(axis), value.shape[dim]
-    up = [(i, (i + 1) % size) for i in range(size)]
-    down = [(j, i) for i, j in up]
+    length = value.shape[dim]
     last = lax.slice_in_dim(value, length - 1, length, axis=dim)
     initial = lax.slice_in_dim(value, 0, 1, axis=dim)
-    return lax.ppermute(last, axis, up), lax.ppermute(initial, axis, down)
+    return shift(last, axis, 1), shift(initial, axis, -1)
 
 
 anywhere = pl.BlockSpec(memory_space=pl.ANY)
@@ -77,6 +80,55 @@
 
     def wait(self, slot):
         self.copy(slot, self.source, 0).wait()
+
+
+def in_sections(x_local, size, loads, stores, start_up, body):
+    count = x_local // size
+
+    def cut(ref, first, planes):
+        part = pl.ds(first, planes)
+        return ref.at[:, part] if len(ref.shape) == 4 else ref.at[part]
+
+    def moves(kinds, section, first, planes):
+        return [
+            pltpu.make_async_copy(
+                cut(source, first, planes), cut(target, first, planes), semaphores.at[section]
+            )
+            for source, target, semaphores in kinds
+        ]
+
+    def begin(section, state):
+        for move in moves(loads, section, section * size, size):
+            move.start()
+        return state
+
+    lax.fori_loop(0, count, begin, 0)
+
+    def work(section, first, planes):
+        for move in moves(loads, section, section * size, size):
+            move.wait()
+        if isinstance(first, int):
+            start_up()
+        lax.fori_loop(first, first + planes, body, 0)
+        for move in moves(stores, section, first, planes):
+            move.start()
+
+    work(0, 1, size - 2)
+
+    def rest(section, state):
+        work(section, section * size - 1, size)
+        return state
+
+    lax.fori_loop(1, count, rest, 0)
+    for move in moves(stores, 0, 1, size - 2):
+        move.wait()
+
+    def finish(section, state):
+        for move in moves(stores, section, section * size - 1, size):
+            move.wait()
+        return state
+
+    lax.fori_loop(1, count, finish, 0)
 
 
 def edge_list(ref, low, high, x_local):
@@ -227,6 +279,57 @@
     )(*operands)
 
 
+def viscosity_inner(flow, y_sides, warmth, with_heat):
+    _, x_local, y_local, z_cells = flow.shape
+    z_blocks, size = z_cells // 128, 4
+    outputs = 2 if with_heat else 1
+
+    def kernel(flow_ref, before_ref, after_ref, warmth_ref, *rest):
+        out_refs, (cells, cell_sem, warm, warm_sem, *heat) = rest[:outputs], rest[outputs:]
+        outs = [out_refs[0]] + heat[:1]
+
+        def body(slot, state):
+            viscosity_plane(
+                cells,
+                slot,
+                (lambda c: before_ref[c, slot], lambda c: after_ref[c, slot]),
+                warm,
+                slot,
+                outs,
+                slot,
+                y_local,
+                z_cells,
+            )
+            return state
+
+        in_sections(
+            x_local,
+            size,
+            [(flow_ref, cells, cell_sem), (warmth_ref, warm, warm_sem)],
+            [(heat[0], out_refs[1], heat[1])] if with_heat else [],
+            lambda: None,
+            body,
+        )
+
+    shapes = [(x_local, y_local, z_cells), (z_blocks, x_local, y_local, 128)][:outputs]
+    sems = pltpu.SemaphoreType.DMA((x_local // size,))
+    return pl.pallas_call(
+        kernel,
+        in_specs=[anywhere, in_vmem, in_vmem, anywhere],
+        out_specs=[in_vmem, anywhere][:outputs],
+        out_shape=[jax.ShapeDtypeStruct(shape, jnp.float32) for shape in shapes],
+        scratch_shapes=[
+            pltpu.VMEM(flow.shape, jnp.float32),
+            sems,
+            pltpu.VMEM(warmth.shape, jnp.float32),
+            sems,
+        ]
+        + ([pltpu.VMEM(shapes[1], jnp.float32), sems] if with_heat else []),
+        compiler_params=pltpu.CompilerParams(vmem_limit_bytes=vmem_limit),
+        name="viscosity_inner",
+    )(flow, *y_sides, warmth)
+
+
 vmem_limit = 48 << 20
 
 
@@ -391,6 +494,61 @@
         compiler_params=pltpu.CompilerParams(vmem_limit_bytes=vmem_limit),
         name="advance_edge" if edge else "advance_inner",
     )(*operands)
+
+
+def advance_inner(flow, flow_y, mu, mu_y, push):
+    _, x_local, y_local, z_cells = flow.shape
+    size = 4
+
+    def kernel(
+        flow_ref, flow_before, flow_after, mu_ref, mu_before, mu_after, push_ref,
+        out_ref, cells, cell_sem, work, work_sem, out_sem, flux,
+    ):
+        def body(slot, state):
+            advance_plane(
+                cells,
+                mu_ref,
+                slot,
+                (
+                    lambda c: flow_before[c, slot],
+                    lambda c: flow_after[c, slot],
+                    lambda: mu_before[slot],
+                    lambda: mu_after[slot],
+                ),
+                work,
+                slot,
+                flux,
+                y_local,
+                z_cells,
+            )
+            return state
+
+        in_sections(
+            x_local,
+            size,
+            [(flow_ref, cells, cell_sem), (push_ref, work, work_sem)],
+            [(work, out_ref, out_sem)],
+            lambda: first_flux(cells, mu_ref, 1, flux, y_local),
+            body,
+        )
+
+    sems = pltpu.SemaphoreType.DMA((x_local // size,))
+    return pl.pallas_call(
+        kernel,
+        in_specs=[anywhere, in_vmem, in_vmem, in_vmem, in_vmem, in_vmem, anywhere],
+        out_specs=anywhere,
+        out_shape=jax.ShapeDtypeStruct(flow.shape, jnp.float32),
+        scratch_shapes=[
+            pltpu.VMEM(flow.shape, jnp.float32),
+            sems,
+            pltpu.VMEM(flow.shape, jnp.float32),
+            sems,
+            sems,
+            pltpu.VMEM((3, y_local, z_cells), jnp.float32),
+        ],
+        compiler_params=pltpu.CompilerParams(vmem_limit_bytes=vmem_limit),
+        name="advance_inner",
+    )(flow, *flow_y, mu, *mu_y, push)
 
 
 def cosine_sine_basis(points, period, waves):
@@ -726,54 +884,70 @@
 
 def y_forward(spectrum, ratio, wide_count):
     count, x_local, y_local, piece = spectrum.shape
-    y_cells = count * y_local
-    share = y_cells // wide_count
+    y_cells, pairs = count * y_local, x_local // 2
+    share, group = y_cells // wide_count, max(2, x_local // 4)
     table, _ = cosine_sine_basis(y_cells, y_cells, range(y_cells // 2 + 1))
     tables = halves(table.T)
 
-    def kernel(in_ref, high_ref, low_ref, ratio_ref, modes_ref, carry_ref, sums, power):
-        @pl.when(pl.program_id(0) == 0)
-        def _():
-            sums[...] = jnp.zeros_like(sums)
-            power[...] = jnp.ones_like(power)
-
-        planes = [
-            jnp.concatenate([in_ref[n, side] for n in range(count)], 0) for side in range(2)
-        ]
-        modes = triple_product(
-            (high_ref[...], low_ref[...]), split(jnp.concatenate(planes, 1))
-        )
-        r, pw = ratio_ref[...], power[...]
-        for side in range(2):
-            plane = modes[:, side * piece : (side + 1) * piece]
-            modes_ref[side] = plane
-            sums[side] = plane + r * sums[side]
-            sums[2 + side] = sums[2 + side] + pw * plane
-        power[...] = pw * r
-
-        @pl.when(pl.program_id(0) == x_local // 2 - 1)
-        def _():
-            for kind in range(4):
-                carry_ref[:, kind] = sums[kind].reshape(wide_count, share, piece)
+    def kernel(
+        in_ref, high_ref, low_ref, ratio_ref, modes_ref, carry_ref,
+        lines, in_sems, made, out_sems, sums, power,
+    ):
+        def load(k):
+            part = pl.ds(k * group, group)
+            return pltpu.make_async_copy(in_ref.at[:, part], lines.at[:, part], in_sems.at[k])
+
+        def stored(k):
+            part = pl.ds(k * group, group)
+            return pltpu.make_async_copy(made.at[part], modes_ref.at[part], out_sems.at[k])
+
+        for k in range(x_local // group):
+            load(k).start()
+        sums[...] = jnp.zeros_like(sums)
+        power[...] = jnp.ones_like(power)
+
+        def body(t, state):
+            planes = [
+                jnp.concatenate([lines[n, 2 * t + side] for n in range(count)], 0)
+                for side in range(2)
+            ]
+            modes = triple_product(
+                (high_ref[...], low_ref[...]), split(jnp.concatenate(planes, 1))
+            )
+            r, pw = ratio_ref[...], power[...]
+            for side in range(2):
+                plane = modes[:, side * piece : (side + 1) * piece]
+                made[2 * t + side] = plane
+                sums[side] = plane + r * sums[side]
+                sums[2 + side] = sums[2 + side] + pw * plane
+            power[...] = pw * r
+            return state
+
+        def section(k, state):
+            load(k).wait()
+            lax.fori_loop(k * (group // 2), (k + 1) * (group // 2), body, 0)
+            stored(k).start()
+            return state
+
+        lax.fori_loop(0, x_local // group, section, 0)
+        for kind in range(4):
+            carry_ref[:, kind] = sums[kind].reshape(wide_count, share, piece)
+        for k in range(x_local // group):
+            stored(k).wait()
 
     return pl.pallas_call(
         kernel,
-        grid=(x_local // 2,),
-        in_specs=[
-            pl.BlockSpec((count, 2, y_local, piece), lambda i: (0, i, 0, 0)),
-            whole(y_cells, y_cells),
-            whole(y_cells, y_cells),
-            whole(y_cells, piece),
-        ],
-        out_specs=[
-            pl.BlockSpec((2, y_cells, piece), lambda i: (i, 0, 0)),
-            whole(wide_count, 4, share, piece),
-        ],
+        in_specs=[anywhere] + [in_vmem] * 3,
+        out_specs=[anywhere, in_vmem],
         out_shape=[
             jax.ShapeDtypeStruct((x_local, y_cells, piece), jnp.float32),
             jax.ShapeDtypeStruct((wide_count, 4, share, piece), jnp.float32),
         ],
         scratch_shapes=[
+            pltpu.VMEM(spectrum.shape, jnp.float32),
+            pltpu.SemaphoreType.DMA((x_local // group,)),
+            pltpu.VMEM((x_local, y_cells, piece), jnp.float32),
+            pltpu.SemaphoreType.DMA((x_local // group,)),
             pltpu.VMEM((4, y_cells, piece), jnp.float32),
             pltpu.VMEM((y_cells, piece), jnp.float32),
         ],
@@ -809,77 +983,100 @@
 
     return pl.pallas_call(
         kernel,
+        in_specs=[in_vmem] * 2,
+        out_specs=in_vmem,
         out_shape=jax.ShapeDtypeStruct(carries.shape, jnp.float32),
+        compiler_params=pltpu.CompilerParams(vmem_limit_bytes=vmem_limit),
         name="join_carries",
     )(carries, ratio)
 
 
 def y_inverse(modes, carries, ratio, gain, count):
     x_local, y_cells, piece = modes.shape
-    y_local, pairs = y_cells // count, x_local // 2
-    wide_count, _, share, _ = carries.shape
+    y_local, pairs, group = y_cells // count, x_local // 2, max(2, x_local // 4)
     table, _ = cosine_sine_basis(y_cells, y_cells, range(y_cells // 2 + 1))
     tables = halves(table)
 
-    def kernel(modes_ref, carry_ref, high_ref, low_ref, ratio_ref, gain_ref, out_ref, behind, ahead):
-        step = pl.program_id(0)
-        r = ratio_ref[...]
+    def kernel(
+        modes_in, carry_ref, high_ref, low_ref, ratio_ref, gain_ref, out_ref,
+        planes, in_sems, behind, state, cells, out_sems,
+    ):
+        def load(k):
+            part = pl.ds(k * group, group)
+            return pltpu.make_async_copy(modes_in.at[part], planes.at[part], in_sems.at[k])
+
+        def stored(t):
+            part = pl.ds(2 * t, 2)
+            return pltpu.make_async_copy(cells.at[:, part], out_ref.at[:, part], out_sems.at[t])
 
         def carry(kind):
             return carry_ref[:, kind].reshape(y_cells, piece)
 
-        @pl.when(step == 0)
-        def _():
-            ahead[0] = carry(0)
-            ahead[1] = carry(1)
-            behind[2 * pairs + 1] = carry(2)
-
-            def back(i, state):
-                even, odd = state
-                m = pairs - 1 - i
-                behind[2 * m + 2] = r * odd
-                behind[2 * m + 1] = r * even
-                return (
-                    modes_ref[2 * m] + r * even,
-                    modes_ref[2 * m + 1] + r * odd,
-                )
-
-            _, odd = lax.fori_loop(0, pairs, back, (carry(2), carry(3)))
-            behind[0] = r * odd
-
-        even_plane = modes_ref[jnp.minimum(2 * step, x_local - 2)]
-        odd_plane = modes_ref[jnp.maximum(2 * step - 1, 1)]
-        even = r * ahead[0] + jnp.where(step < pairs, even_plane, 0.0)
-        odd = jnp.where(step > 0, odd_plane + r * ahead[1], ahead[1])
-        ahead[0] = even
-        ahead[1] = odd
-        gain_value = gain_ref[...]
-        planes = jnp.concatenate(
-            [gain_value * (odd + behind[2 * step]), gain_value * (even + behind[2 * step + 1])], 1
-        )
-        cells = triple_product((high_ref[...], low_ref[...]), split(planes))
-        for n in range(count):
+        groups = x_local // group
+        for k in range(groups)[::-1]:
+            load(k).start()
+        for kind in range(4):
+            state[kind] = carry(kind)
+        behind[x_local + 1] = carry(2)
+
+        def back(i, done):
+            m = pairs - 1 - i
+            r = ratio_ref[...]
             for side in range(2):
-                out_ref[n, side] = cells[
-                    n * y_local : (n + 1) * y_local, side * piece : (side + 1) * piece
-                ]
-
+                value = r * state[2 + side]
+                behind[2 * m + 1 + side] = value
+                state[2 + side] = planes[2 * m + side] + value
+            return done
+
+        def back_section(k, done):
+            load(groups - 1 - k).wait()
+            lax.fori_loop(k * (group // 2), (k + 1) * (group // 2), back, 0)
+            return done
+
+        lax.fori_loop(0, groups, back_section, 0)
+        behind[0] = ratio_ref[...] * state[3]
+
+        def body(t, done):
+            r, gain_value = ratio_ref[...], gain_ref[...]
+            even_plane = planes[jnp.minimum(2 * t, x_local - 2)]
+            odd_plane = planes[jnp.maximum(2 * t - 1, 1)]
+            even = r * state[0] + jnp.where(t < pairs, even_plane, 0.0)
+            odd = jnp.where(t > 0, odd_plane + r * state[1], state[1])
+            state[0] = even
+            state[1] = odd
+            joined = jnp.concatenate(
+                [gain_value * (odd + behind[2 * t]), gain_value * (even + behind[2 * t + 1])], 1
+            )
+            result = triple_product((high_ref[...], low_ref[...]), split(joined))
+            for n in range(count):
+                for side in range(2):
+                    cells[n, 2 * t + side] = result[
+                        n * y_local : (n + 1) * y_local, side * piece : (side + 1) * piece
+                    ]
+            stored(t).start()
+            return done
+
+        lax.fori_loop(0, pairs + 1, body, 0)
+
+        def finish(t, done):
+            stored(t).wait()
+            return done
+
+        lax.fori_loop(0, pairs + 1, finish, 0)
+
+    made = (count, x_local + 2, y_local, piece)
     return pl.pallas_call(
         kernel,
-        grid=(pairs + 1,),
-        in_specs=[
-            whole(x_local, y_cells, piece),
-            whole(wide_count, 4, share, piece),
-            whole(y_cells, y_cells),
-            whole(y_cells, y_cells),
-            whole(y_cells, piece),
-            whole(y_cells, piece),
-        ],
-        out_specs=pl.BlockSpec((count, 2, y_local, piece), lambda i: (0, i, 0, 0)),
-        out_shape=jax.ShapeDtypeStruct((count, x_local + 2, y_local, piece), jnp.float32),
+        in_specs=[anywhere] + [in_vmem] * 5,
+        out_specs=anywhere,
+        out_shape=jax.ShapeDtypeStruct(made, jnp.float32),
         scratch_shapes=[
+            pltpu.VMEM(modes.shape, jnp.float32),
+            pltpu.SemaphoreType.DMA((x_local // group,)),
             pltpu.VMEM((x_local + 2, y_cells, piece), jnp.float32),
-            pltpu.VMEM((2, y_cells, piece), jnp.float32),
+            pltpu.VMEM((4, y_cells, piece), jnp.float32),
+            pltpu.VMEM(made, jnp.float32),
+            pltpu.SemaphoreType.DMA((pairs + 1,)),
         ],
         name="y_inverse",
     )(modes, carries, *tables, ratio, gain)
@@ -937,17 +1134,21 @@
     current, current_x, current_y = flow, flow_x, flow_y
     for section in range(PASSES):
         last = section + 1 == PASSES
-        inner = viscosity_call(current, current_y, tool_warmth_excess, last)
+        inner = viscosity_inner(current, current_y, tool_warmth_excess, last)
         fields = viscosity_call(current, current_y, tool_warmth_excess, last, current_x, inner)
         mu = fields[0]
         mu_x, mu_y = ring(mu, "wide", 0), ring(mu, "narrow", 1)
-        inner = advance_call(flow, flow_y, mu, mu_y, tool_push_density)
+        inner = advance_inner(flow, flow_y, mu, mu_y, tool_push_density)
         current = advance_call(flow, flow_y, mu, mu_y, tool_push_density, flow_x, mu_x, inner)
         if not last:
             current_x, current_y = ring(current, "wide", 1), ring(current, "narrow", 2)
     heat_cells = fields[1]
     end_x = ring(current[0], "wide", 0)
-    end_y = [side[:, 0] for side in ring(current[1], "narrow", 1)]
+    y_local = flow.shape[2]
+    end_y = [
+        shift(current[1, :, y_local - 1 :], "narrow", 1)[:, 0],
+        shift(current[1, :, :1], "narrow", -1)[:, 0],
+    ]
     modes = divergence_modes(current, lax.axis_size("narrow"))
     spectrum = project(add_halo_modes(modes, end_x, end_y))
     inner = spectrum[:, 1:-1]

time: 381 us -> 350 us (0.919)
  Pallas kernels: 141 us -> 113 us
  local copies, waits for them, and re-layouts: 20.3 us -> 15 us
    pallas_call x3 -> x7, Pallas kernels: 26.7 us -> 74.2 us  [the longest x2 30.2 us: advance_inner(): pl.pallas_call(kernel, in_specs=[anywhere, in_vmem, in_vmem, in_vmem, in_...]
    pallas_call x4 -> x2, Pallas kernels: 46.5 us -> 7.93 us  [advance_call(): pl.pallas_call(kernel, in_specs=specs, out_specs=anywhere, out_shape=jax....]
    pallas_call x4 -> x2, Pallas kernels: 42.8 us -> 5.87 us  [viscosity_call(): pl.pallas_call(kernel, in_specs=specs, out_specs=[anywhere] * outputs, ou...]
    slice x11 -> x10, local copies, waits for them, and re-layouts: 9.52 us -> 9.51 us  [ring(): initial = lax.slice_in_dim(value, 0, 1, axis=dim)]
  transfers between devices with their start and end apart: 34 -> 34, of which waited for: 14 -> 14; matrix products, arithmetic and copies ran while one was open for 15% -> 17% of each run, Pallas kernels for 30% -> 24%
where the time goes in v6:
time: 350 us; the launch traced here: 349 us
  Pallas kernels  113 us (32%)
  waiting for transfers between devices  71.8 us (21%)
  starting transfers between devices  67.6 us (19%)
  other arithmetic  49.2 us (14%)
  blocking collectives  17.3 us (5%)
  local copies, waits for them, and re-layouts  15 us (4%)
  between operations  14.8 us (4%)
    scatter-add x1, other arithmetic, per_device(): partial_value = jnp.zeros((slab_count * component_lines, 128), jnp.float3...  45.8 us
    ppermute x22, starting transfers between devices, shift(): lax.ppermute(value, axis, [(i, (i + by) % size) for i in range(size)])  30.2 us
    pallas_call x2, Pallas kernels, advance_inner(): pl.pallas_call(kernel, in_specs=[anywhere, in_vmem, in_vmem, in_vmem, in_...  30.2 us
    pallas_call x2, Pallas kernels, viscosity_inner(): pl.pallas_call(kernel, in_specs=[anywhere, in_vmem, in_vmem, anywhere], o...  25.7 us
    all_to_all x3, waiting for transfers between devices, turn(): return lax.all_to_all(value, axis, split_axis=0, concat_axis=0, tiled=True)  23.1 us
    ppermute x4, waiting for transfers between devices, with_halo(): before = lax.ppermute(last, axis, up)  21.5 us
    ppermute x22, waiting for transfers between devices, shift(): lax.ppermute(value, axis, [(i, (i + by) % size) for i in range(size)])  21.2 us
    all_to_all x1, blocking collectives, turn(): return lax.all_to_all(value, axis, split_axis=0, concat_axis=0, tiled=True)  17.3 us
  transfers between devices with their start and end apart: 34, of which 14 were waited for; matrix products, arithmetic and copies ran while one was open for 17% of the time, Pallas kernels for 24%

profile of v6, /device:TPU:1, one launch (start us, length us, event | category | flops | bytes accessed | tf_op | source)
XLA Modules:
  0.0 348.9 jit_solution(8991839112723588508)
XLA Ops:
  18.1 4.0 %collective-permute-done.before_ref.refs_1_.flow_before = f32[3,32,1,512]{3,2,1,0:T(1,128)S(1)} collective-permute-done((f32[3,32,1,512]{3,2,1,0:T(1,128)S(1)}, f32[3,32,1,512]{3,2,1,0:T(1,128)S(1)}, u32[]{:S(2)}, u32[]{:S(2)}) %collective-permute-start) | collective-permute-done | bytes 196640 | tf_op jit(solution)/shard_map/ppermute | solution.py:38
  23.7 12.2 %viscosity_inner.2.refs_6_ = f32[32,64,512]{2,1,0:T(8,128)S(1)} custom-call(f32[3,32,64,512]{3,2,1,0:T(8,128)} %refs_0_.5, f32[3,32,1,512]{3,2,1,0:T(1,128)S(1)} %collective-permute-done.before_ref.refs_1_.flow_before, f32[3,32,1,512]{3,2,1,0:T(1,128)S(1)} %collective-permute-done.1.after_ref.refs_2_.flow_after, f32[32,64,512]{2,1,0:T(8,128)} %refs_3_.3), custom_call_target="tpu_custom_call" | custom-call | tf_op jit(solution)/shard_map/viscosity_inner/pallas_call | solution.py:316
  38.6 4.1 %collective-permute-start.7 = (f32[1,64,512]{2,1,0:T(8,128)S(1)}, f32[1,64,512]{2,1,0:T(8,128)S(1)}, u32[]{:S(2)}, u32[]{:S(2)}) collective-permute-start(f32[1,64,512]{2,1,0:T(8,128)S(1)} %get-tuple-element.32), channel_id=1, source_target_pairs={{0,28},{4,0},{8,4},{12,8},{16,12},{20,16},{24,20},{28,24},{1,29},{... | collective-permute-start | bytes 393224 | tf_op jit(solution)/shard_map/ppermute | solution.py:38
  48.0 15.1 %advance_inner.2.refs_11_ = f32[3,32,64,512]{3,2,1,0:T(8,128)} custom-call(f32[3,32,64,512]{3,2,1,0:T(8,128)} %refs_0_.5, f32[3,32,1,512]{3,2,1,0:T(1,128)S(1)} %collective-permute-done.before_ref.refs_1_.flow_before, f32[3,32,1,512]{3,2,1,0:T(1,128)S(1)} %collective-permute-done.1.after_ref.refs_2_.flow_after, ...), custom_call_target="tpu_custom_call" | custom-call | tf_op jit(solution)/shard_map/advance_inner/pallas_call | solution.py:536
  68.3 4.1 %collective-permute-start.11 = (f32[3,1,64,512]{3,2,1,0:T(8,128)S(1)}, f32[3,1,64,512]{3,2,1,0:T(8,128)S(1)}, u32[]{:S(2)}, u32[]{:S(2)}) collective-permute-start(f32[3,1,64,512]{3,2,1,0:T(8,128)S(1)} %get-tuple-element.18), channel_id=1, source_target_pairs={{0,28},{4,0},{8,4},{12,8},{16,12},{20,16},{24,20},{28,24},{1,29},{... | collective-permute-start | bytes 1179656 | tf_op jit(solution)/shard_map/ppermute | solution.py:38
  75.5 4.3 %collective-permute-done.8.before_ref.refs_1_ = f32[3,32,1,512]{3,2,1,0:T(1,128)S(1)} collective-permute-done((f32[3,32,1,512]{3,2,1,0:T(1,128)S(1)}, f32[3,32,1,512]{3,2,1,0:T(1,128)S(1)}, u32[]{:S(2)}, u32[]{:S(2)}) %collective-permute-start.8) | collective-permute-done | bytes 196640 | tf_op jit(solution)/shard_map/ppermute | solution.py:38
  80.9 13.5 %viscosity_inner.3 = (f32[32,64,512]{2,1,0:T(8,128)S(1)}, f32[4,32,64,128]{3,2,1,0:T(8,128)}) custom-call(f32[3,32,64,512]{3,2,1,0:T(8,128)} %advance_edge.2.flow_ref.refs_0_, f32[3,32,1,512]{3,2,1,0:T(1,128)S(1)} %collective-permute-done.8.before_ref.refs_1_, f32[3,32,1,512]{3,2,1,0:T(1,128)S(1)} %collective-permute-done.9.after_ref.refs_2_, ...), custom_call_target="tpu_custom_call" | custom-call | tf_op jit(solution)/shard_map/viscosity_inner/pallas_call | solution.py:316
  97.8 4.1 %collective-permute-start.15 = (f32[1,64,512]{2,1,0:T(8,128)S(1)}, f32[1,64,512]{2,1,0:T(8,128)S(1)}, u32[]{:S(2)}, u32[]{:S(2)}) collective-permute-start(f32[1,64,512]{2,1,0:T(8,128)S(1)} %get-tuple-element.28), channel_id=1, source_target_pairs={{0,28},{4,0},{8,4},{12,8},{16,12},{20,16},{24,20},{28,24},{1,29},{... | collective-permute-start | bytes 393224 | tf_op jit(solution)/shard_map/ppermute | solution.py:38
  107.8 15.1 %advance_inner.3.refs_11_ = f32[3,32,64,512]{3,2,1,0:T(8,128)} custom-call(f32[3,32,64,512]{3,2,1,0:T(8,128)} %refs_0_.5, f32[3,32,1,512]{3,2,1,0:T(1,128)S(1)} %collective-permute-done.before_ref.refs_1_.flow_before, f32[3,32,1,512]{3,2,1,0:T(1,128)S(1)} %collective-permute-done.1.after_ref.refs_2_.flow_after, ...), custom_call_target="tpu_custom_call" | custom-call | tf_op jit(solution)/shard_map/advance_inner/pallas_call | solution.py:536
  122.9 4.0 %advance_edge.3.flow_ref = f32[3,32,64,512]{3,2,1,0:T(8,128)} custom-call(f32[3,32,64,512]{3,2,1,0:T(8,128)} %refs_0_.5, f32[3,32,1,512]{3,2,1,0:T(1,128)S(1)} %collective-permute-done.before_ref.refs_1_.flow_before, f32[3,32,1,512]{3,2,1,0:T(1,128)S(1)} %collective-permute-done.1.after_ref.refs_2_.flow_after, ...), custom_call_target="tpu_custom_call", output_to_operand_aliasing={{}: (11, {})} | custom-call | tf_op jit(solution)/shard_map/advance_edge/pallas_call | solution.py:478
  127.9 4.1 %collective-permute-start.17 = (f32[1,64,512]{2,1,0:T(8,128)S(1)}, f32[1,64,512]{2,1,0:T(8,128)S(1)}, u32[]{:S(2)}, u32[]{:S(2)}) collective-permute-start(f32[1,64,512]{2,1,0:T(8,128)S(1)} %get-tuple-element.16), channel_id=1, source_target_pairs={{0,28},{4,0},{8,4},{12,8},{16,12},{20,16},{24,20},{28,24},{1,29},{... | collective-permute-start | bytes 393224 | tf_op jit(solution)/shard_map/ppermute | solution.py:38
  134.5 10.3 %divergence_modes.1.modes_ref = f32[4,32,64,128]{3,2,1,0:T(8,128)} custom-call(f32[3,32,64,512]{3,2,1,0:T(8,128)} %advance_edge.3.flow_ref, bf16[256,256]{1,0:T(8,128)(2,1)} %constant.68.clone.even_high, bf16[256,256]{1,0:T(8,128)(2,1)} %constant.69.clone.even_low, bf16[256,256]{1,0:T(8,128)(2,1)} %constant.70.clone.odd_high, ...), custom_call_target="tpu_custom_call" | custom-call | tf_op jit(solution)/shard_map/divergence_modes/pallas_call | solution.py:687
  149.4 4.9 %all-to-all-start = ((f32[4,32,64,128]{3,2,1,0:T(8,128)}), f32[4,32,64,128]{3,2,1,0:T(8,128)}, u32[]{:S(2)}, u32[]{:S(2)}) async-start(f32[4,32,64,128]{3,2,1,0:T(8,128)} %add_halo_modes.1), calls=%async_computation | async-start | bytes 8388608 | tf_op jit(solution)/shard_map/all_to_all | solution.py:1086
  156.1 45.8 %scatter_custom_fusion = f32[4096,128]{1,0:T(8,128)} fusion(s32[8192]{0:T(1024)S(1)} %bitcast.41, f32[8192,128]{1,0:T(8,128)} %bitcast.29, f32[]{:T(128)} %constant.26.clone.1), kind=kCustom, calls=%fused_computation.1 | custom fusion | flops 1048576 | bytes 2097664 | tf_op jit(solution)/shard_map/scatter-add | solution.py:1165
  203.5 8.5 %y_forward.1 = (f32[32,256,128]{2,1,0:T(8,128)}, f32[8,4,32,128]{3,2,1,0:T(8,128)}) custom-call(f32[4,32,64,128]{3,2,1,0:T(8,128)} %all-to-all-done.in_ref, bf16[256,256]{1,0:T(8,128)(2,1)} %constant.74.clone.high_ref, bf16[256,256]{1,0:T(8,128)(2,1)} %constant.75.clone.low_ref, f32[256,128]{1,0:T(8,128)} %get-tuple-element.53.ratio_ref), custom_call_target="tpu_custom_call" | custom-call | tf_op jit(solution)/shard_map/y_forward/pallas_call | solution.py:938
  216.2 23.1 %all-to-all-done.1.in_ref = f32[8,4,32,128]{3,2,1,0:T(8,128)S(1)} async-done(((f32[8,4,32,128]{3,2,1,0:T(8,128)}), f32[8,4,32,128]{3,2,1,0:T(8,128)S(1)}, u32[]{:S(2)}, u32[]{:S(2)}) %all-to-all-start.1) | async-done | bytes 524320 | tf_op jit(solution)/shard_map/all_to_all | solution.py:1086
  239.5 17.3 %all_to_all.20.carry_ref = f32[8,4,32,128]{3,2,1,0:T(8,128)} all-to-all(f32[8,4,32,128]{3,2,1,0:T(8,128)S(1)} %join_carries.1), channel_id=1, replica_groups=mesh['wide'=8,'narrow'=4] {'wide'}, dimensions={0} | all-to-all | bytes 1048576 | tf_op jit(solution)/shard_map/all_to_all | solution.py:1086
  256.8 9.7 %y_inverse.1 = f32[4,34,64,128]{3,2,1,0:T(8,128)} custom-call(f32[32,256,128]{2,1,0:T(8,128)} %get-tuple-element.11.modes_in, f32[8,4,32,128]{3,2,1,0:T(8,128)} %all_to_all.20.carry_ref, bf16[256,256]{1,0:T(8,128)(2,1)} %constant.76.clone.high_ref, bf16[256,256]{1,0:T(8,128)(2,1)} %constant.77.clone.low_ref, f32[256,128]{1,0:T(8,128)} %get-tuple-element.53.ratio_ref, ...), custom_call_target="tpu_custom_call" | custom-call | tf_op jit(solution)/shard_map/y_inverse/pallas_call | solution.py:1068
  266.5 6.8 %all-to-all-start.3 = ((f32[4,34,64,128]{3,2,1,0:T(8,128)}), f32[4,34,64,128]{3,2,1,0:T(8,128)}, u32[]{:S(2)}, u32[]{:S(2)}) async-start(f32[4,34,64,128]{3,2,1,0:T(8,128)} %y_inverse.1), calls=%async_computation.3 | async-start | bytes 8912896 | tf_op jit(solution)/shard_map/all_to_all | solution.py:1086
  278.8 4.0 %collective-permute-start.22 = (f32[3,32,128]{2,1,0:T(8,128)S(1)}, f32[3,32,128]{2,1,0:T(8,128)S(1)}, u32[]{:S(2)}, u32[]{:S(2)}) collective-permute-start(f32[3,32,128]{2,1,0:T(8,128)S(1)} %get-tuple-element.50), channel_id=1, source_target_pairs={{0,4},{4,8},{8,12},{12,16},{16,20},{20,24},{24,28},{1,5},{5,9},{9,... | collective-permute-start | bytes 147464 | tf_op jit(solution)/shard_map/ppermute | solution.py:30
  284.2 4.2 %collective-permute-done.23 = f32[3,32,128]{2,1,0:T(8,128)S(1)} collective-permute-done((f32[3,32,128]{2,1,0:T(8,128)S(1)}, f32[3,32,128]{2,1,0:T(8,128)S(1)}, u32[]{:S(2)}, u32[]{:S(2)}) %collective-permute-start.23) | collective-permute-done | bytes 49184 | tf_op jit(solution)/shard_map/ppermute | solution.py:31
  288.4 4.9 %collective-permute-start.24 = (f32[22,3,128]{2,1,0:T(4,128)S(1)}, f32[22,3,128]{2,1,0:T(4,128)S(1)}, u32[]{:S(2)}, u32[]{:S(2)}) collective-permute-start(f32[22,3,128]{2,1,0:T(4,128)S(1)} %get-tuple-element.44), channel_id=1, source_target_pairs={{0,1},{1,2},{2,3},{4,5},{5,6},{6,7},{8,9},{9,10},{10,11},{12,13},{... | collective-permute-start | bytes 101384 | tf_op jit(solution)/shard_map/ppermute | solution.py:30
  300.8 21.5 %collective-permute-done.24 = f32[22,3,128]{2,1,0:T(4,128)S(1)} collective-permute-done((f32[22,3,128]{2,1,0:T(4,128)S(1)}, f32[22,3,128]{2,1,0:T(4,128)S(1)}, u32[]{:S(2)}, u32[]{:S(2)}) %collective-permute-start.24) | collective-permute-done | bytes 33824 | tf_op jit(solution)/shard_map/ppermute | solution.py:30
  331.0 11.0 %corrected.1 = f32[3,32,64,512]{3,2,1,0:T(8,128)} custom-call(f32[3,32,64,512]{3,2,1,0:T(8,128)} %advance_edge.3.flow_ref, f32[4,34,64,128]{3,2,1,0:T(8,128)} %all-to-all-done.3.in_ref, f32[4,32,128]{2,1,0:T(8,128)S(1)} %bitcast.26, f32[4,32,128]{2,1,0:T(8,128)S(1)} %bitcast.27, bf16[256,256]{1,0:T(8,128)(2,1)S(1)} %copy-done, ...), custom_call_target="tpu_custom_call" | custom-call | tf_op jit(solution)/shard_map/corrected/pallas_call | solution.py:866
  (125 shorter events, 77.5 us)
Async XLA Ops:
  8.4 27.5 %collective-permute-start.2 = (f32[3,1,64,512]{3,2,1,0:T(8,128)S(1)}, f32[3,1,64,512]{3,2,1,0:T(8,128)S(1)}, u32[]{:S(2)}, u32[]{:S(2)}) collective-permute-start(f32[3,1,64,512]{3,2,1,0:T(8,128)S(1)} %get-tuple-element.23), channel_id=1, source_target_pairs={{0,4},{4,8},{8,12},{12,16},{16,20},{20,24},{24,28},{28,0},{1,5},{5... | collective-permute-start | bytes 1179656 | tf_op jit(solution)/shard_map/ppermute | solution.py:38
  10.5 25.4 %collective-permute-start.3 = (f32[3,1,64,512]{3,2,1,0:T(8,128)S(1)}, f32[3,1,64,512]{3,2,1,0:T(8,128)S(1)}, u32[]{:S(2)}, u32[]{:S(2)}) collective-permute-start(f32[3,1,64,512]{3,2,1,0:T(8,128)S(1)} %get-tuple-element.22), channel_id=1, source_target_pairs={{0,28},{4,0},{8,4},{12,8},{16,12},{20,16},{24,20},{28,24},{1,29},{... | collective-permute-start | bytes 1179656 | tf_op jit(solution)/shard_map/ppermute | solution.py:38
  15.9 6.2 %collective-permute-start = (f32[3,32,1,512]{3,2,1,0:T(1,128)S(1)}, f32[3,32,1,512]{3,2,1,0:T(1,128)S(1)}, u32[]{:S(2)}, u32[]{:S(2)}) collective-permute-start(f32[3,32,1,512]{3,2,1,0:T(1,128)S(1)} %get-tuple-element.25), channel_id=1, source_target_pairs={{0,1},{1,2},{2,3},{3,0},{4,5},{5,6},{6,7},{7,4},{8,9},{9,10},{10,1... | collective-permute-start | bytes 589832 | tf_op jit(solution)/shard_map/ppermute | solution.py:38
  18.1 5.6 %collective-permute-start.1 = (f32[3,32,1,512]{3,2,1,0:T(1,128)S(1)}, f32[3,32,1,512]{3,2,1,0:T(1,128)S(1)}, u32[]{:S(2)}, u32[]{:S(2)}) collective-permute-start(f32[3,32,1,512]{3,2,1,0:T(1,128)S(1)} %get-tuple-element.24), channel_id=1, source_target_pairs={{0,3},{1,0},{2,1},{3,2},{4,7},{5,4},{6,5},{7,6},{8,11},{9,8},{10,9... | collective-permute-start | bytes 589832 | tf_op jit(solution)/shard_map/ppermute | solution.py:38
  38.5 24.6 %collective-permute-start.6 = (f32[1,64,512]{2,1,0:T(8,128)S(1)}, f32[1,64,512]{2,1,0:T(8,128)S(1)}, u32[]{:S(2)}, u32[]{:S(2)}) collective-permute-start(f32[1,64,512]{2,1,0:T(8,128)S(1)} %get-tuple-element.33), channel_id=1, source_target_pairs={{0,4},{4,8},{8,12},{12,16},{16,20},{20,24},{24,28},{28,0},{1,5},{5... | collective-permute-start | bytes 393224 | tf_op jit(solution)/shard_map/ppermute | solution.py:38
  38.6 24.5 %collective-permute-start.7 = (f32[1,64,512]{2,1,0:T(8,128)S(1)}, f32[1,64,512]{2,1,0:T(8,128)S(1)}, u32[]{:S(2)}, u32[]{:S(2)}) collective-permute-start(f32[1,64,512]{2,1,0:T(8,128)S(1)} %get-tuple-element.32), channel_id=1, source_target_pairs={{0,28},{4,0},{8,4},{12,8},{16,12},{20,16},{24,20},{28,24},{1,29},{... | collective-permute-start | bytes 393224 | tf_op jit(solution)/shard_map/ppermute | solution.py:38
  68.3 26.2 %collective-permute-start.10 = (f32[3,1,64,512]{3,2,1,0:T(8,128)S(1)}, f32[3,1,64,512]{3,2,1,0:T(8,128)S(1)}, u32[]{:S(2)}, u32[]{:S(2)}) collective-permute-start(f32[3,1,64,512]{3,2,1,0:T(8,128)S(1)} %get-tuple-element.19), channel_id=1, source_target_pairs={{0,4},{4,8},{8,12},{12,16},{16,20},{20,24},{24,28},{28,0},{1,5},{5... | collective-permute-start | bytes 1179656 | tf_op jit(solution)/shard_map/ppermute | solution.py:38
  68.3 26.1 %collective-permute-start.11 = (f32[3,1,64,512]{3,2,1,0:T(8,128)S(1)}, f32[3,1,64,512]{3,2,1,0:T(8,128)S(1)}, u32[]{:S(2)}, u32[]{:S(2)}) collective-permute-start(f32[3,1,64,512]{3,2,1,0:T(8,128)S(1)} %get-tuple-element.18), channel_id=1, source_target_pairs={{0,28},{4,0},{8,4},{12,8},{16,12},{20,16},{24,20},{28,24},{1,29},{... | collective-permute-start | bytes 1179656 | tf_op jit(solution)/shard_map/ppermute | solution.py:38
  97.8 25.1 %collective-permute-start.14 = (f32[1,64,512]{2,1,0:T(8,128)S(1)}, f32[1,64,512]{2,1,0:T(8,128)S(1)}, u32[]{:S(2)}, u32[]{:S(2)}) collective-permute-start(f32[1,64,512]{2,1,0:T(8,128)S(1)} %get-tuple-element.29), channel_id=1, source_target_pairs={{0,4},{4,8},{8,12},{12,16},{16,20},{20,24},{24,28},{28,0},{1,5},{5... | collective-permute-start | bytes 393224 | tf_op jit(solution)/shard_map/ppermute | solution.py:38
  97.8 25.1 %collective-permute-start.15 = (f32[1,64,512]{2,1,0:T(8,128)S(1)}, f32[1,64,512]{2,1,0:T(8,128)S(1)}, u32[]{:S(2)}, u32[]{:S(2)}) collective-permute-start(f32[1,64,512]{2,1,0:T(8,128)S(1)} %get-tuple-element.28), channel_id=1, source_target_pairs={{0,28},{4,0},{8,4},{12,8},{16,12},{20,16},{24,20},{28,24},{1,29},{... | collective-permute-start | bytes 393224 | tf_op jit(solution)/shard_map/ppermute | solution.py:38
  127.9 17.0 %collective-permute-start.16 = (f32[1,64,512]{2,1,0:T(8,128)S(1)}, f32[1,64,512]{2,1,0:T(8,128)S(1)}, u32[]{:S(2)}, u32[]{:S(2)}) collective-permute-start(f32[1,64,512]{2,1,0:T(8,128)S(1)} %get-tuple-element.17), channel_id=1, source_target_pairs={{0,4},{4,8},{8,12},{12,16},{16,20},{20,24},{24,28},{28,0},{1,5},{5... | collective-permute-start | bytes 393224 | tf_op jit(solution)/shard_map/ppermute | solution.py:38
  127.9 16.9 %collective-permute-start.17 = (f32[1,64,512]{2,1,0:T(8,128)S(1)}, f32[1,64,512]{2,1,0:T(8,128)S(1)}, u32[]{:S(2)}, u32[]{:S(2)}) collective-permute-start(f32[1,64,512]{2,1,0:T(8,128)S(1)} %get-tuple-element.16), channel_id=1, source_target_pairs={{0,28},{4,0},{8,4},{12,8},{16,12},{20,16},{24,20},{28,24},{1,29},{... | collective-permute-start | bytes 393224 | tf_op jit(solution)/shard_map/ppermute | solution.py:38
  133.4 11.4 %collective-permute-start.18 = (f32[32,1,512]{2,0,1:T(8,128)S(1)}, f32[32,1,512]{2,0,1:T(8,128)S(1)}, u32[]{:S(2)}, u32[]{:S(2)}) collective-permute-start(f32[32,1,512]{2,0,1:T(8,128)S(1)} %bitcast.37), channel_id=1, source_target_pairs={{0,1},{1,2},{2,3},{3,0},{4,5},{5,6},{6,7},{7,4},{8,9},{9,10},{10,1... | collective-permute-start | bytes 196616 | tf_op jit(solution)/shard_map/ppermute | solution.py:38
  134.5 10.4 %collective-permute-start.19 = (f32[32,1,512]{2,0,1:T(8,128)S(1)}, f32[32,1,512]{2,0,1:T(8,128)S(1)}, u32[]{:S(2)}, u32[]{:S(2)}) collective-permute-start(f32[32,1,512]{2,0,1:T(8,128)S(1)} %bitcast.38), channel_id=1, source_target_pairs={{0,3},{1,0},{2,1},{3,2},{4,7},{5,4},{6,5},{7,6},{8,11},{9,8},{10,9... | collective-permute-start | bytes 196616 | tf_op jit(solution)/shard_map/ppermute | solution.py:38
  149.4 54.1 %all-to-all-start = ((f32[4,32,64,128]{3,2,1,0:T(8,128)}), f32[4,32,64,128]{3,2,1,0:T(8,128)}, u32[]{:S(2)}, u32[]{:S(2)}) async-start(f32[4,32,64,128]{3,2,1,0:T(8,128)} %add_halo_modes.1), calls=%async_computation | async-start | bytes 8388608 | tf_op jit(solution)/shard_map/all_to_all | solution.py:1086
  154.3 123.5 %reduce-scatter.2.cloned.1.call-start = ((), (), s32[]{:S(2)}) async-start(), calls=%async_computation.5 | async-start | bytes 2359296 | tf_op jit(solution)/shard_map/reduce_scatter | solution.py:1167
  212.0 27.4 %all-to-all-start.1 = ((f32[8,4,32,128]{3,2,1,0:T(8,128)}), f32[8,4,32,128]{3,2,1,0:T(8,128)S(1)}, u32[]{:S(2)}, u32[]{:S(2)}) async-start(f32[8,4,32,128]{3,2,1,0:T(8,128)} %get-tuple-element.12), calls=%async_computation.1 | async-start | bytes 1048576 | tf_op jit(solution)/shard_map/all_to_all | solution.py:1086
  266.5 58.7 %all-to-all-start.3 = ((f32[4,34,64,128]{3,2,1,0:T(8,128)}), f32[4,34,64,128]{3,2,1,0:T(8,128)}, u32[]{:S(2)}, u32[]{:S(2)}) async-start(f32[4,34,64,128]{3,2,1,0:T(8,128)} %y_inverse.1), calls=%async_computation.3 | async-start | bytes 8912896 | tf_op jit(solution)/shard_map/all_to_all | solution.py:1086
  276.4 7.7 %collective-permute-start.27 = (f32[2,32,128]{2,1,0:T(8,128)S(1)}, f32[2,32,128]{2,1,0:T(8,128)S(1)}, u32[]{:S(2)}, u32[]{:S(2)}) collective-permute-start(f32[2,32,128]{2,1,0:T(8,128)S(1)} %get-tuple-element.48), channel_id=1, source_target_pairs={{4,0},{8,4},{12,8},{16,12},{20,16},{24,20},{28,24},{5,1},{9,5},{13... | collective-permute-start | bytes 98312 | tf_op jit(solution)/shard_map/ppermute | solution.py:31
  282.8 5.5 %collective-permute-start.23 = (f32[3,32,128]{2,1,0:T(8,128)S(1)}, f32[3,32,128]{2,1,0:T(8,128)S(1)}, u32[]{:S(2)}, u32[]{:S(2)}) collective-permute-start(f32[3,32,128]{2,1,0:T(8,128)S(1)} %get-tuple-element.51), channel_id=1, source_target_pairs={{4,0},{8,4},{12,8},{16,12},{20,16},{24,20},{28,24},{5,1},{9,5},{13... | collective-permute-start | bytes 147464 | tf_op jit(solution)/shard_map/ppermute | solution.py:31
  288.4 33.9 %collective-permute-start.24 = (f32[22,3,128]{2,1,0:T(4,128)S(1)}, f32[22,3,128]{2,1,0:T(4,128)S(1)}, u32[]{:S(2)}, u32[]{:S(2)}) collective-permute-start(f32[22,3,128]{2,1,0:T(4,128)S(1)} %get-tuple-element.44), channel_id=1, source_target_pairs={{0,1},{1,2},{2,3},{4,5},{5,6},{6,7},{8,9},{9,10},{10,11},{12,13},{... | collective-permute-start | bytes 101384 | tf_op jit(solution)/shard_map/ppermute | solution.py:30
  293.2 30.8 %collective-permute-start.25 = (f32[22,3,128]{2,1,0:T(4,128)S(1)}, f32[22,3,128]{2,1,0:T(4,128)S(1)}, u32[]{:S(2)}, u32[]{:S(2)}) collective-permute-start(f32[22,3,128]{2,1,0:T(4,128)S(1)} %get-tuple-element.45), channel_id=1, source_target_pairs={{1,0},{2,1},{3,2},{5,4},{6,5},{7,6},{9,8},{10,9},{11,10},{13,12},{... | collective-permute-start | bytes 101384 | tf_op jit(solution)/shard_map/ppermute | solution.py:31
  295.2 29.1 %collective-permute-start.28 = (f32[20,2,128]{2,1,0:T(2,128)S(1)}, f32[20,2,128]{2,1,0:T(2,128)S(1)}, u32[]{:S(2)}, u32[]{:S(2)}) collective-permute-start(f32[20,2,128]{2,1,0:T(2,128)S(1)} %get-tuple-element.46), channel_id=1, source_target_pairs={{0,1},{1,2},{2,3},{4,5},{5,6},{6,7},{8,9},{9,10},{10,11},{12,13},{... | collective-permute-start | bytes 61448 | tf_op jit(solution)/shard_map/ppermute | solution.py:30
  298.8 25.5 %collective-permute-start.29 = (f32[20,2,128]{2,1,0:T(2,128)S(1)}, f32[20,2,128]{2,1,0:T(2,128)S(1)}, u32[]{:S(2)}, u32[]{:S(2)}) collective-permute-start(f32[20,2,128]{2,1,0:T(2,128)S(1)} %get-tuple-element.47), channel_id=1, source_target_pairs={{1,0},{2,1},{3,2},{5,4},{6,5},{7,6},{9,8},{10,9},{11,10},{13,12},{... | collective-permute-start | bytes 61448 | tf_op jit(solution)/shard_map/ppermute | solution.py:31
  (23 other events, 145.8 us)
Sparse Core Ops, SparseCore 0:
  202.0 74.5 reduce-scatter.1

commit v7 on v6

--- a/solution.py
+++ b/solution.py
@@ -48,6 +48,7 @@
 anywhere = pl.BlockSpec(memory_space=pl.ANY)
 in_vmem = pl.BlockSpec(memory_space=pltpu.VMEM)
 scaled_mu = 0.5 * time_step
+vmem_limit = 48 << 20
 
 
 def row_numbers(width):
@@ -63,36 +64,35 @@
 
 
 class Planes:
-    def __init__(self, source, target, semaphores, listed=None):
+    def __init__(self, source, target, semaphores):
         self.source, self.target, self.semaphores = source, target, semaphores
-        self.listed = listed
-
-    def copy(self, slot, ref, plane):
+
+    def copy(self, slot):
         return pltpu.make_async_copy(
-            pick(ref, plane), pick(self.target, slot), self.semaphores.at[slot]
-        )
-
-    def start(self, slot, plane=None):
-        if self.listed is None:
-            self.copy(slot, self.source, slot if plane is None else plane).start()
-        else:
-            self.copy(slot, *self.listed[slot]).start()
+            pick(self.source, slot), pick(self.target, slot), self.semaphores.at[slot]
+        )
+
+    def start(self, slot):
+        self.copy(slot).start()
 
     def wait(self, slot):
-        self.copy(slot, self.source, 0).wait()
+        self.copy(slot).wait()
+
+
+def cut(ref, first, planes, row, rows):
+    part, lines = pl.ds(first, planes), pl.ds(row, rows)
+    return ref.at[:, part, lines] if len(ref.shape) == 4 else ref.at[part, lines]
 
 
 def in_sections(x_local, size, loads, stores, start_up, body):
     count = x_local // size
 
-    def cut(ref, first, planes):
-        part = pl.ds(first, planes)
-        return ref.at[:, part] if len(ref.shape) == 4 else ref.at[part]
-
-    def moves(kinds, section, first, planes):
+    def moves(kinds, section, first, planes, row=0):
         return [
             pltpu.make_async_copy(
-                cut(source, first, planes), cut(target, first, planes), semaphores.at[section]
+                cut(source, first, planes, row, source.shape[-2] - 2 * row),
+                cut(target, first, planes, row, source.shape[-2] - 2 * row),
+                semaphores.at[section],
             )
             for source, target, semaphores in kinds
         ]
@@ -110,7 +110,7 @@
         if isinstance(first, int):
             start_up()
         lax.fori_loop(first, first + planes, body, 0)
-        for move in moves(stores, section, first, planes):
+        for move in moves(stores, section, first, planes, 8):
             move.start()
 
     work(0, 1, size - 2)
@@ -120,34 +120,87 @@
         return state
 
     lax.fori_loop(1, count, rest, 0)
-    for move in moves(stores, 0, 1, size - 2):
+    for move in moves(stores, 0, 1, size - 2, 8):
         move.wait()
 
     def finish(section, state):
-        for move in moves(stores, section, section * size - 1, size):
+        for move in moves(stores, section, section * size - 1, size, 8):
             move.wait()
         return state
 
     lax.fori_loop(1, count, finish, 0)
 
 
-def edge_list(ref, low, high, x_local):
-    return [(low, 0), (ref, 0), (ref, 1), (ref, x_local - 2), (ref, x_local - 1), (high, 0)]
-
-
-def viscosity_plane(cells, slot, edges, warmth, warm_slot, outs, out_slot, y_local, z_cells):
-    strips, rows = y_local // 8, row_numbers(z_cells)
-    before, after = edges
-    values = [[cells[c, slot, rows_of(s), :] for s in range(strips)] for c in range(3)]
-    up = [[pltpu.roll(v, 7, 0) for v in row] for row in values]
-    down = [[pltpu.roll(v, 1, 0) for v in row] for row in values]
-    for s in range(strips):
+def frame_loads(source, low, high, target, semaphores, x_local, y_local):
+    ends = [
+        pltpu.make_async_copy(pick(ref, plane), pick(target, slot), semaphores.at[i])
+        for i, (ref, plane, slot) in enumerate(
+            [
+                (low, 0, 0),
+                (source, 0, 1),
+                (source, 1, 2),
+                (source, x_local - 2, x_local - 1),
+                (source, x_local - 1, x_local),
+                (high, 0, x_local + 1),
+            ]
+        )
+    ]
+    lines = [
+        pltpu.make_async_copy(
+            cut(source, 2, x_local - 4, row, 16),
+            cut(target, 3, x_local - 4, row, 16),
+            semaphores.at[6 + i],
+        )
+        for i, row in enumerate((0, y_local - 16))
+    ]
+    return ends, lines
+
+
+def frame_parts(source, target, semaphores, x_local, y_local):
+    return [
+        pltpu.make_async_copy(pick(source, plane), pick(target, plane), semaphores.at[i])
+        for i, plane in enumerate((0, x_local - 1))
+    ] + [
+        pltpu.make_async_copy(
+            cut(source, 1, x_local - 2, row, 8),
+            cut(target, 1, x_local - 2, row, 8),
+            semaphores.at[2 + i],
+        )
+        for i, row in enumerate((0, y_local - 8))
+    ]
+
+
+def neighbour_rows(span, y_local, take, halo):
+    before = take(8 * span[0] - 1) if span[0] else halo(0)
+    after = take(8 * span[1]) if 8 * span[1] < y_local else halo(1)
+    return before, after
+
+
+def viscosity_plane(cells, slot, span, halo, warmth, warm_slot, outs, out_slot, y_local, z_cells):
+    strips, rows = range(*span), row_numbers(z_cells)
+    values = [{s: cells[c, slot, rows_of(s), :] for s in strips} for c in range(3)]
+    up = [{s: pltpu.roll(v, 7, 0) for s, v in row.items()} for row in values]
+    down = [{s: pltpu.roll(v, 1, 0) for s, v in row.items()} for row in values]
+    sides = [
+        neighbour_rows(
+            span,
+            y_local,
+            lambda row: cells[c, slot, pl.ds(row, 1), :],
+            lambda side: halo[side][c, out_slot],
+        )
+        for c in range(3)
+    ]
+    for s in strips:
         along_x, along_y, along_z = [], [], []
         for c in range(3):
             value = values[c][s]
             along_x.append(cells[c, slot + 1, rows_of(s), :] - cells[c, slot - 1, rows_of(s), :])
-            ahead = jnp.where(rows == 7, up[c][s + 1] if s + 1 < strips else after(c), up[c][s])
-            behind = jnp.where(rows == 0, down[c][s - 1] if s else before(c), down[c][s])
+            ahead = jnp.where(
+                rows == 7, up[c][s + 1] if s + 1 in strips else sides[c][1], up[c][s]
+            )
+            behind = jnp.where(
+                rows == 0, down[c][s - 1] if s - 1 in strips else sides[c][0], down[c][s]
+            )
             along_y.append(ahead - behind)
             along_z.append(pltpu.roll(value, z_cells - 1, 1) - pltpu.roll(value, 1, 1))
         s_xy = along_y[0] + along_x[1]
@@ -170,121 +223,87 @@
                 outs[1][b, out_slot, rows_of(s), :] = heat[:, b * 128 : (b + 1) * 128]
 
 
-def viscosity_call(flow, y_sides, warmth, with_heat, x_sides=None, inner=None):
+def viscosity_frame(flow, x_sides, y_sides, warmth, inner):
     _, x_local, y_local, z_cells = flow.shape
-    z_blocks = z_cells // 128
-    edge = x_sides is not None
-    slots, made = (6, 2) if edge else (x_local, x_local - 2)
-    outputs = 2 if with_heat else 1
-
-    def kernel(*refs):
-        flow_ref, before_ref, after_ref, warmth_ref = refs[:4]
-        rest = list(refs[4:])
-        listed = None
-        if edge:
-            low, high = rest[:2]
-            listed = edge_list(flow_ref, low, high, x_local)
-            rest = rest[2 + outputs :]
-        out_refs, rest = rest[:outputs], rest[outputs:]
+    outputs, strips = len(inner), y_local // 8
+
+    def kernel(flow_ref, low, high, before_ref, after_ref, warmth_ref, *rest):
+        out_refs, rest = rest[outputs : 2 * outputs], rest[2 * outputs :]
         cells, cell_sem, warm, warm_sem = rest[:4]
-        outs, out_sems = rest[4 : 4 + outputs], rest[4 + outputs :]
-        flow_planes = Planes(flow_ref, cells, cell_sem, listed)
-        warm_planes = Planes(warmth_ref, warm, warm_sem)
-
-        def plane_of(i):
-            return i * (x_local - 1) if edge else i + 1
-
-        def slot_of(i):
-            return 3 * i + 1 if edge else i + 1
-
-        def stored(k, i):
-            return pltpu.make_async_copy(
-                pick(outs[k], i), pick(out_refs[k], plane_of(i)), out_sems[k].at[i]
-            )
-
-        if edge:
-            for slot in range(6):
-                flow_planes.start(slot)
-            for i in range(2):
-                warm_planes.start(i, plane_of(i))
-        else:
-            flow_planes.start(0)
-            flow_planes.start(1)
-
-            def begin(i, state):
-                flow_planes.start(i + 2)
-                warm_planes.start(i, i + 1)
-                return state
-
-            lax.fori_loop(0, made, begin, 0)
-            flow_planes.wait(0)
-            flow_planes.wait(1)
-
-        def body(i, state):
-            slot, plane = slot_of(i), plane_of(i)
-            if edge:
-                flow_planes.wait(slot - 1)
-                flow_planes.wait(slot)
-            flow_planes.wait(slot + 1)
-            warm_planes.wait(i)
+        outs, sems = rest[4 : 4 + outputs], rest[4 + outputs :]
+        ends, lines = frame_loads(flow_ref, low, high, cells, cell_sem, x_local, y_local)
+        warms = frame_parts(warmth_ref, warm, warm_sem, x_local, y_local)
+        stores = [
+            frame_parts(outs[k], out_refs[k], sems[k], x_local, y_local) for k in range(outputs)
+        ]
+        for load in ends + warms[:2] + lines + warms[2:]:
+            load.start()
+        for load in ends + warms[:2]:
+            load.wait()
+
+        def work(plane, *span):
             viscosity_plane(
                 cells,
-                slot,
-                (lambda c: before_ref[c, plane], lambda c: after_ref[c, plane]),
+                plane + 1,
+                span,
+                (before_ref, after_ref),
                 warm,
-                i,
+                plane,
                 outs,
-                i,
+                plane,
                 y_local,
                 z_cells,
             )
-            for k in range(outputs):
-                stored(k, i).start()
-            return state
-
-        lax.fori_loop(0, made, body, 0)
-
-        def finish(i, state):
-            for k in range(outputs):
-                stored(k, i).wait()
-            return state
-
-        lax.fori_loop(0, made, finish, 0)
-
-    shapes = [(x_local, y_local, z_cells), (z_blocks, x_local, y_local, 128)][:outputs]
-    held = [(made, y_local, z_cells), (z_blocks, made, y_local, 128)][:outputs]
-    operands = [flow, *y_sides, warmth]
-    specs = [anywhere, in_vmem, in_vmem, anywhere]
-    aliases = {}
-    if edge:
-        operands += [*x_sides, *inner]
-        specs += [anywhere] * (2 + outputs)
-        aliases = {6 + k: k for k in range(outputs)}
+
+        def end_plane(i, state):
+            work(i * (x_local - 1), 0, strips)
+            return state
+
+        lax.fori_loop(0, 2, end_plane, 0)
+        for k in range(outputs):
+            for store in stores[k][:2]:
+                store.start()
+        for load in lines + warms[2:]:
+            load.wait()
+
+        def side_strips(plane, state):
+            work(plane, 0, 1)
+            work(plane, strips - 1, strips)
+            return state
+
+        lax.fori_loop(1, x_local - 1, side_strips, 0)
+        for k in range(outputs):
+            for store in stores[k][2:]:
+                store.start()
+        for k in range(outputs):
+            for store in stores[k]:
+                store.wait()
+
     return pl.pallas_call(
         kernel,
-        in_specs=specs,
+        in_specs=[anywhere] * 3 + [in_vmem] * 2 + [anywhere] * (1 + outputs),
         out_specs=[anywhere] * outputs,
-        out_shape=[jax.ShapeDtypeStruct(shape, jnp.float32) for shape in shapes],
-        input_output_aliases=aliases,
+        out_shape=[jax.ShapeDtypeStruct(field.shape, jnp.float32) for field in inner],
+        input_output_aliases={6 + k: k for k in range(outputs)},
         scratch_shapes=[
-            pltpu.VMEM((3, slots, y_local, z_cells), jnp.float32),
-            pltpu.SemaphoreType.DMA((slots,)),
-            pltpu.VMEM((made, y_local, z_cells), jnp.float32),
-            pltpu.SemaphoreType.DMA((made,)),
+            pltpu.VMEM((3, x_local + 2, y_local, z_cells), jnp.float32),
+            pltpu.SemaphoreType.DMA((8,)),
+            pltpu.VMEM(warmth.shape, jnp.float32),
+            pltpu.SemaphoreType.DMA((4,)),
         ]
-        + [pltpu.VMEM(shape, jnp.float32) for shape in held]
-        + [pltpu.SemaphoreType.DMA((made,))] * outputs,
+        + [pltpu.VMEM(field.shape, jnp.float32) for field in inner]
+        + [pltpu.SemaphoreType.DMA((4,))] * outputs,
         compiler_params=pltpu.CompilerParams(vmem_limit_bytes=vmem_limit),
-        name="viscosity_edge" if edge else "viscosity_inner",
-    )(*operands)
-
-
-def viscosity_inner(flow, y_sides, warmth, with_heat):
+        name="viscosity_frame",
+    )(flow, *x_sides, *y_sides, warmth, *inner)
+
+
+def viscosity_inner(flow, warmth, with_heat):
     _, x_local, y_local, z_cells = flow.shape
     z_blocks, size = z_cells // 128, 4
     outputs = 2 if with_heat else 1
 
-    def kernel(flow_ref, before_ref, after_ref, warmth_ref, *rest):
+    def kernel(flow_ref, warmth_ref, *rest):
         out_refs, (cells, cell_sem, warm, warm_sem, *heat) = rest[:outputs], rest[outputs:]
         outs = [out_refs[0]] + heat[:1]
 
@@ -292,7 +311,8 @@
             viscosity_plane(
                 cells,
                 slot,
-                (lambda c: before_ref[c, slot], lambda c: after_ref[c, slot]),
+                (1, y_local // 8 - 1),
+                None,
                 warm,
                 slot,
                 outs,
@@ -315,7 +335,7 @@
     sems = pltpu.SemaphoreType.DMA((x_local // size,))
     return pl.pallas_call(
         kernel,
-        in_specs=[anywhere, in_vmem, in_vmem, anywhere],
+        in_specs=[anywhere, anywhere],
         out_specs=[in_vmem, anywhere][:outputs],
         out_shape=[jax.ShapeDtypeStruct(shape, jnp.float32) for shape in shapes],
         scratch_shapes=[
@@ -327,36 +347,46 @@
         + ([pltpu.VMEM(shapes[1], jnp.float32), sems] if with_heat else []),
         compiler_params=pltpu.CompilerParams(vmem_limit_bytes=vmem_limit),
         name="viscosity_inner",
-    )(flow, *y_sides, warmth)
-
-
-vmem_limit = 48 << 20
-
-
-def advance_plane(cells, mu, slot, edges, push, out_slot, flux, y_local, z_cells):
-    strips, rows = y_local // 8, row_numbers(z_cells)
-    flow_before, flow_after, mu_before, mu_after = edges
-    m = [mu[slot, rows_of(s), :] for s in range(strips)]
-    m_up = [pltpu.roll(v, 7, 0) for v in m]
-    sums_y = [
-        m[s] + jnp.where(rows == 7, m_up[s + 1] if s + 1 < strips else mu_after(), m_up[s])
-        for s in range(strips)
+    )(flow, warmth)
+
+
+def advance_plane(cells, mu, slot, mu_slot, span, halo, push, plane, flux, y_local, z_cells):
+    strips, rows = range(*span), row_numbers(z_cells)
+    m = {s: mu[mu_slot, rows_of(s), :] for s in strips}
+    m_up = {s: pltpu.roll(v, 7, 0) for s, v in m.items()}
+    mu_before, mu_after = neighbour_rows(
+        span,
+        y_local,
+        lambda row: mu[mu_slot, pl.ds(row, 1), :],
+        lambda side: halo[1][side][plane],
+    )
+    sums_y = {
+        s: m[s] + jnp.where(rows == 7, m_up[s + 1] if s + 1 in strips else mu_after, m_up[s])
+        for s in strips
+    }
+    start = pl.ds(8 * span[0], 1)
+    first_sum = mu_before + mu[mu_slot, start, :]
+    values = [{s: cells[c, slot, rows_of(s), :] for s in strips} for c in range(3)]
+    up = [{s: pltpu.roll(v, 7, 0) for s, v in row.items()} for row in values]
+    sides = [
+        neighbour_rows(
+            span,
+            y_local,
+            lambda row: cells[c, slot, pl.ds(row, 1), :],
+            lambda side: halo[0][side][c, plane],
+        )
+        for c in range(3)
     ]
-    first_sum = mu_before() + mu[slot, pl.ds(0, 1), :]
-    values = [[cells[c, slot, rows_of(s), :] for s in range(strips)] for c in range(3)]
-    up = [[pltpu.roll(v, 7, 0) for v in row] for row in values]
-    carried = [
-        first_sum * (cells[c, slot, pl.ds(0, 1), :] - flow_before(c)) for c in range(3)
-    ]
-    for s in range(strips):
-        sum_x = m[s] + mu[slot + 1, rows_of(s), :]
+    carried = [first_sum * (cells[c, slot, start, :] - sides[c][0]) for c in range(3)]
+    for s in strips:
+        sum_x = m[s] + mu[mu_slot + 1, rows_of(s), :]
         sum_z_ahead = m[s] + pltpu.roll(m[s], z_cells - 1, 1)
         sum_z_behind = m[s] + pltpu.roll(m[s], 1, 1)
         for c in range(3):
             value = values[c][s]
             flux_x = sum_x * (cells[c, slot + 1, rows_of(s), :] - value)
             ahead = jnp.where(
-                rows == 7, up[c][s + 1] if s + 1 < strips else flow_after(c), up[c][s]
+                rows == 7, up[c][s + 1] if s + 1 in strips else sides[c][1], up[c][s]
             )
             flux_y = sums_y[s] * (ahead - value)
             turned = pltpu.roll(flux_y, 1, 0)
@@ -368,158 +398,117 @@
             )
             flux[c, rows_of(s), :] = flux_x
             carried[c] = turned
-            push[c, out_slot, rows_of(s), :] = (
-                value + time_step * push[c, out_slot, rows_of(s), :] + total
-            )
-
-
-def first_flux(cells, mu, slot, flux, y_local):
-    for s in range(y_local // 8):
-        sum_x = mu[slot - 1, rows_of(s), :] + mu[slot, rows_of(s), :]
+            push[c, plane, rows_of(s), :] = (
+                value + time_step * push[c, plane, rows_of(s), :] + total
+            )
+
+
+def first_flux(cells, mu, slot, mu_slot, strips, flux):
+    for s in strips:
+        sum_x = mu[mu_slot - 1, rows_of(s), :] + mu[mu_slot, rows_of(s), :]
         for c in range(3):
             flux[c, rows_of(s), :] = sum_x * (
                 cells[c, slot, rows_of(s), :] - cells[c, slot - 1, rows_of(s), :]
             )
 
 
-def advance_call(flow, flow_y, mu, mu_y, push, flow_x=None, mu_x=None, inner=None):
+def advance_frame(flow, flow_x, flow_y, mu, mu_x, mu_y, push, inner):
     _, x_local, y_local, z_cells = flow.shape
-    edge = flow_x is not None
-    slots, made = (6, 2) if edge else (x_local, x_local - 2)
-
-    def kernel(*refs):
-        flow_ref, flow_before, flow_after, mu_ref, mu_before, mu_after, push_ref = refs[:7]
-        rest = refs[7:]
-        flow_listed = mu_listed = None
-        if edge:
-            flow_listed = edge_list(flow_ref, rest[0], rest[1], x_local)
-            mu_listed = edge_list(mu_ref, rest[2], rest[3], x_local)
-            rest = rest[5:]
-        out_ref, cells, cell_sem, mu_cells, mu_sem, work, work_sem, out_sem, flux = rest
-        flow_planes = Planes(flow_ref, cells, cell_sem, flow_listed)
-        mu_planes = Planes(mu_ref, mu_cells, mu_sem, mu_listed)
-        push_planes = Planes(push_ref, work, work_sem)
-
-        def plane_of(i):
-            return i * (x_local - 1) if edge else i + 1
-
-        def stored(i):
-            return pltpu.make_async_copy(
-                pick(work, i), pick(out_ref, plane_of(i)), out_sem.at[i]
-            )
-
-        if edge:
-            for slot in range(6):
-                flow_planes.start(slot)
-                mu_planes.start(slot)
-            for i in range(2):
-                push_planes.start(i, plane_of(i))
-        else:
-            for slot in range(2):
-                flow_planes.start(slot)
-                mu_planes.start(slot)
-
-            def begin(i, state):
-                flow_planes.start(i + 2)
-                mu_planes.start(i + 2)
-                push_planes.start(i, i + 1)
-                return state
-
-            lax.fori_loop(0, made, begin, 0)
-            for slot in range(2):
-                flow_planes.wait(slot)
-                mu_planes.wait(slot)
-            first_flux(cells, mu_cells, 1, flux, y_local)
-
-        def body(i, state):
-            slot, plane = (3 * i + 1 if edge else i + 1), plane_of(i)
-            if edge:
-                for back in range(2):
-                    flow_planes.wait(slot - back)
-                    mu_planes.wait(slot - back)
-                first_flux(cells, mu_cells, slot, flux, y_local)
-            flow_planes.wait(slot + 1)
-            mu_planes.wait(slot + 1)
-            push_planes.wait(i)
+    strips = y_local // 8
+
+    def kernel(
+        flow_ref, flow_low, flow_high, flow_before, flow_after,
+        mu_ref, mu_low, mu_high, mu_before, mu_after, push_ref, _,
+        out_ref, cells, cell_sem, mu_cells, mu_sem, work, work_sem, out_sem, flux,
+    ):
+        ends, lines = frame_loads(
+            flow_ref, flow_low, flow_high, cells, cell_sem, x_local, y_local
+        )
+        mu_ends, mu_lines = frame_loads(
+            mu_ref, mu_low, mu_high, mu_cells, mu_sem, x_local, y_local
+        )
+        pushes = frame_parts(push_ref, work, work_sem, x_local, y_local)
+        stores = frame_parts(work, out_ref, out_sem, x_local, y_local)
+        early, late = ends + mu_ends + pushes[:2], lines + mu_lines + pushes[2:]
+        for load in early + late:
+            load.start()
+        for load in early:
+            load.wait()
+
+        def advance(plane, *span):
             advance_plane(
                 cells,
                 mu_cells,
-                slot,
-                (
-                    lambda c: flow_before[c, plane],
-                    lambda c: flow_after[c, plane],
-                    lambda: mu_before[plane],
-                    lambda: mu_after[plane],
-                ),
+                plane + 1,
+                plane + 1,
+                span,
+                ((flow_before, flow_after), (mu_before, mu_after)),
                 work,
-                i,
+                plane,
                 flux,
                 y_local,
                 z_cells,
             )
-            stored(i).start()
-            return state
-
-        lax.fori_loop(0, made, body, 0)
-
-        def finish(i, state):
-            stored(i).wait()
-            return state
-
-        lax.fori_loop(0, made, finish, 0)
-
-    operands = [flow, *flow_y, mu, *mu_y, push]
-    specs = [anywhere, in_vmem, in_vmem, anywhere, in_vmem, in_vmem, anywhere]
-    aliases = {}
-    if edge:
-        operands += [*flow_x, *mu_x, inner]
-        specs += [anywhere] * 5
-        aliases = {11: 0}
+
+        def end_plane(i, state):
+            plane = i * (x_local - 1)
+            first_flux(cells, mu_cells, plane + 1, plane + 1, range(strips), flux)
+            advance(plane, 0, strips)
+            return state
+
+        lax.fori_loop(0, 2, end_plane, 0)
+        for store in stores[:2]:
+            store.start()
+        for load in late:
+            load.wait()
+        first_flux(cells, mu_cells, 2, 2, (0, strips - 1), flux)
+
+        def side_strips(plane, state):
+            advance(plane, 0, 1)
+            advance(plane, strips - 1, strips)
+            return state
+
+        lax.fori_loop(1, x_local - 1, side_strips, 0)
+        for store in stores[2:]:
+            store.start()
+        for store in stores:
+            store.wait()
+
     return pl.pallas_call(
         kernel,
-        in_specs=specs,
+        in_specs=[anywhere] * 3
+        + [in_vmem] * 2
+        + [anywhere] * 3
+        + [in_vmem] * 2
+        + [anywhere] * 2,
         out_specs=anywhere,
         out_shape=jax.ShapeDtypeStruct(flow.shape, jnp.float32),
-        input_output_aliases=aliases,
+        input_output_aliases={11: 0},
         scratch_shapes=[
-            pltpu.VMEM((3, slots, y_local, z_cells), jnp.float32),
-            pltpu.SemaphoreType.DMA((slots,)),
-            pltpu.VMEM((slots, y_local, z_cells), jnp.float32),
-            pltpu.SemaphoreType.DMA((slots,)),
-            pltpu.VMEM((3, made, y_local, z_cells), jnp.float32),
-            pltpu.SemaphoreType.DMA((made,)),
-            pltpu.SemaphoreType.DMA((made,)),
+            pltpu.VMEM((3, x_local + 2, y_local, z_cells), jnp.float32),
+            pltpu.SemaphoreType.DMA((8,)),
+            pltpu.VMEM((x_local + 2, y_local, z_cells), jnp.float32),
+            pltpu.SemaphoreType.DMA((8,)),
+            pltpu.VMEM(flow.shape, jnp.float32),
+            pltpu.SemaphoreType.DMA((4,)),
+            pltpu.SemaphoreType.DMA((4,)),
             pltpu.VMEM((3, y_local, z_cells), jnp.float32),
         ],
         compiler_params=pltpu.CompilerParams(vmem_limit_bytes=vmem_limit),
-        name="advance_edge" if edge else "advance_inner",
-    )(*operands)
-
-
-def advance_inner(flow, flow_y, mu, mu_y, push):
+        name="advance_frame",
+    )(flow, *flow_x, *flow_y, mu, *mu_x, *mu_y, push, inner)
+
+
+def advance_inner(flow, mu, push):
     _, x_local, y_local, z_cells = flow.shape
-    size = 4
+    size, span = 4, (1, y_local // 8 - 1)
 
     def kernel(
-        flow_ref, flow_before, flow_after, mu_ref, mu_before, mu_after, push_ref,
-        out_ref, cells, cell_sem, work, work_sem, out_sem, flux,
+        flow_ref, mu_ref, push_ref, out_ref, cells, cell_sem, work, work_sem, out_sem, flux
     ):
         def body(slot, state):
             advance_plane(
-                cells,
-                mu_ref,
-                slot,
-                (
-                    lambda c: flow_before[c, slot],
-                    lambda c: flow_after[c, slot],
-                    lambda: mu_before[slot],
-                    lambda: mu_after[slot],
-                ),
-                work,
-                slot,
-                flux,
-                y_local,
-                z_cells,
+                cells, mu_ref, slot, slot, span, None, work, slot, flux, y_local, z_cells
             )
             return state
 
@@ -528,14 +517,14 @@
             size,
             [(flow_ref, cells, cell_sem), (push_ref, work, work_sem)],
             [(work, out_ref, out_sem)],
-            lambda: first_flux(cells, mu_ref, 1, flux, y_local),
+            lambda: first_flux(cells, mu_ref, 1, 1, range(*span), flux),
             body,
         )
 
     sems = pltpu.SemaphoreType.DMA((x_local // size,))
     return pl.pallas_call(
         kernel,
-        in_specs=[anywhere, in_vmem, in_vmem, in_vmem, in_vmem, in_vmem, anywhere],
+        in_specs=[anywhere, in_vmem, anywhere],
         out_specs=anywhere,
         out_shape=jax.ShapeDtypeStruct(flow.shape, jnp.float32),
         scratch_shapes=[
@@ -548,7 +537,7 @@
         ],
         compiler_params=pltpu.CompilerParams(vmem_limit_bytes=vmem_limit),
         name="advance_inner",
-    )(flow, *flow_y, mu, *mu_y, push)
+    )(flow, mu, push)
 
 
 def cosine_sine_basis(points, period, waves):
@@ -1134,12 +1123,14 @@
     current, current_x, current_y = flow, flow_x, flow_y
     for section in range(PASSES):
         last = section + 1 == PASSES
-        inner = viscosity_inner(current, current_y, tool_warmth_excess, last)
-        fields = viscosity_call(current, current_y, tool_warmth_excess, last, current_x, inner)
+        inner = viscosity_inner(current, tool_warmth_excess, last)
+        fields = viscosity_frame(current, current_x, current_y, tool_warmth_excess, inner)
         mu = fields[0]
         mu_x, mu_y = ring(mu, "wide", 0), ring(mu, "narrow", 1)
-        inner = advance_inner(flow, flow_y, mu, mu_y, tool_push_density)
-        current = advance_call(flow, flow_y, mu, mu_y, tool_push_density, flow_x, mu_x, inner)
+        inner = advance_inner(flow, mu, tool_push_density)
+        current = advance_frame(
+            flow, flow_x, flow_y, mu, mu_x, mu_y, tool_push_density, inner
+        )
         if not last:
             current_x, current_y = ring(current, "wide", 1), ring(current, "narrow", 2)
     heat_cells = fields[1]

time: 350 us -> 356 us (1.017)
  Pallas kernels: 113 us -> 132 us
  waiting for transfers between devices: 71.8 us -> 53.7 us
  starting transfers between devices: 67.6 us -> 73.3 us
    pallas_call x8, Pallas kernels: 69.7 us -> 88.5 us  [the longest x2 25.9 us: advance_inner(): pl.pallas_call(kernel, in_specs=[anywhere, in_vmem, anywhere], out_specs=...]
    ppermute x22, waiting for transfers between devices: 21.2 us -> 3.06 us  [shift(): lax.ppermute(value, axis, [(i, (i + by) % size) for i in range(size)])]
    ppermute x22, starting transfers between devices: 30.2 us -> 35.6 us  [shift(): lax.ppermute(value, axis, [(i, (i + by) % size) for i in range(size)])]
  transfers between devices with their start and end apart: 34 -> 34, of which waited for: 14 -> 7; matrix products, arithmetic and copies ran while one was open for 17% -> 17% of each run, Pallas kernels for 24% -> 21%
where the time goes in v7:
time: 356 us; the launch traced here: 355 us
  Pallas kernels  132 us (37%)
  starting transfers between devices  73.3 us (21%)
  waiting for transfers between devices  53.7 us (15%)
  other arithmetic  49.2 us (14%)
  blocking collectives  17.4 us (5%)
  local copies, waits for them, and re-layouts  15 us (4%)
  between operations  14.8 us (4%)
    scatter-add x1, other arithmetic, per_device(): partial_value = jnp.zeros((slab_count * component_lines, 128), jnp.float3...  45.8 us
    ppermute x22, starting transfers between devices, shift(): lax.ppermute(value, axis, [(i, (i + by) % size) for i in range(size)])  35.6 us
    pallas_call x2, Pallas kernels, advance_inner(): pl.pallas_call(kernel, in_specs=[anywhere, in_vmem, anywhere], out_specs=...  25.9 us
    all_to_all x3, waiting for transfers between devices, turn(): return lax.all_to_all(value, axis, split_axis=0, concat_axis=0, tiled=True)  23.1 us
    pallas_call x2, Pallas kernels, advance_frame(): pl.pallas_call(kernel, in_specs=[anywhere] * 3 + [in_vmem] * 2 + [anywher...  22.6 us
    pallas_call x2, Pallas kernels, viscosity_inner(): pl.pallas_call(kernel, in_specs=[anywhere, anywhere], out_specs=[in_vmem,...  21.7 us
    ppermute x4, waiting for transfers between devices, with_halo(): before = lax.ppermute(last, axis, up)  21.5 us
    pallas_call x2, Pallas kernels, viscosity_frame(): pl.pallas_call(kernel, in_specs=[anywhere] * 3 + [in_vmem] * 2 + [anywher...  18.2 us
  transfers between devices with their start and end apart: 34, of which 7 were waited for; matrix products, arithmetic and copies ran while one was open for 17% of the time, Pallas kernels for 21%

profile of v7, /device:TPU:1, one launch (start us, length us, event | category | flops | bytes accessed | tf_op | source)
XLA Modules:
  0.0 355.4 jit_solution(15703252524955422431)
XLA Ops:
  18.1 10.3 %viscosity_inner.2.rest_0_ = f32[32,64,512]{2,1,0:T(8,128)S(1)} custom-call(f32[3,32,64,512]{3,2,1,0:T(8,128)} %flow_ref.11, f32[32,64,512]{2,1,0:T(8,128)} %warmth_ref.7), custom_call_target="tpu_custom_call" | custom-call | tf_op jit(solution)/shard_map/viscosity_inner/pallas_call | solution.py:336
  28.6 8.6 %viscosity_frame.2.mu_ref = f32[32,64,512]{2,1,0:T(8,128)S(1)} custom-call(f32[3,32,64,512]{3,2,1,0:T(8,128)} %flow_ref.11, f32[3,1,64,512]{3,2,1,0:T(8,128)S(1)} %collective-permute-done.low.flow_low, f32[3,1,64,512]{3,2,1,0:T(8,128)S(1)} %collective-permute-done.1.high.flow_high, ...), custom_call_target="tpu_custom_call", output_to_operand_aliasing={{}: (6, {})} | custom-call | tf_op jit(solution)/shard_map/viscosity_frame/pallas_call | solution.py:282
  45.1 13.0 %advance_inner.2._ = f32[3,32,64,512]{3,2,1,0:T(8,128)} custom-call(f32[3,32,64,512]{3,2,1,0:T(8,128)} %flow_ref.11, f32[32,64,512]{2,1,0:T(8,128)S(1)} %viscosity_frame.2.mu_ref, f32[3,32,64,512]{3,2,1,0:T(8,128)} %push_ref.7), custom_call_target="tpu_custom_call" | custom-call | tf_op jit(solution)/shard_map/advance_inner/pallas_call | solution.py:525
  58.1 11.3 %advance_frame.2.flow_ref = f32[3,32,64,512]{3,2,1,0:T(8,128)} custom-call(f32[3,32,64,512]{3,2,1,0:T(8,128)} %flow_ref.11, f32[3,1,64,512]{3,2,1,0:T(8,128)S(1)} %collective-permute-done.low.flow_low, f32[3,1,64,512]{3,2,1,0:T(8,128)S(1)} %collective-permute-done.1.high.flow_high, ...), custom_call_target="tpu_custom_call", output_to_operand_aliasing={{}: (11, {})} | custom-call | tf_op jit(solution)/shard_map/advance_frame/pallas_call | solution.py:477
  70.7 4.1 %collective-permute-start.9 = (f32[3,1,64,512]{3,2,1,0:T(8,128)S(1)}, f32[3,1,64,512]{3,2,1,0:T(8,128)S(1)}, u32[]{:S(2)}, u32[]{:S(2)}) collective-permute-start(f32[3,1,64,512]{3,2,1,0:T(8,128)S(1)} %get-tuple-element.20), channel_id=1, source_target_pairs={{0,28},{4,0},{8,4},{12,8},{16,12},{20,16},{24,20},{28,24},{1,29},{... | collective-permute-start | bytes 1179656 | tf_op jit(solution)/shard_map/ppermute | solution.py:38
  79.5 11.4 %viscosity_inner.3 = (f32[32,64,512]{2,1,0:T(8,128)S(1)}, f32[4,32,64,128]{3,2,1,0:T(8,128)}) custom-call(f32[3,32,64,512]{3,2,1,0:T(8,128)} %advance_frame.2.flow_ref, f32[32,64,512]{2,1,0:T(8,128)} %warmth_ref.7), custom_call_target="tpu_custom_call" | custom-call | tf_op jit(solution)/shard_map/viscosity_inner/pallas_call | solution.py:336
  91.0 9.7 %viscosity_frame.3 = (f32[32,64,512]{2,1,0:T(8,128)S(1)}, f32[4,32,64,128]{3,2,1,0:T(8,128)}) custom-call(f32[3,32,64,512]{3,2,1,0:T(8,128)} %advance_frame.2.flow_ref, f32[3,1,64,512]{3,2,1,0:T(8,128)S(1)} %collective-permute-done.8.low, f32[3,1,64,512]{3,2,1,0:T(8,128)S(1)} %collective-permute-done.9.high, ...), custom_call_target="tpu_custom_call", output_to_operand_aliasing={{0}: (6, {}), {1}: (7, {})} | custom-call | tf_op jit(solution)/shard_map/viscosity_frame/pallas_call | solution.py:282
  100.7 4.1 %collective-permute-start.13 = (f32[1,64,512]{2,1,0:T(8,128)S(1)}, f32[1,64,512]{2,1,0:T(8,128)S(1)}, u32[]{:S(2)}, u32[]{:S(2)}) collective-permute-start(f32[1,64,512]{2,1,0:T(8,128)S(1)} %get-tuple-element.30), channel_id=1, source_target_pairs={{0,28},{4,0},{8,4},{12,8},{16,12},{20,16},{24,20},{28,24},{1,29},{... | collective-permute-start | bytes 393224 | tf_op jit(solution)/shard_map/ppermute | solution.py:38
  107.3 13.0 %advance_inner.3._ = f32[3,32,64,512]{3,2,1,0:T(8,128)} custom-call(f32[3,32,64,512]{3,2,1,0:T(8,128)} %flow_ref.11, f32[32,64,512]{2,1,0:T(8,128)S(1)} %get-tuple-element.10.mu_ref, f32[3,32,64,512]{3,2,1,0:T(8,128)} %push_ref.7), custom_call_target="tpu_custom_call" | custom-call | tf_op jit(solution)/shard_map/advance_inner/pallas_call | solution.py:525
  120.4 11.3 %advance_frame.3.flow_ref = f32[3,32,64,512]{3,2,1,0:T(8,128)} custom-call(f32[3,32,64,512]{3,2,1,0:T(8,128)} %flow_ref.11, f32[3,1,64,512]{3,2,1,0:T(8,128)S(1)} %collective-permute-done.low.flow_low, f32[3,1,64,512]{3,2,1,0:T(8,128)S(1)} %collective-permute-done.1.high.flow_high, ...), custom_call_target="tpu_custom_call", output_to_operand_aliasing={{}: (11, {})} | custom-call | tf_op jit(solution)/shard_map/advance_frame/pallas_call | solution.py:477
  132.7 4.1 %collective-permute-start.17 = (f32[1,64,512]{2,1,0:T(8,128)S(1)}, f32[1,64,512]{2,1,0:T(8,128)S(1)}, u32[]{:S(2)}, u32[]{:S(2)}) collective-permute-start(f32[1,64,512]{2,1,0:T(8,128)S(1)} %get-tuple-element.16), channel_id=1, source_target_pairs={{0,28},{4,0},{8,4},{12,8},{16,12},{20,16},{24,20},{28,24},{1,29},{... | collective-permute-start | bytes 393224 | tf_op jit(solution)/shard_map/ppermute | solution.py:38
  140.6 10.3 %divergence_modes.1.modes_ref = f32[4,32,64,128]{3,2,1,0:T(8,128)} custom-call(f32[3,32,64,512]{3,2,1,0:T(8,128)} %advance_frame.3.flow_ref, bf16[256,256]{1,0:T(8,128)(2,1)} %constant.68.clone.even_high, bf16[256,256]{1,0:T(8,128)(2,1)} %constant.69.clone.even_low, bf16[256,256]{1,0:T(8,128)(2,1)} %constant.70.clone.odd_high, ...), custom_call_target="tpu_custom_call" | custom-call | tf_op jit(solution)/shard_map/divergence_modes/pallas_call | solution.py:676
  155.5 5.5 %all-to-all-start = ((f32[4,32,64,128]{3,2,1,0:T(8,128)}), f32[4,32,64,128]{3,2,1,0:T(8,128)}, u32[]{:S(2)}, u32[]{:S(2)}) async-start(f32[4,32,64,128]{3,2,1,0:T(8,128)} %add_halo_modes.1), calls=%async_computation | async-start | bytes 8388608 | tf_op jit(solution)/shard_map/all_to_all | solution.py:1075
  162.5 45.8 %scatter_custom_fusion = f32[4096,128]{1,0:T(8,128)} fusion(s32[8192]{0:T(1024)S(1)} %bitcast.41, f32[8192,128]{1,0:T(8,128)} %bitcast.29, f32[]{:T(128)} %constant.26.clone.1), kind=kCustom, calls=%fused_computation.1 | custom fusion | flops 1048576 | bytes 2097664 | tf_op jit(solution)/shard_map/scatter-add | solution.py:1156
  209.9 8.5 %y_forward.1 = (f32[32,256,128]{2,1,0:T(8,128)}, f32[8,4,32,128]{3,2,1,0:T(8,128)}) custom-call(f32[4,32,64,128]{3,2,1,0:T(8,128)} %all-to-all-done.in_ref, bf16[256,256]{1,0:T(8,128)(2,1)} %constant.74.clone.high_ref, bf16[256,256]{1,0:T(8,128)(2,1)} %constant.75.clone.low_ref, f32[256,128]{1,0:T(8,128)} %get-tuple-element.53.ratio_ref), custom_call_target="tpu_custom_call" | custom-call | tf_op jit(solution)/shard_map/y_forward/pallas_call | solution.py:927
  222.7 23.1 %all-to-all-done.1.in_ref = f32[8,4,32,128]{3,2,1,0:T(8,128)S(1)} async-done(((f32[8,4,32,128]{3,2,1,0:T(8,128)}), f32[8,4,32,128]{3,2,1,0:T(8,128)S(1)}, u32[]{:S(2)}, u32[]{:S(2)}) %all-to-all-start.1) | async-done | bytes 524320 | tf_op jit(solution)/shard_map/all_to_all | solution.py:1075
  245.9 17.4 %all_to_all.20.carry_ref = f32[8,4,32,128]{3,2,1,0:T(8,128)} all-to-all(f32[8,4,32,128]{3,2,1,0:T(8,128)S(1)} %join_carries.1), channel_id=1, replica_groups=mesh['wide'=8,'narrow'=4] {'wide'}, dimensions={0} | all-to-all | bytes 1048576 | tf_op jit(solution)/shard_map/all_to_all | solution.py:1075
  263.3 9.7 %y_inverse.1 = f32[4,34,64,128]{3,2,1,0:T(8,128)} custom-call(f32[32,256,128]{2,1,0:T(8,128)} %get-tuple-element.11.modes_in, f32[8,4,32,128]{3,2,1,0:T(8,128)} %all_to_all.20.carry_ref, bf16[256,256]{1,0:T(8,128)(2,1)} %constant.76.clone.high_ref, bf16[256,256]{1,0:T(8,128)(2,1)} %constant.77.clone.low_ref, f32[256,128]{1,0:T(8,128)} %get-tuple-element.53.ratio_ref, ...), custom_call_target="tpu_custom_call" | custom-call | tf_op jit(solution)/shard_map/y_inverse/pallas_call | solution.py:1057
  273.0 6.8 %all-to-all-start.3 = ((f32[4,34,64,128]{3,2,1,0:T(8,128)}), f32[4,34,64,128]{3,2,1,0:T(8,128)}, u32[]{:S(2)}, u32[]{:S(2)}) async-start(f32[4,34,64,128]{3,2,1,0:T(8,128)} %y_inverse.1), calls=%async_computation.3 | async-start | bytes 8912896 | tf_op jit(solution)/shard_map/all_to_all | solution.py:1075
  285.3 4.0 %collective-permute-start.22 = (f32[3,32,128]{2,1,0:T(8,128)S(1)}, f32[3,32,128]{2,1,0:T(8,128)S(1)}, u32[]{:S(2)}, u32[]{:S(2)}) collective-permute-start(f32[3,32,128]{2,1,0:T(8,128)S(1)} %get-tuple-element.50), channel_id=1, source_target_pairs={{0,4},{4,8},{8,12},{12,16},{16,20},{20,24},{24,28},{1,5},{5,9},{9,... | collective-permute-start | bytes 147464 | tf_op jit(solution)/shard_map/ppermute | solution.py:30
  290.7 4.2 %collective-permute-done.23 = f32[3,32,128]{2,1,0:T(8,128)S(1)} collective-permute-done((f32[3,32,128]{2,1,0:T(8,128)S(1)}, f32[3,32,128]{2,1,0:T(8,128)S(1)}, u32[]{:S(2)}, u32[]{:S(2)}) %collective-permute-start.23) | collective-permute-done | bytes 49184 | tf_op jit(solution)/shard_map/ppermute | solution.py:31
  294.9 4.9 %collective-permute-start.24 = (f32[22,3,128]{2,1,0:T(4,128)S(1)}, f32[22,3,128]{2,1,0:T(4,128)S(1)}, u32[]{:S(2)}, u32[]{:S(2)}) collective-permute-start(f32[22,3,128]{2,1,0:T(4,128)S(1)} %get-tuple-element.44), channel_id=1, source_target_pairs={{0,1},{1,2},{2,3},{4,5},{5,6},{6,7},{8,9},{9,10},{10,11},{12,13},{... | collective-permute-start | bytes 101384 | tf_op jit(solution)/shard_map/ppermute | solution.py:30
  307.3 21.5 %collective-permute-done.24 = f32[22,3,128]{2,1,0:T(4,128)S(1)} collective-permute-done((f32[22,3,128]{2,1,0:T(4,128)S(1)}, f32[22,3,128]{2,1,0:T(4,128)S(1)}, u32[]{:S(2)}, u32[]{:S(2)}) %collective-permute-start.24) | collective-permute-done | bytes 33824 | tf_op jit(solution)/shard_map/ppermute | solution.py:30
  337.5 11.0 %corrected.1 = f32[3,32,64,512]{3,2,1,0:T(8,128)} custom-call(f32[3,32,64,512]{3,2,1,0:T(8,128)} %advance_frame.3.flow_ref, f32[4,34,64,128]{3,2,1,0:T(8,128)} %all-to-all-done.3.in_ref, f32[4,32,128]{2,1,0:T(8,128)S(1)} %bitcast.26, f32[4,32,128]{2,1,0:T(8,128)S(1)} %bitcast.27, bf16[256,256]{1,0:T(8,128)(2,1)S(1)} %copy-done, ...), custom_call_target="tpu_custom_call" | custom-call | tf_op jit(solution)/shard_map/corrected/pallas_call | solution.py:855
  (125 shorter events, 67.1 us)
Async XLA Ops:
  8.4 20.0 %collective-permute-start = (f32[3,1,64,512]{3,2,1,0:T(8,128)S(1)}, f32[3,1,64,512]{3,2,1,0:T(8,128)S(1)}, u32[]{:S(2)}, u32[]{:S(2)}) collective-permute-start(f32[3,1,64,512]{3,2,1,0:T(8,128)S(1)} %get-tuple-element.25), channel_id=1, source_target_pairs={{0,4},{4,8},{8,12},{12,16},{16,20},{20,24},{24,28},{28,0},{1,5},{5... | collective-permute-start | bytes 1179656 | tf_op jit(solution)/shard_map/ppermute | solution.py:38
  10.5 18.1 %collective-permute-start.1 = (f32[3,1,64,512]{3,2,1,0:T(8,128)S(1)}, f32[3,1,64,512]{3,2,1,0:T(8,128)S(1)}, u32[]{:S(2)}, u32[]{:S(2)}) collective-permute-start(f32[3,1,64,512]{3,2,1,0:T(8,128)S(1)} %get-tuple-element.24), channel_id=1, source_target_pairs={{0,28},{4,0},{8,4},{12,8},{16,12},{20,16},{24,20},{28,24},{1,29},{... | collective-permute-start | bytes 1179656 | tf_op jit(solution)/shard_map/ppermute | solution.py:38
  37.2 20.9 %collective-permute-start.4 = (f32[1,64,512]{2,1,0:T(8,128)S(1)}, f32[1,64,512]{2,1,0:T(8,128)S(1)}, u32[]{:S(2)}, u32[]{:S(2)}) collective-permute-start(f32[1,64,512]{2,1,0:T(8,128)S(1)} %get-tuple-element.35), channel_id=1, source_target_pairs={{0,4},{4,8},{8,12},{12,16},{16,20},{20,24},{24,28},{28,0},{1,5},{5... | collective-permute-start | bytes 393224 | tf_op jit(solution)/shard_map/ppermute | solution.py:38
  37.6 20.5 %collective-permute-start.5 = (f32[1,64,512]{2,1,0:T(8,128)S(1)}, f32[1,64,512]{2,1,0:T(8,128)S(1)}, u32[]{:S(2)}, u32[]{:S(2)}) collective-permute-start(f32[1,64,512]{2,1,0:T(8,128)S(1)} %get-tuple-element.34), channel_id=1, source_target_pairs={{0,28},{4,0},{8,4},{12,8},{16,12},{20,16},{24,20},{28,24},{1,29},{... | collective-permute-start | bytes 393224 | tf_op jit(solution)/shard_map/ppermute | solution.py:38
  41.6 16.5 %collective-permute-start.6 = (f32[32,1,512]{2,1,0:T(1,128)S(1)}, f32[32,1,512]{2,1,0:T(1,128)S(1)}, u32[]{:S(2)}, u32[]{:S(2)}) collective-permute-start(f32[32,1,512]{2,1,0:T(1,128)S(1)} %get-tuple-element.33), channel_id=1, source_target_pairs={{0,1},{1,2},{2,3},{3,0},{4,5},{5,6},{6,7},{7,4},{8,9},{9,10},{10,1... | collective-permute-start | bytes 196616 | tf_op jit(solution)/shard_map/ppermute | solution.py:38
  45.1 13.0 %collective-permute-start.7 = (f32[32,1,512]{2,1,0:T(1,128)S(1)}, f32[32,1,512]{2,1,0:T(1,128)S(1)}, u32[]{:S(2)}, u32[]{:S(2)}) collective-permute-start(f32[32,1,512]{2,1,0:T(1,128)S(1)} %get-tuple-element.32), channel_id=1, source_target_pairs={{0,3},{1,0},{2,1},{3,2},{4,7},{5,4},{6,5},{7,6},{8,11},{9,8},{10,9... | collective-permute-start | bytes 196616 | tf_op jit(solution)/shard_map/ppermute | solution.py:38
  70.6 20.3 %collective-permute-start.8 = (f32[3,1,64,512]{3,2,1,0:T(8,128)S(1)}, f32[3,1,64,512]{3,2,1,0:T(8,128)S(1)}, u32[]{:S(2)}, u32[]{:S(2)}) collective-permute-start(f32[3,1,64,512]{3,2,1,0:T(8,128)S(1)} %get-tuple-element.21), channel_id=1, source_target_pairs={{0,4},{4,8},{8,12},{12,16},{16,20},{20,24},{24,28},{28,0},{1,5},{5... | collective-permute-start | bytes 1179656 | tf_op jit(solution)/shard_map/ppermute | solution.py:38
  70.7 20.3 %collective-permute-start.9 = (f32[3,1,64,512]{3,2,1,0:T(8,128)S(1)}, f32[3,1,64,512]{3,2,1,0:T(8,128)S(1)}, u32[]{:S(2)}, u32[]{:S(2)}) collective-permute-start(f32[3,1,64,512]{3,2,1,0:T(8,128)S(1)} %get-tuple-element.20), channel_id=1, source_target_pairs={{0,28},{4,0},{8,4},{12,8},{16,12},{20,16},{24,20},{28,24},{1,29},{... | collective-permute-start | bytes 1179656 | tf_op jit(solution)/shard_map/ppermute | solution.py:38
  77.1 13.8 %collective-permute-start.10 = (f32[3,32,1,512]{3,2,1,0:T(1,128)S(1)}, f32[3,32,1,512]{3,2,1,0:T(1,128)S(1)}, u32[]{:S(2)}, u32[]{:S(2)}) collective-permute-start(f32[3,32,1,512]{3,2,1,0:T(1,128)S(1)} %get-tuple-element.19), channel_id=1, source_target_pairs={{0,1},{1,2},{2,3},{3,0},{4,5},{5,6},{6,7},{7,4},{8,9},{9,10},{10,1... | collective-permute-start | bytes 589832 | tf_op jit(solution)/shard_map/ppermute | solution.py:38
  100.7 19.7 %collective-permute-start.12 = (f32[1,64,512]{2,1,0:T(8,128)S(1)}, f32[1,64,512]{2,1,0:T(8,128)S(1)}, u32[]{:S(2)}, u32[]{:S(2)}) collective-permute-start(f32[1,64,512]{2,1,0:T(8,128)S(1)} %get-tuple-element.31), channel_id=1, source_target_pairs={{0,4},{4,8},{8,12},{12,16},{16,20},{20,24},{24,28},{28,0},{1,5},{5... | collective-permute-start | bytes 393224 | tf_op jit(solution)/shard_map/ppermute | solution.py:38
  100.7 19.6 %collective-permute-start.13 = (f32[1,64,512]{2,1,0:T(8,128)S(1)}, f32[1,64,512]{2,1,0:T(8,128)S(1)}, u32[]{:S(2)}, u32[]{:S(2)}) collective-permute-start(f32[1,64,512]{2,1,0:T(8,128)S(1)} %get-tuple-element.30), channel_id=1, source_target_pairs={{0,28},{4,0},{8,4},{12,8},{16,12},{20,16},{24,20},{28,24},{1,29},{... | collective-permute-start | bytes 393224 | tf_op jit(solution)/shard_map/ppermute | solution.py:38
  105.0 15.3 %collective-permute-start.14 = (f32[32,1,512]{2,1,0:T(1,128)S(1)}, f32[32,1,512]{2,1,0:T(1,128)S(1)}, u32[]{:S(2)}, u32[]{:S(2)}) collective-permute-start(f32[32,1,512]{2,1,0:T(1,128)S(1)} %get-tuple-element.29), channel_id=1, source_target_pairs={{0,1},{1,2},{2,3},{3,0},{4,5},{5,6},{6,7},{7,4},{8,9},{9,10},{10,1... | collective-permute-start | bytes 196616 | tf_op jit(solution)/shard_map/ppermute | solution.py:38
  107.3 13.0 %collective-permute-start.15 = (f32[32,1,512]{2,1,0:T(1,128)S(1)}, f32[32,1,512]{2,1,0:T(1,128)S(1)}, u32[]{:S(2)}, u32[]{:S(2)}) collective-permute-start(f32[32,1,512]{2,1,0:T(1,128)S(1)} %get-tuple-element.28), channel_id=1, source_target_pairs={{0,3},{1,0},{2,1},{3,2},{4,7},{5,4},{6,5},{7,6},{8,11},{9,8},{10,9... | collective-permute-start | bytes 196616 | tf_op jit(solution)/shard_map/ppermute | solution.py:38
  132.7 18.3 %collective-permute-start.16 = (f32[1,64,512]{2,1,0:T(8,128)S(1)}, f32[1,64,512]{2,1,0:T(8,128)S(1)}, u32[]{:S(2)}, u32[]{:S(2)}) collective-permute-start(f32[1,64,512]{2,1,0:T(8,128)S(1)} %get-tuple-element.17), channel_id=1, source_target_pairs={{0,4},{4,8},{8,12},{12,16},{16,20},{20,24},{24,28},{28,0},{1,5},{5... | collective-permute-start | bytes 393224 | tf_op jit(solution)/shard_map/ppermute | solution.py:38
  132.7 18.3 %collective-permute-start.17 = (f32[1,64,512]{2,1,0:T(8,128)S(1)}, f32[1,64,512]{2,1,0:T(8,128)S(1)}, u32[]{:S(2)}, u32[]{:S(2)}) collective-permute-start(f32[1,64,512]{2,1,0:T(8,128)S(1)} %get-tuple-element.16), channel_id=1, source_target_pairs={{0,28},{4,0},{8,4},{12,8},{16,12},{20,16},{24,20},{28,24},{1,29},{... | collective-permute-start | bytes 393224 | tf_op jit(solution)/shard_map/ppermute | solution.py:38
  138.2 12.7 %collective-permute-start.18 = (f32[32,1,512]{2,0,1:T(8,128)S(1)}, f32[32,1,512]{2,0,1:T(8,128)S(1)}, u32[]{:S(2)}, u32[]{:S(2)}) collective-permute-start(f32[32,1,512]{2,0,1:T(8,128)S(1)} %bitcast.37), channel_id=1, source_target_pairs={{0,1},{1,2},{2,3},{3,0},{4,5},{5,6},{6,7},{7,4},{8,9},{9,10},{10,1... | collective-permute-start | bytes 196616 | tf_op jit(solution)/shard_map/ppermute | solution.py:38
  155.5 54.4 %all-to-all-start = ((f32[4,32,64,128]{3,2,1,0:T(8,128)}), f32[4,32,64,128]{3,2,1,0:T(8,128)}, u32[]{:S(2)}, u32[]{:S(2)}) async-start(f32[4,32,64,128]{3,2,1,0:T(8,128)} %add_halo_modes.1), calls=%async_computation | async-start | bytes 8388608 | tf_op jit(solution)/shard_map/all_to_all | solution.py:1075
  160.9 123.3 %reduce-scatter.2.cloned.1.call-start = ((), (), s32[]{:S(2)}) async-start(), calls=%async_computation.5 | async-start | bytes 2359296 | tf_op jit(solution)/shard_map/reduce_scatter | solution.py:1158
  218.5 27.4 %all-to-all-start.1 = ((f32[8,4,32,128]{3,2,1,0:T(8,128)}), f32[8,4,32,128]{3,2,1,0:T(8,128)S(1)}, u32[]{:S(2)}, u32[]{:S(2)}) async-start(f32[8,4,32,128]{3,2,1,0:T(8,128)} %get-tuple-element.12), calls=%async_computation.1 | async-start | bytes 1048576 | tf_op jit(solution)/shard_map/all_to_all | solution.py:1075
  273.0 58.7 %all-to-all-start.3 = ((f32[4,34,64,128]{3,2,1,0:T(8,128)}), f32[4,34,64,128]{3,2,1,0:T(8,128)}, u32[]{:S(2)}, u32[]{:S(2)}) async-start(f32[4,34,64,128]{3,2,1,0:T(8,128)} %y_inverse.1), calls=%async_computation.3 | async-start | bytes 8912896 | tf_op jit(solution)/shard_map/all_to_all | solution.py:1075
  294.9 33.9 %collective-permute-start.24 = (f32[22,3,128]{2,1,0:T(4,128)S(1)}, f32[22,3,128]{2,1,0:T(4,128)S(1)}, u32[]{:S(2)}, u32[]{:S(2)}) collective-permute-start(f32[22,3,128]{2,1,0:T(4,128)S(1)} %get-tuple-element.44), channel_id=1, source_target_pairs={{0,1},{1,2},{2,3},{4,5},{5,6},{6,7},{8,9},{9,10},{10,11},{12,13},{... | collective-permute-start | bytes 101384 | tf_op jit(solution)/shard_map/ppermute | solution.py:30
  299.7 30.8 %collective-permute-start.25 = (f32[22,3,128]{2,1,0:T(4,128)S(1)}, f32[22,3,128]{2,1,0:T(4,128)S(1)}, u32[]{:S(2)}, u32[]{:S(2)}) collective-permute-start(f32[22,3,128]{2,1,0:T(4,128)S(1)} %get-tuple-element.45), channel_id=1, source_target_pairs={{1,0},{2,1},{3,2},{5,4},{6,5},{7,6},{9,8},{10,9},{11,10},{13,12},{... | collective-permute-start | bytes 101384 | tf_op jit(solution)/shard_map/ppermute | solution.py:31
  301.7 29.1 %collective-permute-start.28 = (f32[20,2,128]{2,1,0:T(2,128)S(1)}, f32[20,2,128]{2,1,0:T(2,128)S(1)}, u32[]{:S(2)}, u32[]{:S(2)}) collective-permute-start(f32[20,2,128]{2,1,0:T(2,128)S(1)} %get-tuple-element.46), channel_id=1, source_target_pairs={{0,1},{1,2},{2,3},{4,5},{5,6},{6,7},{8,9},{9,10},{10,11},{12,13},{... | collective-permute-start | bytes 61448 | tf_op jit(solution)/shard_map/ppermute | solution.py:30
  305.3 25.5 %collective-permute-start.29 = (f32[20,2,128]{2,1,0:T(2,128)S(1)}, f32[20,2,128]{2,1,0:T(2,128)S(1)}, u32[]{:S(2)}, u32[]{:S(2)}) collective-permute-start(f32[20,2,128]{2,1,0:T(2,128)S(1)} %get-tuple-element.47), channel_id=1, source_target_pairs={{1,0},{2,1},{3,2},{5,4},{6,5},{7,6},{9,8},{10,9},{11,10},{13,12},{... | collective-permute-start | bytes 61448 | tf_op jit(solution)/shard_map/ppermute | solution.py:31
  (23 other events, 180.0 us)
Sparse Core Ops, SparseCore 0:
  208.4 74.4 reduce-scatter.1

commit v8 on v6

--- a/solution.py
+++ b/solution.py
@@ -7,6 +7,7 @@
 from jax.experimental import pallas as pl
 from jax.experimental.pallas import tpu as pltpu
 from jax.sharding import PartitionSpec as P
+
 
 PASSES = 2
 STEPS = 3
@@ -593,10 +594,6 @@
     return even, odd, np.concatenate([eigen_even, eigen_odd])
 
 
-def whole(*shape):
-    return pl.BlockSpec(shape, lambda *index: (0,) * len(shape))
-
-
 def modes_of(lines, even_high, even_low, odd_high, odd_low):
     half = lines.shape[1] // 2
     first, second = lines[:, :half], lines[:, half:]
@@ -618,7 +615,7 @@
 
 def divergence_modes(flow, count):
     _, x_local, y_local, z_cells = flow.shape
-    half, piece, strips = z_cells // 2, z_cells // count, y_local // 8
+    piece, strips = z_cells // count, y_local // 8
     step = min(8, x_local)
     even, odd, _ = z_tables(z_cells)
     tables = halves(even) + halves(odd)
@@ -884,7 +881,7 @@
 
 def y_forward(spectrum, ratio, wide_count):
     count, x_local, y_local, piece = spectrum.shape
-    y_cells, pairs = count * y_local, x_local // 2
+    y_cells = count * y_local
     share, group = y_cells // wide_count, max(2, x_local // 4)
     table, _ = cosine_sine_basis(y_cells, y_cells, range(y_cells // 2 + 1))
     tables = halves(table.T)
@@ -966,7 +963,7 @@
 
 
 def join_carries(carries, ratio, block):
-    count, kinds, share, piece = carries.shape
+    count, kinds, _, _ = carries.shape
 
     def kernel(in_ref, ratio_ref, out_ref):
         step = power_of(ratio_ref[...], block)
@@ -1108,7 +1105,7 @@
     sides = (("wide", 0), ("narrow", 1))
     spread = with_halo(spread, sides, STEPS - 1, False)
     profile = with_halo(profile, sides, STEPS, False)
-    for step in range(STEPS):
+    for _ in range(STEPS):
         center = profile[1:-1, 1:-1]
         near = (
             profile[2:, 1:-1] + profile[:-2, 1:-1] + profile[1:-1, 2:] + profile[1:-1, :-2]
@@ -1120,7 +1117,13 @@
     return profile
 
 
-def per_device(
+def both_rings(value, dim):
+    y_sides = ring(value, "narrow", dim + 1)
+    x_sides = ring(value, "wide", dim)
+    return x_sides, y_sides
+
+
+def device_step(
     material_flow_vector,
     tool_push_density,
     tool_warmth_excess,
@@ -1130,18 +1133,18 @@
     source_part_line,
 ):
     flow = material_flow_vector
-    flow_x, flow_y = ring(flow, "wide", 1), ring(flow, "narrow", 2)
+    flow_x, flow_y = both_rings(flow, 1)
     current, current_x, current_y = flow, flow_x, flow_y
     for section in range(PASSES):
         last = section + 1 == PASSES
         inner = viscosity_inner(current, current_y, tool_warmth_excess, last)
         fields = viscosity_call(current, current_y, tool_warmth_excess, last, current_x, inner)
         mu = fields[0]
-        mu_x, mu_y = ring(mu, "wide", 0), ring(mu, "narrow", 1)
+        mu_x, mu_y = both_rings(mu, 0)
         inner = advance_inner(flow, flow_y, mu, mu_y, tool_push_density)
         current = advance_call(flow, flow_y, mu, mu_y, tool_push_density, flow_x, mu_x, inner)
         if not last:
-            current_x, current_y = ring(current, "wide", 1), ring(current, "narrow", 2)
+            current_x, current_y = both_rings(current, 1)
     heat_cells = fields[1]
     end_x = ring(current[0], "wide", 0)
     y_local = flow.shape[2]
@@ -1178,7 +1181,7 @@
 
 def solution(mesh):
     return jax.shard_map(
-        per_device,
+        device_step,
         mesh=mesh,
         in_specs=(
             P(None, "wide", "narrow", None),

time: 350 us -> 350 us (level)
  no operation moved by 1% of the time
where the time goes in v8:
time: 350 us; the launch traced here: 349 us
  Pallas kernels  113 us (32%)
  waiting for transfers between devices  71.8 us (21%)
  starting transfers between devices  67.6 us (19%)
  other arithmetic  49.2 us (14%)
  blocking collectives  17.3 us (5%)
  local copies, waits for them, and re-layouts  15 us (4%)
  between operations  14.8 us (4%)
    scatter-add x1, other arithmetic, device_step(): partial_value = jnp.zeros((slab_count * component_lines, 128), jnp.float3...  45.8 us
    ppermute x22, starting transfers between devices, shift(): lax.ppermute(value, axis, [(i, (i + by) % size) for i in range(size)])  30.2 us
    pallas_call x2, Pallas kernels, advance_inner(): pl.pallas_call(kernel, in_specs=[anywhere, in_vmem, in_vmem, in_vmem, in_...  30.2 us
    pallas_call x2, Pallas kernels, viscosity_inner(): pl.pallas_call(kernel, in_specs=[anywhere, in_vmem, in_vmem, anywhere], o...  25.7 us
    all_to_all x3, waiting for transfers between devices, turn(): return lax.all_to_all(value, axis, split_axis=0, concat_axis=0, tiled=True)  23.1 us
    ppermute x4, waiting for transfers between devices, with_halo(): before = lax.ppermute(last, axis, up)  21.5 us
    ppermute x22, waiting for transfers between devices, shift(): lax.ppermute(value, axis, [(i, (i + by) % size) for i in range(size)])  21.2 us
    all_to_all x1, blocking collectives, turn(): return lax.all_to_all(value, axis, split_axis=0, concat_axis=0, tiled=True)  17.3 us
  transfers between devices with their start and end apart: 34, of which 14 were waited for; matrix products, arithmetic and copies ran while one was open for 17% of the time, Pallas kernels for 24%

profile of v8, /device:TPU:1, one launch (start us, length us, event | category | flops | bytes accessed | tf_op | source)
XLA Modules:
  0.0 348.9 jit_solution(8991839112723588508)
XLA Ops:
  18.1 4.0 %collective-permute-done.before_ref.refs_1_.flow_before = f32[3,32,1,512]{3,2,1,0:T(1,128)S(1)} collective-permute-done((f32[3,32,1,512]{3,2,1,0:T(1,128)S(1)}, f32[3,32,1,512]{3,2,1,0:T(1,128)S(1)}, u32[]{:S(2)}, u32[]{:S(2)}) %collective-permute-start) | collective-permute-done | bytes 196640 | tf_op jit(solution)/shard_map/ppermute | solution.py:39
  23.7 12.2 %viscosity_inner.2.refs_6_ = f32[32,64,512]{2,1,0:T(8,128)S(1)} custom-call(f32[3,32,64,512]{3,2,1,0:T(8,128)} %refs_0_.5, f32[3,32,1,512]{3,2,1,0:T(1,128)S(1)} %collective-permute-done.before_ref.refs_1_.flow_before, f32[3,32,1,512]{3,2,1,0:T(1,128)S(1)} %collective-permute-done.1.after_ref.refs_2_.flow_after, f32[32,64,512]{2,1,0:T(8,128)} %refs_3_.3), custom_call_target="tpu_custom_call" | custom-call | tf_op jit(solution)/shard_map/viscosity_inner/pallas_call | solution.py:317
  38.6 4.1 %collective-permute-start.7 = (f32[1,64,512]{2,1,0:T(8,128)S(1)}, f32[1,64,512]{2,1,0:T(8,128)S(1)}, u32[]{:S(2)}, u32[]{:S(2)}) collective-permute-start(f32[1,64,512]{2,1,0:T(8,128)S(1)} %get-tuple-element.32), channel_id=1, source_target_pairs={{0,28},{4,0},{8,4},{12,8},{16,12},{20,16},{24,20},{28,24},{1,29},{... | collective-permute-start | bytes 393224 | tf_op jit(solution)/shard_map/ppermute | solution.py:39
  48.0 15.1 %advance_inner.2.refs_11_ = f32[3,32,64,512]{3,2,1,0:T(8,128)} custom-call(f32[3,32,64,512]{3,2,1,0:T(8,128)} %refs_0_.5, f32[3,32,1,512]{3,2,1,0:T(1,128)S(1)} %collective-permute-done.before_ref.refs_1_.flow_before, f32[3,32,1,512]{3,2,1,0:T(1,128)S(1)} %collective-permute-done.1.after_ref.refs_2_.flow_after, ...), custom_call_target="tpu_custom_call" | custom-call | tf_op jit(solution)/shard_map/advance_inner/pallas_call | solution.py:537
  68.3 4.1 %collective-permute-start.11 = (f32[3,1,64,512]{3,2,1,0:T(8,128)S(1)}, f32[3,1,64,512]{3,2,1,0:T(8,128)S(1)}, u32[]{:S(2)}, u32[]{:S(2)}) collective-permute-start(f32[3,1,64,512]{3,2,1,0:T(8,128)S(1)} %get-tuple-element.18), channel_id=1, source_target_pairs={{0,28},{4,0},{8,4},{12,8},{16,12},{20,16},{24,20},{28,24},{1,29},{... | collective-permute-start | bytes 1179656 | tf_op jit(solution)/shard_map/ppermute | solution.py:39
  75.5 4.3 %collective-permute-done.8.before_ref.refs_1_ = f32[3,32,1,512]{3,2,1,0:T(1,128)S(1)} collective-permute-done((f32[3,32,1,512]{3,2,1,0:T(1,128)S(1)}, f32[3,32,1,512]{3,2,1,0:T(1,128)S(1)}, u32[]{:S(2)}, u32[]{:S(2)}) %collective-permute-start.8) | collective-permute-done | bytes 196640 | tf_op jit(solution)/shard_map/ppermute | solution.py:39
  80.9 13.5 %viscosity_inner.3 = (f32[32,64,512]{2,1,0:T(8,128)S(1)}, f32[4,32,64,128]{3,2,1,0:T(8,128)}) custom-call(f32[3,32,64,512]{3,2,1,0:T(8,128)} %advance_edge.2.flow_ref.refs_0_, f32[3,32,1,512]{3,2,1,0:T(1,128)S(1)} %collective-permute-done.8.before_ref.refs_1_, f32[3,32,1,512]{3,2,1,0:T(1,128)S(1)} %collective-permute-done.9.after_ref.refs_2_, ...), custom_call_target="tpu_custom_call" | custom-call | tf_op jit(solution)/shard_map/viscosity_inner/pallas_call | solution.py:317
  97.8 4.1 %collective-permute-start.15 = (f32[1,64,512]{2,1,0:T(8,128)S(1)}, f32[1,64,512]{2,1,0:T(8,128)S(1)}, u32[]{:S(2)}, u32[]{:S(2)}) collective-permute-start(f32[1,64,512]{2,1,0:T(8,128)S(1)} %get-tuple-element.28), channel_id=1, source_target_pairs={{0,28},{4,0},{8,4},{12,8},{16,12},{20,16},{24,20},{28,24},{1,29},{... | collective-permute-start | bytes 393224 | tf_op jit(solution)/shard_map/ppermute | solution.py:39
  107.8 15.1 %advance_inner.3.refs_11_ = f32[3,32,64,512]{3,2,1,0:T(8,128)} custom-call(f32[3,32,64,512]{3,2,1,0:T(8,128)} %refs_0_.5, f32[3,32,1,512]{3,2,1,0:T(1,128)S(1)} %collective-permute-done.before_ref.refs_1_.flow_before, f32[3,32,1,512]{3,2,1,0:T(1,128)S(1)} %collective-permute-done.1.after_ref.refs_2_.flow_after, ...), custom_call_target="tpu_custom_call" | custom-call | tf_op jit(solution)/shard_map/advance_inner/pallas_call | solution.py:537
  122.9 4.0 %advance_edge.3.flow_ref = f32[3,32,64,512]{3,2,1,0:T(8,128)} custom-call(f32[3,32,64,512]{3,2,1,0:T(8,128)} %refs_0_.5, f32[3,32,1,512]{3,2,1,0:T(1,128)S(1)} %collective-permute-done.before_ref.refs_1_.flow_before, f32[3,32,1,512]{3,2,1,0:T(1,128)S(1)} %collective-permute-done.1.after_ref.refs_2_.flow_after, ...), custom_call_target="tpu_custom_call", output_to_operand_aliasing={{}: (11, {})} | custom-call | tf_op jit(solution)/shard_map/advance_edge/pallas_call | solution.py:479
  127.9 4.1 %collective-permute-start.17 = (f32[1,64,512]{2,1,0:T(8,128)S(1)}, f32[1,64,512]{2,1,0:T(8,128)S(1)}, u32[]{:S(2)}, u32[]{:S(2)}) collective-permute-start(f32[1,64,512]{2,1,0:T(8,128)S(1)} %get-tuple-element.16), channel_id=1, source_target_pairs={{0,28},{4,0},{8,4},{12,8},{16,12},{20,16},{24,20},{28,24},{1,29},{... | collective-permute-start | bytes 393224 | tf_op jit(solution)/shard_map/ppermute | solution.py:39
  134.5 10.3 %divergence_modes.1.modes_ref = f32[4,32,64,128]{3,2,1,0:T(8,128)} custom-call(f32[3,32,64,512]{3,2,1,0:T(8,128)} %advance_edge.3.flow_ref, bf16[256,256]{1,0:T(8,128)(2,1)} %constant.68.clone.even_high, bf16[256,256]{1,0:T(8,128)(2,1)} %constant.69.clone.even_low, bf16[256,256]{1,0:T(8,128)(2,1)} %constant.70.clone.odd_high, ...), custom_call_target="tpu_custom_call" | custom-call | tf_op jit(solution)/shard_map/divergence_modes/pallas_call | solution.py:684
  149.4 4.9 %all-to-all-start = ((f32[4,32,64,128]{3,2,1,0:T(8,128)}), f32[4,32,64,128]{3,2,1,0:T(8,128)}, u32[]{:S(2)}, u32[]{:S(2)}) async-start(f32[4,32,64,128]{3,2,1,0:T(8,128)} %add_halo_modes.1), calls=%async_computation | async-start | bytes 8388608 | tf_op jit(solution)/shard_map/all_to_all | solution.py:1083
  156.1 45.8 %scatter_custom_fusion = f32[4096,128]{1,0:T(8,128)} fusion(s32[8192]{0:T(1024)S(1)} %bitcast.41, f32[8192,128]{1,0:T(8,128)} %bitcast.29, f32[]{:T(128)} %constant.26.clone.1), kind=kCustom, calls=%fused_computation.1 | custom fusion | flops 1048576 | bytes 2097664 | tf_op jit(solution)/shard_map/scatter-add | solution.py:1168
  203.5 8.5 %y_forward.1 = (f32[32,256,128]{2,1,0:T(8,128)}, f32[8,4,32,128]{3,2,1,0:T(8,128)}) custom-call(f32[4,32,64,128]{3,2,1,0:T(8,128)} %all-to-all-done.in_ref, bf16[256,256]{1,0:T(8,128)(2,1)} %constant.74.clone.high_ref, bf16[256,256]{1,0:T(8,128)(2,1)} %constant.75.clone.low_ref, f32[256,128]{1,0:T(8,128)} %get-tuple-element.53.ratio_ref), custom_call_target="tpu_custom_call" | custom-call | tf_op jit(solution)/shard_map/y_forward/pallas_call | solution.py:935
  216.2 23.1 %all-to-all-done.1.in_ref = f32[8,4,32,128]{3,2,1,0:T(8,128)S(1)} async-done(((f32[8,4,32,128]{3,2,1,0:T(8,128)}), f32[8,4,32,128]{3,2,1,0:T(8,128)S(1)}, u32[]{:S(2)}, u32[]{:S(2)}) %all-to-all-start.1) | async-done | bytes 524320 | tf_op jit(solution)/shard_map/all_to_all | solution.py:1083
  239.5 17.3 %all_to_all.20.carry_ref = f32[8,4,32,128]{3,2,1,0:T(8,128)} all-to-all(f32[8,4,32,128]{3,2,1,0:T(8,128)S(1)} %join_carries.1), channel_id=1, replica_groups=mesh['wide'=8,'narrow'=4] {'wide'}, dimensions={0} | all-to-all | bytes 1048576 | tf_op jit(solution)/shard_map/all_to_all | solution.py:1083
  256.8 9.7 %y_inverse.1 = f32[4,34,64,128]{3,2,1,0:T(8,128)} custom-call(f32[32,256,128]{2,1,0:T(8,128)} %get-tuple-element.11.modes_in, f32[8,4,32,128]{3,2,1,0:T(8,128)} %all_to_all.20.carry_ref, bf16[256,256]{1,0:T(8,128)(2,1)} %constant.76.clone.high_ref, bf16[256,256]{1,0:T(8,128)(2,1)} %constant.77.clone.low_ref, f32[256,128]{1,0:T(8,128)} %get-tuple-element.53.ratio_ref, ...), custom_call_target="tpu_custom_call" | custom-call | tf_op jit(solution)/shard_map/y_inverse/pallas_call | solution.py:1065
  266.5 6.8 %all-to-all-start.3 = ((f32[4,34,64,128]{3,2,1,0:T(8,128)}), f32[4,34,64,128]{3,2,1,0:T(8,128)}, u32[]{:S(2)}, u32[]{:S(2)}) async-start(f32[4,34,64,128]{3,2,1,0:T(8,128)} %y_inverse.1), calls=%async_computation.3 | async-start | bytes 8912896 | tf_op jit(solution)/shard_map/all_to_all | solution.py:1083
  278.8 4.0 %collective-permute-start.22 = (f32[3,32,128]{2,1,0:T(8,128)S(1)}, f32[3,32,128]{2,1,0:T(8,128)S(1)}, u32[]{:S(2)}, u32[]{:S(2)}) collective-permute-start(f32[3,32,128]{2,1,0:T(8,128)S(1)} %get-tuple-element.50), channel_id=1, source_target_pairs={{0,4},{4,8},{8,12},{12,16},{16,20},{20,24},{24,28},{1,5},{5,9},{9,... | collective-permute-start | bytes 147464 | tf_op jit(solution)/shard_map/ppermute | solution.py:31
  284.2 4.2 %collective-permute-done.23 = f32[3,32,128]{2,1,0:T(8,128)S(1)} collective-permute-done((f32[3,32,128]{2,1,0:T(8,128)S(1)}, f32[3,32,128]{2,1,0:T(8,128)S(1)}, u32[]{:S(2)}, u32[]{:S(2)}) %collective-permute-start.23) | collective-permute-done | bytes 49184 | tf_op jit(solution)/shard_map/ppermute | solution.py:32
  288.4 4.9 %collective-permute-start.24 = (f32[22,3,128]{2,1,0:T(4,128)S(1)}, f32[22,3,128]{2,1,0:T(4,128)S(1)}, u32[]{:S(2)}, u32[]{:S(2)}) collective-permute-start(f32[22,3,128]{2,1,0:T(4,128)S(1)} %get-tuple-element.44), channel_id=1, source_target_pairs={{0,1},{1,2},{2,3},{4,5},{5,6},{6,7},{8,9},{9,10},{10,11},{12,13},{... | collective-permute-start | bytes 101384 | tf_op jit(solution)/shard_map/ppermute | solution.py:31
  300.8 21.5 %collective-permute-done.24 = f32[22,3,128]{2,1,0:T(4,128)S(1)} collective-permute-done((f32[22,3,128]{2,1,0:T(4,128)S(1)}, f32[22,3,128]{2,1,0:T(4,128)S(1)}, u32[]{:S(2)}, u32[]{:S(2)}) %collective-permute-start.24) | collective-permute-done | bytes 33824 | tf_op jit(solution)/shard_map/ppermute | solution.py:31
  331.0 11.0 %corrected.1 = f32[3,32,64,512]{3,2,1,0:T(8,128)} custom-call(f32[3,32,64,512]{3,2,1,0:T(8,128)} %advance_edge.3.flow_ref, f32[4,34,64,128]{3,2,1,0:T(8,128)} %all-to-all-done.3.in_ref, f32[4,32,128]{2,1,0:T(8,128)S(1)} %bitcast.26, f32[4,32,128]{2,1,0:T(8,128)S(1)} %bitcast.27, bf16[256,256]{1,0:T(8,128)(2,1)S(1)} %copy-done, ...), custom_call_target="tpu_custom_call" | custom-call | tf_op jit(solution)/shard_map/corrected/pallas_call | solution.py:863
  (125 shorter events, 77.5 us)
Async XLA Ops:
  8.4 27.5 %collective-permute-start.2 = (f32[3,1,64,512]{3,2,1,0:T(8,128)S(1)}, f32[3,1,64,512]{3,2,1,0:T(8,128)S(1)}, u32[]{:S(2)}, u32[]{:S(2)}) collective-permute-start(f32[3,1,64,512]{3,2,1,0:T(8,128)S(1)} %get-tuple-element.23), channel_id=1, source_target_pairs={{0,4},{4,8},{8,12},{12,16},{16,20},{20,24},{24,28},{28,0},{1,5},{5... | collective-permute-start | bytes 1179656 | tf_op jit(solution)/shard_map/ppermute | solution.py:39
  10.5 25.4 %collective-permute-start.3 = (f32[3,1,64,512]{3,2,1,0:T(8,128)S(1)}, f32[3,1,64,512]{3,2,1,0:T(8,128)S(1)}, u32[]{:S(2)}, u32[]{:S(2)}) collective-permute-start(f32[3,1,64,512]{3,2,1,0:T(8,128)S(1)} %get-tuple-element.22), channel_id=1, source_target_pairs={{0,28},{4,0},{8,4},{12,8},{16,12},{20,16},{24,20},{28,24},{1,29},{... | collective-permute-start | bytes 1179656 | tf_op jit(solution)/shard_map/ppermute | solution.py:39
  15.9 6.2 %collective-permute-start = (f32[3,32,1,512]{3,2,1,0:T(1,128)S(1)}, f32[3,32,1,512]{3,2,1,0:T(1,128)S(1)}, u32[]{:S(2)}, u32[]{:S(2)}) collective-permute-start(f32[3,32,1,512]{3,2,1,0:T(1,128)S(1)} %get-tuple-element.25), channel_id=1, source_target_pairs={{0,1},{1,2},{2,3},{3,0},{4,5},{5,6},{6,7},{7,4},{8,9},{9,10},{10,1... | collective-permute-start | bytes 589832 | tf_op jit(solution)/shard_map/ppermute | solution.py:39
  18.1 5.6 %collective-permute-start.1 = (f32[3,32,1,512]{3,2,1,0:T(1,128)S(1)}, f32[3,32,1,512]{3,2,1,0:T(1,128)S(1)}, u32[]{:S(2)}, u32[]{:S(2)}) collective-permute-start(f32[3,32,1,512]{3,2,1,0:T(1,128)S(1)} %get-tuple-element.24), channel_id=1, source_target_pairs={{0,3},{1,0},{2,1},{3,2},{4,7},{5,4},{6,5},{7,6},{8,11},{9,8},{10,9... | collective-permute-start | bytes 589832 | tf_op jit(solution)/shard_map/ppermute | solution.py:39
  38.5 24.6 %collective-permute-start.6 = (f32[1,64,512]{2,1,0:T(8,128)S(1)}, f32[1,64,512]{2,1,0:T(8,128)S(1)}, u32[]{:S(2)}, u32[]{:S(2)}) collective-permute-start(f32[1,64,512]{2,1,0:T(8,128)S(1)} %get-tuple-element.33), channel_id=1, source_target_pairs={{0,4},{4,8},{8,12},{12,16},{16,20},{20,24},{24,28},{28,0},{1,5},{5... | collective-permute-start | bytes 393224 | tf_op jit(solution)/shard_map/ppermute | solution.py:39
  38.6 24.5 %collective-permute-start.7 = (f32[1,64,512]{2,1,0:T(8,128)S(1)}, f32[1,64,512]{2,1,0:T(8,128)S(1)}, u32[]{:S(2)}, u32[]{:S(2)}) collective-permute-start(f32[1,64,512]{2,1,0:T(8,128)S(1)} %get-tuple-element.32), channel_id=1, source_target_pairs={{0,28},{4,0},{8,4},{12,8},{16,12},{20,16},{24,20},{28,24},{1,29},{... | collective-permute-start | bytes 393224 | tf_op jit(solution)/shard_map/ppermute | solution.py:39
  68.3 26.2 %collective-permute-start.10 = (f32[3,1,64,512]{3,2,1,0:T(8,128)S(1)}, f32[3,1,64,512]{3,2,1,0:T(8,128)S(1)}, u32[]{:S(2)}, u32[]{:S(2)}) collective-permute-start(f32[3,1,64,512]{3,2,1,0:T(8,128)S(1)} %get-tuple-element.19), channel_id=1, source_target_pairs={{0,4},{4,8},{8,12},{12,16},{16,20},{20,24},{24,28},{28,0},{1,5},{5... | collective-permute-start | bytes 1179656 | tf_op jit(solution)/shard_map/ppermute | solution.py:39
  68.3 26.1 %collective-permute-start.11 = (f32[3,1,64,512]{3,2,1,0:T(8,128)S(1)}, f32[3,1,64,512]{3,2,1,0:T(8,128)S(1)}, u32[]{:S(2)}, u32[]{:S(2)}) collective-permute-start(f32[3,1,64,512]{3,2,1,0:T(8,128)S(1)} %get-tuple-element.18), channel_id=1, source_target_pairs={{0,28},{4,0},{8,4},{12,8},{16,12},{20,16},{24,20},{28,24},{1,29},{... | collective-permute-start | bytes 1179656 | tf_op jit(solution)/shard_map/ppermute | solution.py:39
  97.8 25.1 %collective-permute-start.14 = (f32[1,64,512]{2,1,0:T(8,128)S(1)}, f32[1,64,512]{2,1,0:T(8,128)S(1)}, u32[]{:S(2)}, u32[]{:S(2)}) collective-permute-start(f32[1,64,512]{2,1,0:T(8,128)S(1)} %get-tuple-element.29), channel_id=1, source_target_pairs={{0,4},{4,8},{8,12},{12,16},{16,20},{20,24},{24,28},{28,0},{1,5},{5... | collective-permute-start | bytes 393224 | tf_op jit(solution)/shard_map/ppermute | solution.py:39
  97.8 25.1 %collective-permute-start.15 = (f32[1,64,512]{2,1,0:T(8,128)S(1)}, f32[1,64,512]{2,1,0:T(8,128)S(1)}, u32[]{:S(2)}, u32[]{:S(2)}) collective-permute-start(f32[1,64,512]{2,1,0:T(8,128)S(1)} %get-tuple-element.28), channel_id=1, source_target_pairs={{0,28},{4,0},{8,4},{12,8},{16,12},{20,16},{24,20},{28,24},{1,29},{... | collective-permute-start | bytes 393224 | tf_op jit(solution)/shard_map/ppermute | solution.py:39
  127.9 17.0 %collective-permute-start.16 = (f32[1,64,512]{2,1,0:T(8,128)S(1)}, f32[1,64,512]{2,1,0:T(8,128)S(1)}, u32[]{:S(2)}, u32[]{:S(2)}) collective-permute-start(f32[1,64,512]{2,1,0:T(8,128)S(1)} %get-tuple-element.17), channel_id=1, source_target_pairs={{0,4},{4,8},{8,12},{12,16},{16,20},{20,24},{24,28},{28,0},{1,5},{5... | collective-permute-start | bytes 393224 | tf_op jit(solution)/shard_map/ppermute | solution.py:39
  127.9 16.9 %collective-permute-start.17 = (f32[1,64,512]{2,1,0:T(8,128)S(1)}, f32[1,64,512]{2,1,0:T(8,128)S(1)}, u32[]{:S(2)}, u32[]{:S(2)}) collective-permute-start(f32[1,64,512]{2,1,0:T(8,128)S(1)} %get-tuple-element.16), channel_id=1, source_target_pairs={{0,28},{4,0},{8,4},{12,8},{16,12},{20,16},{24,20},{28,24},{1,29},{... | collective-permute-start | bytes 393224 | tf_op jit(solution)/shard_map/ppermute | solution.py:39
  133.4 11.4 %collective-permute-start.18 = (f32[32,1,512]{2,0,1:T(8,128)S(1)}, f32[32,1,512]{2,0,1:T(8,128)S(1)}, u32[]{:S(2)}, u32[]{:S(2)}) collective-permute-start(f32[32,1,512]{2,0,1:T(8,128)S(1)} %bitcast.37), channel_id=1, source_target_pairs={{0,1},{1,2},{2,3},{3,0},{4,5},{5,6},{6,7},{7,4},{8,9},{9,10},{10,1... | collective-permute-start | bytes 196616 | tf_op jit(solution)/shard_map/ppermute | solution.py:39
  134.5 10.4 %collective-permute-start.19 = (f32[32,1,512]{2,0,1:T(8,128)S(1)}, f32[32,1,512]{2,0,1:T(8,128)S(1)}, u32[]{:S(2)}, u32[]{:S(2)}) collective-permute-start(f32[32,1,512]{2,0,1:T(8,128)S(1)} %bitcast.38), channel_id=1, source_target_pairs={{0,3},{1,0},{2,1},{3,2},{4,7},{5,4},{6,5},{7,6},{8,11},{9,8},{10,9... | collective-permute-start | bytes 196616 | tf_op jit(solution)/shard_map/ppermute | solution.py:39
  149.4 54.1 %all-to-all-start = ((f32[4,32,64,128]{3,2,1,0:T(8,128)}), f32[4,32,64,128]{3,2,1,0:T(8,128)}, u32[]{:S(2)}, u32[]{:S(2)}) async-start(f32[4,32,64,128]{3,2,1,0:T(8,128)} %add_halo_modes.1), calls=%async_computation | async-start | bytes 8388608 | tf_op jit(solution)/shard_map/all_to_all | solution.py:1083
  154.3 123.5 %reduce-scatter.2.cloned.1.call-start = ((), (), s32[]{:S(2)}) async-start(), calls=%async_computation.5 | async-start | bytes 2359296 | tf_op jit(solution)/shard_map/reduce_scatter | solution.py:1170
  212.0 27.4 %all-to-all-start.1 = ((f32[8,4,32,128]{3,2,1,0:T(8,128)}), f32[8,4,32,128]{3,2,1,0:T(8,128)S(1)}, u32[]{:S(2)}, u32[]{:S(2)}) async-start(f32[8,4,32,128]{3,2,1,0:T(8,128)} %get-tuple-element.12), calls=%async_computation.1 | async-start | bytes 1048576 | tf_op jit(solution)/shard_map/all_to_all | solution.py:1083
  266.5 58.7 %all-to-all-start.3 = ((f32[4,34,64,128]{3,2,1,0:T(8,128)}), f32[4,34,64,128]{3,2,1,0:T(8,128)}, u32[]{:S(2)}, u32[]{:S(2)}) async-start(f32[4,34,64,128]{3,2,1,0:T(8,128)} %y_inverse.1), calls=%async_computation.3 | async-start | bytes 8912896 | tf_op jit(solution)/shard_map/all_to_all | solution.py:1083
  276.4 7.7 %collective-permute-start.27 = (f32[2,32,128]{2,1,0:T(8,128)S(1)}, f32[2,32,128]{2,1,0:T(8,128)S(1)}, u32[]{:S(2)}, u32[]{:S(2)}) collective-permute-start(f32[2,32,128]{2,1,0:T(8,128)S(1)} %get-tuple-element.48), channel_id=1, source_target_pairs={{4,0},{8,4},{12,8},{16,12},{20,16},{24,20},{28,24},{5,1},{9,5},{13... | collective-permute-start | bytes 98312 | tf_op jit(solution)/shard_map/ppermute | solution.py:32
  282.8 5.5 %collective-permute-start.23 = (f32[3,32,128]{2,1,0:T(8,128)S(1)}, f32[3,32,128]{2,1,0:T(8,128)S(1)}, u32[]{:S(2)}, u32[]{:S(2)}) collective-permute-start(f32[3,32,128]{2,1,0:T(8,128)S(1)} %get-tuple-element.51), channel_id=1, source_target_pairs={{4,0},{8,4},{12,8},{16,12},{20,16},{24,20},{28,24},{5,1},{9,5},{13... | collective-permute-start | bytes 147464 | tf_op jit(solution)/shard_map/ppermute | solution.py:32
  288.4 33.9 %collective-permute-start.24 = (f32[22,3,128]{2,1,0:T(4,128)S(1)}, f32[22,3,128]{2,1,0:T(4,128)S(1)}, u32[]{:S(2)}, u32[]{:S(2)}) collective-permute-start(f32[22,3,128]{2,1,0:T(4,128)S(1)} %get-tuple-element.44), channel_id=1, source_target_pairs={{0,1},{1,2},{2,3},{4,5},{5,6},{6,7},{8,9},{9,10},{10,11},{12,13},{... | collective-permute-start | bytes 101384 | tf_op jit(solution)/shard_map/ppermute | solution.py:31
  293.2 30.8 %collective-permute-start.25 = (f32[22,3,128]{2,1,0:T(4,128)S(1)}, f32[22,3,128]{2,1,0:T(4,128)S(1)}, u32[]{:S(2)}, u32[]{:S(2)}) collective-permute-start(f32[22,3,128]{2,1,0:T(4,128)S(1)} %get-tuple-element.45), channel_id=1, source_target_pairs={{1,0},{2,1},{3,2},{5,4},{6,5},{7,6},{9,8},{10,9},{11,10},{13,12},{... | collective-permute-start | bytes 101384 | tf_op jit(solution)/shard_map/ppermute | solution.py:32
  295.2 29.1 %collective-permute-start.28 = (f32[20,2,128]{2,1,0:T(2,128)S(1)}, f32[20,2,128]{2,1,0:T(2,128)S(1)}, u32[]{:S(2)}, u32[]{:S(2)}) collective-permute-start(f32[20,2,128]{2,1,0:T(2,128)S(1)} %get-tuple-element.46), channel_id=1, source_target_pairs={{0,1},{1,2},{2,3},{4,5},{5,6},{6,7},{8,9},{9,10},{10,11},{12,13},{... | collective-permute-start | bytes 61448 | tf_op jit(solution)/shard_map/ppermute | solution.py:31
  298.8 25.5 %collective-permute-start.29 = (f32[20,2,128]{2,1,0:T(2,128)S(1)}, f32[20,2,128]{2,1,0:T(2,128)S(1)}, u32[]{:S(2)}, u32[]{:S(2)}) collective-permute-start(f32[20,2,128]{2,1,0:T(2,128)S(1)} %get-tuple-element.47), channel_id=1, source_target_pairs={{1,0},{2,1},{3,2},{5,4},{6,5},{7,6},{9,8},{10,9},{11,10},{13,12},{... | collective-permute-start | bytes 61448 | tf_op jit(solution)/shard_map/ppermute | solution.py:32
  (23 other events, 145.8 us)
Sparse Core Ops, SparseCore 0:
  202.0 74.5 reduce-scatter.1

commit v9 on v8

--- a/solution.py
+++ b/solution.py
@@ -1083,7 +1083,7 @@
     return lax.all_to_all(value, axis, split_axis=0, concat_axis=0, tiled=True)
 
 
-def project(spectrum):
+def project(spectrum, late):
     count, x_local, y_local, piece = spectrum.shape
     y_cells, z_cells = count * y_local, count * piece
     wide_count = lax.axis_size("wide")
@@ -1096,9 +1096,11 @@
     gain = -4.0 / root
     share = y_cells // wide_count
     own_ratio = lax.dynamic_slice_in_dim(ratio, lax.axis_index("wide") * share, share)
-    modes, carries = y_forward(turn(spectrum, "narrow"), ratio, wide_count)
-    carries = turn(join_carries(turn(carries, "wide"), own_ratio, x_local // 2), "wide")
-    return turn(y_inverse(modes, carries, ratio, gain, count), "narrow")
+    spectrum = turn(spectrum, "narrow")
+    modes, carries = y_forward(spectrum, ratio, wide_count)
+    carries, late = lax.optimization_barrier((turn(carries, "wide"), late))
+    carries = turn(join_carries(carries, own_ratio, x_local // 2), "wide")
+    return turn(y_inverse(modes, carries, ratio, gain, count), "narrow"), late
 
 
 def conduct(profile, spread):
@@ -1153,11 +1155,6 @@
         shift(current[1, :, :1], "narrow", -1)[:, 0],
     ]
     modes = divergence_modes(current, lax.axis_size("narrow"))
-    spectrum = project(add_halo_modes(modes, end_x, end_y))
-    inner = spectrum[:, 1:-1]
-    corrected_flow_vector = corrected(
-        current, spectrum, [side[:, :, 0] for side in ring(inner, "narrow", 2)]
-    )
     z_blocks = heat_cells.shape[0]
     slab_count = lax.axis_size("wide")
     component_lines = substrate_warmth_excess.shape[0] * substrate_warmth_excess.shape[1]
@@ -1166,6 +1163,11 @@
         jnp.zeros((slab_count * component_lines, 128), jnp.float32)
         .at[targets.reshape(-1, z_blocks).T.reshape(-1)]
         .add(heat_cells.reshape(-1, 128))
+    )
+    spectrum, partial_value = project(add_halo_modes(modes, end_x, end_y), partial_value)
+    inner = spectrum[:, 1:-1]
+    corrected_flow_vector = corrected(
+        current, spectrum, [side[:, :, 0] for side in ring(inner, "narrow", 2)]
     )
     substrate_energy_input = lax.psum_scatter(
         partial_value.reshape(slab_count, component_lines, 128),

time: 350 us -> 386 us (1.10)
  waiting for transfers between devices: 71.8 us -> 89.1 us
  starting transfers between devices: 67.6 us -> 78.9 us
  blocking collectives: 17.3 us -> 24.5 us
    all_to_all x3, waiting for transfers between devices: 23.1 us -> 49.5 us  [turn(): return lax.all_to_all(value, axis, split_axis=0, concat_axis=0, tiled=True)]
    ppermute x4, waiting for transfers between devices: 21.5 us -> 0.01 us  [with_halo(): before = lax.ppermute(last, axis, up)]
    reduce_scatter x1, waiting for transfers between devices: 0.02 us -> 18.9 us  [device_step(): lax.psum_scatter(partial_value.reshape(slab_count, component_lines, 128),...]
    all_to_all x3, starting transfers between devices: 15.1 us -> 23.9 us  [turn(): return lax.all_to_all(value, axis, split_axis=0, concat_axis=0, tiled=True)]
    all_to_all x1, blocking collectives: 17.3 us -> 24.5 us  [turn(): return lax.all_to_all(value, axis, split_axis=0, concat_axis=0, tiled=True)]
    ppermute x22, waiting for transfers between devices: 21.2 us -> 17 us  [shift(): lax.ppermute(value, axis, [(i, (i + by) % size) for i in range(size)])]
  transfers between devices with their start and end apart: 34 -> 34, of which waited for: 14 -> 9; matrix products, arithmetic and copies ran while one was open for 17% -> 16% of each run, Pallas kernels for 24% -> 20%
where the time goes in v9:
time: 386 us; the launch traced here: 385 us
  Pallas kernels  113 us (29%)
  waiting for transfers between devices  89.1 us (23%)
  starting transfers between devices  78.9 us (20%)
  other arithmetic  49.2 us (13%)
  blocking collectives  24.5 us (6%)
  local copies, waits for them, and re-layouts  15 us (4%)
  between operations  14.7 us (4%)
    all_to_all x3, waiting for transfers between devices, turn(): return lax.all_to_all(value, axis, split_axis=0, concat_axis=0, tiled=True)  49.5 us
    scatter-add x1, other arithmetic, device_step(): partial_value = jnp.zeros((slab_count * component_lines, 128), jnp.float3...  45.7 us
    ppermute x22, starting transfers between devices, shift(): lax.ppermute(value, axis, [(i, (i + by) % size) for i in range(size)])  33.9 us
    pallas_call x2, Pallas kernels, advance_inner(): pl.pallas_call(kernel, in_specs=[anywhere, in_vmem, in_vmem, in_vmem, in_...  30.2 us
    pallas_call x2, Pallas kernels, viscosity_inner(): pl.pallas_call(kernel, in_specs=[anywhere, in_vmem, in_vmem, anywhere], o...  25.7 us
    all_to_all x1, blocking collectives, turn(): return lax.all_to_all(value, axis, split_axis=0, concat_axis=0, tiled=True)  24.5 us
    all_to_all x3, starting transfers between devices, turn(): return lax.all_to_all(value, axis, split_axis=0, concat_axis=0, tiled=True)  23.9 us
    reduce_scatter x1, waiting for transfers between devices, device_step(): lax.psum_scatter(partial_value.reshape(slab_count, component_lines, 128),...  18.9 us
  transfers between devices with their start and end apart: 34, of which 9 were waited for; matrix products, arithmetic and copies ran while one was open for 16% of the time, Pallas kernels for 20%

profile of v9, /device:TPU:1, one launch (start us, length us, event | category | flops | bytes accessed | tf_op | source)
XLA Modules:
  0.0 384.6 jit_solution(16480686524876937176)
XLA Ops:
  8.4 5.1 %collective-permute-start.3 = (f32[3,1,64,512]{3,2,1,0:T(8,128)S(1)}, f32[3,1,64,512]{3,2,1,0:T(8,128)S(1)}, u32[]{:S(2)}, u32[]{:S(2)}) collective-permute-start(f32[3,1,64,512]{3,2,1,0:T(8,128)S(1)} %get-tuple-element.26), channel_id=1, source_target_pairs={{0,28},{4,0},{8,4},{12,8},{16,12},{20,16},{24,20},{28,24},{1,29},{... | collective-permute-start | bytes 1179656 | tf_op jit(solution)/shard_map/ppermute | solution.py:39
  18.0 5.1 %collective-permute-done.1.after_ref.refs_2_.flow_after = f32[3,32,1,512]{3,2,1,0:T(1,128)S(1)} collective-permute-done((f32[3,32,1,512]{3,2,1,0:T(1,128)S(1)}, f32[3,32,1,512]{3,2,1,0:T(1,128)S(1)}, u32[]{:S(2)}, u32[]{:S(2)}) %collective-permute-start.1) | collective-permute-done | bytes 196640 | tf_op jit(solution)/shard_map/ppermute | solution.py:39
  23.1 12.2 %viscosity_inner.2.refs_6_ = f32[32,64,512]{2,1,0:T(8,128)S(1)} custom-call(f32[3,32,64,512]{3,2,1,0:T(8,128)} %refs_0_.5, f32[3,32,1,512]{3,2,1,0:T(1,128)S(1)} %collective-permute-done.before_ref.refs_1_.flow_before, f32[3,32,1,512]{3,2,1,0:T(1,128)S(1)} %collective-permute-done.1.after_ref.refs_2_.flow_after, f32[32,64,512]{2,1,0:T(8,128)} %refs_3_.3), custom_call_target="tpu_custom_call" | custom-call | tf_op jit(solution)/shard_map/viscosity_inner/pallas_call | solution.py:317
  37.9 4.8 %collective-permute-start.7 = (f32[1,64,512]{2,1,0:T(8,128)S(1)}, f32[1,64,512]{2,1,0:T(8,128)S(1)}, u32[]{:S(2)}, u32[]{:S(2)}) collective-permute-start(f32[1,64,512]{2,1,0:T(8,128)S(1)} %get-tuple-element.36), channel_id=1, source_target_pairs={{0,28},{4,0},{8,4},{12,8},{16,12},{20,16},{24,20},{28,24},{1,29},{... | collective-permute-start | bytes 393224 | tf_op jit(solution)/shard_map/ppermute | solution.py:39
  47.1 15.1 %advance_inner.2.refs_11_ = f32[3,32,64,512]{3,2,1,0:T(8,128)} custom-call(f32[3,32,64,512]{3,2,1,0:T(8,128)} %refs_0_.5, f32[3,32,1,512]{3,2,1,0:T(1,128)S(1)} %collective-permute-done.before_ref.refs_1_.flow_before, f32[3,32,1,512]{3,2,1,0:T(1,128)S(1)} %collective-permute-done.1.after_ref.refs_2_.flow_after, ...), custom_call_target="tpu_custom_call" | custom-call | tf_op jit(solution)/shard_map/advance_inner/pallas_call | solution.py:537
  67.4 4.0 %collective-permute-start.11 = (f32[3,1,64,512]{3,2,1,0:T(8,128)S(1)}, f32[3,1,64,512]{3,2,1,0:T(8,128)S(1)}, u32[]{:S(2)}, u32[]{:S(2)}) collective-permute-start(f32[3,1,64,512]{3,2,1,0:T(8,128)S(1)} %get-tuple-element.22), channel_id=1, source_target_pairs={{0,28},{4,0},{8,4},{12,8},{16,12},{20,16},{24,20},{28,24},{1,29},{... | collective-permute-start | bytes 1179656 | tf_op jit(solution)/shard_map/ppermute | solution.py:39
  75.8 5.2 %collective-permute-done.9.after_ref.refs_2_ = f32[3,32,1,512]{3,2,1,0:T(1,128)S(1)} collective-permute-done((f32[3,32,1,512]{3,2,1,0:T(1,128)S(1)}, f32[3,32,1,512]{3,2,1,0:T(1,128)S(1)}, u32[]{:S(2)}, u32[]{:S(2)}) %collective-permute-start.9) | collective-permute-done | bytes 196640 | tf_op jit(solution)/shard_map/ppermute | solution.py:39
  81.0 13.5 %viscosity_inner.3 = (f32[32,64,512]{2,1,0:T(8,128)S(1)}, f32[4,32,64,128]{3,2,1,0:T(8,128)}) custom-call(f32[3,32,64,512]{3,2,1,0:T(8,128)} %advance_edge.2.flow_ref.refs_0_, f32[3,32,1,512]{3,2,1,0:T(1,128)S(1)} %collective-permute-done.8.before_ref.refs_1_, f32[3,32,1,512]{3,2,1,0:T(1,128)S(1)} %collective-permute-done.9.after_ref.refs_2_, ...), custom_call_target="tpu_custom_call" | custom-call | tf_op jit(solution)/shard_map/viscosity_inner/pallas_call | solution.py:317
  97.9 4.6 %collective-permute-start.15 = (f32[1,64,512]{2,1,0:T(8,128)S(1)}, f32[1,64,512]{2,1,0:T(8,128)S(1)}, u32[]{:S(2)}, u32[]{:S(2)}) collective-permute-start(f32[1,64,512]{2,1,0:T(8,128)S(1)} %get-tuple-element.32), channel_id=1, source_target_pairs={{0,28},{4,0},{8,4},{12,8},{16,12},{20,16},{24,20},{28,24},{1,29},{... | collective-permute-start | bytes 393224 | tf_op jit(solution)/shard_map/ppermute | solution.py:39
  106.9 15.1 %advance_inner.3.refs_11_ = f32[3,32,64,512]{3,2,1,0:T(8,128)} custom-call(f32[3,32,64,512]{3,2,1,0:T(8,128)} %refs_0_.5, f32[3,32,1,512]{3,2,1,0:T(1,128)S(1)} %collective-permute-done.before_ref.refs_1_.flow_before, f32[3,32,1,512]{3,2,1,0:T(1,128)S(1)} %collective-permute-done.1.after_ref.refs_2_.flow_after, ...), custom_call_target="tpu_custom_call" | custom-call | tf_op jit(solution)/shard_map/advance_inner/pallas_call | solution.py:537
  127.0 4.1 %collective-permute-start.17 = (f32[1,64,512]{2,1,0:T(8,128)S(1)}, f32[1,64,512]{2,1,0:T(8,128)S(1)}, u32[]{:S(2)}, u32[]{:S(2)}) collective-permute-start(f32[1,64,512]{2,1,0:T(8,128)S(1)} %get-tuple-element.20), channel_id=1, source_target_pairs={{0,28},{4,0},{8,4},{12,8},{16,12},{20,16},{24,20},{28,24},{1,29},{... | collective-permute-start | bytes 393224 | tf_op jit(solution)/shard_map/ppermute | solution.py:39
  134.6 10.3 %divergence_modes.1.modes_ref = f32[4,32,64,128]{3,2,1,0:T(8,128)} custom-call(f32[3,32,64,512]{3,2,1,0:T(8,128)} %advance_edge.3.flow_ref, bf16[256,256]{1,0:T(8,128)(2,1)} %constant.68.clone.even_high, bf16[256,256]{1,0:T(8,128)(2,1)} %constant.69.clone.even_low, bf16[256,256]{1,0:T(8,128)(2,1)} %constant.70.clone.odd_high, ...), custom_call_target="tpu_custom_call" | custom-call | tf_op jit(solution)/shard_map/divergence_modes/pallas_call | solution.py:684
  149.5 6.0 %all-to-all-start = ((f32[4,32,64,128]{3,2,1,0:T(8,128)}), f32[4,32,64,128]{3,2,1,0:T(8,128)}, u32[]{:S(2)}, u32[]{:S(2)}) async-start(f32[4,32,64,128]{3,2,1,0:T(8,128)} %add_halo_modes.1), calls=%async_computation | async-start | bytes 8388608 | tf_op jit(solution)/shard_map/all_to_all | solution.py:1083
  158.6 44.1 %all-to-all-done.in_ref = f32[4,32,64,128]{3,2,1,0:T(8,128)} async-done(((f32[4,32,64,128]{3,2,1,0:T(8,128)}), f32[4,32,64,128]{3,2,1,0:T(8,128)}, u32[]{:S(2)}, u32[]{:S(2)}) %all-to-all-start) | async-done | bytes 4194336 | tf_op jit(solution)/shard_map/all_to_all | solution.py:1083
  202.8 8.5 %y_forward.1 = (f32[32,256,128]{2,1,0:T(8,128)}, f32[8,4,32,128]{3,2,1,0:T(8,128)}) custom-call(f32[4,32,64,128]{3,2,1,0:T(8,128)} %all-to-all-done.in_ref, bf16[256,256]{1,0:T(8,128)(2,1)} %constant.74.clone.high_ref, bf16[256,256]{1,0:T(8,128)(2,1)} %constant.75.clone.low_ref, f32[256,128]{1,0:T(8,128)} %get-tuple-element.57.ratio_ref), custom_call_target="tpu_custom_call" | custom-call | tf_op jit(solution)/shard_map/y_forward/pallas_call | solution.py:935
  211.3 5.7 %all-to-all-start.1 = ((f32[8,4,32,128]{3,2,1,0:T(8,128)}), f32[8,4,32,128]{3,2,1,0:T(8,128)S(1)}, u32[]{:S(2)}, u32[]{:S(2)}) async-start(f32[8,4,32,128]{3,2,1,0:T(8,128)} %get-tuple-element.14), calls=%async_computation.1 | async-start | bytes 1048576 | tf_op jit(solution)/shard_map/all_to_all | solution.py:1083
  217.3 45.7 %scatter_custom_fusion = f32[4096,128]{1,0:T(8,128)} fusion(s32[8192]{0:T(1024)S(1)} %bitcast.41, f32[8192,128]{1,0:T(8,128)} %bitcast.29, f32[]{:T(128)} %constant.21.clone.1), kind=kCustom, calls=%fused_computation.1 | custom fusion | flops 1048576 | bytes 2097664 | tf_op jit(solution)/shard_map/scatter-add | solution.py:1165
  263.8 24.5 %all_to_all.20.carry_ref = f32[8,4,32,128]{3,2,1,0:T(8,128)} all-to-all(f32[8,4,32,128]{3,2,1,0:T(8,128)S(1)} %join_carries.1), channel_id=1, replica_groups=mesh['wide'=8,'narrow'=4] {'wide'}, dimensions={0} | all-to-all | bytes 1048576 | tf_op jit(solution)/shard_map/all_to_all | solution.py:1083
  288.4 9.8 %y_inverse.1 = f32[4,34,64,128]{3,2,1,0:T(8,128)} custom-call(f32[32,256,128]{2,1,0:T(8,128)} %get-tuple-element.13.modes_in, f32[8,4,32,128]{3,2,1,0:T(8,128)} %all_to_all.20.carry_ref, bf16[256,256]{1,0:T(8,128)(2,1)} %constant.76.clone.high_ref, bf16[256,256]{1,0:T(8,128)(2,1)} %constant.77.clone.low_ref, f32[256,128]{1,0:T(8,128)} %get-tuple-element.57.ratio_ref, ...), custom_call_target="tpu_custom_call" | custom-call | tf_op jit(solution)/shard_map/y_inverse/pallas_call | solution.py:1065
  298.2 12.2 %all-to-all-start.3 = ((f32[4,34,64,128]{3,2,1,0:T(8,128)}), f32[4,34,64,128]{3,2,1,0:T(8,128)}, u32[]{:S(2)}, u32[]{:S(2)}) async-start(f32[4,34,64,128]{3,2,1,0:T(8,128)} %y_inverse.1), calls=%async_computation.3 | async-start | bytes 8912896 | tf_op jit(solution)/shard_map/all_to_all | solution.py:1083
  318.6 18.9 %reduce-scatter.2.cloned.1.call-done = f32[1,512,128]{2,1,0:T(8,128)} async-done(((f32[8,512,128]{2,1,0:T(8,128)}), f32[1,512,128]{2,1,0:T(8,128)}) %reduce-scatter.2.cloned.1.call-update) | async-done | bytes 262160 | tf_op jit(solution)/shard_map/reduce_scatter | solution.py:1172
  342.3 5.3 %collective-permute-start.28 = (f32[20,2,128]{2,1,0:T(2,128)S(1)}, f32[20,2,128]{2,1,0:T(2,128)S(1)}, u32[]{:S(2)}, u32[]{:S(2)}) collective-permute-start(f32[20,2,128]{2,1,0:T(2,128)S(1)} %get-tuple-element.50), channel_id=1, source_target_pairs={{0,1},{1,2},{2,3},{4,5},{5,6},{6,7},{8,9},{9,10},{10,11},{12,13},{... | collective-permute-start | bytes 61448 | tf_op jit(solution)/shard_map/ppermute | solution.py:31
  355.1 5.4 %all-to-all-done.3.in_ref = f32[4,34,64,128]{3,2,1,0:T(8,128)} async-done(((f32[4,34,64,128]{3,2,1,0:T(8,128)}), f32[4,34,64,128]{3,2,1,0:T(8,128)}, u32[]{:S(2)}, u32[]{:S(2)}) %all-to-all-start.3) | async-done | bytes 4456480 | tf_op jit(solution)/shard_map/all_to_all | solution.py:1083
  366.8 11.0 %corrected.1 = f32[3,32,64,512]{3,2,1,0:T(8,128)} custom-call(f32[3,32,64,512]{3,2,1,0:T(8,128)} %advance_edge.3.flow_ref, f32[4,34,64,128]{3,2,1,0:T(8,128)} %all-to-all-done.3.in_ref, f32[4,32,128]{2,1,0:T(8,128)S(1)} %bitcast.26, f32[4,32,128]{2,1,0:T(8,128)S(1)} %bitcast.27, bf16[256,256]{1,0:T(8,128)(2,1)S(1)} %copy-done.3, ...), custom_call_target="tpu_custom_call" | custom-call | tf_op jit(solution)/shard_map/corrected/pallas_call | solution.py:863
  (125 shorter events, 73.6 us)
Async XLA Ops:
  8.4 26.9 %collective-permute-start.3 = (f32[3,1,64,512]{3,2,1,0:T(8,128)S(1)}, f32[3,1,64,512]{3,2,1,0:T(8,128)S(1)}, u32[]{:S(2)}, u32[]{:S(2)}) collective-permute-start(f32[3,1,64,512]{3,2,1,0:T(8,128)S(1)} %get-tuple-element.26), channel_id=1, source_target_pairs={{0,28},{4,0},{8,4},{12,8},{16,12},{20,16},{24,20},{28,24},{1,29},{... | collective-permute-start | bytes 1179656 | tf_op jit(solution)/shard_map/ppermute | solution.py:39
  13.5 21.7 %collective-permute-start.2 = (f32[3,1,64,512]{3,2,1,0:T(8,128)S(1)}, f32[3,1,64,512]{3,2,1,0:T(8,128)S(1)}, u32[]{:S(2)}, u32[]{:S(2)}) collective-permute-start(f32[3,1,64,512]{3,2,1,0:T(8,128)S(1)} %get-tuple-element.27), channel_id=1, source_target_pairs={{0,4},{4,8},{8,12},{12,16},{16,20},{20,24},{24,28},{28,0},{1,5},{5... | collective-permute-start | bytes 1179656 | tf_op jit(solution)/shard_map/ppermute | solution.py:39
  15.8 7.3 %collective-permute-start.1 = (f32[3,32,1,512]{3,2,1,0:T(1,128)S(1)}, f32[3,32,1,512]{3,2,1,0:T(1,128)S(1)}, u32[]{:S(2)}, u32[]{:S(2)}) collective-permute-start(f32[3,32,1,512]{3,2,1,0:T(1,128)S(1)} %get-tuple-element.28), channel_id=1, source_target_pairs={{0,3},{1,0},{2,1},{3,2},{4,7},{5,4},{6,5},{7,6},{8,11},{9,8},{10,9... | collective-permute-start | bytes 589832 | tf_op jit(solution)/shard_map/ppermute | solution.py:39
  37.9 24.3 %collective-permute-start.7 = (f32[1,64,512]{2,1,0:T(8,128)S(1)}, f32[1,64,512]{2,1,0:T(8,128)S(1)}, u32[]{:S(2)}, u32[]{:S(2)}) collective-permute-start(f32[1,64,512]{2,1,0:T(8,128)S(1)} %get-tuple-element.36), channel_id=1, source_target_pairs={{0,28},{4,0},{8,4},{12,8},{16,12},{20,16},{24,20},{28,24},{1,29},{... | collective-permute-start | bytes 393224 | tf_op jit(solution)/shard_map/ppermute | solution.py:39
  42.6 19.6 %collective-permute-start.6 = (f32[1,64,512]{2,1,0:T(8,128)S(1)}, f32[1,64,512]{2,1,0:T(8,128)S(1)}, u32[]{:S(2)}, u32[]{:S(2)}) collective-permute-start(f32[1,64,512]{2,1,0:T(8,128)S(1)} %get-tuple-element.37), channel_id=1, source_target_pairs={{0,4},{4,8},{8,12},{12,16},{16,20},{20,24},{24,28},{28,0},{1,5},{5... | collective-permute-start | bytes 393224 | tf_op jit(solution)/shard_map/ppermute | solution.py:39
  67.4 27.2 %collective-permute-start.11 = (f32[3,1,64,512]{3,2,1,0:T(8,128)S(1)}, f32[3,1,64,512]{3,2,1,0:T(8,128)S(1)}, u32[]{:S(2)}, u32[]{:S(2)}) collective-permute-start(f32[3,1,64,512]{3,2,1,0:T(8,128)S(1)} %get-tuple-element.22), channel_id=1, source_target_pairs={{0,28},{4,0},{8,4},{12,8},{16,12},{20,16},{24,20},{28,24},{1,29},{... | collective-permute-start | bytes 1179656 | tf_op jit(solution)/shard_map/ppermute | solution.py:39
  71.4 23.1 %collective-permute-start.10 = (f32[3,1,64,512]{3,2,1,0:T(8,128)S(1)}, f32[3,1,64,512]{3,2,1,0:T(8,128)S(1)}, u32[]{:S(2)}, u32[]{:S(2)}) collective-permute-start(f32[3,1,64,512]{3,2,1,0:T(8,128)S(1)} %get-tuple-element.23), channel_id=1, source_target_pairs={{0,4},{4,8},{8,12},{12,16},{16,20},{20,24},{24,28},{28,0},{1,5},{5... | collective-permute-start | bytes 1179656 | tf_op jit(solution)/shard_map/ppermute | solution.py:39
  73.7 7.3 %collective-permute-start.9 = (f32[3,32,1,512]{3,2,1,0:T(1,128)S(1)}, f32[3,32,1,512]{3,2,1,0:T(1,128)S(1)}, u32[]{:S(2)}, u32[]{:S(2)}) collective-permute-start(f32[3,32,1,512]{3,2,1,0:T(1,128)S(1)} %get-tuple-element.24), channel_id=1, source_target_pairs={{0,3},{1,0},{2,1},{3,2},{4,7},{5,4},{6,5},{7,6},{8,11},{9,8},{10,9... | collective-permute-start | bytes 589832 | tf_op jit(solution)/shard_map/ppermute | solution.py:39
  97.9 24.1 %collective-permute-start.15 = (f32[1,64,512]{2,1,0:T(8,128)S(1)}, f32[1,64,512]{2,1,0:T(8,128)S(1)}, u32[]{:S(2)}, u32[]{:S(2)}) collective-permute-start(f32[1,64,512]{2,1,0:T(8,128)S(1)} %get-tuple-element.32), channel_id=1, source_target_pairs={{0,28},{4,0},{8,4},{12,8},{16,12},{20,16},{24,20},{28,24},{1,29},{... | collective-permute-start | bytes 393224 | tf_op jit(solution)/shard_map/ppermute | solution.py:39
  102.5 19.5 %collective-permute-start.14 = (f32[1,64,512]{2,1,0:T(8,128)S(1)}, f32[1,64,512]{2,1,0:T(8,128)S(1)}, u32[]{:S(2)}, u32[]{:S(2)}) collective-permute-start(f32[1,64,512]{2,1,0:T(8,128)S(1)} %get-tuple-element.33), channel_id=1, source_target_pairs={{0,4},{4,8},{8,12},{12,16},{16,20},{20,24},{24,28},{28,0},{1,5},{5... | collective-permute-start | bytes 393224 | tf_op jit(solution)/shard_map/ppermute | solution.py:39
  127.0 17.9 %collective-permute-start.17 = (f32[1,64,512]{2,1,0:T(8,128)S(1)}, f32[1,64,512]{2,1,0:T(8,128)S(1)}, u32[]{:S(2)}, u32[]{:S(2)}) collective-permute-start(f32[1,64,512]{2,1,0:T(8,128)S(1)} %get-tuple-element.20), channel_id=1, source_target_pairs={{0,28},{4,0},{8,4},{12,8},{16,12},{20,16},{24,20},{28,24},{1,29},{... | collective-permute-start | bytes 393224 | tf_op jit(solution)/shard_map/ppermute | solution.py:39
  131.1 13.8 %collective-permute-start.16 = (f32[1,64,512]{2,1,0:T(8,128)S(1)}, f32[1,64,512]{2,1,0:T(8,128)S(1)}, u32[]{:S(2)}, u32[]{:S(2)}) collective-permute-start(f32[1,64,512]{2,1,0:T(8,128)S(1)} %get-tuple-element.21), channel_id=1, source_target_pairs={{0,4},{4,8},{8,12},{12,16},{16,20},{20,24},{24,28},{28,0},{1,5},{5... | collective-permute-start | bytes 393224 | tf_op jit(solution)/shard_map/ppermute | solution.py:39
  132.5 12.4 %collective-permute-start.18 = (f32[32,1,512]{2,0,1:T(8,128)S(1)}, f32[32,1,512]{2,0,1:T(8,128)S(1)}, u32[]{:S(2)}, u32[]{:S(2)}) collective-permute-start(f32[32,1,512]{2,0,1:T(8,128)S(1)} %bitcast.38), channel_id=1, source_target_pairs={{0,1},{1,2},{2,3},{3,0},{4,5},{5,6},{6,7},{7,4},{8,9},{9,10},{10,1... | collective-permute-start | bytes 196616 | tf_op jit(solution)/shard_map/ppermute | solution.py:39
  134.6 10.4 %collective-permute-start.19 = (f32[32,1,512]{2,0,1:T(8,128)S(1)}, f32[32,1,512]{2,0,1:T(8,128)S(1)}, u32[]{:S(2)}, u32[]{:S(2)}) collective-permute-start(f32[32,1,512]{2,0,1:T(8,128)S(1)} %bitcast.37), channel_id=1, source_target_pairs={{0,3},{1,0},{2,1},{3,2},{4,7},{5,4},{6,5},{7,6},{8,11},{9,8},{10,9... | collective-permute-start | bytes 196616 | tf_op jit(solution)/shard_map/ppermute | solution.py:39
  149.5 53.3 %all-to-all-start = ((f32[4,32,64,128]{3,2,1,0:T(8,128)}), f32[4,32,64,128]{3,2,1,0:T(8,128)}, u32[]{:S(2)}, u32[]{:S(2)}) async-start(f32[4,32,64,128]{3,2,1,0:T(8,128)} %add_halo_modes.1), calls=%async_computation | async-start | bytes 8388608 | tf_op jit(solution)/shard_map/all_to_all | solution.py:1083
  211.3 51.7 %all-to-all-start.1 = ((f32[8,4,32,128]{3,2,1,0:T(8,128)}), f32[8,4,32,128]{3,2,1,0:T(8,128)S(1)}, u32[]{:S(2)}, u32[]{:S(2)}) async-start(f32[8,4,32,128]{3,2,1,0:T(8,128)} %get-tuple-element.14), calls=%async_computation.1 | async-start | bytes 1048576 | tf_op jit(solution)/shard_map/all_to_all | solution.py:1083
  217.0 120.5 %reduce-scatter.2.cloned.1.call-start = ((), (), s32[]{:S(2)}) async-start(), calls=%async_computation.5 | async-start | bytes 2359296 | tf_op jit(solution)/shard_map/reduce_scatter | solution.py:1172
  298.2 62.3 %all-to-all-start.3 = ((f32[4,34,64,128]{3,2,1,0:T(8,128)}), f32[4,34,64,128]{3,2,1,0:T(8,128)}, u32[]{:S(2)}, u32[]{:S(2)}) async-start(f32[4,34,64,128]{3,2,1,0:T(8,128)} %y_inverse.1), calls=%async_computation.3 | async-start | bytes 8912896 | tf_op jit(solution)/shard_map/all_to_all | solution.py:1083
  338.6 10.9 %collective-permute-start.22 = (f32[3,32,128]{2,1,0:T(8,128)S(1)}, f32[3,32,128]{2,1,0:T(8,128)S(1)}, u32[]{:S(2)}, u32[]{:S(2)}) collective-permute-start(f32[3,32,128]{2,1,0:T(8,128)S(1)} %get-tuple-element.54), channel_id=1, source_target_pairs={{0,4},{4,8},{8,12},{12,16},{16,20},{20,24},{24,28},{1,5},{5,9},{9,... | collective-permute-start | bytes 147464 | tf_op jit(solution)/shard_map/ppermute | solution.py:31
  340.9 8.6 %collective-permute-start.23 = (f32[3,32,128]{2,1,0:T(8,128)S(1)}, f32[3,32,128]{2,1,0:T(8,128)S(1)}, u32[]{:S(2)}, u32[]{:S(2)}) collective-permute-start(f32[3,32,128]{2,1,0:T(8,128)S(1)} %get-tuple-element.55), channel_id=1, source_target_pairs={{4,0},{8,4},{12,8},{16,12},{20,16},{24,20},{28,24},{5,1},{9,5},{13... | collective-permute-start | bytes 147464 | tf_op jit(solution)/shard_map/ppermute | solution.py:32
  342.3 21.0 %collective-permute-start.28 = (f32[20,2,128]{2,1,0:T(2,128)S(1)}, f32[20,2,128]{2,1,0:T(2,128)S(1)}, u32[]{:S(2)}, u32[]{:S(2)}) collective-permute-start(f32[20,2,128]{2,1,0:T(2,128)S(1)} %get-tuple-element.50), channel_id=1, source_target_pairs={{0,1},{1,2},{2,3},{4,5},{5,6},{6,7},{8,9},{9,10},{10,11},{12,13},{... | collective-permute-start | bytes 61448 | tf_op jit(solution)/shard_map/ppermute | solution.py:31
  347.6 15.7 %collective-permute-start.29 = (f32[20,2,128]{2,1,0:T(2,128)S(1)}, f32[20,2,128]{2,1,0:T(2,128)S(1)}, u32[]{:S(2)}, u32[]{:S(2)}) collective-permute-start(f32[20,2,128]{2,1,0:T(2,128)S(1)} %get-tuple-element.51), channel_id=1, source_target_pairs={{1,0},{2,1},{3,2},{5,4},{6,5},{7,6},{9,8},{10,9},{11,10},{13,12},{... | collective-permute-start | bytes 61448 | tf_op jit(solution)/shard_map/ppermute | solution.py:32
  349.5 13.5 %collective-permute-start.24 = (f32[22,3,128]{2,1,0:T(4,128)S(1)}, f32[22,3,128]{2,1,0:T(4,128)S(1)}, u32[]{:S(2)}, u32[]{:S(2)}) collective-permute-start(f32[22,3,128]{2,1,0:T(4,128)S(1)} %get-tuple-element.48), channel_id=1, source_target_pairs={{0,1},{1,2},{2,3},{4,5},{5,6},{6,7},{8,9},{9,10},{10,11},{12,13},{... | collective-permute-start | bytes 101384 | tf_op jit(solution)/shard_map/ppermute | solution.py:31
  353.2 9.9 %collective-permute-start.25 = (f32[22,3,128]{2,1,0:T(4,128)S(1)}, f32[22,3,128]{2,1,0:T(4,128)S(1)}, u32[]{:S(2)}, u32[]{:S(2)}) collective-permute-start(f32[22,3,128]{2,1,0:T(4,128)S(1)} %get-tuple-element.49), channel_id=1, source_target_pairs={{1,0},{2,1},{3,2},{5,4},{6,5},{7,6},{9,8},{10,9},{11,10},{13,12},{... | collective-permute-start | bytes 101384 | tf_op jit(solution)/shard_map/ppermute | solution.py:32
  (23 other events, 131.9 us)
Sparse Core Ops, SparseCore 0:
  263.1 74.3 reduce-scatter.1

commit v10 on v8

--- a/solution.py
+++ b/solution.py
@@ -795,7 +795,6 @@
         even_high, even_low, odd_high, odd_low, out_ref,
         modes, mode_sem, pressure, sides, work, flow_sem, out_sem,
     ):
-        flow_planes = Planes(flow_ref, work, flow_sem)
         table_refs = (even_high, even_low, odd_high, odd_low)
 
         def load(k):
@@ -805,11 +804,12 @@
         load(0).start()
         load(1).start()
 
-        def begin(i, state):
-            flow_planes.start(i)
-            return state
-
-        lax.fori_loop(0, x_local, begin, 0)
+        def brought(k):
+            span = pl.ds(k * (part - 2), part - 2 if k == 0 else x_local + 2 - part)
+            return pltpu.make_async_copy(flow_ref.at[:, span], work.at[:, span], flow_sem.at[k])
+
+        brought(0).start()
+        brought(1).start()
         sides[...] = cells_of(
             jnp.concatenate(
                 [
@@ -826,7 +826,6 @@
             return pltpu.make_async_copy(pick(work, i), pick(out_ref, i), out_sem.at[i])
 
         def plane(j, state):
-            flow_planes.wait(j)
             values = [pressure[j + 1, rows_of(s), :] for s in range(strips)]
             up = [pltpu.roll(v, 7, 0) for v in values]
             down = [pltpu.roll(v, 1, 0) for v in values]
@@ -852,6 +851,7 @@
                 ),
                 *table_refs,
             ).reshape(part, y_local, z_cells)
+            brought(k).wait()
             lax.fori_loop(k * (part - 2), (part - 2) if k == 0 else x_local, plane, 0)
 
         def finish(i, state):
@@ -871,7 +871,7 @@
             pltpu.VMEM((planes, y_local, z_cells), jnp.float32),
             pltpu.VMEM((2 * x_local, z_cells), jnp.float32),
             pltpu.VMEM(flow.shape, jnp.float32),
-            pltpu.SemaphoreType.DMA((x_local,)),
+            pltpu.SemaphoreType.DMA((2,)),
             pltpu.SemaphoreType.DMA((x_local,)),
         ],
         compiler_params=pltpu.CompilerParams(vmem_limit_bytes=vmem_limit),

time: 350 us -> 350 us (level)
  no operation moved by 1% of the time
where the time goes in v10:
time: 350 us; the launch traced here: 349 us
  Pallas kernels  114 us (33%)
  waiting for transfers between devices  71.8 us (21%)
  starting transfers between devices  67.6 us (19%)
  other arithmetic  49.2 us (14%)
  blocking collectives  17.3 us (5%)
  local copies, waits for them, and re-layouts  15 us (4%)
  between operations  14.8 us (4%)
    scatter-add x1, other arithmetic, device_step(): partial_value = jnp.zeros((slab_count * component_lines, 128), jnp.float3...  45.8 us
    ppermute x22, starting transfers between devices, shift(): lax.ppermute(value, axis, [(i, (i + by) % size) for i in range(size)])  30.2 us
    pallas_call x2, Pallas kernels, advance_inner(): pl.pallas_call(kernel, in_specs=[anywhere, in_vmem, in_vmem, in_vmem, in_...  30.2 us
    pallas_call x2, Pallas kernels, viscosity_inner(): pl.pallas_call(kernel, in_specs=[anywhere, in_vmem, in_vmem, anywhere], o...  25.7 us
    all_to_all x3, waiting for transfers between devices, turn(): return lax.all_to_all(value, axis, split_axis=0, concat_axis=0, tiled=True)  23.1 us
    ppermute x4, waiting for transfers between devices, with_halo(): before = lax.ppermute(last, axis, up)  21.5 us
    ppermute x22, waiting for transfers between devices, shift(): lax.ppermute(value, axis, [(i, (i + by) % size) for i in range(size)])  21.2 us
    all_to_all x1, blocking collectives, turn(): return lax.all_to_all(value, axis, split_axis=0, concat_axis=0, tiled=True)  17.3 us
  transfers between devices with their start and end apart: 34, of which 14 were waited for; matrix products, arithmetic and copies ran while one was open for 17% of the time, Pallas kernels for 24%

profile of v10, /device:TPU:1, one launch (start us, length us, event | category | flops | bytes accessed | tf_op | source)
XLA Modules:
  0.0 349.3 jit_solution(12678657348331192421)
XLA Ops:
  18.1 4.0 %collective-permute-done.before_ref.refs_1_.flow_before = f32[3,32,1,512]{3,2,1,0:T(1,128)S(1)} collective-permute-done((f32[3,32,1,512]{3,2,1,0:T(1,128)S(1)}, f32[3,32,1,512]{3,2,1,0:T(1,128)S(1)}, u32[]{:S(2)}, u32[]{:S(2)}) %collective-permute-start) | collective-permute-done | bytes 196640 | tf_op jit(solution)/shard_map/ppermute | solution.py:39
  23.7 12.2 %viscosity_inner.2.refs_6_ = f32[32,64,512]{2,1,0:T(8,128)S(1)} custom-call(f32[3,32,64,512]{3,2,1,0:T(8,128)} %refs_0_.5, f32[3,32,1,512]{3,2,1,0:T(1,128)S(1)} %collective-permute-done.before_ref.refs_1_.flow_before, f32[3,32,1,512]{3,2,1,0:T(1,128)S(1)} %collective-permute-done.1.after_ref.refs_2_.flow_after, f32[32,64,512]{2,1,0:T(8,128)} %refs_3_.3), custom_call_target="tpu_custom_call" | custom-call | tf_op jit(solution)/shard_map/viscosity_inner/pallas_call | solution.py:317
  38.6 4.1 %collective-permute-start.7 = (f32[1,64,512]{2,1,0:T(8,128)S(1)}, f32[1,64,512]{2,1,0:T(8,128)S(1)}, u32[]{:S(2)}, u32[]{:S(2)}) collective-permute-start(f32[1,64,512]{2,1,0:T(8,128)S(1)} %get-tuple-element.32), channel_id=1, source_target_pairs={{0,28},{4,0},{8,4},{12,8},{16,12},{20,16},{24,20},{28,24},{1,29},{... | collective-permute-start | bytes 393224 | tf_op jit(solution)/shard_map/ppermute | solution.py:39
  48.0 15.1 %advance_inner.2.refs_11_ = f32[3,32,64,512]{3,2,1,0:T(8,128)} custom-call(f32[3,32,64,512]{3,2,1,0:T(8,128)} %refs_0_.5, f32[3,32,1,512]{3,2,1,0:T(1,128)S(1)} %collective-permute-done.before_ref.refs_1_.flow_before, f32[3,32,1,512]{3,2,1,0:T(1,128)S(1)} %collective-permute-done.1.after_ref.refs_2_.flow_after, ...), custom_call_target="tpu_custom_call" | custom-call | tf_op jit(solution)/shard_map/advance_inner/pallas_call | solution.py:537
  68.3 4.1 %collective-permute-start.11 = (f32[3,1,64,512]{3,2,1,0:T(8,128)S(1)}, f32[3,1,64,512]{3,2,1,0:T(8,128)S(1)}, u32[]{:S(2)}, u32[]{:S(2)}) collective-permute-start(f32[3,1,64,512]{3,2,1,0:T(8,128)S(1)} %get-tuple-element.18), channel_id=1, source_target_pairs={{0,28},{4,0},{8,4},{12,8},{16,12},{20,16},{24,20},{28,24},{1,29},{... | collective-permute-start | bytes 1179656 | tf_op jit(solution)/shard_map/ppermute | solution.py:39
  75.5 4.3 %collective-permute-done.8.before_ref.refs_1_ = f32[3,32,1,512]{3,2,1,0:T(1,128)S(1)} collective-permute-done((f32[3,32,1,512]{3,2,1,0:T(1,128)S(1)}, f32[3,32,1,512]{3,2,1,0:T(1,128)S(1)}, u32[]{:S(2)}, u32[]{:S(2)}) %collective-permute-start.8) | collective-permute-done | bytes 196640 | tf_op jit(solution)/shard_map/ppermute | solution.py:39
  80.9 13.5 %viscosity_inner.3 = (f32[32,64,512]{2,1,0:T(8,128)S(1)}, f32[4,32,64,128]{3,2,1,0:T(8,128)}) custom-call(f32[3,32,64,512]{3,2,1,0:T(8,128)} %advance_edge.2.flow_ref.refs_0_, f32[3,32,1,512]{3,2,1,0:T(1,128)S(1)} %collective-permute-done.8.before_ref.refs_1_, f32[3,32,1,512]{3,2,1,0:T(1,128)S(1)} %collective-permute-done.9.after_ref.refs_2_, ...), custom_call_target="tpu_custom_call" | custom-call | tf_op jit(solution)/shard_map/viscosity_inner/pallas_call | solution.py:317
  97.8 4.1 %collective-permute-start.15 = (f32[1,64,512]{2,1,0:T(8,128)S(1)}, f32[1,64,512]{2,1,0:T(8,128)S(1)}, u32[]{:S(2)}, u32[]{:S(2)}) collective-permute-start(f32[1,64,512]{2,1,0:T(8,128)S(1)} %get-tuple-element.28), channel_id=1, source_target_pairs={{0,28},{4,0},{8,4},{12,8},{16,12},{20,16},{24,20},{28,24},{1,29},{... | collective-permute-start | bytes 393224 | tf_op jit(solution)/shard_map/ppermute | solution.py:39
  107.8 15.1 %advance_inner.3.refs_11_ = f32[3,32,64,512]{3,2,1,0:T(8,128)} custom-call(f32[3,32,64,512]{3,2,1,0:T(8,128)} %refs_0_.5, f32[3,32,1,512]{3,2,1,0:T(1,128)S(1)} %collective-permute-done.before_ref.refs_1_.flow_before, f32[3,32,1,512]{3,2,1,0:T(1,128)S(1)} %collective-permute-done.1.after_ref.refs_2_.flow_after, ...), custom_call_target="tpu_custom_call" | custom-call | tf_op jit(solution)/shard_map/advance_inner/pallas_call | solution.py:537
  122.9 4.0 %advance_edge.3.flow_ref = f32[3,32,64,512]{3,2,1,0:T(8,128)} custom-call(f32[3,32,64,512]{3,2,1,0:T(8,128)} %refs_0_.5, f32[3,32,1,512]{3,2,1,0:T(1,128)S(1)} %collective-permute-done.before_ref.refs_1_.flow_before, f32[3,32,1,512]{3,2,1,0:T(1,128)S(1)} %collective-permute-done.1.after_ref.refs_2_.flow_after, ...), custom_call_target="tpu_custom_call", output_to_operand_aliasing={{}: (11, {})} | custom-call | tf_op jit(solution)/shard_map/advance_edge/pallas_call | solution.py:479
  127.9 4.1 %collective-permute-start.17 = (f32[1,64,512]{2,1,0:T(8,128)S(1)}, f32[1,64,512]{2,1,0:T(8,128)S(1)}, u32[]{:S(2)}, u32[]{:S(2)}) collective-permute-start(f32[1,64,512]{2,1,0:T(8,128)S(1)} %get-tuple-element.16), channel_id=1, source_target_pairs={{0,28},{4,0},{8,4},{12,8},{16,12},{20,16},{24,20},{28,24},{1,29},{... | collective-permute-start | bytes 393224 | tf_op jit(solution)/shard_map/ppermute | solution.py:39
  134.5 10.3 %divergence_modes.1.modes_ref = f32[4,32,64,128]{3,2,1,0:T(8,128)} custom-call(f32[3,32,64,512]{3,2,1,0:T(8,128)} %advance_edge.3.flow_ref, bf16[256,256]{1,0:T(8,128)(2,1)} %constant.68.clone.even_high, bf16[256,256]{1,0:T(8,128)(2,1)} %constant.69.clone.even_low, bf16[256,256]{1,0:T(8,128)(2,1)} %constant.70.clone.odd_high, ...), custom_call_target="tpu_custom_call" | custom-call | tf_op jit(solution)/shard_map/divergence_modes/pallas_call | solution.py:684
  149.4 4.9 %all-to-all-start = ((f32[4,32,64,128]{3,2,1,0:T(8,128)}), f32[4,32,64,128]{3,2,1,0:T(8,128)}, u32[]{:S(2)}, u32[]{:S(2)}) async-start(f32[4,32,64,128]{3,2,1,0:T(8,128)} %add_halo_modes.1), calls=%async_computation | async-start | bytes 8388608 | tf_op jit(solution)/shard_map/all_to_all | solution.py:1083
  156.1 45.8 %scatter_custom_fusion = f32[4096,128]{1,0:T(8,128)} fusion(s32[8192]{0:T(1024)S(1)} %bitcast.41, f32[8192,128]{1,0:T(8,128)} %bitcast.29, f32[]{:T(128)} %constant.26.clone.1), kind=kCustom, calls=%fused_computation.1 | custom fusion | flops 1048576 | bytes 2097664 | tf_op jit(solution)/shard_map/scatter-add | solution.py:1168
  203.5 8.5 %y_forward.1 = (f32[32,256,128]{2,1,0:T(8,128)}, f32[8,4,32,128]{3,2,1,0:T(8,128)}) custom-call(f32[4,32,64,128]{3,2,1,0:T(8,128)} %all-to-all-done.in_ref, bf16[256,256]{1,0:T(8,128)(2,1)} %constant.74.clone.high_ref, bf16[256,256]{1,0:T(8,128)(2,1)} %constant.75.clone.low_ref, f32[256,128]{1,0:T(8,128)} %get-tuple-element.53.ratio_ref), custom_call_target="tpu_custom_call" | custom-call | tf_op jit(solution)/shard_map/y_forward/pallas_call | solution.py:935
  216.2 23.1 %all-to-all-done.1.in_ref = f32[8,4,32,128]{3,2,1,0:T(8,128)S(1)} async-done(((f32[8,4,32,128]{3,2,1,0:T(8,128)}), f32[8,4,32,128]{3,2,1,0:T(8,128)S(1)}, u32[]{:S(2)}, u32[]{:S(2)}) %all-to-all-start.1) | async-done | bytes 524320 | tf_op jit(solution)/shard_map/all_to_all | solution.py:1083
  239.5 17.3 %all_to_all.20.carry_ref = f32[8,4,32,128]{3,2,1,0:T(8,128)} all-to-all(f32[8,4,32,128]{3,2,1,0:T(8,128)S(1)} %join_carries.1), channel_id=1, replica_groups=mesh['wide'=8,'narrow'=4] {'wide'}, dimensions={0} | all-to-all | bytes 1048576 | tf_op jit(solution)/shard_map/all_to_all | solution.py:1083
  256.8 9.7 %y_inverse.1 = f32[4,34,64,128]{3,2,1,0:T(8,128)} custom-call(f32[32,256,128]{2,1,0:T(8,128)} %get-tuple-element.11.modes_in, f32[8,4,32,128]{3,2,1,0:T(8,128)} %all_to_all.20.carry_ref, bf16[256,256]{1,0:T(8,128)(2,1)} %constant.76.clone.high_ref, bf16[256,256]{1,0:T(8,128)(2,1)} %constant.77.clone.low_ref, f32[256,128]{1,0:T(8,128)} %get-tuple-element.53.ratio_ref, ...), custom_call_target="tpu_custom_call" | custom-call | tf_op jit(solution)/shard_map/y_inverse/pallas_call | solution.py:1065
  266.5 6.8 %all-to-all-start.3 = ((f32[4,34,64,128]{3,2,1,0:T(8,128)}), f32[4,34,64,128]{3,2,1,0:T(8,128)}, u32[]{:S(2)}, u32[]{:S(2)}) async-start(f32[4,34,64,128]{3,2,1,0:T(8,128)} %y_inverse.1), calls=%async_computation.3 | async-start | bytes 8912896 | tf_op jit(solution)/shard_map/all_to_all | solution.py:1083
  278.8 4.0 %collective-permute-start.22 = (f32[3,32,128]{2,1,0:T(8,128)S(1)}, f32[3,32,128]{2,1,0:T(8,128)S(1)}, u32[]{:S(2)}, u32[]{:S(2)}) collective-permute-start(f32[3,32,128]{2,1,0:T(8,128)S(1)} %get-tuple-element.50), channel_id=1, source_target_pairs={{0,4},{4,8},{8,12},{12,16},{16,20},{20,24},{24,28},{1,5},{5,9},{9,... | collective-permute-start | bytes 147464 | tf_op jit(solution)/shard_map/ppermute | solution.py:31
  284.2 4.2 %collective-permute-done.23 = f32[3,32,128]{2,1,0:T(8,128)S(1)} collective-permute-done((f32[3,32,128]{2,1,0:T(8,128)S(1)}, f32[3,32,128]{2,1,0:T(8,128)S(1)}, u32[]{:S(2)}, u32[]{:S(2)}) %collective-permute-start.23) | collective-permute-done | bytes 49184 | tf_op jit(solution)/shard_map/ppermute | solution.py:32
  288.4 4.9 %collective-permute-start.24 = (f32[22,3,128]{2,1,0:T(4,128)S(1)}, f32[22,3,128]{2,1,0:T(4,128)S(1)}, u32[]{:S(2)}, u32[]{:S(2)}) collective-permute-start(f32[22,3,128]{2,1,0:T(4,128)S(1)} %get-tuple-element.44), channel_id=1, source_target_pairs={{0,1},{1,2},{2,3},{4,5},{5,6},{6,7},{8,9},{9,10},{10,11},{12,13},{... | collective-permute-start | bytes 101384 | tf_op jit(solution)/shard_map/ppermute | solution.py:31
  300.8 21.5 %collective-permute-done.24 = f32[22,3,128]{2,1,0:T(4,128)S(1)} collective-permute-done((f32[22,3,128]{2,1,0:T(4,128)S(1)}, f32[22,3,128]{2,1,0:T(4,128)S(1)}, u32[]{:S(2)}, u32[]{:S(2)}) %collective-permute-start.24) | collective-permute-done | bytes 33824 | tf_op jit(solution)/shard_map/ppermute | solution.py:31
  331.0 11.4 %corrected.1 = f32[3,32,64,512]{3,2,1,0:T(8,128)} custom-call(f32[3,32,64,512]{3,2,1,0:T(8,128)} %advance_edge.3.flow_ref, f32[4,34,64,128]{3,2,1,0:T(8,128)} %all-to-all-done.3.in_ref, f32[4,32,128]{2,1,0:T(8,128)S(1)} %bitcast.26, f32[4,32,128]{2,1,0:T(8,128)S(1)} %bitcast.27, bf16[256,256]{1,0:T(8,128)(2,1)S(1)} %copy-done, ...), custom_call_target="tpu_custom_call" | custom-call | tf_op jit(solution)/shard_map/corrected/pallas_call | solution.py:863
  (125 shorter events, 77.5 us)
Async XLA Ops:
  8.4 27.5 %collective-permute-start.2 = (f32[3,1,64,512]{3,2,1,0:T(8,128)S(1)}, f32[3,1,64,512]{3,2,1,0:T(8,128)S(1)}, u32[]{:S(2)}, u32[]{:S(2)}) collective-permute-start(f32[3,1,64,512]{3,2,1,0:T(8,128)S(1)} %get-tuple-element.23), channel_id=1, source_target_pairs={{0,4},{4,8},{8,12},{12,16},{16,20},{20,24},{24,28},{28,0},{1,5},{5... | collective-permute-start | bytes 1179656 | tf_op jit(solution)/shard_map/ppermute | solution.py:39
  10.5 25.4 %collective-permute-start.3 = (f32[3,1,64,512]{3,2,1,0:T(8,128)S(1)}, f32[3,1,64,512]{3,2,1,0:T(8,128)S(1)}, u32[]{:S(2)}, u32[]{:S(2)}) collective-permute-start(f32[3,1,64,512]{3,2,1,0:T(8,128)S(1)} %get-tuple-element.22), channel_id=1, source_target_pairs={{0,28},{4,0},{8,4},{12,8},{16,12},{20,16},{24,20},{28,24},{1,29},{... | collective-permute-start | bytes 1179656 | tf_op jit(solution)/shard_map/ppermute | solution.py:39
  15.9 6.2 %collective-permute-start = (f32[3,32,1,512]{3,2,1,0:T(1,128)S(1)}, f32[3,32,1,512]{3,2,1,0:T(1,128)S(1)}, u32[]{:S(2)}, u32[]{:S(2)}) collective-permute-start(f32[3,32,1,512]{3,2,1,0:T(1,128)S(1)} %get-tuple-element.25), channel_id=1, source_target_pairs={{0,1},{1,2},{2,3},{3,0},{4,5},{5,6},{6,7},{7,4},{8,9},{9,10},{10,1... | collective-permute-start | bytes 589832 | tf_op jit(solution)/shard_map/ppermute | solution.py:39
  18.1 5.6 %collective-permute-start.1 = (f32[3,32,1,512]{3,2,1,0:T(1,128)S(1)}, f32[3,32,1,512]{3,2,1,0:T(1,128)S(1)}, u32[]{:S(2)}, u32[]{:S(2)}) collective-permute-start(f32[3,32,1,512]{3,2,1,0:T(1,128)S(1)} %get-tuple-element.24), channel_id=1, source_target_pairs={{0,3},{1,0},{2,1},{3,2},{4,7},{5,4},{6,5},{7,6},{8,11},{9,8},{10,9... | collective-permute-start | bytes 589832 | tf_op jit(solution)/shard_map/ppermute | solution.py:39
  38.5 24.6 %collective-permute-start.6 = (f32[1,64,512]{2,1,0:T(8,128)S(1)}, f32[1,64,512]{2,1,0:T(8,128)S(1)}, u32[]{:S(2)}, u32[]{:S(2)}) collective-permute-start(f32[1,64,512]{2,1,0:T(8,128)S(1)} %get-tuple-element.33), channel_id=1, source_target_pairs={{0,4},{4,8},{8,12},{12,16},{16,20},{20,24},{24,28},{28,0},{1,5},{5... | collective-permute-start | bytes 393224 | tf_op jit(solution)/shard_map/ppermute | solution.py:39
  38.6 24.5 %collective-permute-start.7 = (f32[1,64,512]{2,1,0:T(8,128)S(1)}, f32[1,64,512]{2,1,0:T(8,128)S(1)}, u32[]{:S(2)}, u32[]{:S(2)}) collective-permute-start(f32[1,64,512]{2,1,0:T(8,128)S(1)} %get-tuple-element.32), channel_id=1, source_target_pairs={{0,28},{4,0},{8,4},{12,8},{16,12},{20,16},{24,20},{28,24},{1,29},{... | collective-permute-start | bytes 393224 | tf_op jit(solution)/shard_map/ppermute | solution.py:39
  68.3 26.2 %collective-permute-start.10 = (f32[3,1,64,512]{3,2,1,0:T(8,128)S(1)}, f32[3,1,64,512]{3,2,1,0:T(8,128)S(1)}, u32[]{:S(2)}, u32[]{:S(2)}) collective-permute-start(f32[3,1,64,512]{3,2,1,0:T(8,128)S(1)} %get-tuple-element.19), channel_id=1, source_target_pairs={{0,4},{4,8},{8,12},{12,16},{16,20},{20,24},{24,28},{28,0},{1,5},{5... | collective-permute-start | bytes 1179656 | tf_op jit(solution)/shard_map/ppermute | solution.py:39
  68.3 26.1 %collective-permute-start.11 = (f32[3,1,64,512]{3,2,1,0:T(8,128)S(1)}, f32[3,1,64,512]{3,2,1,0:T(8,128)S(1)}, u32[]{:S(2)}, u32[]{:S(2)}) collective-permute-start(f32[3,1,64,512]{3,2,1,0:T(8,128)S(1)} %get-tuple-element.18), channel_id=1, source_target_pairs={{0,28},{4,0},{8,4},{12,8},{16,12},{20,16},{24,20},{28,24},{1,29},{... | collective-permute-start | bytes 1179656 | tf_op jit(solution)/shard_map/ppermute | solution.py:39
  97.8 25.1 %collective-permute-start.14 = (f32[1,64,512]{2,1,0:T(8,128)S(1)}, f32[1,64,512]{2,1,0:T(8,128)S(1)}, u32[]{:S(2)}, u32[]{:S(2)}) collective-permute-start(f32[1,64,512]{2,1,0:T(8,128)S(1)} %get-tuple-element.29), channel_id=1, source_target_pairs={{0,4},{4,8},{8,12},{12,16},{16,20},{20,24},{24,28},{28,0},{1,5},{5... | collective-permute-start | bytes 393224 | tf_op jit(solution)/shard_map/ppermute | solution.py:39
  97.8 25.1 %collective-permute-start.15 = (f32[1,64,512]{2,1,0:T(8,128)S(1)}, f32[1,64,512]{2,1,0:T(8,128)S(1)}, u32[]{:S(2)}, u32[]{:S(2)}) collective-permute-start(f32[1,64,512]{2,1,0:T(8,128)S(1)} %get-tuple-element.28), channel_id=1, source_target_pairs={{0,28},{4,0},{8,4},{12,8},{16,12},{20,16},{24,20},{28,24},{1,29},{... | collective-permute-start | bytes 393224 | tf_op jit(solution)/shard_map/ppermute | solution.py:39
  127.9 17.0 %collective-permute-start.16 = (f32[1,64,512]{2,1,0:T(8,128)S(1)}, f32[1,64,512]{2,1,0:T(8,128)S(1)}, u32[]{:S(2)}, u32[]{:S(2)}) collective-permute-start(f32[1,64,512]{2,1,0:T(8,128)S(1)} %get-tuple-element.17), channel_id=1, source_target_pairs={{0,4},{4,8},{8,12},{12,16},{16,20},{20,24},{24,28},{28,0},{1,5},{5... | collective-permute-start | bytes 393224 | tf_op jit(solution)/shard_map/ppermute | solution.py:39
  127.9 16.9 %collective-permute-start.17 = (f32[1,64,512]{2,1,0:T(8,128)S(1)}, f32[1,64,512]{2,1,0:T(8,128)S(1)}, u32[]{:S(2)}, u32[]{:S(2)}) collective-permute-start(f32[1,64,512]{2,1,0:T(8,128)S(1)} %get-tuple-element.16), channel_id=1, source_target_pairs={{0,28},{4,0},{8,4},{12,8},{16,12},{20,16},{24,20},{28,24},{1,29},{... | collective-permute-start | bytes 393224 | tf_op jit(solution)/shard_map/ppermute | solution.py:39
  133.4 11.4 %collective-permute-start.18 = (f32[32,1,512]{2,0,1:T(8,128)S(1)}, f32[32,1,512]{2,0,1:T(8,128)S(1)}, u32[]{:S(2)}, u32[]{:S(2)}) collective-permute-start(f32[32,1,512]{2,0,1:T(8,128)S(1)} %bitcast.37), channel_id=1, source_target_pairs={{0,1},{1,2},{2,3},{3,0},{4,5},{5,6},{6,7},{7,4},{8,9},{9,10},{10,1... | collective-permute-start | bytes 196616 | tf_op jit(solution)/shard_map/ppermute | solution.py:39
  134.5 10.4 %collective-permute-start.19 = (f32[32,1,512]{2,0,1:T(8,128)S(1)}, f32[32,1,512]{2,0,1:T(8,128)S(1)}, u32[]{:S(2)}, u32[]{:S(2)}) collective-permute-start(f32[32,1,512]{2,0,1:T(8,128)S(1)} %bitcast.38), channel_id=1, source_target_pairs={{0,3},{1,0},{2,1},{3,2},{4,7},{5,4},{6,5},{7,6},{8,11},{9,8},{10,9... | collective-permute-start | bytes 196616 | tf_op jit(solution)/shard_map/ppermute | solution.py:39
  149.4 54.1 %all-to-all-start = ((f32[4,32,64,128]{3,2,1,0:T(8,128)}), f32[4,32,64,128]{3,2,1,0:T(8,128)}, u32[]{:S(2)}, u32[]{:S(2)}) async-start(f32[4,32,64,128]{3,2,1,0:T(8,128)} %add_halo_modes.1), calls=%async_computation | async-start | bytes 8388608 | tf_op jit(solution)/shard_map/all_to_all | solution.py:1083
  154.3 123.5 %reduce-scatter.2.cloned.1.call-start = ((), (), s32[]{:S(2)}) async-start(), calls=%async_computation.5 | async-start | bytes 2359296 | tf_op jit(solution)/shard_map/reduce_scatter | solution.py:1170
  212.0 27.4 %all-to-all-start.1 = ((f32[8,4,32,128]{3,2,1,0:T(8,128)}), f32[8,4,32,128]{3,2,1,0:T(8,128)S(1)}, u32[]{:S(2)}, u32[]{:S(2)}) async-start(f32[8,4,32,128]{3,2,1,0:T(8,128)} %get-tuple-element.12), calls=%async_computation.1 | async-start | bytes 1048576 | tf_op jit(solution)/shard_map/all_to_all | solution.py:1083
  266.5 58.7 %all-to-all-start.3 = ((f32[4,34,64,128]{3,2,1,0:T(8,128)}), f32[4,34,64,128]{3,2,1,0:T(8,128)}, u32[]{:S(2)}, u32[]{:S(2)}) async-start(f32[4,34,64,128]{3,2,1,0:T(8,128)} %y_inverse.1), calls=%async_computation.3 | async-start | bytes 8912896 | tf_op jit(solution)/shard_map/all_to_all | solution.py:1083
  276.4 7.7 %collective-permute-start.27 = (f32[2,32,128]{2,1,0:T(8,128)S(1)}, f32[2,32,128]{2,1,0:T(8,128)S(1)}, u32[]{:S(2)}, u32[]{:S(2)}) collective-permute-start(f32[2,32,128]{2,1,0:T(8,128)S(1)} %get-tuple-element.48), channel_id=1, source_target_pairs={{4,0},{8,4},{12,8},{16,12},{20,16},{24,20},{28,24},{5,1},{9,5},{13... | collective-permute-start | bytes 98312 | tf_op jit(solution)/shard_map/ppermute | solution.py:32
  282.8 5.5 %collective-permute-start.23 = (f32[3,32,128]{2,1,0:T(8,128)S(1)}, f32[3,32,128]{2,1,0:T(8,128)S(1)}, u32[]{:S(2)}, u32[]{:S(2)}) collective-permute-start(f32[3,32,128]{2,1,0:T(8,128)S(1)} %get-tuple-element.51), channel_id=1, source_target_pairs={{4,0},{8,4},{12,8},{16,12},{20,16},{24,20},{28,24},{5,1},{9,5},{13... | collective-permute-start | bytes 147464 | tf_op jit(solution)/shard_map/ppermute | solution.py:32
  288.4 33.9 %collective-permute-start.24 = (f32[22,3,128]{2,1,0:T(4,128)S(1)}, f32[22,3,128]{2,1,0:T(4,128)S(1)}, u32[]{:S(2)}, u32[]{:S(2)}) collective-permute-start(f32[22,3,128]{2,1,0:T(4,128)S(1)} %get-tuple-element.44), channel_id=1, source_target_pairs={{0,1},{1,2},{2,3},{4,5},{5,6},{6,7},{8,9},{9,10},{10,11},{12,13},{... | collective-permute-start | bytes 101384 | tf_op jit(solution)/shard_map/ppermute | solution.py:31
  293.2 30.8 %collective-permute-start.25 = (f32[22,3,128]{2,1,0:T(4,128)S(1)}, f32[22,3,128]{2,1,0:T(4,128)S(1)}, u32[]{:S(2)}, u32[]{:S(2)}) collective-permute-start(f32[22,3,128]{2,1,0:T(4,128)S(1)} %get-tuple-element.45), channel_id=1, source_target_pairs={{1,0},{2,1},{3,2},{5,4},{6,5},{7,6},{9,8},{10,9},{11,10},{13,12},{... | collective-permute-start | bytes 101384 | tf_op jit(solution)/shard_map/ppermute | solution.py:32
  295.2 29.1 %collective-permute-start.28 = (f32[20,2,128]{2,1,0:T(2,128)S(1)}, f32[20,2,128]{2,1,0:T(2,128)S(1)}, u32[]{:S(2)}, u32[]{:S(2)}) collective-permute-start(f32[20,2,128]{2,1,0:T(2,128)S(1)} %get-tuple-element.46), channel_id=1, source_target_pairs={{0,1},{1,2},{2,3},{4,5},{5,6},{6,7},{8,9},{9,10},{10,11},{12,13},{... | collective-permute-start | bytes 61448 | tf_op jit(solution)/shard_map/ppermute | solution.py:31
  298.8 25.5 %collective-permute-start.29 = (f32[20,2,128]{2,1,0:T(2,128)S(1)}, f32[20,2,128]{2,1,0:T(2,128)S(1)}, u32[]{:S(2)}, u32[]{:S(2)}) collective-permute-start(f32[20,2,128]{2,1,0:T(2,128)S(1)} %get-tuple-element.47), channel_id=1, source_target_pairs={{1,0},{2,1},{3,2},{5,4},{6,5},{7,6},{9,8},{10,9},{11,10},{13,12},{... | collective-permute-start | bytes 61448 | tf_op jit(solution)/shard_map/ppermute | solution.py:32
  (23 other events, 145.8 us)
Sparse Core Ops, SparseCore 0:
  202.0 74.5 reduce-scatter.1
